TPU v7x, 128 devices: a whole 4x4x4 slice. The times are simulated.
128 devices in a mesh: dp: 16 (over x, z), mp: 8 (over y, core).
Axes of the slice: x: 4, y: 4, z: 4, core: 2. Of those that a mesh axis runs over, the one named last changes fastest.
Arguments:
- context: bfloat16 [4096, 4096], P('dp', 'mp'), may hold values from -6 to 6
- w_out: bfloat16 [4096, 8192], P('mp'), may hold values from -0.09375 to 0.09375
- residual: bfloat16 [4096, 8192], P('dp', 'mp'), may hold values from -6 to 6
- norm_gain: float32 [8192], P('mp'), may hold values from 0.25 to 1.75
- w_join: bfloat16 [8192, 4096], P('mp'), may hold values from -0.0625 to 0.0625
- dec_state: bfloat16 [6144, 4096], P('dp', 'mp'), may hold values from -6 to 6
- gate_s: float32 [4096], P('mp'), may hold values from -1 to 1
- gate_h: float32 [4096], P('mp'), may hold values from 0.5 to 2
- gate_bias: float32 [4096], P('mp'), may hold values from -1 to 1
- owner: int32 [4096, 1], P('dp'), may hold values from 0 to 15; in each aligned block of 256 rows (0 to 255, 256 to 511, ...) at most 24 rows name the same one
- pad_mask: int32 [4096], P('dp'), may hold values 0 or 1
- cotangent: bfloat16 [6144, 4096], P('dp', 'mp'), may hold values from -6 to 6
Outputs:
- joined: bfloat16 [6144, 4096], P('dp', 'mp')
- state_grad: bfloat16 [6144, 4096], P('dp', 'mp')
- join_grad: float32 [8192, 4096], P('mp', 'dp')
Inputs may be any that keep to these rules, and one draw needn't show every extreme that they name: `owner`: within each shard of 256 tokens no pair group is named more than 24 times, and in some shard one group is named exactly 24 times.
All inputs are finite; a program needn't handle non-finite values. No bound on the sum of `pad_mask` on one device may be relied on, other than what follows from the above.
Results may differ from a plain program's by a relative error of at most 0.02.
Values may be sent and summed in bfloat16 or wider, within the bound.
No kernel may reach another device: no remote copies, remote signals or barrier semaphores. Data moves between devices by JAX's collectives and lax.ppermute only.
A program may use at most 128 MiB of HBM per device.

v0:
```python
import jax
import jax.numpy as jnp
from jax import lax
from jax.sharding import PartitionSpec as P


def owner_slots(owner, n_owner, most):
    target = owner[:, 0]
    onehot = (target[:, None] == jnp.arange(n_owner, dtype=jnp.int32)[None, :]).astype(jnp.int32)
    before = jnp.cumsum(onehot, axis=0) - onehot
    rank = jnp.sum(before * onehot, axis=1)
    return target * most + rank


def body(
    context,
    w_out,
    residual,
    norm_gain,
    w_join,
    dec_state,
    gate_s,
    gate_h,
    gate_bias,
    owner,
    pad_mask,
    cotangent,
):
    n_owner = lax.axis_size("dp")
    width = residual.shape[1]
    term = jnp.dot(context, w_out, preferred_element_type=jnp.float32)
    summed = lax.psum_scatter(
        term.astype(jnp.bfloat16), "mp", scatter_dimension=1, tiled=True
    ).astype(jnp.float32)
    mixed = residual.astype(jnp.float32) + summed
    total = lax.psum(jnp.sum(mixed * mixed, axis=1), "mp")
    full_width = width * lax.axis_size("mp")
    scale = lax.rsqrt(total / full_width + 1e-05)
    normed = (
        mixed * scale[:, None] * norm_gain[None, :] * pad_mask.astype(jnp.float32)[:, None]
    ).astype(jnp.bfloat16)
    slot_rows = dec_state.shape[0]
    most = slot_rows // n_owner
    slots = owner_slots(owner, n_owner, most)
    outgoing = jnp.zeros((slot_rows, width), jnp.bfloat16).at[slots].set(normed)
    arrived = lax.all_to_all(
        outgoing.reshape(n_owner, most, width), "dp", split_axis=0, concat_axis=0, tiled=True
    ).reshape(slot_rows, width)
    join_term = jnp.dot(arrived, w_join, preferred_element_type=jnp.float32)
    hidden = lax.psum_scatter(
        join_term.astype(jnp.bfloat16), "mp", scatter_dimension=1, tiled=True
    ).astype(jnp.float32)
    state = dec_state.astype(jnp.float32)
    gate = jax.nn.sigmoid(gate_s[None, :] * state + gate_h[None, :] * hidden + gate_bias[None, :])
    joined = (state + gate * hidden).astype(jnp.bfloat16)
    outer = cotangent.astype(jnp.float32)
    slope = gate * (1.0 - gate) * hidden
    hidden_grad = (outer * (gate + slope * gate_h[None, :])).astype(jnp.bfloat16)
    state_grad = (outer * (1.0 + slope * gate_s[None, :])).astype(jnp.bfloat16)
    local_grad = lax.dot_general(
        arrived,
        lax.all_gather(hidden_grad, "mp", axis=1, tiled=True),
        (((0,), (0,)), ((), ())),
        preferred_element_type=jnp.float32,
    )
    join_grad = lax.psum_scatter(
        local_grad.astype(jnp.bfloat16), "dp", scatter_dimension=1, tiled=True
    ).astype(jnp.float32)
    return (joined, state_grad, join_grad)


def solution(mesh):
    in_specs = (
        P("dp", "mp"),
        P("mp", None),
        P("dp", "mp"),
        P("mp"),
        P("mp", None),
        P("dp", "mp"),
        P("mp"),
        P("mp"),
        P("mp"),
        P("dp", None),
        P("dp"),
        P("dp", "mp"),
    )
    out_specs = (P("dp", "mp"), P("dp", "mp"), P("mp", "dp"))
    return jax.shard_map(body, mesh=mesh, in_specs=in_specs, out_specs=out_specs, check_vma=False)
```

profile of v0, /device:TPU:0, one launch (start us, length us, event | category | flops | bytes accessed | tf_op | source)
XLA Modules:
  0.0 265.3 jit_solution(11250096342205545324)
XLA Ops:
  7.2 0.0 copy-start
  7.2 0.0 copy-start.9
  7.2 0.0 copy-start.4
  7.2 0.0 copy-start.1
  7.2 0.0 copy-start.5
  7.2 0.0 reduce-scatter.4.cloned.1.call-start
  7.3 0.9 copy-done
  8.1 7.7 %convolution_convert_fusion = bf16[256,8192]{1,0:T(8,128)(2,1)} fusion(bf16[256,512]{1,0:T(8,128)(2,1)S(1)} %copy-done, bf16[512,8192]{1,0:T(8,128)(2,1)} %param.13), kind=kOutput, calls=%fused_computation.1 | convolution fusion | flops 2149580800 | bytes 12845056 | tf_op jit(solution)/shard_map/dot_general | solution.py:31
  15.8 0.0 reduce-scatter.4.cloned.1.call-update
  15.8 0.0 reduce-scatter.6.cloned.1.call-start
  15.9 0.0 copy-done.9
  15.9 0.0 copy-done.4
  15.9 0.6 reduce-window.6
  16.5 0.2 slice_reduce_fusion
  16.7 0.1 fusion.16
  16.8 39.4 %reduce-scatter.4.cloned.1.call-done = bf16[256,1024]{1,0:T(8,128)(2,1)} async-done(((bf16[256,8192]{1,0:T(8,128)(2,1)}), bf16[256,1024]{1,0:T(8,128)(2,1)}) %reduce-scatter.4.cloned.1.call-update) | async-done | bytes 524304 | tf_op jit(solution)/shard_map/reduce_scatter | solution.py:32
  56.2 0.0 copy-done.1
  56.2 1.3 multiply_reduce_fusion
  57.5 13.0 %psum.7 = f32[256]{0:T(256)S(1)} all-reduce(f32[256]{0:T(256)S(1)} %multiply_reduce_fusion), channel_id=1, replica_groups=mesh['dp'=16,'mp'=8] {'mp'}, use_global_device_ids=true, to_apply=%region_5.6 | all-reduce | flops 256 | bytes 2048 | tf_op jit(solution)/shard_map/psum | solution.py:36
  70.5 0.0 copy-done.5
  70.5 2.6 scatter_custom_fusion
  73.1 20.3 %all_to_all.5 = bf16[16,24,1024]{2,1,0:T(8,128)(2,1)S(1)} all-to-all(bf16[16,24,1024]{2,1,0:T(8,128)(2,1)S(1)} %bitcast.32), channel_id=1, replica_groups=mesh['dp'=16,'mp'=8] {'dp'}, dimensions={0} | all-to-all | bytes 1572864 | tf_op jit(solution)/shard_map/all_to_all | solution.py:46
  93.5 0.0 copy-start.2
  93.5 0.0 copy-start.3
  93.5 0.0 copy-start.6
  93.5 0.0 copy-start.7
  93.5 0.0 copy-start.8
  93.5 8.2 %convolution_convert_fusion.2 = bf16[384,4096]{1,0:T(8,128)(2,1)} fusion(bf16[384,1024]{1,0:T(8,128)(2,1)S(1)} %bitcast.33, bf16[1024,4096]{1,0:T(8,128)(2,1)} %param.16), kind=kOutput, calls=%fused_computation.3 | convolution fusion | flops 3222798336 | bytes 12320768 | tf_op jit(solution)/shard_map/dot_general | solution.py:49
  101.7 0.0 reduce-scatter.6.cloned.1.call-update
  101.7 0.0 all-gather.2.cloned.1.call-start
  101.8 31.5 %reduce-scatter.6.cloned.1.call-done = bf16[384,512]{1,0:T(8,128)(2,1)} async-done(((bf16[384,4096]{1,0:T(8,128)(2,1)}), bf16[384,512]{1,0:T(8,128)(2,1)}) %reduce-scatter.6.cloned.1.call-update) | async-done | bytes 393232 | tf_op jit(solution)/shard_map/reduce_scatter | solution.py:50
  133.2 0.0 copy-done.2
  133.2 0.0 copy-done.3
  133.2 0.0 copy-done.6
  133.3 0.0 copy-done.7
  133.3 0.0 copy-done.8
  133.3 2.7 %fusion.8 = (bf16[384,512]{1,0:T(8,128)(2,1)}, bf16[384,512]{1,0:T(8,128)(2,1)}, bf16[384,512]{1,0:T(8,128)(2,1)}) fusion(bf16[384,512]{1,0:T(8,128)(2,1)S(1)} %copy-done.2, bf16[384,512]{1,0:T(8,128)(2,1)} %reduce-scatter.6.cloned.1.call-done, f32[512]{0:T(512)S(1)} %copy-done.6, f32[512]{0:T(512)S(1)} %copy-done.7, bf16[384,512]{1,0:T(8,128)(2,1)S(1)} %copy-done.3, ...), kind=kLoop, calls=%fused_computation.23 | loop fusion | flops 4718592 | bytes 2365440 | tf_op jit(solution)/shard_map/convert_element_type | solution.py:58
  135.9 0.0 all-gather.2.cloned.1.call-update
  136.0 0.0 reduce-scatter.8.cloned.1.call-start
  136.0 26.7 %all-gather.2.cloned.1.call-done = bf16[384,4096]{1,0:T(8,128)(2,1)} async-done(((bf16[384,512]{1,0:T(8,128)(2,1)}), bf16[384,4096]{1,0:T(8,128)(2,1)}) %all-gather.2.cloned.1.call-update) | async-done | bytes 3145744 | tf_op jit(solution)/shard_map/all_gather | solution.py:62
  162.7 8.6 %convolution_convert_fusion.1 = bf16[1024,4096]{1,0:T(8,128)(2,1)} fusion(bf16[384,1024]{1,0:T(8,128)(2,1)S(1)} %bitcast.34, bf16[384,4096]{1,0:T(8,128)(2,1)} %all-gather.2.cloned.1.call-done), kind=kOutput, calls=%fused_computation.2 | convolution fusion | flops 3225419776 | bytes 12320768 | tf_op jit(solution)/shard_map/dot_general | solution.py:60
  171.4 0.0 reduce-scatter.8.cloned.1.call-update
  171.4 85.3 %reduce-scatter.8.cloned.1.call-done = bf16[1024,256]{1,0:T(8,128)(2,1)} async-done(((bf16[1024,4096]{1,0:T(8,128)(2,1)}), bf16[1024,256]{1,0:T(8,128)(2,1)}) %reduce-scatter.8.cloned.1.call-update) | async-done | bytes 524304 | tf_op jit(solution)/shard_map/reduce_scatter | solution.py:66
  256.7 2.1 convert_element_type.64
  (6 shorter events, 0.1 us)
Async XLA Ops:
  7.2 1.0 copy-start
  7.2 8.7 %copy-start.9 = (s32[256]{0:T(256)S(1)}, s32[256]{0:T(256)}, u32[]{:S(2)}) copy-start(s32[256]{0:T(256)} %param.22) | copy-start | bytes 3076
  7.2 8.7 %copy-start.4 = (s32[256,1]{0,1:T(1,128)S(1)}, s32[256,1]{0,1:T(1,128)}, u32[]{:S(2)}) copy-start(s32[256,1]{0,1:T(1,128)} %param.21) | copy-start | bytes 3076
  7.2 49.0 %copy-start.1 = (bf16[256,1024]{1,0:T(8,128)(2,1)S(1)}, bf16[256,1024]{1,0:T(8,128)(2,1)}, u32[]{:S(2)}) copy-start(bf16[256,1024]{1,0:T(8,128)(2,1)} %param.14) | copy-start | bytes 1572868
  7.2 63.3 %copy-start.5 = (f32[1024]{0:T(1024)S(1)}, f32[1024]{0:T(1024)}, u32[]{:S(2)}) copy-start(f32[1024]{0:T(1024)} %param.15) | copy-start | bytes 12292
  7.2 49.0 %reduce-scatter.4.cloned.1.call-start = ((), (), s32[]{:S(2)}) async-start(), calls=%async_computation.4 | async-start | bytes 4718592 | tf_op jit(solution)/shard_map/reduce_scatter | solution.py:32
  15.8 117.4 %reduce-scatter.6.cloned.1.call-start = ((), (), s32[]{:S(2)}) async-start(), calls=%async_computation.5 | async-start | bytes 3538944 | tf_op jit(solution)/shard_map/reduce_scatter | solution.py:50
  93.5 39.8 %copy-start.2 = (bf16[384,512]{1,0:T(8,128)(2,1)S(1)}, bf16[384,512]{1,0:T(8,128)(2,1)}, u32[]{:S(2)}) copy-start(bf16[384,512]{1,0:T(8,128)(2,1)} %param.23) | copy-start | bytes 1179652
  93.5 39.8 %copy-start.3 = (bf16[384,512]{1,0:T(8,128)(2,1)S(1)}, bf16[384,512]{1,0:T(8,128)(2,1)}, u32[]{:S(2)}) copy-start(bf16[384,512]{1,0:T(8,128)(2,1)} %param.17) | copy-start | bytes 1179652
  93.5 39.8 %copy-start.6 = (f32[512]{0:T(512)S(1)}, f32[512]{0:T(512)}, u32[]{:S(2)}) copy-start(f32[512]{0:T(512)} %param.19) | copy-start | bytes 6148
  93.5 39.8 %copy-start.7 = (f32[512]{0:T(512)S(1)}, f32[512]{0:T(512)}, u32[]{:S(2)}) copy-start(f32[512]{0:T(512)} %param.20) | copy-start | bytes 6148
  93.5 39.8 %copy-start.8 = (f32[512]{0:T(512)S(1)}, f32[512]{0:T(512)}, u32[]{:S(2)}) copy-start(f32[512]{0:T(512)} %param.18) | copy-start | bytes 6148
  101.7 61.0 %all-gather.2.cloned.1.call-start = ((), (), s32[]{:S(2)}) async-start(), calls=%async_computation.6 | async-start | bytes 3538944 | tf_op jit(solution)/shard_map/all_gather | solution.py:62
  136.0 120.7 %reduce-scatter.8.cloned.1.call-start = ((), (), s32[]{:S(2)}) async-start(), calls=%async_computation.7 | async-start | bytes 8912896 | tf_op jit(solution)/shard_map/reduce_scatter | solution.py:66
Sparse Core Ops, SparseCore 0:
  15.9 40.2 reduce-scatter.3
  101.9 31.3 reduce-scatter.5
  136.1 26.5 all-gather.1
  171.5 85.1 reduce-scatter.7
where the time goes:
time: 266 us; the launch traced here: 265 us
  waiting for transfers between devices  183 us (69%)
  blocking collectives  33.3 us (13%)
  matrix products  24.5 us (9%)
  between operations  13.9 us (5%)
  other arithmetic  9.39 us (4%)
    reduce_scatter x1, waiting for transfers between devices, body(): lax.psum_scatter(local_grad.astype(jnp.bfloat16), 'dp', scatter_dimension...  85.3 us
    reduce_scatter x1, waiting for transfers between devices, body(): lax.psum_scatter(term.astype(jnp.bfloat16), 'mp', scatter_dimension=1, ti...  39.4 us
    reduce_scatter x1, waiting for transfers between devices, body(): lax.psum_scatter(join_term.astype(jnp.bfloat16), 'mp', scatter_dimension=...  31.5 us
    all_gather x1, waiting for transfers between devices, body(): lax.all_gather(hidden_grad, 'mp', axis=1, tiled=True)  26.7 us
    all_to_all x1, blocking collectives, body(): lax.all_to_all(outgoing.reshape(n_owner, most, width), 'dp', split_axis=0...  20.3 us
    psum x1, blocking collectives, body(): total = lax.psum(jnp.sum(mixed * mixed, axis=1), 'mp')  13 us
    dot_general x1, matrix products, body(): lax.dot_general(arrived, lax.all_gather(hidden_grad, 'mp', axis=1, tiled=...  8.63 us
    dot_general x1, matrix products, body(): join_term = jnp.dot(arrived, w_join, preferred_element_type=jnp.float32)  8.24 us
  transfers between devices with their start and end apart: 4, of which 4 were waited for; matrix products, arithmetic and copies ran while one was open for 0% of the time, Pallas kernels for 0%

commit v1 on v0

v1 whole, which is shorter than its diff:
```python
import jax
import jax.numpy as jnp
from jax import lax
from jax.sharding import Mesh, PartitionSpec as P

AXES = ("x", "z", "y", "c")
N = 4
BF = jnp.bfloat16
F32 = jnp.float32


def move(value, where):
    pairs = []
    for x in range(N):
        for z in range(N):
            for y in range(N):
                for c in range(2):
                    tx, tz, ty, tc = where(x, z, y, c)
                    pairs.append(
                        (
                            ((x * N + z) * N + y) * 2 + c,
                            (((tx % N) * N + tz % N) * N + ty % N) * 2 + tc % 2,
                        )
                    )
    return lax.ppermute(value, AXES, pairs)


def swap(value):
    return move(value, lambda x, z, y, c: (x, z, y, 1 - c))


def along_y(value, step):
    return move(value, lambda x, z, y, c: (x, z, y + step, c))


def along_z(value, step):
    return move(value, lambda x, z, y, c: (x, z + step, y, c))


def add(*terms):
    total = terms[0].astype(F32)
    for term in terms[1:]:
        total = total + term.astype(F32)
    return total


def ring_scatter(chunk, shift):
    far = chunk(2).astype(BF)
    half = far.shape[0] // 2
    from_left = shift(far[:half], 1)
    from_right = shift(far[half:], -1)
    right = chunk(1)
    left = chunk(-1)
    low_b = shift(right[half:].astype(BF), 1)
    up_a = shift(left[:half].astype(BF), -1)
    low_a = shift(add(right[:half], from_left).astype(BF), 1)
    up_b = shift(add(left[half:], from_right).astype(BF), -1)
    own = chunk(0)
    return jnp.concatenate([add(own[:half], up_a, low_a), add(own[half:], low_b, up_b)], axis=0)


def pair_scatter(rows, weights, width):
    y, c = lax.axis_index("y"), lax.axis_index("c")

    def term(step, core):
        start = (lax.rem(y + step + N, N) * 2 + core) * width
        columns = lax.dynamic_slice_in_dim(weights, start, width, 1)
        return jnp.dot(rows, columns, preferred_element_type=F32)

    arrived = {d: swap(term(d, 1 - c).astype(BF)) for d in (2, 1, -1, 0)}
    return lambda d: add(term(d, c), arrived[d])


def body(
    context, w_out, residual, norm_gain, w_join, dec_state, gate_s, gate_h, gate_bias, owner, pad_mask, cotangent
):
    x, z, y, c = (lax.axis_index(a) for a in AXES)
    n_owner = N * N
    tokens, width = residual.shape
    slot_rows, features = dec_state.shape
    most = slot_rows // n_owner

    onehot = (owner == jnp.arange(n_owner, dtype=jnp.int32)[None, :]).astype(BF)
    ahead = jnp.tril(jnp.ones((tokens, tokens), BF), -1)
    before = jnp.dot(ahead, onehot, preferred_element_type=F32)
    rank = jnp.sum(before * onehot.astype(F32), axis=1).astype(jnp.int32)
    slots = owner[:, 0] * most + rank
    select = (slots[:, None] == jnp.arange(slot_rows, dtype=jnp.int32)[None, :]).astype(BF)

    both = jnp.concatenate([dec_state, cotangent], axis=1).reshape(n_owner, most, 2 * features)
    both = lax.all_to_all(both, ("x", "z"), 0, 0, tiled=True).reshape(slot_rows, 2 * features)
    both = jnp.dot(select, both, preferred_element_type=F32).astype(BF)
    state_t, outer_t = both[:, :features].astype(F32), both[:, features:].astype(F32)

    summed = ring_scatter(pair_scatter(context, w_out, width), along_y)
    mixed = residual.astype(F32) + summed
    squares = jnp.sum(mixed * mixed, axis=1)
    rows = (mixed * norm_gain[None, :] * pad_mask.astype(F32)[:, None]).astype(BF)
    rows_t = lax.all_gather(rows.T, "x")

    total = squares.reshape(2, -1)
    total = total + swap(total)
    total = total + move(total, lambda x, z, y, c: (x, z, y ^ 1, c))
    total = total + move(total, lambda x, z, y, c: (x, z, y ^ 2, c))
    scale = lax.rsqrt(total.reshape(-1) / (width * N * 2) + 1e-05)[:, None]

    part = pair_scatter(rows, w_join, features)
    sums = [along_y(part(d).astype(BF), d) for d in (2, 1, -1)]
    hidden = (add(part(0), *sums) * scale).astype(BF)

    def gates(state, hidden):
        gate = jax.nn.sigmoid(gate_s[None, :] * state + gate_h[None, :] * hidden + gate_bias[None, :])
        return gate, gate * (1.0 - gate) * hidden

    gate, slope = gates(state_t, hidden.astype(F32))
    grad = (outer_t * (gate + slope * gate_h[None, :]) * scale).astype(BF)

    grad = move(grad, lambda x, z, y, c: (y, z, x, c))
    pieces = [grad] + [along_y(grad, -d) for d in (1, 2, 3)]
    pieces = [(piece, swap(piece)) for piece in pieces]
    stacked = jnp.stack(
        [jnp.concatenate([jnp.where(c == 0, a, b), jnp.where(c == 0, b, a)], axis=1) for a, b in pieces]
    )
    order = lax.rem(y + jnp.arange(N), N)
    rows_y = jnp.take(rows_t, order, axis=0)

    def grad_term(step):
        start = lax.rem(z + step + N, N) * (2 * features // N)
        columns = lax.dynamic_slice_in_dim(stacked, start, 2 * features // N, 2)
        return lax.dot_general(rows_y, columns, (((0, 2), (0, 1)), ((), ())), preferred_element_type=F32)

    join_grad = ring_scatter(grad_term, along_z)

    placed = lax.dot_general(select, hidden, (((0,), (0,)), ((), ())), preferred_element_type=F32)
    placed = placed.astype(BF).reshape(n_owner, most, features)
    placed = lax.all_to_all(placed, ("x", "z"), 0, 0, tiled=True).reshape(slot_rows, features).astype(F32)
    state = dec_state.astype(F32)
    gate, slope = gates(state, placed)
    joined = (state + gate * placed).astype(BF)
    state_grad = (cotangent.astype(F32) * (1.0 + slope * gate_s[None, :])).astype(BF)
    return joined, state_grad, join_grad


def solution(mesh):
    fine = Mesh(mesh.devices.reshape(N, N, N, 2), AXES)
    dp, mp = ("x", "z"), ("y", "c")
    in_specs = (
        P(dp, mp),
        P(mp, None),
        P(dp, mp),
        P(mp),
        P(mp, None),
        P(dp, mp),
        P(mp),
        P(mp),
        P(mp),
        P(dp, None),
        P(dp),
        P(dp, mp),
    )
    out_specs = (P(dp, mp), P(dp, mp), P(mp, dp))
    return jax.shard_map(body, mesh=fine, in_specs=in_specs, out_specs=out_specs, check_vma=False)
```

time: 266 us -> 175 us (0.66)
  waiting for transfers between devices: 183 us -> 39.4 us
  starting transfers between devices: 0.16 us -> 62.9 us
  blocking collectives: 33.3 us -> 0 us
  matrix products: 24.5 us -> 37.9 us
  local copies, waits for them, and re-layouts: 1.09 us -> 8.34 us
    reduce_scatter x3 -> x0, waiting for transfers between devices: 156 us -> none  [the longest x1 85.3 us: body(): lax.psum_scatter(local_grad.astype(jnp.bfloat16), 'dp', scatter_dimension...]
    ppermute x0 -> x34, starting transfers between devices: none -> 44.3 us  [move(): return lax.ppermute(value, AXES, pairs)]
    ppermute x0 -> x34, waiting for transfers between devices: none -> 39.4 us  [move(): return lax.ppermute(value, AXES, pairs)]
    all_gather x1, waiting for transfers between devices: 26.7 us -> 0.01 us  [body(): rows_t = lax.all_gather(rows.T, 'x')]
    all_to_all x1 -> x0, blocking collectives: 20.3 us -> none  [body(): lax.all_to_all(outgoing.reshape(n_owner, most, width), 'dp', split_axis=0...]
    all_to_all x0 -> x2, starting transfers between devices: none -> 18.5 us  [the longest x1 10.5 us: body(): lax.all_to_all(placed, ('x', 'z'), 0, 0, tiled=True)]
    dot_general x3 -> x23, matrix products: 24.5 us -> 37.9 us  [the longest x16 31.2 us: term(): return jnp.dot(rows, columns, preferred_element_type=F32)]
    psum x1 -> x0, blocking collectives: 13 us -> none  [body(): total = lax.psum(jnp.sum(mixed * mixed, axis=1), 'mp')]
  transfers between devices with their start and end apart: 4 -> 37, of which waited for: 4 -> 14; matrix products, arithmetic and copies ran while one was open for 0% -> 23% of each run, Pallas kernels for 0% -> 0%
where the time goes in v1:
time: 175 us; the launch traced here: 174 us
  starting transfers between devices  62.9 us (36%)
  waiting for transfers between devices  39.4 us (23%)
  matrix products  37.9 us (22%)
  between operations  14.7 us (8%)
  other arithmetic  10.7 us (6%)
  local copies, waits for them, and re-layouts  8.34 us (5%)
    ppermute x34, starting transfers between devices, move(): return lax.ppermute(value, AXES, pairs)  44.3 us
    ppermute x34, waiting for transfers between devices, move(): return lax.ppermute(value, AXES, pairs)  39.4 us
    dot_general x16, matrix products, term(): return jnp.dot(rows, columns, preferred_element_type=F32)  31.2 us
    all_to_all x1, starting transfers between devices, body(): lax.all_to_all(placed, ('x', 'z'), 0, 0, tiled=True)  10.5 us
    all_to_all x1, starting transfers between devices, body(): lax.all_to_all(both, ('x', 'z'), 0, 0, tiled=True)  7.96 us
    dot_general x4, matrix products, grad_term(): lax.dot_general(rows_y, columns, (((0, 2), (0, 1)), ((), ())), preferred_...  4.84 us
  transfers between devices with their start and end apart: 37, of which 14 were waited for; matrix products, arithmetic and copies ran while one was open for 23% of the time, Pallas kernels for 0%

profile of v1, /device:TPU:0, one launch (start us, length us, event | category | flops | bytes accessed | tf_op | source)
XLA Modules:
  0.0 174.0 jit_solution(8824140547024195277)
XLA Ops:
  7.2 0.9 copy-done
  8.1 2.5 %fusion.4 = bf16[256,1024]{1,0:T(8,128)(2,1)} fusion(bf16[256,512]{1,0:T(8,128)(2,1)S(1)} %copy-done, bf16[512,8192]{1,0:T(8,128)(2,1)} %param.13, s32[]{:T(128)S(6)} %select_n.128), kind=kOutput, calls=%fused_computation.21 | convolution fusion | flops 268697600 | bytes 1835012 | tf_op jit(solution)/shard_map/dot_general | solution.py:68
  10.6 1.7 fusion.3
  12.3 0.6 collective-permute-start.3
  12.9 2.5 %fusion.2 = bf16[256,1024]{1,0:T(8,128)(2,1)} fusion(bf16[256,512]{1,0:T(8,128)(2,1)S(1)} %copy-done, bf16[512,8192]{1,0:T(8,128)(2,1)} %param.13, s32[]{:T(128)S(6)} %select_n.124), kind=kOutput, calls=%fused_computation.19 | convolution fusion | flops 268697600 | bytes 1835012 | tf_op jit(solution)/shard_map/dot_general | solution.py:68
  15.5 2.5 %fusion.1 = bf16[256,1024]{1,0:T(8,128)(2,1)} fusion(bf16[256,512]{1,0:T(8,128)(2,1)S(1)} %copy-done, bf16[512,8192]{1,0:T(8,128)(2,1)} %param.13, s32[]{:T(128)S(6)} %select_n.122), kind=kOutput, calls=%fused_computation.18 | convolution fusion | flops 268697600 | bytes 1835012 | tf_op jit(solution)/shard_map/dot_general | solution.py:68
  18.3 1.0 pad_maximum_fusion.2
  19.3 8.0 %all-to-all-start.1 = ((bf16[16,24,1024]{2,1,0:T(8,128)(2,1)}), bf16[16,24,1024]{2,1,0:T(8,128)(2,1)S(1)}, u32[]{:S(2)}, u32[]{:S(2)}) async-start(bf16[16,24,1024]{2,1,0:T(8,128)(2,1)} %bitcast.19), calls=%async_computation.1 | async-start | bytes 1572864 | tf_op jit(solution)/shard_map/all_to_all | solution.py:91
  27.9 1.7 add_convert_fusion
  29.6 1.6 collective-permute-start.5
  31.2 1.7 collective-permute-start.8
  32.9 1.8 %convert_add_fusion.1 = f32[256,1024]{1,0:T(8,128)S(1)} fusion(bf16[256,1024]{1,0:T(8,128)(2,1)} %collective-permute-done.1, bf16[256,512]{1,0:T(8,128)(2,1)S(1)} %copy-done, bf16[512,8192]{1,0:T(8,128)(2,1)} %param.13, s32[]{:T(128)S(6)} %select_n.123), kind=kOutput, calls=%fused_computation.54 | convolution fusion | flops 268959744 | bytes 2883588 | tf_op jit(solution)/shard_map/dot_general | solution.py:68
  34.7 0.7 slice.129
  35.4 1.8 %collective-permute-start.2 = (bf16[128,1024]{1,0:T(8,128)(2,1)}, bf16[128,1024]{1,0:T(8,128)(2,1)}, u32[]{:S(2)}, u32[]{:S(2)}) collective-permute-start(bf16[128,1024]{1,0:T(8,128)(2,1)} %slice.129), channel_id=1, source_target_pairs={{0,6},{1,7},{2,0},{3,1},{4,2},{5,3},{6,4},{7,5},{8,14},{9,15},{10,... | collective-permute-start | bytes 786440 | tf_op jit(solution)/shard_map/ppermute | solution.py:25
  37.2 1.7 convert_add_fusion
  38.9 0.8 slice.128
  39.9 0.8 fusion.62
  41.0 0.8 fusion.60
  41.8 2.9 %collective-permute-start.9 = (bf16[128,1024]{1,0:T(8,128)(2,1)}, bf16[128,1024]{1,0:T(8,128)(2,1)}, u32[]{:S(2)}, u32[]{:S(2)}) collective-permute-start(bf16[128,1024]{1,0:T(8,128)(2,1)} %fusion.60), channel_id=1, source_target_pairs={{0,6},{1,7},{2,0},{3,1},{4,2},{5,3},{6,4},{7,5},{8,14},{9,15},{10,... | collective-permute-start | bytes 786440 | tf_op jit(solution)/shard_map/ppermute | solution.py:25
  44.6 1.8 %convert_add_fusion.2 = f32[256,1024]{1,0:T(8,128)S(1)} fusion(bf16[256,1024]{1,0:T(8,128)(2,1)} %collective-permute-done, bf16[256,512]{1,0:T(8,128)(2,1)S(1)} %copy-done, bf16[512,8192]{1,0:T(8,128)(2,1)} %param.13, s32[]{:T(128)S(6)} %select_n.121), kind=kOutput, calls=%fused_computation.57 | convolution fusion | flops 268959744 | bytes 2883588 | tf_op jit(solution)/shard_map/dot_general | solution.py:68
  47.0 3.4 %collective-permute-done.7 = bf16[128,1024]{1,0:T(8,128)(2,1)} collective-permute-done((bf16[128,1024]{1,0:T(8,128)(2,1)}, bf16[128,1024]{1,0:T(8,128)(2,1)}, u32[]{:S(2)}, u32[]{:S(2)}) %collective-permute-start.7) | collective-permute-done | bytes 262176 | tf_op jit(solution)/shard_map/ppermute | solution.py:25
  50.4 3.6 %collective-permute-done.6 = bf16[128,1024]{1,0:T(8,128)(2,1)} collective-permute-done((bf16[128,1024]{1,0:T(8,128)(2,1)}, bf16[128,1024]{1,0:T(8,128)(2,1)}, u32[]{:S(2)}, u32[]{:S(2)}) %collective-permute-start.6) | collective-permute-done | bytes 262176 | tf_op jit(solution)/shard_map/ppermute | solution.py:25
  54.0 1.4 fusion.63
  55.8 1.9 %convolution_convert_fusion.8 = bf16[256,512]{1,0:T(8,128)(2,1)S(1)} fusion(bf16[256,1024]{1,0:T(8,128)(2,1)S(1)} %get-tuple-element.5, bf16[1024,4096]{1,0:T(8,128)(2,1)} %param.16, s32[]{:T(128)S(6)} %select_n.132), kind=kOutput, calls=%fused_computation.24 | convolution fusion | flops 268566528 | bytes 1835012 | tf_op jit(solution)/shard_map/dot_general | solution.py:68
  57.8 2.4 %convolution_convert_fusion.7 = bf16[256,512]{1,0:T(8,128)(2,1)} fusion(bf16[256,1024]{1,0:T(8,128)(2,1)S(1)} %get-tuple-element.5, bf16[1024,4096]{1,0:T(8,128)(2,1)} %param.16, s32[]{:T(128)S(6)} %select_n.134), kind=kOutput, calls=%fused_computation.23 | convolution fusion | flops 268566528 | bytes 1835012 | tf_op jit(solution)/shard_map/dot_general | solution.py:68
  60.7 2.4 %convolution_convert_fusion.6 = bf16[256,512]{1,0:T(8,128)(2,1)} fusion(bf16[256,1024]{1,0:T(8,128)(2,1)S(1)} %get-tuple-element.5, bf16[1024,4096]{1,0:T(8,128)(2,1)} %param.16, s32[]{:T(128)S(6)} %select_n.136), kind=kOutput, calls=%fused_computation.22 | convolution fusion | flops 268566528 | bytes 1835012 | tf_op jit(solution)/shard_map/dot_general | solution.py:68
  63.6 1.7 convolution_convert_fusion.9
  65.5 1.7 collective-permute-done.18
  67.1 1.8 %add_convert_fusion.3 = bf16[256,512]{1,0:T(8,128)(2,1)S(1)} fusion(bf16[256,512]{1,0:T(8,128)(2,1)S(1)} %collective-permute-done.11, bf16[256,1024]{1,0:T(8,128)(2,1)} %copy-done.1, bf16[1024,4096]{1,0:T(8,128)(2,1)} %param.16, s32[]{:T(128)S(6)} %select_n.131), kind=kOutput, calls=%fused_computation.119 | convolution fusion | flops 268828672 | bytes 2097156 | tf_op jit(solution)/shard_map/dot_general | solution.py:68
  69.0 3.6 %collective-permute-start.12 = (bf16[256,512]{1,0:T(8,128)(2,1)S(1)}, bf16[256,512]{1,0:T(8,128)(2,1)S(1)}, u32[]{:S(2)}, u32[]{:S(2)}) collective-permute-start(bf16[256,512]{1,0:T(8,128)(2,1)S(1)} %add_convert_fusion.3), channel_id=1, source_target_pairs={{0,4},{1,5},{2,6},{3,7},{4,0},{5,1},{6,2},{7,3},{8,12},{9,13},{10,... | collective-permute-start | bytes 786440 | tf_op jit(solution)/shard_map/ppermute | solution.py:25
  72.6 1.7 add_convert_fusion.2
  74.3 0.6 collective-permute-start.14
  74.9 1.7 %add_convert_fusion.1 = bf16[256,512]{1,0:T(8,128)(2,1)S(1)} fusion(bf16[256,512]{1,0:T(8,128)(2,1)S(1)} %collective-permute-done.15, bf16[256,1024]{1,0:T(8,128)(2,1)S(1)} %copy-done.2, bf16[1024,4096]{1,0:T(8,128)(2,1)} %param.16, s32[]{:T(128)S(6)} %select_n.135), kind=kOutput, calls=%fused_computation.117 | convolution fusion | flops 268828672 | bytes 2097156 | tf_op jit(solution)/shard_map/dot_general | solution.py:68
  76.6 2.9 %collective-permute-start.16 = (bf16[256,512]{1,0:T(8,128)(2,1)S(1)}, bf16[256,512]{1,0:T(8,128)(2,1)S(1)}, u32[]{:S(2)}, u32[]{:S(2)}) collective-permute-start(bf16[256,512]{1,0:T(8,128)(2,1)S(1)} %add_convert_fusion.1), channel_id=1, source_target_pairs={{0,6},{1,7},{2,0},{3,1},{4,2},{5,3},{6,4},{7,5},{8,14},{9,15},{10,... | collective-permute-start | bytes 786440 | tf_op jit(solution)/shard_map/ppermute | solution.py:25
  79.6 1.7 fusion.16
  81.3 2.6 %collective-permute-done.14 = bf16[256,512]{1,0:T(8,128)(2,1)S(1)} collective-permute-done((bf16[256,512]{1,0:T(8,128)(2,1)S(1)}, bf16[256,512]{1,0:T(8,128)(2,1)S(1)}, u32[]{:S(2)}, u32[]{:S(2)}) %collective-permute-start.14) | collective-permute-done | bytes 262176 | tf_op jit(solution)/shard_map/ppermute | solution.py:25
  83.9 1.0 collective-permute-done.16
  85.0 1.5 fusion.55
  86.4 0.7 collective-permute-start.20
  87.1 1.1 convolution_convert_fusion.5
  88.3 10.5 %all-to-all-start = ((bf16[16,24,512]{2,1,0:T(8,128)(2,1)}), bf16[16,24,512]{2,1,0:T(8,128)(2,1)S(1)}, u32[]{:S(2)}, u32[]{:S(2)}) async-start(bf16[16,24,512]{2,1,0:T(8,128)(2,1)} %bitcast.13), calls=%async_computation | async-start | bytes 786432 | tf_op jit(solution)/shard_map/all_to_all | solution.py:136
  98.8 14.4 %collective-permute-start.22 = (bf16[256,512]{1,0:T(8,128)(2,1)S(1)}, bf16[256,512]{1,0:T(8,128)(2,1)S(1)}, u32[]{:S(2)}, u32[]{:S(2)}) collective-permute-start(bf16[256,512]{1,0:T(8,128)(2,1)S(1)} %collective-permute-done.20), channel_id=1, source_target_pairs={{0,6},{1,7},{2,0},{3,1},{4,2},{5,3},{6,4},{7,5},{8,14},{9,15},{10,... | collective-permute-start | bytes 786440 | tf_op jit(solution)/shard_map/ppermute | solution.py:25
  113.4 1.5 collective-permute-start.24
  114.9 2.5 %collective-permute-done.22 = bf16[256,512]{1,0:T(8,128)(2,1)S(1)} collective-permute-done((bf16[256,512]{1,0:T(8,128)(2,1)S(1)}, bf16[256,512]{1,0:T(8,128)(2,1)S(1)}, u32[]{:S(2)}, u32[]{:S(2)}) %collective-permute-start.22) | collective-permute-done | bytes 262176 | tf_op jit(solution)/shard_map/ppermute | solution.py:25
  117.4 1.4 fusion.44
  118.9 10.0 %collective-permute-done.26 = bf16[256,512]{1,0:T(8,128)(2,1)S(1)} collective-permute-done((bf16[256,512]{1,0:T(8,128)(2,1)S(1)}, bf16[256,512]{1,0:T(8,128)(2,1)S(1)}, u32[]{:S(2)}, u32[]{:S(2)}) %collective-permute-start.26) | collective-permute-done | bytes 262176 | tf_op jit(solution)/shard_map/ppermute | solution.py:25
  128.9 0.5 collective-permute-start.25
  129.6 0.8 collective-permute-done.27
  131.0 1.6 pad_maximum_fusion
  132.6 3.3 %copy.37 = bf16[4096,256]{1,0:T(8,128)(2,1)S(1)} copy(bf16[4096,256]{0,1:T(8,128)(2,1)} %all-gather.3.cloned.1.call-done) | data formatting | bytes 4194304 | tf_op jit(solution)/shard_map/all_gather | solution.py:99
  135.9 2.0 %gather_fusion = bf16[4,1024,256]{2,1,0:T(8,128)(2,1)} fusion(bf16[4,1024,256]{2,1,0:T(8,128)(2,1)S(1)} %bitcast.86, s32[1024]{0:T(1024)S(1)} %pad_clamp_fusion), kind=kCustom, calls=%fused_computation | custom fusion | bytes 4194320 | tf_op jit(solution)/shard_map/jit(_take)/gather | solution.py:125
  137.9 2.6 %convolution_bitcast_fusion.2 = f32[1024,256]{1,0:T(8,128)S(1)} fusion(bf16[4,256,1024]{2,1,0:T(8,128)(2,1)} %pad_maximum_fusion, s32[]{:T(128)S(6)} %select_n.150, bf16[4,1024,256]{2,1,0:T(8,128)(2,1)} %gather_fusion, pred[4]{0:T(512)(128)(4,1)S(1)} %compare_and_fusion), kind=kOutput, calls=%fused_computation.5 | convolution fusion | flops 537919488 | bytes 3670024 | tf_op jit(solution)/shard_map/dot_general | solution.py:130
  141.0 0.8 fusion
  141.8 3.0 %collective-permute-start.32 = (bf16[512,256]{1,0:T(8,128)(2,1)S(1)}, bf16[512,256]{1,0:T(8,128)(2,1)S(1)}, u32[]{:S(2)}, u32[]{:S(2)}) collective-permute-start(bf16[512,256]{1,0:T(8,128)(2,1)S(1)} %get-tuple-element.14), channel_id=1, source_target_pairs={{0,24},{1,25},{2,26},{3,27},{4,28},{5,29},{6,30},{7,31},{8,0},{9,1... | collective-permute-start | bytes 786440 | tf_op jit(solution)/shard_map/ppermute | solution.py:25
  144.8 0.8 collective-permute-start.28
  145.6 1.2 collective-permute-start.29
  146.9 0.7 convolution_bitcast_fusion.1
  147.8 3.7 %collective-permute-done.32 = bf16[512,256]{1,0:T(8,128)(2,1)S(1)} collective-permute-done((bf16[512,256]{1,0:T(8,128)(2,1)S(1)}, bf16[512,256]{1,0:T(8,128)(2,1)S(1)}, u32[]{:S(2)}, u32[]{:S(2)}) %collective-permute-start.32) | collective-permute-done | bytes 262176 | tf_op jit(solution)/shard_map/ppermute | solution.py:25
  151.5 3.8 %collective-permute-start.33 = (bf16[512,256]{1,0:T(8,128)(2,1)S(1)}, bf16[512,256]{1,0:T(8,128)(2,1)S(1)}, u32[]{:S(2)}, u32[]{:S(2)}) collective-permute-start(bf16[512,256]{1,0:T(8,128)(2,1)S(1)} %fusion.56), channel_id=1, source_target_pairs={{0,24},{1,25},{2,26},{3,27},{4,28},{5,29},{6,30},{7,31},{8,0},{9,1... | collective-permute-start | bytes 786440 | tf_op jit(solution)/shard_map/ppermute | solution.py:25
  155.3 0.8 collective-permute-done.29
  156.3 0.7 convolution_bitcast_fusion.3
  157.1 4.7 %collective-permute-done.31 = bf16[512,256]{1,0:T(8,128)(2,1)S(1)} collective-permute-done((bf16[512,256]{1,0:T(8,128)(2,1)S(1)}, bf16[512,256]{1,0:T(8,128)(2,1)S(1)}, u32[]{:S(2)}, u32[]{:S(2)}) %collective-permute-start.31) | collective-permute-done | bytes 262176 | tf_op jit(solution)/shard_map/ppermute | solution.py:25
  161.9 4.0 %collective-permute-done.30 = bf16[512,256]{1,0:T(8,128)(2,1)S(1)} collective-permute-done((bf16[512,256]{1,0:T(8,128)(2,1)S(1)}, bf16[512,256]{1,0:T(8,128)(2,1)S(1)}, u32[]{:S(2)}, u32[]{:S(2)}) %collective-permute-start.30) | collective-permute-done | bytes 262176 | tf_op jit(solution)/shard_map/ppermute | solution.py:25
  166.1 1.0 pad_maximum_fusion.1
  (98 shorter events, 5.9 us)
Async XLA Ops:
  7.2 1.0 copy-start
  10.6 17.3 %collective-permute-start.4 = (bf16[256,1024]{1,0:T(8,128)(2,1)}, bf16[256,1024]{1,0:T(8,128)(2,1)S(1)}, u32[]{:S(2)}, u32[]{:S(2)}) collective-permute-start(bf16[256,1024]{1,0:T(8,128)(2,1)} %fusion.4), channel_id=1, source_target_pairs={{0,1},{1,0},{2,3},{3,2},{4,5},{5,4},{6,7},{7,6},{8,9},{9,8},{10,11... | collective-permute-start | bytes 1572872 | tf_op jit(solution)/shard_map/ppermute | solution.py:25
  12.3 6.1 %copy-start.5 = (bf16[384,512]{1,0:T(8,128)(2,1)S(1)}, bf16[384,512]{1,0:T(8,128)(2,1)}, u32[]{:S(2)}) copy-start(bf16[384,512]{1,0:T(8,128)(2,1)} %param.23) | copy-start | bytes 1179652
  12.3 6.1 %copy-start.6 = (bf16[384,512]{1,0:T(8,128)(2,1)S(1)}, bf16[384,512]{1,0:T(8,128)(2,1)}, u32[]{:S(2)}) copy-start(bf16[384,512]{1,0:T(8,128)(2,1)} %param.17) | copy-start | bytes 1179652
  12.3 25.0 %collective-permute-start.3 = (bf16[256,1024]{1,0:T(8,128)(2,1)S(1)}, bf16[256,1024]{1,0:T(8,128)(2,1)S(1)}, u32[]{:S(2)}, u32[]{:S(2)}) collective-permute-start(bf16[256,1024]{1,0:T(8,128)(2,1)S(1)} %fusion.3), channel_id=1, source_target_pairs={{0,1},{1,0},{2,3},{3,2},{4,5},{5,4},{6,7},{7,6},{8,9},{9,8},{10,11... | collective-permute-start | bytes 1572872 | tf_op jit(solution)/shard_map/ppermute | solution.py:25
  15.3 17.5 %collective-permute-start.1 = (bf16[256,1024]{1,0:T(8,128)(2,1)}, bf16[256,1024]{1,0:T(8,128)(2,1)}, u32[]{:S(2)}, u32[]{:S(2)}) collective-permute-start(bf16[256,1024]{1,0:T(8,128)(2,1)} %fusion.2), channel_id=1, source_target_pairs={{0,1},{1,0},{2,3},{3,2},{4,5},{5,4},{6,7},{7,6},{8,9},{9,8},{10,11... | collective-permute-start | bytes 1572872 | tf_op jit(solution)/shard_map/ppermute | solution.py:25
  15.5 11.9 %copy-start.12 = (s32[256,1]{0,1:T(1,128)S(1)}, s32[256,1]{0,1:T(1,128)}, u32[]{:S(2)}) copy-start(s32[256,1]{0,1:T(1,128)} %param.21) | copy-start | bytes 3076
  17.9 9.8 %copy-start.13 = (s32[256]{0:T(256)S(1)}, s32[256]{0:T(256)}, u32[]{:S(2)}) copy-start(s32[256]{0:T(256)} %param.22) | copy-start | bytes 3076
  17.9 26.7 %collective-permute-start = (bf16[256,1024]{1,0:T(8,128)(2,1)}, bf16[256,1024]{1,0:T(8,128)(2,1)}, u32[]{:S(2)}, u32[]{:S(2)}) collective-permute-start(bf16[256,1024]{1,0:T(8,128)(2,1)} %fusion.1), channel_id=1, source_target_pairs={{0,1},{1,0},{2,3},{3,2},{4,5},{5,4},{6,7},{7,6},{8,9},{9,8},{10,11... | collective-permute-start | bytes 1572872 | tf_op jit(solution)/shard_map/ppermute | solution.py:25
  19.3 27.1 %all-to-all-start.1 = ((bf16[16,24,1024]{2,1,0:T(8,128)(2,1)}), bf16[16,24,1024]{2,1,0:T(8,128)(2,1)S(1)}, u32[]{:S(2)}, u32[]{:S(2)}) async-start(bf16[16,24,1024]{2,1,0:T(8,128)(2,1)} %bitcast.19), calls=%async_computation.1 | async-start | bytes 1572864 | tf_op jit(solution)/shard_map/all_to_all | solution.py:91
  27.3 105.3 %all-gather.3.cloned.1.call-start = ((), (), s32[]{:S(2)}) async-start(), calls=%async_computation.2 | async-start | bytes 2621440 | tf_op jit(solution)/shard_map/all_gather | solution.py:99
  29.6 10.3 %collective-permute-start.5 = (bf16[128,1024]{1,0:T(8,128)(2,1)S(1)}, bf16[128,1024]{1,0:T(8,128)(2,1)S(1)}, u32[]{:S(2)}, u32[]{:S(2)}) collective-permute-start(bf16[128,1024]{1,0:T(8,128)(2,1)S(1)} %get-tuple-element.23), channel_id=1, source_target_pairs={{0,2},{1,3},{2,4},{3,5},{4,6},{5,7},{6,0},{7,1},{8,10},{9,11},{10,... | collective-permute-start | bytes 786440 | tf_op jit(solution)/shard_map/ppermute | solution.py:25
  31.2 9.8 %collective-permute-start.8 = (bf16[128,1024]{1,0:T(8,128)(2,1)S(1)}, bf16[128,1024]{1,0:T(8,128)(2,1)S(1)}, u32[]{:S(2)}, u32[]{:S(2)}) collective-permute-start(bf16[128,1024]{1,0:T(8,128)(2,1)S(1)} %get-tuple-element.24), channel_id=1, source_target_pairs={{0,6},{1,7},{2,0},{3,1},{4,2},{5,3},{6,4},{7,5},{8,14},{9,15},{10,... | collective-permute-start | bytes 786440 | tf_op jit(solution)/shard_map/ppermute | solution.py:25
  35.4 11.6 %collective-permute-start.2 = (bf16[128,1024]{1,0:T(8,128)(2,1)}, bf16[128,1024]{1,0:T(8,128)(2,1)}, u32[]{:S(2)}, u32[]{:S(2)}) collective-permute-start(bf16[128,1024]{1,0:T(8,128)(2,1)} %slice.129), channel_id=1, source_target_pairs={{0,6},{1,7},{2,0},{3,1},{4,2},{5,3},{6,4},{7,5},{8,14},{9,15},{10,... | collective-permute-start | bytes 786440 | tf_op jit(solution)/shard_map/ppermute | solution.py:25
  39.7 10.8 %collective-permute-start.7 = (bf16[128,1024]{1,0:T(8,128)(2,1)}, bf16[128,1024]{1,0:T(8,128)(2,1)}, u32[]{:S(2)}, u32[]{:S(2)}) collective-permute-start(bf16[128,1024]{1,0:T(8,128)(2,1)} %slice.128), channel_id=1, source_target_pairs={{0,2},{1,3},{2,4},{3,5},{4,6},{5,7},{6,0},{7,1},{8,10},{9,11},{10,... | collective-permute-start | bytes 786440 | tf_op jit(solution)/shard_map/ppermute | solution.py:25
  40.6 13.4 %collective-permute-start.6 = (bf16[128,1024]{1,0:T(8,128)(2,1)}, bf16[128,1024]{1,0:T(8,128)(2,1)}, u32[]{:S(2)}, u32[]{:S(2)}) collective-permute-start(bf16[128,1024]{1,0:T(8,128)(2,1)} %fusion.62), channel_id=1, source_target_pairs={{0,2},{1,3},{2,4},{3,5},{4,6},{5,7},{6,0},{7,1},{8,10},{9,11},{10,... | collective-permute-start | bytes 786440 | tf_op jit(solution)/shard_map/ppermute | solution.py:25
  41.8 12.2 %collective-permute-start.9 = (bf16[128,1024]{1,0:T(8,128)(2,1)}, bf16[128,1024]{1,0:T(8,128)(2,1)}, u32[]{:S(2)}, u32[]{:S(2)}) collective-permute-start(bf16[128,1024]{1,0:T(8,128)(2,1)} %fusion.60), channel_id=1, source_target_pairs={{0,6},{1,7},{2,0},{3,1},{4,2},{5,3},{6,4},{7,5},{8,14},{9,15},{10,... | collective-permute-start | bytes 786440 | tf_op jit(solution)/shard_map/ppermute | solution.py:25
  46.5 9.0 %copy-start.7 = (bf16[256,1024]{1,0:T(8,128)(2,1)S(1)}, bf16[256,1024]{1,0:T(8,128)(2,1)}, u32[]{:S(2)}) copy-start(bf16[256,1024]{1,0:T(8,128)(2,1)} %param.14) | copy-start | bytes 1572868
  46.5 8.9 %copy-start.11 = (f32[1024]{0:T(1024)S(1)}, f32[1024]{0:T(1024)}, u32[]{:S(2)}) copy-start(f32[1024]{0:T(1024)} %param.15) | copy-start | bytes 12292
  55.8 7.8 %copy-start.1 = (bf16[256,1024]{1,0:T(8,128)(2,1)}, bf16[256,1024]{1,0:T(8,128)(2,1)S(1)}, u32[]{:S(2)}) copy-start(bf16[256,1024]{1,0:T(8,128)(2,1)S(1)} %get-tuple-element.5) | copy-start | bytes 1572868
  57.7 9.4 %collective-permute-start.11 = (bf16[256,512]{1,0:T(8,128)(2,1)S(1)}, bf16[256,512]{1,0:T(8,128)(2,1)S(1)}, u32[]{:S(2)}, u32[]{:S(2)}) collective-permute-start(bf16[256,512]{1,0:T(8,128)(2,1)S(1)} %convolution_convert_fusion.8), channel_id=1, source_target_pairs={{0,1},{1,0},{2,3},{3,2},{4,5},{5,4},{6,7},{7,6},{8,9},{9,8},{10,11... | collective-permute-start | bytes 786440 | tf_op jit(solution)/shard_map/ppermute | solution.py:25
  60.2 12.4 %collective-permute-start.13 = (bf16[256,512]{1,0:T(8,128)(2,1)}, bf16[256,512]{1,0:T(8,128)(2,1)S(1)}, u32[]{:S(2)}, u32[]{:S(2)}) collective-permute-start(bf16[256,512]{1,0:T(8,128)(2,1)} %convolution_convert_fusion.7), channel_id=1, source_target_pairs={{0,1},{1,0},{2,3},{3,2},{4,5},{5,4},{6,7},{7,6},{8,9},{9,8},{10,11... | collective-permute-start | bytes 786440 | tf_op jit(solution)/shard_map/ppermute | solution.py:25
  60.7 2.9 %collective-permute-start.17 = (f32[2,128]{1,0:T(2,128)S(1)}, f32[2,128]{1,0:T(2,128)S(1)}, u32[]{:S(2)}, u32[]{:S(2)}) collective-permute-start(f32[2,128]{1,0:T(2,128)S(1)} %bitcast.88), channel_id=1, source_target_pairs={{0,1},{1,0},{2,3},{3,2},{4,5},{5,4},{6,7},{7,6},{8,9},{9,8},{10,11... | collective-permute-start | bytes 3080 | tf_op jit(solution)/shard_map/ppermute | solution.py:25
  63.1 11.8 %collective-permute-start.15 = (bf16[256,512]{1,0:T(8,128)(2,1)}, bf16[256,512]{1,0:T(8,128)(2,1)S(1)}, u32[]{:S(2)}, u32[]{:S(2)}) collective-permute-start(bf16[256,512]{1,0:T(8,128)(2,1)} %convolution_convert_fusion.6), channel_id=1, source_target_pairs={{0,1},{1,0},{2,3},{3,2},{4,5},{5,4},{6,7},{7,6},{8,9},{9,8},{10,11... | collective-permute-start | bytes 786440 | tf_op jit(solution)/shard_map/ppermute | solution.py:25
  63.6 3.6 %collective-permute-start.18 = (f32[2,128]{1,0:T(2,128)S(1)}, f32[2,128]{1,0:T(2,128)S(1)}, u32[]{:S(2)}, u32[]{:S(2)}) collective-permute-start(f32[2,128]{1,0:T(2,128)S(1)} %bitcast_add_fusion), channel_id=1, source_target_pairs={{0,2},{1,3},{2,0},{3,1},{4,6},{5,7},{6,4},{7,5},{8,10},{9,11},{10,... | collective-permute-start | bytes 3080 | tf_op jit(solution)/shard_map/ppermute | solution.py:25
  65.3 7.3 %copy-start.2 = (bf16[256,1024]{1,0:T(8,128)(2,1)S(1)}, bf16[256,1024]{1,0:T(8,128)(2,1)}, u32[]{:S(2)}) copy-start(bf16[256,1024]{1,0:T(8,128)(2,1)} %copy-done.1) | copy-start | bytes 1572868
  65.3 16.0 %collective-permute-start.10 = (bf16[256,512]{1,0:T(8,128)(2,1)S(1)}, bf16[256,512]{1,0:T(8,128)(2,1)}, u32[]{:S(2)}, u32[]{:S(2)}) collective-permute-start(bf16[256,512]{1,0:T(8,128)(2,1)S(1)} %convolution_convert_fusion.9), channel_id=1, source_target_pairs={{0,1},{1,0},{2,3},{3,2},{4,5},{5,4},{6,7},{7,6},{8,9},{9,8},{10,11... | collective-permute-start | bytes 786440 | tf_op jit(solution)/shard_map/ppermute | solution.py:25
  67.1 14.1 %collective-permute-start.19 = (f32[2,128]{1,0:T(2,128)S(1)}, f32[2,128]{1,0:T(2,128)S(1)}, u32[]{:S(2)}, u32[]{:S(2)}) collective-permute-start(f32[2,128]{1,0:T(2,128)S(1)} %fusion.128), channel_id=1, source_target_pairs={{0,4},{1,5},{2,6},{3,7},{4,0},{5,1},{6,2},{7,3},{8,12},{9,13},{10,... | collective-permute-start | bytes 3080 | tf_op jit(solution)/shard_map/ppermute | solution.py:25
  69.0 12.3 %collective-permute-start.12 = (bf16[256,512]{1,0:T(8,128)(2,1)S(1)}, bf16[256,512]{1,0:T(8,128)(2,1)S(1)}, u32[]{:S(2)}, u32[]{:S(2)}) collective-permute-start(bf16[256,512]{1,0:T(8,128)(2,1)S(1)} %add_convert_fusion.3), channel_id=1, source_target_pairs={{0,4},{1,5},{2,6},{3,7},{4,0},{5,1},{6,2},{7,3},{8,12},{9,13},{10,... | collective-permute-start | bytes 786440 | tf_op jit(solution)/shard_map/ppermute | solution.py:25
  74.3 10.7 %copy-start.8 = (f32[512]{0:T(512)S(1)}, f32[512]{0:T(512)}, u32[]{:S(2)}) copy-start(f32[512]{0:T(512)} %param.20) | copy-start | bytes 6148
  74.3 10.7 %copy-start.9 = (f32[512]{0:T(512)S(1)}, f32[512]{0:T(512)}, u32[]{:S(2)}) copy-start(f32[512]{0:T(512)} %param.19) | copy-start | bytes 6148
  74.3 10.7 %copy-start.10 = (f32[512]{0:T(512)S(1)}, f32[512]{0:T(512)}, u32[]{:S(2)}) copy-start(f32[512]{0:T(512)} %param.18) | copy-start | bytes 6148
  74.3 9.6 %collective-permute-start.14 = (bf16[256,512]{1,0:T(8,128)(2,1)S(1)}, bf16[256,512]{1,0:T(8,128)(2,1)S(1)}, u32[]{:S(2)}, u32[]{:S(2)}) collective-permute-start(bf16[256,512]{1,0:T(8,128)(2,1)S(1)} %add_convert_fusion.2), channel_id=1, source_target_pairs={{0,2},{1,3},{2,4},{3,5},{4,6},{5,7},{6,0},{7,1},{8,10},{9,11},{10,... | collective-permute-start | bytes 786440 | tf_op jit(solution)/shard_map/ppermute | solution.py:25
  76.6 8.3 %collective-permute-start.16 = (bf16[256,512]{1,0:T(8,128)(2,1)S(1)}, bf16[256,512]{1,0:T(8,128)(2,1)S(1)}, u32[]{:S(2)}, u32[]{:S(2)}) collective-permute-start(bf16[256,512]{1,0:T(8,128)(2,1)S(1)} %add_convert_fusion.1), channel_id=1, source_target_pairs={{0,6},{1,7},{2,0},{3,1},{4,2},{5,3},{6,4},{7,5},{8,14},{9,15},{10,... | collective-permute-start | bytes 786440 | tf_op jit(solution)/shard_map/ppermute | solution.py:25
  86.4 12.4 %collective-permute-start.20 = (bf16[256,512]{1,0:T(8,128)(2,1)S(1)}, bf16[256,512]{1,0:T(8,128)(2,1)S(1)}, u32[]{:S(2)}, u32[]{:S(2)}) collective-permute-start(bf16[256,512]{1,0:T(8,128)(2,1)S(1)} %get-tuple-element.3), channel_id=1, source_target_pairs={{0,0},{1,1},{2,32},{3,33},{4,64},{5,65},{6,96},{7,97},{8,8},{9,9},... | collective-permute-start | bytes 786440 | tf_op jit(solution)/shard_map/ppermute | solution.py:25
  88.3 29.2 %all-to-all-start = ((bf16[16,24,512]{2,1,0:T(8,128)(2,1)}), bf16[16,24,512]{2,1,0:T(8,128)(2,1)S(1)}, u32[]{:S(2)}, u32[]{:S(2)}) async-start(bf16[16,24,512]{2,1,0:T(8,128)(2,1)} %bitcast.13), calls=%async_computation | async-start | bytes 786432 | tf_op jit(solution)/shard_map/all_to_all | solution.py:136
  98.8 18.6 %collective-permute-start.22 = (bf16[256,512]{1,0:T(8,128)(2,1)S(1)}, bf16[256,512]{1,0:T(8,128)(2,1)S(1)}, u32[]{:S(2)}, u32[]{:S(2)}) collective-permute-start(bf16[256,512]{1,0:T(8,128)(2,1)S(1)} %collective-permute-done.20), channel_id=1, source_target_pairs={{0,6},{1,7},{2,0},{3,1},{4,2},{5,3},{6,4},{7,5},{8,14},{9,15},{10,... | collective-permute-start | bytes 786440 | tf_op jit(solution)/shard_map/ppermute | solution.py:25
  113.2 16.2 %collective-permute-start.21 = (bf16[256,512]{1,0:T(8,128)(2,1)S(1)}, bf16[256,512]{1,0:T(8,128)(2,1)S(1)}, u32[]{:S(2)}, u32[]{:S(2)}) collective-permute-start(bf16[256,512]{1,0:T(8,128)(2,1)S(1)} %collective-permute-done.20), channel_id=1, source_target_pairs={{0,1},{1,0},{2,3},{3,2},{4,5},{5,4},{6,7},{7,6},{8,9},{9,8},{10,11... | collective-permute-start | bytes 786440 | tf_op jit(solution)/shard_map/ppermute | solution.py:25
  113.3 15.6 %collective-permute-start.26 = (bf16[256,512]{1,0:T(8,128)(2,1)S(1)}, bf16[256,512]{1,0:T(8,128)(2,1)S(1)}, u32[]{:S(2)}, u32[]{:S(2)}) collective-permute-start(bf16[256,512]{1,0:T(8,128)(2,1)S(1)} %collective-permute-done.20), channel_id=1, source_target_pairs={{0,2},{1,3},{2,4},{3,5},{4,6},{5,7},{6,0},{7,1},{8,10},{9,11},{10,... | collective-permute-start | bytes 786440 | tf_op jit(solution)/shard_map/ppermute | solution.py:25
  113.4 15.5 %collective-permute-start.24 = (bf16[256,512]{1,0:T(8,128)(2,1)S(1)}, bf16[256,512]{1,0:T(8,128)(2,1)S(1)}, u32[]{:S(2)}, u32[]{:S(2)}) collective-permute-start(bf16[256,512]{1,0:T(8,128)(2,1)S(1)} %collective-permute-done.20), channel_id=1, source_target_pairs={{0,4},{1,5},{2,6},{3,7},{4,0},{5,1},{6,2},{7,3},{8,12},{9,13},{10,... | collective-permute-start | bytes 786440 | tf_op jit(solution)/shard_map/ppermute | solution.py:25
  117.4 12.0 %collective-permute-start.23 = (bf16[256,512]{1,0:T(8,128)(2,1)S(1)}, bf16[256,512]{1,0:T(8,128)(2,1)S(1)}, u32[]{:S(2)}, u32[]{:S(2)}) collective-permute-start(bf16[256,512]{1,0:T(8,128)(2,1)S(1)} %collective-permute-done.22), channel_id=1, source_target_pairs={{0,1},{1,0},{2,3},{3,2},{4,5},{5,4},{6,7},{7,6},{8,9},{9,8},{10,11... | collective-permute-start | bytes 786440 | tf_op jit(solution)/shard_map/ppermute | solution.py:25
  128.9 1.5 collective-permute-start.27
  128.9 1.9 %collective-permute-start.25 = (bf16[256,512]{1,0:T(8,128)(2,1)S(1)}, bf16[256,512]{1,0:T(8,128)(2,1)S(1)}, u32[]{:S(2)}, u32[]{:S(2)}) collective-permute-start(bf16[256,512]{1,0:T(8,128)(2,1)S(1)} %collective-permute-done.24), channel_id=1, source_target_pairs={{0,1},{1,0},{2,3},{3,2},{4,5},{5,4},{6,7},{7,6},{8,9},{9,8},{10,11... | collective-permute-start | bytes 786440 | tf_op jit(solution)/shard_map/ppermute | solution.py:25
  137.9 2.6 %copy-start.3 = (bf16[4,256,1024]{2,1,0:T(8,128)(2,1)S(1)}, bf16[4,256,1024]{2,1,0:T(8,128)(2,1)}, u32[]{:S(2)}) copy-start(bf16[4,256,1024]{2,1,0:T(8,128)(2,1)} %pad_maximum_fusion) | copy-start | bytes 6291460
  137.9 3.0 %copy-start.4 = (bf16[4,1024,256]{2,1,0:T(8,128)(2,1)S(1)}, bf16[4,1024,256]{2,1,0:T(8,128)(2,1)}, u32[]{:S(2)}) copy-start(bf16[4,1024,256]{2,1,0:T(8,128)(2,1)} %gather_fusion) | copy-start | bytes 6291460
  141.8 9.7 %collective-permute-start.32 = (bf16[512,256]{1,0:T(8,128)(2,1)S(1)}, bf16[512,256]{1,0:T(8,128)(2,1)S(1)}, u32[]{:S(2)}, u32[]{:S(2)}) collective-permute-start(bf16[512,256]{1,0:T(8,128)(2,1)S(1)} %get-tuple-element.14), channel_id=1, source_target_pairs={{0,24},{1,25},{2,26},{3,27},{4,28},{5,29},{6,30},{7,31},{8,0},{9,1... | collective-permute-start | bytes 786440 | tf_op jit(solution)/shard_map/ppermute | solution.py:25
  144.8 12.3 %collective-permute-start.28 = (bf16[512,256]{1,0:T(8,128)(2,1)S(1)}, bf16[512,256]{1,0:T(8,128)(2,1)S(1)}, u32[]{:S(2)}, u32[]{:S(2)}) collective-permute-start(bf16[512,256]{1,0:T(8,128)(2,1)S(1)} %slice.127), channel_id=1, source_target_pairs={{0,24},{1,25},{2,26},{3,27},{4,28},{5,29},{6,30},{7,31},{8,0},{9,1... | collective-permute-start | bytes 786440 | tf_op jit(solution)/shard_map/ppermute | solution.py:25
  145.6 10.4 %collective-permute-start.29 = (bf16[512,256]{1,0:T(8,128)(2,1)S(1)}, bf16[512,256]{1,0:T(8,128)(2,1)S(1)}, u32[]{:S(2)}, u32[]{:S(2)}) collective-permute-start(bf16[512,256]{1,0:T(8,128)(2,1)S(1)} %get-tuple-element.13), channel_id=1, source_target_pairs={{0,8},{1,9},{2,10},{3,11},{4,12},{5,13},{6,14},{7,15},{8,16},{9,17... | collective-permute-start | bytes 786440 | tf_op jit(solution)/shard_map/ppermute | solution.py:25
  147.7 14.0 %collective-permute-start.31 = (bf16[512,256]{1,0:T(8,128)(2,1)S(1)}, bf16[512,256]{1,0:T(8,128)(2,1)S(1)}, u32[]{:S(2)}, u32[]{:S(2)}) collective-permute-start(bf16[512,256]{1,0:T(8,128)(2,1)S(1)} %slice.126), channel_id=1, source_target_pairs={{0,8},{1,9},{2,10},{3,11},{4,12},{5,13},{6,14},{7,15},{8,16},{9,17... | collective-permute-start | bytes 786440 | tf_op jit(solution)/shard_map/ppermute | solution.py:25
  151.5 10.4 %collective-permute-start.33 = (bf16[512,256]{1,0:T(8,128)(2,1)S(1)}, bf16[512,256]{1,0:T(8,128)(2,1)S(1)}, u32[]{:S(2)}, u32[]{:S(2)}) collective-permute-start(bf16[512,256]{1,0:T(8,128)(2,1)S(1)} %fusion.56), channel_id=1, source_target_pairs={{0,24},{1,25},{2,26},{3,27},{4,28},{5,29},{6,30},{7,31},{8,0},{9,1... | collective-permute-start | bytes 786440 | tf_op jit(solution)/shard_map/ppermute | solution.py:25
  156.2 9.7 %collective-permute-start.30 = (bf16[512,256]{1,0:T(8,128)(2,1)S(1)}, bf16[512,256]{1,0:T(8,128)(2,1)S(1)}, u32[]{:S(2)}, u32[]{:S(2)}) collective-permute-start(bf16[512,256]{1,0:T(8,128)(2,1)S(1)} %fusion.58), channel_id=1, source_target_pairs={{0,8},{1,9},{2,10},{3,11},{4,12},{5,13},{6,14},{7,15},{8,16},{9,17... | collective-permute-start | bytes 786440 | tf_op jit(solution)/shard_map/ppermute | solution.py:25
Sparse Core Ops, SparseCore 0:
  65.6 42.5 all-gather.2

commit v2 on v1

v2 whole, which is shorter than its diff:
```python
import functools

import jax
import jax.numpy as jnp
from jax import lax
from jax.experimental import pallas as pl
from jax.experimental.pallas import tpu as pltpu
from jax.sharding import Mesh, PartitionSpec as P

AXES = ("x", "z", "y", "c")
N = 4
BF = jnp.bfloat16
F32 = jnp.float32


def move(value, where):
    pairs = []
    for x in range(N):
        for z in range(N):
            for y in range(N):
                for c in range(2):
                    tx, tz, ty, tc = where(x, z, y, c)
                    pairs.append(
                        (
                            ((x * N + z) * N + y) * 2 + c,
                            (((tx % N) * N + tz % N) * N + ty % N) * 2 + tc % 2,
                        )
                    )
    return lax.ppermute(value, AXES, pairs)


def swap(value):
    return move(value, lambda x, z, y, c: (x, z, y, 1 - c))


def along_y(value, step):
    return move(value, lambda x, z, y, c: (x, z, y + step, c))


def along_x(value, step):
    return move(value, lambda x, z, y, c: (x + step, z, y, c))


def add(*terms):
    total = terms[0].astype(F32)
    for term in terms[1:]:
        total = total + term.astype(F32)
    return total


def after(value, *others):
    return lax.optimization_barrier((value, *others))[0]


def product_kernel(n, width, n_in, emit, starts, rows, weights, *refs):
    extra, outs = refs[:n_in], refs[n_in:-2]
    blocks, arrived = refs[-2:]
    copies = []
    for i in range(n):
        columns = pl.ds(pl.multiple_of(starts[i], width), width)
        copies.append(pltpu.make_async_copy(weights.at[:, columns], blocks.at[i], arrived.at[i]))
        copies[i].start()
    for i in range(n):
        copies[i].wait()
        emit(i, jnp.dot(rows[...], blocks[i], preferred_element_type=F32), starts, extra, outs)


def products(rows, weights, starts, n, width, emit, out_shapes, extra=()):
    depth = rows.shape[1]
    whole = pl.BlockSpec(memory_space=pltpu.VMEM)
    return pl.pallas_call(
        functools.partial(product_kernel, n, width, len(extra), emit),
        out_shape=out_shapes,
        in_specs=[pl.BlockSpec(memory_space=pltpu.SMEM), whole, pl.BlockSpec(memory_space=pltpu.HBM)] + [whole] * len(extra),
        out_specs=[whole] * len(out_shapes),
        scratch_shapes=[pltpu.VMEM((n, depth, width), BF), pltpu.SemaphoreType.DMA((n,))],
        compiler_params=pltpu.CompilerParams(vmem_limit_bytes=40 << 20),
        cost_estimate=pl.CostEstimate(
            flops=2 * n * rows.shape[0] * depth * width, bytes_accessed=2 * n * depth * width, transcendentals=0
        ),
    )(starts, rows, weights, *extra)


def shape(rows, columns, dtype):
    return jax.ShapeDtypeStruct((rows, columns), dtype)


def project(context, w_out, width):
    y, c = lax.axis_index("y"), lax.axis_index("c")
    tokens = context.shape[0]
    half = tokens // 2

    def starts(core, *steps):
        return jnp.stack([(lax.rem(y + d + N, N) * 2 + core) * width for d in steps]).astype(jnp.int32)

    def emit_plain(i, value, starts, extra, outs):
        outs[i][...] = value.astype(BF)

    (send_2,) = products(context, w_out, starts(1 - c, 2), 1, width, emit_plain, [shape(tokens, width, BF)])
    got_2 = swap(send_2)
    sends = products(
        context, w_out, starts(1 - c, 1, -1, 0), 3, width, emit_plain, [shape(tokens, width, BF)] * 3
    )
    got_r, got_l, got_o = [swap(s) for s in sends]

    def emit_far(i, value, starts, extra, outs):
        value = value + extra[0][...].astype(F32)
        outs[0][...] = value[:half].astype(BF)
        outs[1][...] = value[half:].astype(BF)

    far_a, far_b = products(
        context, w_out, starts(c, 2), 1, width, emit_far, [shape(half, width, BF)] * 2, (got_2,)
    )
    from_left, from_right = along_y(far_a, 1), along_y(far_b, -1)

    def emit_near(i, value, starts, extra, outs):
        value = value + extra[i][...].astype(F32)
        outs[2 * i][...] = value[:half].astype(outs[2 * i].dtype)
        outs[2 * i + 1][...] = value[half:].astype(outs[2 * i + 1].dtype)

    right_a, right_b, left_a, left_b, own_a, own_b = products(
        context,
        w_out,
        starts(c, 1, -1, 0),
        3,
        width,
        emit_near,
        [shape(half, width, t) for t in (F32, BF, BF, F32, F32, F32)],
        (got_r, got_l, got_o),
    )
    low_b, up_a = along_y(right_b, 1), along_y(left_a, -1)
    low_a = along_y(add(right_a, from_left).astype(BF), 1)
    up_b = along_y(add(left_b, from_right).astype(BF), -1)
    return add(own_a, up_a, low_a), add(own_b, low_b, up_b), (low_b, up_a)


def join(rows, w_join, width):
    y, c = lax.axis_index("y"), lax.axis_index("c")
    half = rows.shape[0] // 2

    def emit(i, value, starts, extra, outs):
        first, second = value[:half], value[half:]
        mine = starts[2] == 0
        outs[2 * i][...] = jnp.where(mine, second, first).astype(BF)
        outs[2 * i + 1][...] = jnp.where(mine, first, second)

    def pair(*steps):
        starts = jnp.stack([lax.rem(y + d + N, N) * width for d in steps] + [c]).astype(jnp.int32)
        shapes = [shape(half, width, BF), shape(half, width, F32)] * 2
        return products(rows, w_join, starts, 2, width, emit, shapes)

    s2, o2, s1, o1 = pair(2, 1)
    g2, g1 = swap(s2), swap(s1)
    s3, o3, s0, o0 = pair(-1, 0)
    g3, g0 = swap(s3), swap(s0)
    terms = [along_y(add(o, g).astype(BF), d) for o, g, d in ((o2, g2, 2), (o1, g1, 1), (o3, g3, -1))]
    return add(o0, g0, *terms)


def body(
    context, w_out, residual, norm_gain, w_join, dec_state, gate_s, gate_h, gate_bias, owner, pad_mask, cotangent
):
    x, z, y, c = (lax.axis_index(a) for a in AXES)
    n_owner = N * N
    tokens, width = residual.shape
    half = tokens // 2
    slot_rows, features = dec_state.shape
    most = slot_rows // n_owner

    onehot = (owner == jnp.arange(n_owner, dtype=jnp.int32)[None, :]).astype(BF)
    ahead = jnp.tril(jnp.ones((tokens, tokens), BF), -1)
    before = jnp.dot(ahead, onehot, preferred_element_type=F32)
    rank = jnp.sum(before * onehot.astype(F32), axis=1).astype(jnp.int32)
    slots = owner[:, 0] * most + rank
    select = (slots[:, None] == jnp.arange(slot_rows, dtype=jnp.int32)[None, :]).astype(BF)

    sum_a, sum_b, late = project(context, w_out, width)

    both = jnp.concatenate([dec_state, cotangent], axis=1).reshape(n_owner, most, 2 * features)
    both = lax.all_to_all(after(both, *late), ("x", "z"), 0, 0, tiled=True).reshape(slot_rows, 2 * features)
    both = jnp.dot(select, both, preferred_element_type=F32).astype(BF)
    first = c == 0
    keep = jnp.where(first, both[:half], both[half:])
    got = swap(jnp.where(first, both[half:], both[:half]))

    def widen(mine, other):
        return jnp.where(
            first, jnp.concatenate([mine, other], axis=-1), jnp.concatenate([other, mine], axis=-1)
        )

    state_t = widen(keep[:, :features], got[:, :features]).astype(F32)
    outer_t = widen(keep[:, features:], got[:, features:]).astype(F32)
    params = jnp.stack([gate_s, gate_h, gate_bias])
    params_t = widen(params, swap(params))

    gain, mask = norm_gain[None, :], pad_mask.astype(F32)[:, None]
    residual = residual.astype(F32)
    mixed = jnp.concatenate([residual[:half] + sum_a, residual[half:] + sum_b], axis=0)
    squares = jnp.sum(mixed * mixed, axis=1)
    rows = (mixed * gain * mask).astype(BF)
    rows_z = lax.all_gather(rows, "z", axis=0, tiled=True)

    total = squares.reshape(2, -1)
    total = total + swap(total)
    total = total + move(total, lambda x, z, y, c: (x, z, y ^ 1, c))
    total = total + move(total, lambda x, z, y, c: (x, z, y ^ 2, c))
    scale = lax.rsqrt(total / (width * N * 2) + 1e-05)
    scale = jnp.where(first, scale[0], scale[1])[:, None]

    hidden = (join(rows, w_join, 2 * features) * scale).astype(BF)

    def gates(params, state, hidden):
        gate = jax.nn.sigmoid(params[0][None, :] * state + params[1][None, :] * hidden + params[2][None, :])
        return gate, gate * (1.0 - gate) * hidden

    gate, slope = gates(params_t, state_t, hidden.astype(F32))
    grad = (outer_t * (gate + slope * params_t[1][None, :]) * scale).astype(BF)

    grad = grad.reshape(half, N, -1).transpose(1, 0, 2)
    grad = lax.all_to_all(grad, "z", 0, 0, tiled=True)
    pieces = [grad] + [along_y(grad, -d) for d in (1, 2, 3)]
    swapped = [swap(piece) for piece in pieces]
    grads = jnp.stack(
        [jnp.where(first, jnp.concatenate([a, b], axis=1), jnp.concatenate([b, a], axis=1)) for a, b in zip(pieces, swapped)]
    )
    grads = grads.reshape(N, N * tokens, -1)

    def grad_term(step, part):
        columns = lax.dynamic_index_in_dim(grads, lax.rem(x + step - y + 2 * N, N), 0, keepdims=False)
        rows = rows_z[:, : width // 2] if part == 0 else rows_z[:, width // 2 :]
        return lax.dot_general(rows, columns, (((0,), (0,)), ((), ())), preferred_element_type=F32)

    from_left = along_x(grad_term(2, 0).astype(BF), 1)
    from_right = along_x(grad_term(2, 1).astype(BF), -1)
    low_b = along_x(grad_term(1, 1).astype(BF), 1)
    up_a = along_x(grad_term(-1, 0).astype(BF), -1)
    low_a = along_x(add(grad_term(1, 0), from_left).astype(BF), 1)
    up_b = along_x(add(grad_term(-1, 1), from_right).astype(BF), -1)
    join_grad = jnp.concatenate(
        [add(grad_term(0, 0), up_a, low_a), add(grad_term(0, 1), low_b, up_b)], axis=0
    )

    late_hidden = after(hidden, swapped[0])
    keep = jnp.where(first, late_hidden[:, :features], late_hidden[:, features:])
    got = swap(jnp.where(first, late_hidden[:, features:], late_hidden[:, :features]))
    rows_h = jnp.where(first, jnp.concatenate([keep, got], axis=0), jnp.concatenate([got, keep], axis=0))
    placed = lax.dot_general(select, rows_h, (((0,), (0,)), ((), ())), preferred_element_type=F32)
    placed = placed.astype(BF).reshape(n_owner, most, features)
    placed = lax.all_to_all(placed, ("x", "z"), 0, 0, tiled=True).reshape(slot_rows, features).astype(F32)
    state = dec_state.astype(F32)
    gate, slope = gates(params, state, placed)
    joined = (state + gate * placed).astype(BF)
    state_grad = (cotangent.astype(F32) * (1.0 + slope * gate_s[None, :])).astype(BF)
    return joined, state_grad, join_grad


def solution(mesh):
    fine = Mesh(mesh.devices.reshape(N, N, N, 2), AXES)
    dp, mp = ("x", "z"), ("y", "c")
    in_specs = (
        P(dp, mp),
        P(mp, None),
        P(dp, mp),
        P(mp),
        P(mp, None),
        P(dp, mp),
        P(mp),
        P(mp),
        P(mp),
        P(dp, None),
        P(dp),
        P(dp, mp),
    )
    out_specs = (P(dp, mp), P(dp, mp), P(mp, dp))
    return jax.shard_map(body, mesh=fine, in_specs=in_specs, out_specs=out_specs, check_vma=False)
```

time: 175 us -> 176 us (level)
  matrix products: 37.9 us -> 7.12 us
  starting transfers between devices: 62.9 us -> 43.3 us
  Pallas kernels: 0 us -> 13 us
  waiting for transfers between devices: 39.4 us -> 51.7 us
  blocking collectives: 0 us -> 11.3 us
  local copies, waits for them, and re-layouts: 8.34 us -> 19.5 us
  other arithmetic: 10.7 us -> 14.8 us
    dot_general x21 -> x9, matrix products: 37.2 us -> 6.38 us  [the longest x8 5.24 us: grad_term(): lax.dot_general(rows, columns, (((0,), (0,)), ((), ())), preferred_elemen...]
    unnamed x28 -> x46, local copies, waits for them, and re-layouts: 1.42 us -> 18.9 us
    ppermute x34 -> x36, starting transfers between devices: 44.3 us -> 30.4 us  [move(): return lax.ppermute(value, AXES, pairs)]
    pallas_call x0 -> x6, Pallas kernels: none -> 13 us  [products(): pl.pallas_call(functools.partial(product_kernel, n, width, len(extra), em...]
    all_to_all x0 -> x1, blocking collectives: none -> 11.3 us  [body(): grad = lax.all_to_all(grad, 'z', 0, 0, tiled=True)]
    all_to_all x1, waiting for transfers between devices: 0.01 us -> 9.49 us  [body(): lax.all_to_all(placed, ('x', 'z'), 0, 0, tiled=True)]
    all_to_all x1, starting transfers between devices: 10.5 us -> 4.97 us  [body(): lax.all_to_all(placed, ('x', 'z'), 0, 0, tiled=True)]
    all_gather x1 -> x0, local copies, waits for them, and re-layouts: 3.27 us -> none  [body(): rows_t = lax.all_gather(rows.T, 'x')]
  transfers between devices with their start and end apart: 37 -> 39, of which waited for: 14 -> 11; matrix products, arithmetic and copies ran while one was open for 23% -> 10% of each run, Pallas kernels for 0% -> 7%
where the time goes in v2:
time: 176 us; the launch traced here: 175 us
  waiting for transfers between devices  51.7 us (29%)
  starting transfers between devices  43.3 us (25%)
  local copies, waits for them, and re-layouts  19.5 us (11%)
  other arithmetic  14.8 us (8%)
  between operations  14.6 us (8%)
  Pallas kernels  13 us (7%)
  blocking collectives  11.3 us (6%)
  matrix products  7.12 us (4%)
    ppermute x36, waiting for transfers between devices, move(): return lax.ppermute(value, AXES, pairs)  41.5 us
    ppermute x36, starting transfers between devices, move(): return lax.ppermute(value, AXES, pairs)  30.4 us
    unnamed x46, local copies, waits for them, and re-layouts  18.9 us
    pallas_call x6, Pallas kernels, products(): pl.pallas_call(functools.partial(product_kernel, n, width, len(extra), em...  13 us
    all_to_all x1, blocking collectives, body(): grad = lax.all_to_all(grad, 'z', 0, 0, tiled=True)  11.3 us
    all_to_all x1, waiting for transfers between devices, body(): lax.all_to_all(placed, ('x', 'z'), 0, 0, tiled=True)  9.49 us
    all_to_all x1, starting transfers between devices, body(): lax.all_to_all(after(both, *late), ('x', 'z'), 0, 0, tiled=True)  7.88 us
    dot_general x8, matrix products, grad_term(): lax.dot_general(rows, columns, (((0,), (0,)), ((), ())), preferred_elemen...  5.24 us
  transfers between devices with their start and end apart: 39, of which 11 were waited for; matrix products, arithmetic and copies ran while one was open for 10% of the time, Pallas kernels for 7%

profile of v2, /device:TPU:0, one launch (start us, length us, event | category | flops | bytes accessed | tf_op | source)
XLA Modules:
  0.0 175.3 jit_solution(7385666444683188483)
XLA Ops:
  7.2 3.4 %copy-done = bf16[512,8192]{1,0:T(8,128)(2,1)S(1)} copy-done((bf16[512,8192]{1,0:T(8,128)(2,1)S(1)}, bf16[512,8192]{1,0:T(8,128)(2,1)}, u32[]{:S(2)}) %copy-start) | copy-done | bytes 8388632
  10.6 0.9 copy-done.6
  11.5 0.6 shard_map.141
  12.5 3.4 %copy-done.1 = bf16[512,8192]{1,0:T(8,128)(2,1)S(1)} copy-done((bf16[512,8192]{1,0:T(8,128)(2,1)S(1)}, bf16[512,8192]{1,0:T(8,128)(2,1)}, u32[]{:S(2)}) %copy-start.1) | copy-done | bytes 8388632
  15.9 3.0 %shard_map.139 = (bf16[256,1024]{1,0:T(8,128)(2,1)}, bf16[256,1024]{1,0:T(8,128)(2,1)}, bf16[256,1024]{1,0:T(8,128)(2,1)S(1)}) custom-call(s32[3]{0:T(128)S(1)} %pad_add_fusion.1.starts, bf16[256,512]{1,0:T(8,128)(2,1)S(1)} %copy-done.7, bf16[512,8192]{1,0:T(8,128)(2,1)S(1)} %copy-done.1), custom_call_target="tpu_custom_call" | custom-call | flops 805306368 | bytes 3145728 | tf_op jit(solution)/shard_map/pallas_call | solution.py:71
  19.9 0.6 pad_maximum_fusion.4
  21.0 3.4 %copy-done.2 = bf16[512,8192]{1,0:T(8,128)(2,1)S(1)} copy-done((bf16[512,8192]{1,0:T(8,128)(2,1)S(1)}, bf16[512,8192]{1,0:T(8,128)(2,1)}, u32[]{:S(2)}) %copy-start.2) | copy-done | bytes 8388632
  24.4 0.6 shard_map.142
  25.0 1.7 collective-permute-start.5
  26.8 0.6 multiply_add_fusion
  27.4 1.6 collective-permute-start.8
  28.9 3.0 %shard_map.140 = (f32[128,1024]{1,0:T(8,128)S(1)}, bf16[128,1024]{1,0:T(8,128)(2,1)}, bf16[128,1024]{1,0:T(8,128)(2,1)}, f32[128,1024]{1,0:T(8,128)S(1)}, f32[12...) custom-call(s32[3]{0:T(128)S(1)} %pad_add_fusion.starts, bf16[256,512]{1,0:T(8,128)(2,1)S(1)} %copy-done.7, ...), custom_call_target="tpu_custom_call" | custom-call | flops 805306368 | bytes 3145728 | tf_op jit(solution)/shard_map/pallas_call | solution.py:71
  32.0 2.0 %collective-permute-start.3 = (bf16[128,1024]{1,0:T(8,128)(2,1)}, bf16[128,1024]{1,0:T(8,128)(2,1)S(1)}, u32[]{:S(2)}, u32[]{:S(2)}) collective-permute-start(bf16[128,1024]{1,0:T(8,128)(2,1)} %get-tuple-element.28), channel_id=1, source_target_pairs={{0,6},{1,7},{2,0},{3,1},{4,2},{5,3},{6,4},{7,5},{8,14},{9,15},{10,... | collective-permute-start | bytes 786440 | tf_op jit(solution)/shard_map/ppermute | solution.py:29
  34.1 0.9 collective-permute-done.5
  35.5 0.9 collective-permute-done.8
  36.4 3.0 %collective-permute-start.9 = (bf16[128,1024]{1,0:T(8,128)(2,1)S(1)}, bf16[128,1024]{1,0:T(8,128)(2,1)S(1)}, u32[]{:S(2)}, u32[]{:S(2)}) collective-permute-start(bf16[128,1024]{1,0:T(8,128)(2,1)S(1)} %add_convert_fusion.5), channel_id=1, source_target_pairs={{0,6},{1,7},{2,0},{3,1},{4,2},{5,3},{6,4},{7,5},{8,14},{9,15},{10,... | collective-permute-start | bytes 786440 | tf_op jit(solution)/shard_map/ppermute | solution.py:29
  39.4 1.0 pad_maximum_fusion.3
  40.6 0.7 convert_element_type.172
  41.3 0.8 maximum_select_fusion.8
  42.1 2.5 %collective-permute-done.7 = bf16[128,1024]{1,0:T(8,128)(2,1)S(1)} collective-permute-done((bf16[128,1024]{1,0:T(8,128)(2,1)}, bf16[128,1024]{1,0:T(8,128)(2,1)S(1)}, u32[]{:S(2)}, u32[]{:S(2)}) %collective-permute-start.7) | collective-permute-done | bytes 262176 | tf_op jit(solution)/shard_map/ppermute | solution.py:29
  44.6 4.1 %collective-permute-done.6 = bf16[128,1024]{1,0:T(8,128)(2,1)S(1)} collective-permute-done((bf16[128,1024]{1,0:T(8,128)(2,1)S(1)}, bf16[128,1024]{1,0:T(8,128)(2,1)S(1)}, u32[]{:S(2)}, u32[]{:S(2)}) %collective-permute-start.6) | collective-permute-done | bytes 262176 | tf_op jit(solution)/shard_map/ppermute | solution.py:29
  49.5 1.0 multiply_convert_fusion
  50.5 0.6 fusion.88
  51.1 7.9 %all-to-all-start = ((bf16[16,24,1024]{2,1,0:T(8,128)(2,1)}), bf16[16,24,1024]{2,1,0:T(8,128)(2,1)S(1)}, u32[]{:S(2)}, u32[]{:S(2)}) async-start(bf16[16,24,1024]{2,1,0:T(8,128)(2,1)} %bitcast.18), calls=%async_computation | async-start | bytes 1572864 | tf_op jit(solution)/shard_map/all_to_all | solution.py:180
  59.0 0.7 all-gather.2.cloned.1.call-update
  59.8 3.4 %copy-done.3 = bf16[1024,4096]{1,0:T(8,128)(2,1)S(1)} copy-done((bf16[1024,4096]{1,0:T(8,128)(2,1)S(1)}, bf16[1024,4096]{1,0:T(8,128)(2,1)}, u32[]{:S(2)}) %copy-start.3) | copy-done | bytes 8388632
  63.2 2.8 %shard_map.144 = (bf16[128,1024]{1,0:T(8,128)(2,1)S(1)}, f32[128,1024]{1,0:T(8,128)S(1)}, bf16[128,1024]{1,0:T(8,128)(2,1)S(1)}, f32[128,1024]{1,0:T(8,128)S(1)}) custom-call(s32[3]{0:T(128)S(1)} %get-tuple-element.65.starts, bf16[256,1024]{1,0:T(8,128)(2,1)S(1)} %copy-done.5, bf16[1024,4096]{1,0:T(8,128)(2,1)S(1)} %copy-done.3), custom_call_target="tpu_custom_call" | custom-call | flops 1073741824 | bytes 4194304 | tf_op jit(solution)/shard_map/pallas_call | solution.py:71
  66.6 2.5 %collective-permute-start.19 = (f32[2,128]{1,0:T(2,128)S(1)}, f32[2,128]{1,0:T(2,128)S(1)}, u32[]{:S(2)}, u32[]{:S(2)}) collective-permute-start(f32[2,128]{1,0:T(2,128)S(1)} %fusion.90), channel_id=1, source_target_pairs={{0,4},{1,5},{2,6},{3,7},{4,0},{5,1},{6,2},{7,3},{8,12},{9,13},{10,... | collective-permute-start | bytes 3080 | tf_op jit(solution)/shard_map/ppermute | solution.py:29
  69.1 3.8 %copy-done.4 = bf16[1024,4096]{1,0:T(8,128)(2,1)S(1)} copy-done((bf16[1024,4096]{1,0:T(8,128)(2,1)S(1)}, bf16[1024,4096]{1,0:T(8,128)(2,1)}, u32[]{:S(2)}) %copy-start.4) | copy-done | bytes 8388632
  73.0 2.8 %shard_map.143 = (bf16[128,1024]{1,0:T(8,128)(2,1)S(1)}, f32[128,1024]{1,0:T(8,128)S(1)}, bf16[128,1024]{1,0:T(8,128)(2,1)S(1)}, f32[128,1024]{1,0:T(8,128)S(1)}) custom-call(s32[3]{0:T(128)S(1)} %get-tuple-element.64.starts, bf16[256,1024]{1,0:T(8,128)(2,1)S(1)} %copy-done.5, bf16[1024,4096]{1,0:T(8,128)(2,1)S(1)} %copy-done.4), custom_call_target="tpu_custom_call" | custom-call | flops 1073741824 | bytes 4194304 | tf_op jit(solution)/shard_map/pallas_call | solution.py:71
  75.8 0.5 collective-permute-start.10
  76.4 0.5 fusion.82
  76.9 0.8 add_convert_fusion.4
  77.6 0.7 collective-permute-start.12
  78.3 0.8 add_convert_fusion.3
  79.1 2.2 %collective-permute-start.14 = (bf16[128,1024]{1,0:T(8,128)(2,1)}, bf16[128,1024]{1,0:T(8,128)(2,1)}, u32[]{:S(2)}, u32[]{:S(2)}) collective-permute-start(bf16[128,1024]{1,0:T(8,128)(2,1)} %add_convert_fusion.3), channel_id=1, source_target_pairs={{0,2},{1,3},{2,4},{3,5},{4,6},{5,7},{6,0},{7,1},{8,10},{9,11},{10,... | collective-permute-start | bytes 786440 | tf_op jit(solution)/shard_map/ppermute | solution.py:29
  82.0 1.0 add_convert_fusion.2
  83.0 1.1 collective-permute-start.16
  84.2 4.5 %collective-permute-done.12 = bf16[128,1024]{1,0:T(8,128)(2,1)} collective-permute-done((bf16[128,1024]{1,0:T(8,128)(2,1)}, bf16[128,1024]{1,0:T(8,128)(2,1)}, u32[]{:S(2)}, u32[]{:S(2)}) %collective-permute-start.12) | collective-permute-done | bytes 262176 | tf_op jit(solution)/shard_map/ppermute | solution.py:29
  88.6 4.9 %collective-permute-done.14 = bf16[128,1024]{1,0:T(8,128)(2,1)} collective-permute-done((bf16[128,1024]{1,0:T(8,128)(2,1)}, bf16[128,1024]{1,0:T(8,128)(2,1)}, u32[]{:S(2)}, u32[]{:S(2)}) %collective-permute-start.14) | collective-permute-done | bytes 262176 | tf_op jit(solution)/shard_map/ppermute | solution.py:29
  93.6 1.6 fusion.34
  95.2 11.3 %all_to_all.15 = bf16[4,128,256]{2,1,0:T(8,128)(2,1)S(1)} all-to-all(bf16[4,128,256]{2,1,0:T(8,128)(2,1)S(1)} %bitcast.94), channel_id=1, replica_groups=mesh['x'=4,'z'=4,'y'=4,'c'=2] {'z'}, dimensions={0} | all-to-all | bytes 524288 | tf_op jit(solution)/shard_map/all_to_all | solution.py:220
  106.6 2.1 %collective-permute-start.24 = (bf16[4,128,256]{2,1,0:T(8,128)(2,1)S(1)}, bf16[4,128,256]{2,1,0:T(8,128)(2,1)S(1)}, u32[]{:S(2)}, u32[]{:S(2)}) collective-permute-start(bf16[4,128,256]{2,1,0:T(8,128)(2,1)S(1)} %all_to_all.15), channel_id=1, source_target_pairs={{0,6},{1,7},{2,0},{3,1},{4,2},{5,3},{6,4},{7,5},{8,14},{9,15},{10,... | collective-permute-start | bytes 786440 | tf_op jit(solution)/shard_map/ppermute | solution.py:29
  108.7 0.9 collective-permute-start.28
  109.7 10.9 %collective-permute-done.24 = bf16[4,128,256]{2,1,0:T(8,128)(2,1)S(1)} collective-permute-done((bf16[4,128,256]{2,1,0:T(8,128)(2,1)S(1)}, bf16[4,128,256]{2,1,0:T(8,128)(2,1)S(1)}, u32[]{:S(2)}, u32[]{:S(2)}) %collective-permute-start.24) | collective-permute-done | bytes 262176 | tf_op jit(solution)/shard_map/ppermute | solution.py:29
  120.8 0.6 collective-permute-start.27
  121.4 2.6 %collective-permute-done.28 = bf16[4,128,256]{2,1,0:T(8,128)(2,1)S(1)} collective-permute-done((bf16[4,128,256]{2,1,0:T(8,128)(2,1)S(1)}, bf16[4,128,256]{2,1,0:T(8,128)(2,1)S(1)}, u32[]{:S(2)}, u32[]{:S(2)}) %collective-permute-start.28) | collective-permute-done | bytes 262176 | tf_op jit(solution)/shard_map/ppermute | solution.py:29
  124.0 1.1 convolution_convert_fusion.1
  125.1 5.0 %all-to-all-start.2 = ((bf16[16,24,512]{2,1,0:T(8,128)(2,1)}), bf16[16,24,512]{2,1,0:T(8,128)(2,1)S(1)}, u32[]{:S(2)}, u32[]{:S(2)}) async-start(bf16[16,24,512]{2,1,0:T(8,128)(2,1)} %bitcast.27), calls=%async_computation.2 | async-start | bytes 786432 | tf_op jit(solution)/shard_map/all_to_all | solution.py:249
  131.1 9.5 %all-to-all-done.2 = bf16[16,24,512]{2,1,0:T(8,128)(2,1)S(1)} async-done(((bf16[16,24,512]{2,1,0:T(8,128)(2,1)}), bf16[16,24,512]{2,1,0:T(8,128)(2,1)S(1)}, u32[]{:S(2)}, u32[]{:S(2)}) %all-to-all-start.2) | async-done | bytes 393248 | tf_op jit(solution)/shard_map/all_to_all | solution.py:249
  140.6 2.4 %fusion.11 = (bf16[384,512]{1,0:T(8,128)(2,1)}, bf16[384,512]{1,0:T(8,128)(2,1)}) fusion(bf16[384,512]{1,0:T(8,128)(2,1)S(1)} %copy-done.8, bf16[16,24,512]{2,1,0:T(8,128)(2,1)S(1)} %all-to-all-done.2, bf16[384,512]{1,0:T(8,128)(2,1)} %param.17, f32[512]{0:T(512)S(1)} %copy-done.11, f32[512]{0:T(512)S(1)} %copy-done.12, f32[512]{0:T(512)S(1)} %copy-done.14), kind=kLoop, calls=%fused_computation.29 | loop fusion | flops 3932160 | bytes 1972224 | tf_op jit(solution)/shard_map/convert_element_type | solution.py:253
  143.0 1.9 %convolution_convert_fusion.5 = bf16[512,256]{1,0:T(8,128)(2,1)S(1)} fusion(bf16[1024,1024]{1,0:T(8,128)(2,1)} %all-gather.2.cloned.1.call-done, bf16[4,1024,256]{2,1,0:T(8,128)(2,1)S(1)} %pad_maximum_fusion, s32[]{:T(128)S(6)} %select_n.174), kind=kOutput, calls=%fused_computation.6 | convolution fusion | flops 268566528 | bytes 1835012 | tf_op jit(solution)/shard_map/dot_general | solution.py:231
  144.9 1.4 collective-permute-start.30
  146.2 0.5 convolution_convert_fusion.4
  146.7 0.8 collective-permute-start.31
  147.5 0.5 convolution_convert_fusion.3
  148.1 0.5 convolution_convert_fusion.2
  148.6 3.3 %collective-permute-start.34 = (bf16[512,256]{1,0:T(8,128)(2,1)S(1)}, bf16[512,256]{1,0:T(8,128)(2,1)S(1)}, u32[]{:S(2)}, u32[]{:S(2)}) collective-permute-start(bf16[512,256]{1,0:T(8,128)(2,1)S(1)} %convolution_convert_fusion.2), channel_id=1, source_target_pairs={{0,96},{1,97},{2,98},{3,99},{4,100},{5,101},{6,102},{7,103},{8,104... | collective-permute-start | bytes 786440 | tf_op jit(solution)/shard_map/ppermute | solution.py:29
  151.9 5.4 %collective-permute-done.31 = bf16[512,256]{1,0:T(8,128)(2,1)S(1)} collective-permute-done((bf16[512,256]{1,0:T(8,128)(2,1)S(1)}, bf16[512,256]{1,0:T(8,128)(2,1)S(1)}, u32[]{:S(2)}, u32[]{:S(2)}) %collective-permute-start.31) | collective-permute-done | bytes 262176 | tf_op jit(solution)/shard_map/ppermute | solution.py:29
  157.3 0.5 add_convert_fusion.1
  157.8 0.5 add_convert_fusion
  158.3 3.3 %collective-permute-start.35 = (bf16[512,256]{1,0:T(8,128)(2,1)S(1)}, bf16[512,256]{1,0:T(8,128)(2,1)S(1)}, u32[]{:S(2)}, u32[]{:S(2)}) collective-permute-start(bf16[512,256]{1,0:T(8,128)(2,1)S(1)} %add_convert_fusion), channel_id=1, source_target_pairs={{0,96},{1,97},{2,98},{3,99},{4,100},{5,101},{6,102},{7,103},{8,104... | collective-permute-start | bytes 786440 | tf_op jit(solution)/shard_map/ppermute | solution.py:29
  161.6 4.8 %collective-permute-done.32 = bf16[512,256]{1,0:T(8,128)(2,1)S(1)} collective-permute-done((bf16[512,256]{1,0:T(8,128)(2,1)S(1)}, bf16[512,256]{1,0:T(8,128)(2,1)S(1)}, u32[]{:S(2)}, u32[]{:S(2)}) %collective-permute-start.32) | collective-permute-done | bytes 262176 | tf_op jit(solution)/shard_map/ppermute | solution.py:29
  167.4 1.0 pad_maximum_fusion.2
  (115 shorter events, 7.2 us)
Async XLA Ops:
  7.2 3.4 %copy-start = (bf16[512,8192]{1,0:T(8,128)(2,1)S(1)}, bf16[512,8192]{1,0:T(8,128)(2,1)}, u32[]{:S(2)}) copy-start(bf16[512,8192]{1,0:T(8,128)(2,1)} %weights.9) | copy-start | bytes 25165828
  10.6 0.9 copy-start.6
  11.5 0.9 copy-start.7
  12.2 8.8 %collective-permute-start.4 = (bf16[256,1024]{1,0:T(8,128)(2,1)S(1)}, bf16[256,1024]{1,0:T(8,128)(2,1)S(1)}, u32[]{:S(2)}, u32[]{:S(2)}) collective-permute-start(bf16[256,1024]{1,0:T(8,128)(2,1)S(1)} %shard_map.141), channel_id=1, source_target_pairs={{0,1},{1,0},{2,3},{3,2},{4,5},{5,4},{6,7},{7,6},{8,9},{9,8},{10,11... | collective-permute-start | bytes 1572872 | tf_op jit(solution)/shard_map/ppermute | solution.py:29
  12.5 3.4 %copy-start.1 = (bf16[512,8192]{1,0:T(8,128)(2,1)S(1)}, bf16[512,8192]{1,0:T(8,128)(2,1)}, u32[]{:S(2)}) copy-start(bf16[512,8192]{1,0:T(8,128)(2,1)} %weights.9) | copy-start | bytes 25165828
  15.8 4.0 %copy-start.11 = (f32[512]{0:T(512)S(1)}, f32[512]{0:T(512)}, u32[]{:S(2)}) copy-start(f32[512]{0:T(512)} %param.20) | copy-start | bytes 6148
  15.8 4.0 %copy-start.12 = (f32[512]{0:T(512)S(1)}, f32[512]{0:T(512)}, u32[]{:S(2)}) copy-start(f32[512]{0:T(512)} %param.19) | copy-start | bytes 6148
  15.9 4.0 %copy-start.13 = (f32[512]{0:T(512)S(1)}, f32[512]{0:T(512)}, u32[]{:S(2)}) copy-start(f32[512]{0:T(512)} %param.18) | copy-start | bytes 6148
  15.9 4.8 %copy-start.21 = (s32[256,1]{0,1:T(1,128)S(1)}, s32[256,1]{0,1:T(1,128)}, u32[]{:S(2)}) copy-start(s32[256,1]{0,1:T(1,128)} %param.21) | copy-start | bytes 3076
  18.9 8.5 %collective-permute-start = (bf16[256,1024]{1,0:T(8,128)(2,1)}, bf16[256,1024]{1,0:T(8,128)(2,1)S(1)}, u32[]{:S(2)}, u32[]{:S(2)}) collective-permute-start(bf16[256,1024]{1,0:T(8,128)(2,1)} %get-tuple-element.24), channel_id=1, source_target_pairs={{0,1},{1,0},{2,3},{3,2},{4,5},{5,4},{6,7},{7,6},{8,9},{9,8},{10,11... | collective-permute-start | bytes 1572872 | tf_op jit(solution)/shard_map/ppermute | solution.py:29
  19.4 9.6 %collective-permute-start.1 = (bf16[256,1024]{1,0:T(8,128)(2,1)}, bf16[256,1024]{1,0:T(8,128)(2,1)S(1)}, u32[]{:S(2)}, u32[]{:S(2)}) collective-permute-start(bf16[256,1024]{1,0:T(8,128)(2,1)} %get-tuple-element.25), channel_id=1, source_target_pairs={{0,1},{1,0},{2,3},{3,2},{4,5},{5,4},{6,7},{7,6},{8,9},{9,8},{10,11... | collective-permute-start | bytes 1572872 | tf_op jit(solution)/shard_map/ppermute | solution.py:29
  19.5 9.5 %collective-permute-start.2 = (bf16[256,1024]{1,0:T(8,128)(2,1)S(1)}, bf16[256,1024]{1,0:T(8,128)(2,1)S(1)}, u32[]{:S(2)}, u32[]{:S(2)}) collective-permute-start(bf16[256,1024]{1,0:T(8,128)(2,1)S(1)} %get-tuple-element.26), channel_id=1, source_target_pairs={{0,1},{1,0},{2,3},{3,2},{4,5},{5,4},{6,7},{7,6},{8,9},{9,8},{10,11... | collective-permute-start | bytes 1572872 | tf_op jit(solution)/shard_map/ppermute | solution.py:29
  20.5 20.8 %collective-permute-start.21 = (f32[3,512]{1,0:T(4,128)}, f32[3,512]{1,0:T(4,128)}, u32[]{:S(2)}, u32[]{:S(2)}) collective-permute-start(f32[3,512]{1,0:T(4,128)} %pad_maximum_fusion.4), channel_id=1, source_target_pairs={{0,1},{1,0},{2,3},{3,2},{4,5},{5,4},{6,7},{7,6},{8,9},{9,8},{10,11... | collective-permute-start | bytes 18440 | tf_op jit(solution)/shard_map/ppermute | solution.py:29
  21.0 3.4 %copy-start.2 = (bf16[512,8192]{1,0:T(8,128)(2,1)S(1)}, bf16[512,8192]{1,0:T(8,128)(2,1)}, u32[]{:S(2)}) copy-start(bf16[512,8192]{1,0:T(8,128)(2,1)} %weights.9) | copy-start | bytes 25165828
  25.0 10.0 %collective-permute-start.5 = (bf16[128,1024]{1,0:T(8,128)(2,1)S(1)}, bf16[128,1024]{1,0:T(8,128)(2,1)S(1)}, u32[]{:S(2)}, u32[]{:S(2)}) collective-permute-start(bf16[128,1024]{1,0:T(8,128)(2,1)S(1)} %get-tuple-element.30), channel_id=1, source_target_pairs={{0,2},{1,3},{2,4},{3,5},{4,6},{5,7},{6,0},{7,1},{8,10},{9,11},{10,... | collective-permute-start | bytes 786440 | tf_op jit(solution)/shard_map/ppermute | solution.py:29
  27.4 9.0 %collective-permute-start.8 = (bf16[128,1024]{1,0:T(8,128)(2,1)S(1)}, bf16[128,1024]{1,0:T(8,128)(2,1)S(1)}, u32[]{:S(2)}, u32[]{:S(2)}) collective-permute-start(bf16[128,1024]{1,0:T(8,128)(2,1)S(1)} %get-tuple-element.34), channel_id=1, source_target_pairs={{0,6},{1,7},{2,0},{3,1},{4,2},{5,3},{6,4},{7,5},{8,14},{9,15},{10,... | collective-permute-start | bytes 786440 | tf_op jit(solution)/shard_map/ppermute | solution.py:29
  32.0 7.4 %copy-start.8 = (bf16[384,512]{1,0:T(8,128)(2,1)S(1)}, bf16[384,512]{1,0:T(8,128)(2,1)}, u32[]{:S(2)}) copy-start(bf16[384,512]{1,0:T(8,128)(2,1)} %param.23) | copy-start | bytes 1179652
  32.0 7.4 %copy-start.9 = (bf16[384,512]{1,0:T(8,128)(2,1)S(1)}, bf16[384,512]{1,0:T(8,128)(2,1)}, u32[]{:S(2)}) copy-start(bf16[384,512]{1,0:T(8,128)(2,1)} %param.17) | copy-start | bytes 1179652
  32.0 8.5 %copy-start.10 = (bf16[256,1024]{1,0:T(8,128)(2,1)S(1)}, bf16[256,1024]{1,0:T(8,128)(2,1)}, u32[]{:S(2)}) copy-start(bf16[256,1024]{1,0:T(8,128)(2,1)} %param.14) | copy-start | bytes 1572868
  32.0 10.1 %collective-permute-start.3 = (bf16[128,1024]{1,0:T(8,128)(2,1)}, bf16[128,1024]{1,0:T(8,128)(2,1)S(1)}, u32[]{:S(2)}, u32[]{:S(2)}) collective-permute-start(bf16[128,1024]{1,0:T(8,128)(2,1)} %get-tuple-element.28), channel_id=1, source_target_pairs={{0,6},{1,7},{2,0},{3,1},{4,2},{5,3},{6,4},{7,5},{8,14},{9,15},{10,... | collective-permute-start | bytes 786440 | tf_op jit(solution)/shard_map/ppermute | solution.py:29
  34.0 10.7 %collective-permute-start.7 = (bf16[128,1024]{1,0:T(8,128)(2,1)}, bf16[128,1024]{1,0:T(8,128)(2,1)S(1)}, u32[]{:S(2)}, u32[]{:S(2)}) collective-permute-start(bf16[128,1024]{1,0:T(8,128)(2,1)} %get-tuple-element.32), channel_id=1, source_target_pairs={{0,2},{1,3},{2,4},{3,5},{4,6},{5,7},{6,0},{7,1},{8,10},{9,11},{10,... | collective-permute-start | bytes 786440 | tf_op jit(solution)/shard_map/ppermute | solution.py:29
  35.1 13.7 %collective-permute-start.6 = (bf16[128,1024]{1,0:T(8,128)(2,1)S(1)}, bf16[128,1024]{1,0:T(8,128)(2,1)S(1)}, u32[]{:S(2)}, u32[]{:S(2)}) collective-permute-start(bf16[128,1024]{1,0:T(8,128)(2,1)S(1)} %add_convert_fusion.6), channel_id=1, source_target_pairs={{0,2},{1,3},{2,4},{3,5},{4,6},{5,7},{6,0},{7,1},{8,10},{9,11},{10,... | collective-permute-start | bytes 786440 | tf_op jit(solution)/shard_map/ppermute | solution.py:29
  36.4 12.3 %collective-permute-start.9 = (bf16[128,1024]{1,0:T(8,128)(2,1)S(1)}, bf16[128,1024]{1,0:T(8,128)(2,1)S(1)}, u32[]{:S(2)}, u32[]{:S(2)}) collective-permute-start(bf16[128,1024]{1,0:T(8,128)(2,1)S(1)} %add_convert_fusion.5), channel_id=1, source_target_pairs={{0,6},{1,7},{2,0},{3,1},{4,2},{5,3},{6,4},{7,5},{8,14},{9,15},{10,... | collective-permute-start | bytes 786440 | tf_op jit(solution)/shard_map/ppermute | solution.py:29
  48.8 0.7 copy-start.17
  50.5 9.3 %copy-start.5 = (bf16[256,1024]{1,0:T(8,128)(2,1)S(1)}, bf16[256,1024]{1,0:T(8,128)(2,1)}, u32[]{:S(2)}) copy-start(bf16[256,1024]{1,0:T(8,128)(2,1)} %get-tuple-element.47.rows) | copy-start | bytes 1572868
  50.5 9.2 %collective-permute-start.17 = (f32[2,128]{1,0:T(2,128)S(1)}, f32[2,128]{1,0:T(2,128)S(1)}, u32[]{:S(2)}, u32[]{:S(2)}) collective-permute-start(f32[2,128]{1,0:T(2,128)S(1)} %bitcast.112), channel_id=1, source_target_pairs={{0,1},{1,0},{2,3},{3,2},{4,5},{5,4},{6,7},{7,6},{8,9},{9,8},{10,11... | collective-permute-start | bytes 3080 | tf_op jit(solution)/shard_map/ppermute | solution.py:29
  51.1 30.3 %all-to-all-start = ((bf16[16,24,1024]{2,1,0:T(8,128)(2,1)}), bf16[16,24,1024]{2,1,0:T(8,128)(2,1)S(1)}, u32[]{:S(2)}, u32[]{:S(2)}) async-start(bf16[16,24,1024]{2,1,0:T(8,128)(2,1)} %bitcast.18), calls=%async_computation | async-start | bytes 1572864 | tf_op jit(solution)/shard_map/all_to_all | solution.py:180
  59.0 84.0 %all-gather.2.cloned.1.call-start = ((), (), s32[]{:S(2)}) async-start(), calls=%async_computation.3 | async-start | bytes 2621440 | tf_op jit(solution)/shard_map/all_gather | solution.py:201
  59.7 6.9 %collective-permute-start.18 = (f32[2,128]{1,0:T(2,128)S(1)}, f32[2,128]{1,0:T(2,128)S(1)}, u32[]{:S(2)}, u32[]{:S(2)}) collective-permute-start(f32[2,128]{1,0:T(2,128)S(1)} %bitcast_add_fusion), channel_id=1, source_target_pairs={{0,2},{1,3},{2,0},{3,1},{4,6},{5,7},{6,4},{7,5},{8,10},{9,11},{10,... | collective-permute-start | bytes 3080 | tf_op jit(solution)/shard_map/ppermute | solution.py:29
  59.8 3.4 %copy-start.3 = (bf16[1024,4096]{1,0:T(8,128)(2,1)S(1)}, bf16[1024,4096]{1,0:T(8,128)(2,1)}, u32[]{:S(2)}) copy-start(bf16[1024,4096]{1,0:T(8,128)(2,1)} %weights.11) | copy-start | bytes 25165828
  66.0 10.9 %collective-permute-start.11 = (bf16[128,1024]{1,0:T(8,128)(2,1)S(1)}, bf16[128,1024]{1,0:T(8,128)(2,1)S(1)}, u32[]{:S(2)}, u32[]{:S(2)}) collective-permute-start(bf16[128,1024]{1,0:T(8,128)(2,1)S(1)} %get-tuple-element.38), channel_id=1, source_target_pairs={{0,1},{1,0},{2,3},{3,2},{4,5},{5,4},{6,7},{7,6},{8,9},{9,8},{10,11... | collective-permute-start | bytes 786440 | tf_op jit(solution)/shard_map/ppermute | solution.py:29
  66.3 12.0 %collective-permute-start.13 = (bf16[128,1024]{1,0:T(8,128)(2,1)S(1)}, bf16[128,1024]{1,0:T(8,128)(2,1)S(1)}, u32[]{:S(2)}, u32[]{:S(2)}) collective-permute-start(bf16[128,1024]{1,0:T(8,128)(2,1)S(1)} %get-tuple-element.40), channel_id=1, source_target_pairs={{0,1},{1,0},{2,3},{3,2},{4,5},{5,4},{6,7},{7,6},{8,9},{9,8},{10,11... | collective-permute-start | bytes 786440 | tf_op jit(solution)/shard_map/ppermute | solution.py:29
  66.6 9.7 %collective-permute-start.19 = (f32[2,128]{1,0:T(2,128)S(1)}, f32[2,128]{1,0:T(2,128)S(1)}, u32[]{:S(2)}, u32[]{:S(2)}) collective-permute-start(f32[2,128]{1,0:T(2,128)S(1)} %fusion.90), channel_id=1, source_target_pairs={{0,4},{1,5},{2,6},{3,7},{4,0},{5,1},{6,2},{7,3},{8,12},{9,13},{10,... | collective-permute-start | bytes 3080 | tf_op jit(solution)/shard_map/ppermute | solution.py:29
  69.1 3.8 %copy-start.4 = (bf16[1024,4096]{1,0:T(8,128)(2,1)S(1)}, bf16[1024,4096]{1,0:T(8,128)(2,1)}, u32[]{:S(2)}) copy-start(bf16[1024,4096]{1,0:T(8,128)(2,1)} %weights.11) | copy-start | bytes 25165828
  75.7 5.6 %copy-start.18 = (s32[256,1]{0,1:T(1,128)S(1)}, s32[256,1]{0,1:T(1,128)}, u32[]{:S(2)}) copy-start(s32[256,1]{0,1:T(1,128)} %multiply_add_fusion) | copy-start | bytes 3076
  75.8 6.2 %collective-permute-start.15 = (bf16[128,1024]{1,0:T(8,128)(2,1)S(1)}, bf16[128,1024]{1,0:T(8,128)(2,1)}, u32[]{:S(2)}, u32[]{:S(2)}) collective-permute-start(bf16[128,1024]{1,0:T(8,128)(2,1)S(1)} %get-tuple-element.42), channel_id=1, source_target_pairs={{0,1},{1,0},{2,3},{3,2},{4,5},{5,4},{6,7},{7,6},{8,9},{9,8},{10,11... | collective-permute-start | bytes 786440 | tf_op jit(solution)/shard_map/ppermute | solution.py:29
  75.8 8.3 %collective-permute-start.10 = (bf16[128,1024]{1,0:T(8,128)(2,1)S(1)}, bf16[128,1024]{1,0:T(8,128)(2,1)S(1)}, u32[]{:S(2)}, u32[]{:S(2)}) collective-permute-start(bf16[128,1024]{1,0:T(8,128)(2,1)S(1)} %get-tuple-element.36), channel_id=1, source_target_pairs={{0,1},{1,0},{2,3},{3,2},{4,5},{5,4},{6,7},{7,6},{8,9},{9,8},{10,11... | collective-permute-start | bytes 786440 | tf_op jit(solution)/shard_map/ppermute | solution.py:29
  77.6 11.0 %collective-permute-start.12 = (bf16[128,1024]{1,0:T(8,128)(2,1)}, bf16[128,1024]{1,0:T(8,128)(2,1)}, u32[]{:S(2)}, u32[]{:S(2)}) collective-permute-start(bf16[128,1024]{1,0:T(8,128)(2,1)} %add_convert_fusion.4), channel_id=1, source_target_pairs={{0,4},{1,5},{2,6},{3,7},{4,0},{5,1},{6,2},{7,3},{8,12},{9,13},{10,... | collective-permute-start | bytes 786440 | tf_op jit(solution)/shard_map/ppermute | solution.py:29
  79.1 14.5 %collective-permute-start.14 = (bf16[128,1024]{1,0:T(8,128)(2,1)}, bf16[128,1024]{1,0:T(8,128)(2,1)}, u32[]{:S(2)}, u32[]{:S(2)}) collective-permute-start(bf16[128,1024]{1,0:T(8,128)(2,1)} %add_convert_fusion.3), channel_id=1, source_target_pairs={{0,2},{1,3},{2,4},{3,5},{4,6},{5,7},{6,0},{7,1},{8,10},{9,11},{10,... | collective-permute-start | bytes 786440 | tf_op jit(solution)/shard_map/ppermute | solution.py:29
  81.4 12.2 %copy-start.15 = (f32[1,1024]{1,0:T(1,128)S(1)}, f32[1,1024]{1,0:T(1,128)}, u32[]{:S(2)}) copy-start(f32[1,1024]{1,0:T(1,128)} %get-tuple-element.62) | copy-start | bytes 12292
  81.4 12.2 %copy-start.16 = (f32[1,1024]{1,0:T(1,128)S(1)}, f32[1,1024]{1,0:T(1,128)}, u32[]{:S(2)}) copy-start(f32[1,1024]{1,0:T(1,128)} %get-tuple-element.63) | copy-start | bytes 12292
  81.4 12.2 %copy-start.20 = (f32[128]{0:T(128)S(1)}, f32[128]{0:T(128)}, u32[]{:S(2)}) copy-start(f32[128]{0:T(128)} %fusion.82) | copy-start | bytes 1540
  81.9 2.2 %collective-permute-start.20 = (bf16[128,1024]{1,0:T(8,128)(2,1)S(1)}, bf16[128,1024]{1,0:T(8,128)(2,1)S(1)}, u32[]{:S(2)}, u32[]{:S(2)}) collective-permute-start(bf16[128,1024]{1,0:T(8,128)(2,1)S(1)} %get-tuple-element.54), channel_id=1, source_target_pairs={{0,1},{1,0},{2,3},{3,2},{4,5},{5,4},{6,7},{7,6},{8,9},{9,8},{10,11... | collective-permute-start | bytes 786440 | tf_op jit(solution)/shard_map/ppermute | solution.py:29
  83.0 10.5 %collective-permute-start.16 = (bf16[128,1024]{1,0:T(8,128)(2,1)S(1)}, bf16[128,1024]{1,0:T(8,128)(2,1)S(1)}, u32[]{:S(2)}, u32[]{:S(2)}) collective-permute-start(bf16[128,1024]{1,0:T(8,128)(2,1)S(1)} %add_convert_fusion.2), channel_id=1, source_target_pairs={{0,6},{1,7},{2,0},{3,1},{4,2},{5,3},{6,4},{7,5},{8,14},{9,15},{10,... | collective-permute-start | bytes 786440 | tf_op jit(solution)/shard_map/ppermute | solution.py:29
  93.6 30.4 %copy-start.19 = (s32[256,1]{0,1:T(1,128)S(1)}, s32[256,1]{0,1:T(1,128)}, u32[]{:S(2)}) copy-start(s32[256,1]{0,1:T(1,128)} %multiply_add_fusion) | copy-start | bytes 3076
  106.6 3.0 %collective-permute-start.22 = (bf16[4,128,256]{2,1,0:T(8,128)(2,1)S(1)}, bf16[4,128,256]{2,1,0:T(8,128)(2,1)S(1)}, u32[]{:S(2)}, u32[]{:S(2)}) collective-permute-start(bf16[4,128,256]{2,1,0:T(8,128)(2,1)S(1)} %all_to_all.15), channel_id=1, source_target_pairs={{0,1},{1,0},{2,3},{3,2},{4,5},{5,4},{6,7},{7,6},{8,9},{9,8},{10,11... | collective-permute-start | bytes 786440 | tf_op jit(solution)/shard_map/ppermute | solution.py:29
  106.6 14.0 %collective-permute-start.24 = (bf16[4,128,256]{2,1,0:T(8,128)(2,1)S(1)}, bf16[4,128,256]{2,1,0:T(8,128)(2,1)S(1)}, u32[]{:S(2)}, u32[]{:S(2)}) collective-permute-start(bf16[4,128,256]{2,1,0:T(8,128)(2,1)S(1)} %all_to_all.15), channel_id=1, source_target_pairs={{0,6},{1,7},{2,0},{3,1},{4,2},{5,3},{6,4},{7,5},{8,14},{9,15},{10,... | collective-permute-start | bytes 786440 | tf_op jit(solution)/shard_map/ppermute | solution.py:29
  108.7 12.1 %collective-permute-start.26 = (bf16[4,128,256]{2,1,0:T(8,128)(2,1)S(1)}, bf16[4,128,256]{2,1,0:T(8,128)(2,1)S(1)}, u32[]{:S(2)}, u32[]{:S(2)}) collective-permute-start(bf16[4,128,256]{2,1,0:T(8,128)(2,1)S(1)} %all_to_all.15), channel_id=1, source_target_pairs={{0,4},{1,5},{2,6},{3,7},{4,0},{5,1},{6,2},{7,3},{8,12},{9,13},{10,... | collective-permute-start | bytes 786440 | tf_op jit(solution)/shard_map/ppermute | solution.py:29
  108.7 15.3 %collective-permute-start.28 = (bf16[4,128,256]{2,1,0:T(8,128)(2,1)S(1)}, bf16[4,128,256]{2,1,0:T(8,128)(2,1)S(1)}, u32[]{:S(2)}, u32[]{:S(2)}) collective-permute-start(bf16[4,128,256]{2,1,0:T(8,128)(2,1)S(1)} %all_to_all.15), channel_id=1, source_target_pairs={{0,2},{1,3},{2,4},{3,5},{4,6},{5,7},{6,0},{7,1},{8,10},{9,11},{10,... | collective-permute-start | bytes 786440 | tf_op jit(solution)/shard_map/ppermute | solution.py:29
  109.6 14.4 %collective-permute-start.23 = (bf16[128,512]{1,0:T(8,128)(2,1)S(1)}, bf16[128,512]{1,0:T(8,128)(2,1)S(1)}, u32[]{:S(2)}, u32[]{:S(2)}) collective-permute-start(bf16[128,512]{1,0:T(8,128)(2,1)S(1)} %get-tuple-element.56), channel_id=1, source_target_pairs={{0,1},{1,0},{2,3},{3,2},{4,5},{5,4},{6,7},{7,6},{8,9},{9,8},{10,11... | collective-permute-start | bytes 393224 | tf_op jit(solution)/shard_map/ppermute | solution.py:29
  120.6 9.5 %collective-permute-start.25 = (bf16[4,128,256]{2,1,0:T(8,128)(2,1)S(1)}, bf16[4,128,256]{2,1,0:T(8,128)(2,1)S(1)}, u32[]{:S(2)}, u32[]{:S(2)}) collective-permute-start(bf16[4,128,256]{2,1,0:T(8,128)(2,1)S(1)} %collective-permute-done.24), channel_id=1, source_target_pairs={{0,1},{1,0},{2,3},{3,2},{4,5},{5,4},{6,7},{7,6},{8,9},{9,8},{10,11... | collective-permute-start | bytes 786440 | tf_op jit(solution)/shard_map/ppermute | solution.py:29
  120.8 9.5 %collective-permute-start.27 = (bf16[4,128,256]{2,1,0:T(8,128)(2,1)S(1)}, bf16[4,128,256]{2,1,0:T(8,128)(2,1)S(1)}, u32[]{:S(2)}, u32[]{:S(2)}) collective-permute-start(bf16[4,128,256]{2,1,0:T(8,128)(2,1)S(1)} %collective-permute-done.26), channel_id=1, source_target_pairs={{0,1},{1,0},{2,3},{3,2},{4,5},{5,4},{6,7},{7,6},{8,9},{9,8},{10,11... | collective-permute-start | bytes 786440 | tf_op jit(solution)/shard_map/ppermute | solution.py:29
  124.0 6.6 %collective-permute-start.29 = (bf16[4,128,256]{2,1,0:T(8,128)(2,1)S(1)}, bf16[4,128,256]{2,1,0:T(8,128)(2,1)S(1)}, u32[]{:S(2)}, u32[]{:S(2)}) collective-permute-start(bf16[4,128,256]{2,1,0:T(8,128)(2,1)S(1)} %collective-permute-done.28), channel_id=1, source_target_pairs={{0,1},{1,0},{2,3},{3,2},{4,5},{5,4},{6,7},{7,6},{8,9},{9,8},{10,11... | collective-permute-start | bytes 786440 | tf_op jit(solution)/shard_map/ppermute | solution.py:29
  125.1 15.5 %all-to-all-start.2 = ((bf16[16,24,512]{2,1,0:T(8,128)(2,1)}), bf16[16,24,512]{2,1,0:T(8,128)(2,1)S(1)}, u32[]{:S(2)}, u32[]{:S(2)}) async-start(bf16[16,24,512]{2,1,0:T(8,128)(2,1)} %bitcast.27), calls=%async_computation.2 | async-start | bytes 786432 | tf_op jit(solution)/shard_map/all_to_all | solution.py:249
  130.8 9.8 %copy-start.14 = (f32[512]{0:T(512)S(1)}, f32[512]{0:T(512)}, u32[]{:S(2)}) copy-start(f32[512]{0:T(512)} %param.18) | copy-start | bytes 6148
  143.0 3.2 %copy-start.22 = (bf16[1024,1024]{1,0:T(8,128)(2,1)S(1)}, bf16[1024,1024]{1,0:T(8,128)(2,1)}, u32[]{:S(2)}) copy-start(bf16[1024,1024]{1,0:T(8,128)(2,1)} %all-gather.2.cloned.1.call-done) | copy-start | bytes 6291460
  144.9 16.8 %collective-permute-start.30 = (bf16[512,256]{1,0:T(8,128)(2,1)S(1)}, bf16[512,256]{1,0:T(8,128)(2,1)S(1)}, u32[]{:S(2)}, u32[]{:S(2)}) collective-permute-start(bf16[512,256]{1,0:T(8,128)(2,1)S(1)} %convolution_convert_fusion.5), channel_id=1, source_target_pairs={{0,96},{1,97},{2,98},{3,99},{4,100},{5,101},{6,102},{7,103},{8,104... | collective-permute-start | bytes 786440 | tf_op jit(solution)/shard_map/ppermute | solution.py:29
  146.7 10.5 %collective-permute-start.31 = (bf16[512,256]{1,0:T(8,128)(2,1)S(1)}, bf16[512,256]{1,0:T(8,128)(2,1)S(1)}, u32[]{:S(2)}, u32[]{:S(2)}) collective-permute-start(bf16[512,256]{1,0:T(8,128)(2,1)S(1)} %convolution_convert_fusion.4), channel_id=1, source_target_pairs={{0,32},{1,33},{2,34},{3,35},{4,36},{5,37},{6,38},{7,39},{8,40},{9,... | collective-permute-start | bytes 786440 | tf_op jit(solution)/shard_map/ppermute | solution.py:29
  148.0 18.9 %collective-permute-start.33 = (bf16[512,256]{1,0:T(8,128)(2,1)S(1)}, bf16[512,256]{1,0:T(8,128)(2,1)S(1)}, u32[]{:S(2)}, u32[]{:S(2)}) collective-permute-start(bf16[512,256]{1,0:T(8,128)(2,1)S(1)} %convolution_convert_fusion.3), channel_id=1, source_target_pairs={{0,32},{1,33},{2,34},{3,35},{4,36},{5,37},{6,38},{7,39},{8,40},{9,... | collective-permute-start | bytes 786440 | tf_op jit(solution)/shard_map/ppermute | solution.py:29
  148.6 9.2 %collective-permute-start.34 = (bf16[512,256]{1,0:T(8,128)(2,1)S(1)}, bf16[512,256]{1,0:T(8,128)(2,1)S(1)}, u32[]{:S(2)}, u32[]{:S(2)}) collective-permute-start(bf16[512,256]{1,0:T(8,128)(2,1)S(1)} %convolution_convert_fusion.2), channel_id=1, source_target_pairs={{0,96},{1,97},{2,98},{3,99},{4,100},{5,101},{6,102},{7,103},{8,104... | collective-permute-start | bytes 786440 | tf_op jit(solution)/shard_map/ppermute | solution.py:29
  157.8 8.6 %collective-permute-start.32 = (bf16[512,256]{1,0:T(8,128)(2,1)S(1)}, bf16[512,256]{1,0:T(8,128)(2,1)S(1)}, u32[]{:S(2)}, u32[]{:S(2)}) collective-permute-start(bf16[512,256]{1,0:T(8,128)(2,1)S(1)} %add_convert_fusion.1), channel_id=1, source_target_pairs={{0,32},{1,33},{2,34},{3,35},{4,36},{5,37},{6,38},{7,39},{8,40},{9,... | collective-permute-start | bytes 786440 | tf_op jit(solution)/shard_map/ppermute | solution.py:29
  158.3 8.5 %collective-permute-start.35 = (bf16[512,256]{1,0:T(8,128)(2,1)S(1)}, bf16[512,256]{1,0:T(8,128)(2,1)S(1)}, u32[]{:S(2)}, u32[]{:S(2)}) collective-permute-start(bf16[512,256]{1,0:T(8,128)(2,1)S(1)} %add_convert_fusion), channel_id=1, source_target_pairs={{0,96},{1,97},{2,98},{3,99},{4,100},{5,101},{6,102},{7,103},{8,104... | collective-permute-start | bytes 786440 | tf_op jit(solution)/shard_map/ppermute | solution.py:29
Sparse Core Ops, SparseCore 0:
  61.5 30.6 all-gather.1

commit v3 on v2

--- a/solution.py
+++ b/solution.py
@@ -37,6 +37,10 @@
     return move(value, lambda x, z, y, c: (x, z, y + step, c))
 
 
+def along_z(value, step):
+    return move(value, lambda x, z, y, c: (x, z + step, y, c))
+
+
 def along_x(value, step):
     return move(value, lambda x, z, y, c: (x + step, z, y, c))
 
@@ -74,11 +78,11 @@
         in_specs=[pl.BlockSpec(memory_space=pltpu.SMEM), whole, pl.BlockSpec(memory_space=pltpu.HBM)] + [whole] * len(extra),
         out_specs=[whole] * len(out_shapes),
         scratch_shapes=[pltpu.VMEM((n, depth, width), BF), pltpu.SemaphoreType.DMA((n,))],
-        compiler_params=pltpu.CompilerParams(vmem_limit_bytes=40 << 20),
+        compiler_params=pltpu.CompilerParams(vmem_limit_bytes=32 << 20),
         cost_estimate=pl.CostEstimate(
             flops=2 * n * rows.shape[0] * depth * width, bytes_accessed=2 * n * depth * width, transcendentals=0
         ),
-    )(starts, rows, weights, *extra)
+    )(starts, rows, pltpu.with_memory_space_constraint(weights, pltpu.HBM), *extra)
 
 
 def shape(rows, columns, dtype):
@@ -89,72 +93,49 @@
     y, c = lax.axis_index("y"), lax.axis_index("c")
     tokens = context.shape[0]
     half = tokens // 2
-
-    def starts(core, *steps):
-        return jnp.stack([(lax.rem(y + d + N, N) * 2 + core) * width for d in steps]).astype(jnp.int32)
-
-    def emit_plain(i, value, starts, extra, outs):
-        outs[i][...] = value.astype(BF)
-
-    (send_2,) = products(context, w_out, starts(1 - c, 2), 1, width, emit_plain, [shape(tokens, width, BF)])
-    got_2 = swap(send_2)
-    sends = products(
-        context, w_out, starts(1 - c, 1, -1, 0), 3, width, emit_plain, [shape(tokens, width, BF)] * 3
-    )
-    got_r, got_l, got_o = [swap(s) for s in sends]
-
-    def emit_far(i, value, starts, extra, outs):
-        value = value + extra[0][...].astype(F32)
-        outs[0][...] = value[:half].astype(BF)
-        outs[1][...] = value[half:].astype(BF)
-
-    far_a, far_b = products(
-        context, w_out, starts(c, 2), 1, width, emit_far, [shape(half, width, BF)] * 2, (got_2,)
-    )
-    from_left, from_right = along_y(far_a, 1), along_y(far_b, -1)
-
-    def emit_near(i, value, starts, extra, outs):
-        value = value + extra[i][...].astype(F32)
-        outs[2 * i][...] = value[:half].astype(outs[2 * i].dtype)
-        outs[2 * i + 1][...] = value[half:].astype(outs[2 * i + 1].dtype)
-
-    right_a, right_b, left_a, left_b, own_a, own_b = products(
-        context,
-        w_out,
-        starts(c, 1, -1, 0),
-        3,
-        width,
-        emit_near,
-        [shape(half, width, t) for t in (F32, BF, BF, F32, F32, F32)],
-        (got_r, got_l, got_o),
-    )
+    steps = (2, 1, -1, 0)
+
+    def emit(i, value, starts, extra, outs):
+        value = value.astype(BF)
+        if i < N:
+            outs[i][...] = value
+        else:
+            outs[2 * i - N][...] = value[:half]
+            outs[2 * i - N + 1][...] = value[half:]
+
+    starts = jnp.stack(
+        [(lax.rem(y + d + N, N) * 2 + core) * width for core in (1 - c, c) for d in steps]
+    ).astype(jnp.int32)
+    shapes = [shape(tokens, width, BF)] * N + [shape(half, width, BF)] * (2 * N)
+    outs = products(context, w_out, starts, 2 * N, width, emit, shapes)
+    got = [swap(out) for out in outs[:N]]
+    far, right, left, own = [
+        (add(outs[N + 2 * i], got[i][:half]), add(outs[N + 2 * i + 1], got[i][half:])) for i in range(N)
+    ]
+    from_left, from_right = along_y(far[0].astype(BF), 1), along_y(far[1].astype(BF), -1)
+    right_b, left_a = right[1].astype(BF), left[0].astype(BF)
     low_b, up_a = along_y(right_b, 1), along_y(left_a, -1)
-    low_a = along_y(add(right_a, from_left).astype(BF), 1)
-    up_b = along_y(add(left_b, from_right).astype(BF), -1)
-    return add(own_a, up_a, low_a), add(own_b, low_b, up_b), (low_b, up_a)
+    last = add(right[0], from_left).astype(BF), add(left[1], from_right).astype(BF)
+    low_a, up_b = along_y(last[0], 1), along_y(last[1], -1)
+    return add(own[0], up_a, low_a), add(own[1], low_b, up_b), last
 
 
 def join(rows, w_join, width):
     y, c = lax.axis_index("y"), lax.axis_index("c")
     half = rows.shape[0] // 2
+    steps = (2, 1, -1, 0)
 
     def emit(i, value, starts, extra, outs):
-        first, second = value[:half], value[half:]
-        mine = starts[2] == 0
-        outs[2 * i][...] = jnp.where(mine, second, first).astype(BF)
+        first, second = value[:half].astype(BF), value[half:].astype(BF)
+        mine = starts[N] == 0
+        outs[2 * i][...] = jnp.where(mine, second, first)
         outs[2 * i + 1][...] = jnp.where(mine, first, second)
 
-    def pair(*steps):
-        starts = jnp.stack([lax.rem(y + d + N, N) * width for d in steps] + [c]).astype(jnp.int32)
-        shapes = [shape(half, width, BF), shape(half, width, F32)] * 2
-        return products(rows, w_join, starts, 2, width, emit, shapes)
-
-    s2, o2, s1, o1 = pair(2, 1)
-    g2, g1 = swap(s2), swap(s1)
-    s3, o3, s0, o0 = pair(-1, 0)
-    g3, g0 = swap(s3), swap(s0)
-    terms = [along_y(add(o, g).astype(BF), d) for o, g, d in ((o2, g2, 2), (o1, g1, 1), (o3, g3, -1))]
-    return add(o0, g0, *terms)
+    starts = jnp.stack([lax.rem(y + d + N, N) * width for d in steps] + [c]).astype(jnp.int32)
+    outs = products(rows, w_join, starts, N, width, emit, [shape(half, width, BF)] * (2 * N))
+    got = [swap(out) for out in outs[::2]]
+    terms = [along_y(add(outs[2 * i + 1], got[i]).astype(BF), steps[i]) for i in range(N - 1)]
+    return [*terms, outs[-1], got[-1]]
 
 
 def body(
@@ -166,6 +147,7 @@
     half = tokens // 2
     slot_rows, features = dec_state.shape
     most = slot_rows // n_owner
+    first = c == 0
 
     onehot = (owner == jnp.arange(n_owner, dtype=jnp.int32)[None, :]).astype(BF)
     ahead = jnp.tril(jnp.ones((tokens, tokens), BF), -1)
@@ -174,25 +156,10 @@
     slots = owner[:, 0] * most + rank
     select = (slots[:, None] == jnp.arange(slot_rows, dtype=jnp.int32)[None, :]).astype(BF)
 
-    sum_a, sum_b, late = project(context, w_out, width)
-
     both = jnp.concatenate([dec_state, cotangent], axis=1).reshape(n_owner, most, 2 * features)
-    both = lax.all_to_all(after(both, *late), ("x", "z"), 0, 0, tiled=True).reshape(slot_rows, 2 * features)
-    both = jnp.dot(select, both, preferred_element_type=F32).astype(BF)
-    first = c == 0
-    keep = jnp.where(first, both[:half], both[half:])
-    got = swap(jnp.where(first, both[half:], both[:half]))
-
-    def widen(mine, other):
-        return jnp.where(
-            first, jnp.concatenate([mine, other], axis=-1), jnp.concatenate([other, mine], axis=-1)
-        )
-
-    state_t = widen(keep[:, :features], got[:, :features]).astype(F32)
-    outer_t = widen(keep[:, features:], got[:, features:]).astype(F32)
-    params = jnp.stack([gate_s, gate_h, gate_bias])
-    params_t = widen(params, swap(params))
-
+
+    sum_a, sum_b, last = project(context, w_out, width)
+    both = lax.all_to_all(after(both, *last), ("x", "z"), 0, 0, tiled=True).reshape(slot_rows, 2 * features)
     gain, mask = norm_gain[None, :], pad_mask.astype(F32)[:, None]
     residual = residual.astype(F32)
     mixed = jnp.concatenate([residual[:half] + sum_a, residual[half:] + sum_b], axis=0)
@@ -207,7 +174,23 @@
     scale = lax.rsqrt(total / (width * N * 2) + 1e-05)
     scale = jnp.where(first, scale[0], scale[1])[:, None]
 
-    hidden = (join(rows, w_join, 2 * features) * scale).astype(BF)
+    gated, both = lax.optimization_barrier((rows, both))
+    terms = join(gated, w_join, 2 * features)
+    both = jnp.dot(select, after(both, terms[1]), preferred_element_type=F32).astype(BF)
+    keep = jnp.where(first, both[:half], both[half:])
+    got = swap(jnp.where(first, both[half:], both[:half]))
+
+    def widen(mine, other):
+        return jnp.where(
+            first, jnp.concatenate([mine, other], axis=-1), jnp.concatenate([other, mine], axis=-1)
+        )
+
+    state_t = widen(keep[:, :features], got[:, :features]).astype(F32)
+    outer_t = widen(keep[:, features:], got[:, features:]).astype(F32)
+    params = jnp.stack([gate_s, gate_h, gate_bias])
+    params_t = widen(params, swap(params))
+
+    hidden = (add(*terms) * scale).astype(BF)
 
     def gates(params, state, hidden):
         gate = jax.nn.sigmoid(params[0][None, :] * state + params[1][None, :] * hidden + params[2][None, :])
@@ -216,9 +199,16 @@
     gate, slope = gates(params_t, state_t, hidden.astype(F32))
     grad = (outer_t * (gate + slope * params_t[1][None, :]) * scale).astype(BF)
 
-    grad = grad.reshape(half, N, -1).transpose(1, 0, 2)
-    grad = lax.all_to_all(grad, "z", 0, 0, tiled=True)
-    pieces = [grad] + [along_y(grad, -d) for d in (1, 2, 3)]
+    quarter = 2 * features // N
+
+    def quarter_for(step):
+        return lax.dynamic_slice_in_dim(grad, lax.rem(z + step + N, N) * quarter, quarter, 1)
+
+    others = {f: along_z(quarter_for(-f), -f) for f in (2, 1, 3)}
+    block = jnp.stack([quarter_for(0), others[1], others[2], others[3]] * 2)
+    block = lax.dynamic_slice_in_dim(block, lax.rem(N - z, N), N, 0)
+    arrived = {d: along_y(block, -d) for d in (2, 1, 3)}
+    pieces = [block, arrived[1], arrived[2], arrived[3]]
     swapped = [swap(piece) for piece in pieces]
     grads = jnp.stack(
         [jnp.where(first, jnp.concatenate([a, b], axis=1), jnp.concatenate([b, a], axis=1)) for a, b in zip(pieces, swapped)]
@@ -232,15 +222,15 @@
 
     from_left = along_x(grad_term(2, 0).astype(BF), 1)
     from_right = along_x(grad_term(2, 1).astype(BF), -1)
-    low_b = along_x(grad_term(1, 1).astype(BF), 1)
-    up_a = along_x(grad_term(-1, 0).astype(BF), -1)
+    near = grad_term(1, 1).astype(BF), grad_term(-1, 0).astype(BF)
+    low_b, up_a = along_x(near[0], 1), along_x(near[1], -1)
     low_a = along_x(add(grad_term(1, 0), from_left).astype(BF), 1)
     up_b = along_x(add(grad_term(-1, 1), from_right).astype(BF), -1)
     join_grad = jnp.concatenate(
         [add(grad_term(0, 0), up_a, low_a), add(grad_term(0, 1), low_b, up_b)], axis=0
     )
 
-    late_hidden = after(hidden, swapped[0])
+    late_hidden = after(hidden, block)
     keep = jnp.where(first, late_hidden[:, :features], late_hidden[:, features:])
     got = swap(jnp.where(first, late_hidden[:, features:], late_hidden[:, :features]))
     rows_h = jnp.where(first, jnp.concatenate([keep, got], axis=0), jnp.concatenate([got, keep], axis=0))

time: 176 us -> 151 us (0.86)
  local copies, waits for them, and re-layouts: 19.5 us -> 1.38 us
  blocking collectives: 11.3 us -> 0 us
  starting transfers between devices: 43.3 us -> 52.8 us
  other arithmetic: 14.8 us -> 11 us
  Pallas kernels: 13 us -> 10.4 us
    unnamed x46 -> x35, local copies, waits for them, and re-layouts: 18.9 us -> 1.06 us
    all_to_all x1 -> x0, blocking collectives: 11.3 us -> none  [body(): grad = lax.all_to_all(grad, 'z', 0, 0, tiled=True)]
    ppermute x36 -> x39, starting transfers between devices: 30.4 us -> 39.4 us  [move(): return lax.ppermute(value, AXES, pairs)]
    ppermute x36 -> x39, waiting for transfers between devices: 41.5 us -> 50 us  [move(): return lax.ppermute(value, AXES, pairs)]
    all_to_all x1, waiting for transfers between devices: 9.49 us -> 2.37 us  [body(): lax.all_to_all(placed, ('x', 'z'), 0, 0, tiled=True)]
    pallas_call x6 -> x2, Pallas kernels: 13 us -> 10.4 us  [products(): pl.pallas_call(functools.partial(product_kernel, n, width, len(extra), em...]
  transfers between devices with their start and end apart: 39 -> 42, of which waited for: 11 -> 19; matrix products, arithmetic and copies ran while one was open for 10% -> 10% of each run, Pallas kernels for 7% -> 3%
where the time goes in v3:
time: 151 us
  waiting for transfers between devices  53.4 us (35%)
  starting transfers between devices  52.8 us (35%)
  between operations  14.8 us (10%)
  other arithmetic  11 us (7%)
  Pallas kernels  10.4 us (7%)
  matrix products  7.13 us (5%)
    ppermute x39, waiting for transfers between devices, move(): return lax.ppermute(value, AXES, pairs)  50 us
    ppermute x39, starting transfers between devices, move(): return lax.ppermute(value, AXES, pairs)  39.4 us
    pallas_call x2, Pallas kernels, products(): pl.pallas_call(functools.partial(product_kernel, n, width, len(extra), em...  10.4 us
    all_to_all x1, starting transfers between devices, body(): lax.all_to_all(after(both, *last), ('x', 'z'), 0, 0, tiled=True)  7.89 us
    all_to_all x1, starting transfers between devices, body(): lax.all_to_all(placed, ('x', 'z'), 0, 0, tiled=True)  5.46 us
    dot_general x8, matrix products, grad_term(): lax.dot_general(rows, columns, (((0,), (0,)), ((), ())), preferred_elemen...  5.25 us
  transfers between devices with their start and end apart: 42, of which 19 were waited for; matrix products, arithmetic and copies ran while one was open for 10% of the time, Pallas kernels for 3%

profile of v3, /device:TPU:0, one launch (start us, length us, event | category | flops | bytes accessed | tf_op | source)
XLA Modules:
  0.0 150.9 jit_solution(16496076017403665599)
XLA Ops:
  7.3 1.0 copy-done.1
  8.2 5.4 %shard_map.139 = (bf16[256,1024]{1,0:T(8,128)(2,1)S(1)}, bf16[256,1024]{1,0:T(8,128)(2,1)S(1)}, bf16[256,1024]{1,0:T(8,128)(2,1)S(1)}, bf16[256,1024]{1,0:T(8,12...) custom-call(s32[8]{0:T(128)S(1)} %stack.97.starts, ...), custom_call_target="tpu_custom_call" | custom-call | flops 2147483648 | bytes 8388608 | tf_op jit(solution)/shard_map/pallas_call | solution.py:75
  13.7 0.5 collective-permute-start.1
  14.7 0.9 collective-permute-done.4
  15.8 3.2 %collective-permute-start.8 = (bf16[128,1024]{1,0:T(8,128)(2,1)S(1)}, bf16[128,1024]{1,0:T(8,128)(2,1)S(1)}, u32[]{:S(2)}, u32[]{:S(2)}) collective-permute-start(bf16[128,1024]{1,0:T(8,128)(2,1)S(1)} %get-tuple-element.68), channel_id=1, source_target_pairs={{0,6},{1,7},{2,0},{3,1},{4,2},{5,3},{6,4},{7,5},{8,14},{9,15},{10,... | collective-permute-start | bytes 786440 | tf_op jit(solution)/shard_map/ppermute | solution.py:29
  19.3 1.0 pad_maximum_fusion.3
  20.4 4.5 %collective-permute-done.8 = bf16[128,1024]{1,0:T(8,128)(2,1)S(1)} collective-permute-done((bf16[128,1024]{1,0:T(8,128)(2,1)S(1)}, bf16[128,1024]{1,0:T(8,128)(2,1)S(1)}, u32[]{:S(2)}, u32[]{:S(2)}) %collective-permute-start.8) | collective-permute-done | bytes 262176 | tf_op jit(solution)/shard_map/ppermute | solution.py:29
  24.9 1.0 add_convert_fusion.10
  25.9 3.7 %collective-permute-start.2 = (bf16[128,1024]{1,0:T(8,128)(2,1)}, bf16[128,1024]{1,0:T(8,128)(2,1)}, u32[]{:S(2)}, u32[]{:S(2)}) collective-permute-start(bf16[128,1024]{1,0:T(8,128)(2,1)} %get-tuple-element.63), channel_id=1, source_target_pairs={{0,6},{1,7},{2,0},{3,1},{4,2},{5,3},{6,4},{7,5},{8,14},{9,15},{10,... | collective-permute-start | bytes 786440 | tf_op jit(solution)/shard_map/ppermute | solution.py:29
  29.6 1.0 add_convert_fusion.8
  30.7 2.0 %collective-permute-start.6 = (bf16[128,1024]{1,0:T(8,128)(2,1)}, bf16[128,1024]{1,0:T(8,128)(2,1)}, u32[]{:S(2)}, u32[]{:S(2)}) collective-permute-start(bf16[128,1024]{1,0:T(8,128)(2,1)} %get-tuple-element.65), channel_id=1, source_target_pairs={{0,2},{1,3},{2,4},{3,5},{4,6},{5,7},{6,0},{7,1},{8,10},{9,11},{10,... | collective-permute-start | bytes 786440 | tf_op jit(solution)/shard_map/ppermute | solution.py:29
  32.9 7.9 %all-to-all-start = ((bf16[16,24,1024]{2,1,0:T(8,128)(2,1)}), bf16[16,24,1024]{2,1,0:T(8,128)(2,1)S(1)}, u32[]{:S(2)}, u32[]{:S(2)}) async-start(bf16[16,24,1024]{2,1,0:T(8,128)(2,1)} %bitcast.16), calls=%async_computation | async-start | bytes 1572864 | tf_op jit(solution)/shard_map/all_to_all | solution.py:162
  41.0 0.5 collective-permute-done.6
  41.4 3.6 %collective-permute-done.7 = bf16[128,1024]{1,0:T(8,128)(2,1)} collective-permute-done((bf16[128,1024]{1,0:T(8,128)(2,1)}, bf16[128,1024]{1,0:T(8,128)(2,1)}, u32[]{:S(2)}, u32[]{:S(2)}) %collective-permute-start.7) | collective-permute-done | bytes 262176 | tf_op jit(solution)/shard_map/ppermute | solution.py:29
  45.0 1.7 %slice_add_fusion.1 = (f32[128,1024]{1,0:T(8,128)S(1)}, f32[128,1024]{1,0:T(8,128)S(1)}) fusion(f32[256,1024]{1,0:T(8,128)S(1)} %convert_element_type.235, bf16[128,1024]{1,0:T(8,128)(2,1)} %collective-permute-done.6, bf16[128,1024]{1,0:T(8,128)(2,1)} %collective-permute-done.2, bf16[128,1024]{1,0:T(8,128)(2,1)S(1)} %get-tuple-element.28, ...), kind=kLoop, calls=%fused_computation.58 | loop fusion | flops 2097152 | bytes 4194304 | tf_op jit(solution)/shard_map/add | solution.py:165
  47.4 1.0 collective-permute-done.17
  48.4 0.5 collective-permute-start.18
  48.9 3.0 %collective-permute-done.18 = f32[2,128]{1,0:T(2,128)S(1)} collective-permute-done((f32[2,128]{1,0:T(2,128)S(1)}, f32[2,128]{1,0:T(2,128)S(1)}, u32[]{:S(2)}, u32[]{:S(2)}) %collective-permute-start.18) | collective-permute-done | bytes 1056 | tf_op jit(solution)/shard_map/ppermute | solution.py:29
  51.9 0.8 collective-permute-start.19
  52.8 1.0 all-to-all-done
  53.7 5.0 %shard_map.140 = (bf16[128,1024]{1,0:T(8,128)(2,1)S(1)}, bf16[128,1024]{1,0:T(8,128)(2,1)S(1)}, bf16[128,1024]{1,0:T(8,128)(2,1)S(1)}, bf16[128,1024]{1,0:T(8,12...) custom-call(s32[5]{0:T(128)S(1)} %stack.88.starts, ...), custom_call_target="tpu_custom_call" | custom-call | flops 2147483648 | bytes 8388608 | tf_op jit(solution)/shard_map/pallas_call | solution.py:75
  58.9 0.6 collective-permute-start.10
  59.5 0.9 collective-permute-done.12
  60.5 0.5 collective-permute-start.13
  61.0 0.5 collective-permute-start.16
  61.6 4.2 %collective-permute-start.11 = (bf16[128,1024]{1,0:T(8,128)(2,1)S(1)}, bf16[128,1024]{1,0:T(8,128)(2,1)S(1)}, u32[]{:S(2)}, u32[]{:S(2)}) collective-permute-start(bf16[128,1024]{1,0:T(8,128)(2,1)S(1)} %add_convert_fusion.4), channel_id=1, source_target_pairs={{0,4},{1,5},{2,6},{3,7},{4,0},{5,1},{6,2},{7,3},{8,12},{9,13},{10,... | collective-permute-start | bytes 786440 | tf_op jit(solution)/shard_map/ppermute | solution.py:29
  65.8 4.5 %collective-permute-done.13 = bf16[128,1024]{1,0:T(8,128)(2,1)S(1)} collective-permute-done((bf16[128,1024]{1,0:T(8,128)(2,1)S(1)}, bf16[128,1024]{1,0:T(8,128)(2,1)S(1)}, u32[]{:S(2)}, u32[]{:S(2)}) %collective-permute-start.13) | collective-permute-done | bytes 262176 | tf_op jit(solution)/shard_map/ppermute | solution.py:29
  70.3 0.5 convolution_convert_fusion
  71.0 2.6 %collective-permute-start.15 = (bf16[128,1024]{1,0:T(8,128)(2,1)S(1)}, bf16[128,1024]{1,0:T(8,128)(2,1)S(1)}, u32[]{:S(2)}, u32[]{:S(2)}) collective-permute-start(bf16[128,1024]{1,0:T(8,128)(2,1)S(1)} %add_convert_fusion.2), channel_id=1, source_target_pairs={{0,6},{1,7},{2,0},{3,1},{4,2},{5,3},{6,4},{7,5},{8,14},{9,15},{10,... | collective-permute-start | bytes 786440 | tf_op jit(solution)/shard_map/ppermute | solution.py:29
  73.6 3.4 %collective-permute-done.11 = bf16[128,1024]{1,0:T(8,128)(2,1)S(1)} collective-permute-done((bf16[128,1024]{1,0:T(8,128)(2,1)S(1)}, bf16[128,1024]{1,0:T(8,128)(2,1)S(1)}, u32[]{:S(2)}, u32[]{:S(2)}) %collective-permute-start.11) | collective-permute-done | bytes 262176 | tf_op jit(solution)/shard_map/ppermute | solution.py:29
  77.0 5.5 %collective-permute-done.15 = bf16[128,1024]{1,0:T(8,128)(2,1)S(1)} collective-permute-done((bf16[128,1024]{1,0:T(8,128)(2,1)S(1)}, bf16[128,1024]{1,0:T(8,128)(2,1)S(1)}, u32[]{:S(2)}, u32[]{:S(2)}) %collective-permute-start.15) | collective-permute-done | bytes 262176 | tf_op jit(solution)/shard_map/ppermute | solution.py:29
  82.6 0.6 fusion.34
  83.2 3.2 %collective-permute-start.22 = (bf16[128,256]{1,0:T(8,128)(2,1)S(1)}, bf16[128,256]{1,0:T(8,128)(2,1)S(1)}, u32[]{:S(2)}, u32[]{:S(2)}) collective-permute-start(bf16[128,256]{1,0:T(8,128)(2,1)S(1)} %get-tuple-element.73), channel_id=1, source_target_pairs={{0,24},{1,25},{2,26},{3,27},{4,28},{5,29},{6,30},{7,31},{8,0},{9,1... | collective-permute-start | bytes 196616 | tf_op jit(solution)/shard_map/ppermute | solution.py:29
  86.4 1.3 collective-permute-start.24
  87.7 2.1 %collective-permute-done.22 = bf16[128,256]{1,0:T(8,128)(2,1)S(1)} collective-permute-done((bf16[128,256]{1,0:T(8,128)(2,1)S(1)}, bf16[128,256]{1,0:T(8,128)(2,1)S(1)}, u32[]{:S(2)}, u32[]{:S(2)}) %collective-permute-start.22) | collective-permute-done | bytes 65568 | tf_op jit(solution)/shard_map/ppermute | solution.py:29
  89.8 3.1 %collective-permute-done.23 = bf16[128,256]{1,0:T(8,128)(2,1)S(1)} collective-permute-done((bf16[128,256]{1,0:T(8,128)(2,1)S(1)}, bf16[128,256]{1,0:T(8,128)(2,1)S(1)}, u32[]{:S(2)}, u32[]{:S(2)}) %collective-permute-start.23) | collective-permute-done | bytes 65568 | tf_op jit(solution)/shard_map/ppermute | solution.py:29
  92.9 0.7 collective-permute-done.24
  93.9 0.5 collective-permute-start.26
  94.4 2.7 %collective-permute-start.27 = (bf16[4,128,256]{2,1,0:T(8,128)(2,1)S(1)}, bf16[4,128,256]{2,1,0:T(8,128)(2,1)S(1)}, u32[]{:S(2)}, u32[]{:S(2)}) collective-permute-start(bf16[4,128,256]{2,1,0:T(8,128)(2,1)S(1)} %constant_dynamic-slice_fusion), channel_id=1, source_target_pairs={{0,6},{1,7},{2,0},{3,1},{4,2},{5,3},{6,4},{7,5},{8,14},{9,15},{10,... | collective-permute-start | bytes 786440 | tf_op jit(solution)/shard_map/ppermute | solution.py:29
  97.1 1.0 collective-permute-start.29
  98.1 1.0 collective-permute-start.31
  99.0 1.1 convolution_convert_fusion.1
  100.2 5.5 %all-to-all-start.1 = ((bf16[16,24,512]{2,1,0:T(8,128)(2,1)}), bf16[16,24,512]{2,1,0:T(8,128)(2,1)S(1)}, u32[]{:S(2)}, u32[]{:S(2)}) async-start(bf16[16,24,512]{2,1,0:T(8,128)(2,1)} %bitcast.30), calls=%async_computation.1 | async-start | bytes 786432 | tf_op jit(solution)/shard_map/all_to_all | solution.py:239
  105.7 2.9 %collective-permute-done.27 = bf16[4,128,256]{2,1,0:T(8,128)(2,1)S(1)} collective-permute-done((bf16[4,128,256]{2,1,0:T(8,128)(2,1)S(1)}, bf16[4,128,256]{2,1,0:T(8,128)(2,1)S(1)}, u32[]{:S(2)}, u32[]{:S(2)}) %collective-permute-start.27) | collective-permute-done | bytes 262176 | tf_op jit(solution)/shard_map/ppermute | solution.py:29
  108.6 0.5 collective-permute-start.30
  109.1 3.2 %collective-permute-done.31 = bf16[4,128,256]{2,1,0:T(8,128)(2,1)S(1)} collective-permute-done((bf16[4,128,256]{2,1,0:T(8,128)(2,1)S(1)}, bf16[4,128,256]{2,1,0:T(8,128)(2,1)S(1)}, u32[]{:S(2)}, u32[]{:S(2)}) %collective-permute-start.31) | collective-permute-done | bytes 262176 | tf_op jit(solution)/shard_map/ppermute | solution.py:29
  112.5 2.4 %all-to-all-done.1 = bf16[16,24,512]{2,1,0:T(8,128)(2,1)S(1)} async-done(((bf16[16,24,512]{2,1,0:T(8,128)(2,1)}), bf16[16,24,512]{2,1,0:T(8,128)(2,1)S(1)}, u32[]{:S(2)}, u32[]{:S(2)}) %all-to-all-start.1) | async-done | bytes 393248 | tf_op jit(solution)/shard_map/all_to_all | solution.py:239
  114.9 1.4 fusion.11
  116.8 1.2 maximum_select_fusion.3
  118.3 1.9 %convolution_convert_fusion.5 = bf16[512,256]{1,0:T(8,128)(2,1)S(1)} fusion(bf16[1024,1024]{1,0:T(8,128)(2,1)} %all-gather.2.cloned.1.call-done, bf16[4,1024,256]{2,1,0:T(8,128)(2,1)S(1)} %pad_maximum_fusion, s32[]{:T(128)S(6)} %select_n.194), kind=kOutput, calls=%fused_computation.6 | convolution fusion | flops 268566528 | bytes 1835012 | tf_op jit(solution)/shard_map/dot_general | solution.py:221
  120.2 1.4 collective-permute-start.33
  121.5 0.5 convolution_convert_fusion.4
  122.0 0.8 collective-permute-start.34
  122.8 0.5 convolution_convert_fusion.3
  123.5 0.5 convolution_convert_fusion.2
  124.0 3.4 %collective-permute-start.37 = (bf16[512,256]{1,0:T(8,128)(2,1)S(1)}, bf16[512,256]{1,0:T(8,128)(2,1)S(1)}, u32[]{:S(2)}, u32[]{:S(2)}) collective-permute-start(bf16[512,256]{1,0:T(8,128)(2,1)S(1)} %convolution_convert_fusion.2), channel_id=1, source_target_pairs={{0,96},{1,97},{2,98},{3,99},{4,100},{5,101},{6,102},{7,103},{8,104... | collective-permute-start | bytes 786440 | tf_op jit(solution)/shard_map/ppermute | solution.py:29
  127.4 5.2 %collective-permute-done.34 = bf16[512,256]{1,0:T(8,128)(2,1)S(1)} collective-permute-done((bf16[512,256]{1,0:T(8,128)(2,1)S(1)}, bf16[512,256]{1,0:T(8,128)(2,1)S(1)}, u32[]{:S(2)}, u32[]{:S(2)}) %collective-permute-start.34) | collective-permute-done | bytes 262176 | tf_op jit(solution)/shard_map/ppermute | solution.py:29
  132.6 0.5 add_convert_fusion.1
  133.2 0.5 add_convert_fusion
  133.7 3.3 %collective-permute-start.38 = (bf16[512,256]{1,0:T(8,128)(2,1)S(1)}, bf16[512,256]{1,0:T(8,128)(2,1)S(1)}, u32[]{:S(2)}, u32[]{:S(2)}) collective-permute-start(bf16[512,256]{1,0:T(8,128)(2,1)S(1)} %add_convert_fusion), channel_id=1, source_target_pairs={{0,96},{1,97},{2,98},{3,99},{4,100},{5,101},{6,102},{7,103},{8,104... | collective-permute-start | bytes 786440 | tf_op jit(solution)/shard_map/ppermute | solution.py:29
  136.9 5.1 %collective-permute-done.35 = bf16[512,256]{1,0:T(8,128)(2,1)S(1)} collective-permute-done((bf16[512,256]{1,0:T(8,128)(2,1)S(1)}, bf16[512,256]{1,0:T(8,128)(2,1)S(1)}, u32[]{:S(2)}, u32[]{:S(2)}) %collective-permute-start.35) | collective-permute-done | bytes 262176 | tf_op jit(solution)/shard_map/ppermute | solution.py:29
  142.0 0.5 convert_add_fusion.2
  142.5 0.5 convert_add_fusion.1
  143.0 1.0 pad_maximum_fusion.2
  (108 shorter events, 4.1 us)
Async XLA Ops:
  7.3 1.0 copy-start.1
  8.2 10.8 %copy-start.11 = (s32[256,1]{0,1:T(1,128)S(1)}, s32[256,1]{0,1:T(1,128)}, u32[]{:S(2)}) copy-start(s32[256,1]{0,1:T(1,128)} %param.21) | copy-start | bytes 3076
  13.6 5.7 %copy-start.2 = (bf16[384,512]{1,0:T(8,128)(2,1)S(1)}, bf16[384,512]{1,0:T(8,128)(2,1)}, u32[]{:S(2)}) copy-start(bf16[384,512]{1,0:T(8,128)(2,1)} %param.23) | copy-start | bytes 1179652
  13.6 5.7 %copy-start.4 = (bf16[384,512]{1,0:T(8,128)(2,1)S(1)}, bf16[384,512]{1,0:T(8,128)(2,1)}, u32[]{:S(2)}) copy-start(bf16[384,512]{1,0:T(8,128)(2,1)} %param.17) | copy-start | bytes 1179652
  13.6 2.0 %collective-permute-start.4 = (bf16[256,1024]{1,0:T(8,128)(2,1)S(1)}, bf16[256,1024]{1,0:T(8,128)(2,1)S(1)}, u32[]{:S(2)}, u32[]{:S(2)}) collective-permute-start(bf16[256,1024]{1,0:T(8,128)(2,1)S(1)} %get-tuple-element.35), channel_id=1, source_target_pairs={{0,1},{1,0},{2,3},{3,2},{4,5},{5,4},{6,7},{7,6},{8,9},{9,8},{10,11... | collective-permute-start | bytes 1572872 | tf_op jit(solution)/shard_map/ppermute | solution.py:29
  13.7 6.6 %collective-permute-start.1 = (bf16[256,1024]{1,0:T(8,128)(2,1)S(1)}, bf16[256,1024]{1,0:T(8,128)(2,1)S(1)}, u32[]{:S(2)}, u32[]{:S(2)}) collective-permute-start(bf16[256,1024]{1,0:T(8,128)(2,1)S(1)} %get-tuple-element.31), channel_id=1, source_target_pairs={{0,1},{1,0},{2,3},{3,2},{4,5},{5,4},{6,7},{7,6},{8,9},{9,8},{10,11... | collective-permute-start | bytes 1572872 | tf_op jit(solution)/shard_map/ppermute | solution.py:29
  14.2 15.4 %collective-permute-start.3 = (bf16[256,1024]{1,0:T(8,128)(2,1)S(1)}, bf16[256,1024]{1,0:T(8,128)(2,1)S(1)}, u32[]{:S(2)}, u32[]{:S(2)}) collective-permute-start(bf16[256,1024]{1,0:T(8,128)(2,1)S(1)} %get-tuple-element.33), channel_id=1, source_target_pairs={{0,1},{1,0},{2,3},{3,2},{4,5},{5,4},{6,7},{7,6},{8,9},{9,8},{10,11... | collective-permute-start | bytes 1572872 | tf_op jit(solution)/shard_map/ppermute | solution.py:29
  14.3 26.5 %collective-permute-start = (bf16[256,1024]{1,0:T(8,128)(2,1)S(1)}, bf16[256,1024]{1,0:T(8,128)(2,1)}, u32[]{:S(2)}, u32[]{:S(2)}) collective-permute-start(bf16[256,1024]{1,0:T(8,128)(2,1)S(1)} %get-tuple-element.29), channel_id=1, source_target_pairs={{0,1},{1,0},{2,3},{3,2},{4,5},{5,4},{6,7},{7,6},{8,9},{9,8},{10,11... | collective-permute-start | bytes 1572872 | tf_op jit(solution)/shard_map/ppermute | solution.py:29
  15.8 9.0 %collective-permute-start.8 = (bf16[128,1024]{1,0:T(8,128)(2,1)S(1)}, bf16[128,1024]{1,0:T(8,128)(2,1)S(1)}, u32[]{:S(2)}, u32[]{:S(2)}) collective-permute-start(bf16[128,1024]{1,0:T(8,128)(2,1)S(1)} %get-tuple-element.68), channel_id=1, source_target_pairs={{0,6},{1,7},{2,0},{3,1},{4,2},{5,3},{6,4},{7,5},{8,14},{9,15},{10,... | collective-permute-start | bytes 786440 | tf_op jit(solution)/shard_map/ppermute | solution.py:29
  20.3 12.4 %copy-start.7 = (f32[512]{0:T(512)S(1)}, f32[512]{0:T(512)}, u32[]{:S(2)}) copy-start(f32[512]{0:T(512)} %param.20) | copy-start | bytes 6148
  20.3 12.4 %copy-start.8 = (f32[512]{0:T(512)S(1)}, f32[512]{0:T(512)}, u32[]{:S(2)}) copy-start(f32[512]{0:T(512)} %param.19) | copy-start | bytes 6148
  20.3 12.4 %copy-start.9 = (f32[512]{0:T(512)S(1)}, f32[512]{0:T(512)}, u32[]{:S(2)}) copy-start(f32[512]{0:T(512)} %param.18) | copy-start | bytes 6148
  20.3 12.4 %copy-start.6 = (bf16[256,1024]{1,0:T(8,128)(2,1)S(1)}, bf16[256,1024]{1,0:T(8,128)(2,1)}, u32[]{:S(2)}) copy-start(bf16[256,1024]{1,0:T(8,128)(2,1)} %param.14) | copy-start | bytes 1572868
  20.3 9.3 %collective-permute-start.5 = (bf16[128,1024]{1,0:T(8,128)(2,1)S(1)}, bf16[128,1024]{1,0:T(8,128)(2,1)S(1)}, u32[]{:S(2)}, u32[]{:S(2)}) collective-permute-start(bf16[128,1024]{1,0:T(8,128)(2,1)S(1)} %get-tuple-element.67), channel_id=1, source_target_pairs={{0,2},{1,3},{2,4},{3,5},{4,6},{5,7},{6,0},{7,1},{8,10},{9,11},{10,... | collective-permute-start | bytes 786440 | tf_op jit(solution)/shard_map/ppermute | solution.py:29
  25.9 7.0 %copy-start.12 = (s32[256]{0:T(256)S(1)}, s32[256]{0:T(256)}, u32[]{:S(2)}) copy-start(s32[256]{0:T(256)} %param.22) | copy-start | bytes 3076
  25.9 15.1 %collective-permute-start.2 = (bf16[128,1024]{1,0:T(8,128)(2,1)}, bf16[128,1024]{1,0:T(8,128)(2,1)}, u32[]{:S(2)}, u32[]{:S(2)}) collective-permute-start(bf16[128,1024]{1,0:T(8,128)(2,1)} %get-tuple-element.63), channel_id=1, source_target_pairs={{0,6},{1,7},{2,0},{3,1},{4,2},{5,3},{6,4},{7,5},{8,14},{9,15},{10,... | collective-permute-start | bytes 786440 | tf_op jit(solution)/shard_map/ppermute | solution.py:29
  29.6 11.4 %collective-permute-start.9 = (bf16[128,1024]{1,0:T(8,128)(2,1)}, bf16[128,1024]{1,0:T(8,128)(2,1)}, u32[]{:S(2)}, u32[]{:S(2)}) collective-permute-start(bf16[128,1024]{1,0:T(8,128)(2,1)} %get-tuple-element.64), channel_id=1, source_target_pairs={{0,6},{1,7},{2,0},{3,1},{4,2},{5,3},{6,4},{7,5},{8,14},{9,15},{10,... | collective-permute-start | bytes 786440 | tf_op jit(solution)/shard_map/ppermute | solution.py:29
  30.7 10.8 %collective-permute-start.6 = (bf16[128,1024]{1,0:T(8,128)(2,1)}, bf16[128,1024]{1,0:T(8,128)(2,1)}, u32[]{:S(2)}, u32[]{:S(2)}) collective-permute-start(bf16[128,1024]{1,0:T(8,128)(2,1)} %get-tuple-element.65), channel_id=1, source_target_pairs={{0,2},{1,3},{2,4},{3,5},{4,6},{5,7},{6,0},{7,1},{8,10},{9,11},{10,... | collective-permute-start | bytes 786440 | tf_op jit(solution)/shard_map/ppermute | solution.py:29
  32.6 12.4 %collective-permute-start.7 = (bf16[128,1024]{1,0:T(8,128)(2,1)}, bf16[128,1024]{1,0:T(8,128)(2,1)}, u32[]{:S(2)}, u32[]{:S(2)}) collective-permute-start(bf16[128,1024]{1,0:T(8,128)(2,1)} %get-tuple-element.66), channel_id=1, source_target_pairs={{0,2},{1,3},{2,4},{3,5},{4,6},{5,7},{6,0},{7,1},{8,10},{9,11},{10,... | collective-permute-start | bytes 786440 | tf_op jit(solution)/shard_map/ppermute | solution.py:29
  32.9 20.8 %all-to-all-start = ((bf16[16,24,1024]{2,1,0:T(8,128)(2,1)}), bf16[16,24,1024]{2,1,0:T(8,128)(2,1)S(1)}, u32[]{:S(2)}, u32[]{:S(2)}) async-start(bf16[16,24,1024]{2,1,0:T(8,128)(2,1)} %bitcast.16), calls=%async_computation | async-start | bytes 1572864 | tf_op jit(solution)/shard_map/all_to_all | solution.py:162
  40.8 77.5 %all-gather.2.cloned.1.call-start = ((), (), s32[]{:S(2)}) async-start(), calls=%async_computation.2 | async-start | bytes 2621440 | tf_op jit(solution)/shard_map/all_gather | solution.py:168
  40.9 8.0 %collective-permute-start.21 = (f32[3,512]{1,0:T(4,128)S(1)}, f32[3,512]{1,0:T(4,128)S(1)}, u32[]{:S(2)}, u32[]{:S(2)}) collective-permute-start(f32[3,512]{1,0:T(4,128)S(1)} %pad_maximum_fusion.4), channel_id=1, source_target_pairs={{0,1},{1,0},{2,3},{3,2},{4,5},{5,4},{6,7},{7,6},{8,9},{9,8},{10,11... | collective-permute-start | bytes 18440 | tf_op jit(solution)/shard_map/ppermute | solution.py:29
  45.0 1.7 %copy-start.10 = (f32[1024]{0:T(1024)S(1)}, f32[1024]{0:T(1024)}, u32[]{:S(2)}) copy-start(f32[1024]{0:T(1024)} %param.15) | copy-start | bytes 12292
  47.1 11.6 %copy-start = (bf16[256,1024]{1,0:T(8,128)(2,1)}, bf16[256,1024]{1,0:T(8,128)(2,1)S(1)}, u32[]{:S(2)}) copy-start(bf16[256,1024]{1,0:T(8,128)(2,1)S(1)} %get-tuple-element.41.rows) | copy-start | bytes 1572868
  47.1 1.2 collective-permute-start.17
  48.4 3.6 %collective-permute-start.18 = (f32[2,128]{1,0:T(2,128)S(1)}, f32[2,128]{1,0:T(2,128)S(1)}, u32[]{:S(2)}, u32[]{:S(2)}) collective-permute-start(f32[2,128]{1,0:T(2,128)S(1)} %bitcast_add_fusion), channel_id=1, source_target_pairs={{0,2},{1,3},{2,0},{3,1},{4,6},{5,7},{6,4},{7,5},{8,10},{9,11},{10,... | collective-permute-start | bytes 3080 | tf_op jit(solution)/shard_map/ppermute | solution.py:29
  51.9 7.0 %collective-permute-start.19 = (f32[2,128]{1,0:T(2,128)S(1)}, f32[2,128]{1,0:T(2,128)S(1)}, u32[]{:S(2)}, u32[]{:S(2)}) collective-permute-start(f32[2,128]{1,0:T(2,128)S(1)} %fusion.91), channel_id=1, source_target_pairs={{0,4},{1,5},{2,6},{3,7},{4,0},{5,1},{6,2},{7,3},{8,12},{9,13},{10,... | collective-permute-start | bytes 3080 | tf_op jit(solution)/shard_map/ppermute | solution.py:29
  58.8 1.6 %collective-permute-start.12 = (bf16[128,1024]{1,0:T(8,128)(2,1)S(1)}, bf16[128,1024]{1,0:T(8,128)(2,1)S(1)}, u32[]{:S(2)}, u32[]{:S(2)}) collective-permute-start(bf16[128,1024]{1,0:T(8,128)(2,1)S(1)} %get-tuple-element.45), channel_id=1, source_target_pairs={{0,1},{1,0},{2,3},{3,2},{4,5},{5,4},{6,7},{7,6},{8,9},{9,8},{10,11... | collective-permute-start | bytes 786440 | tf_op jit(solution)/shard_map/ppermute | solution.py:29
  58.9 2.6 %collective-permute-start.10 = (bf16[128,1024]{1,0:T(8,128)(2,1)S(1)}, bf16[128,1024]{1,0:T(8,128)(2,1)S(1)}, u32[]{:S(2)}, u32[]{:S(2)}) collective-permute-start(bf16[128,1024]{1,0:T(8,128)(2,1)S(1)} %get-tuple-element.43), channel_id=1, source_target_pairs={{0,1},{1,0},{2,3},{3,2},{4,5},{5,4},{6,7},{7,6},{8,9},{9,8},{10,11... | collective-permute-start | bytes 786440 | tf_op jit(solution)/shard_map/ppermute | solution.py:29
  60.5 9.8 %collective-permute-start.13 = (bf16[128,1024]{1,0:T(8,128)(2,1)S(1)}, bf16[128,1024]{1,0:T(8,128)(2,1)S(1)}, u32[]{:S(2)}, u32[]{:S(2)}) collective-permute-start(bf16[128,1024]{1,0:T(8,128)(2,1)S(1)} %add_convert_fusion.3), channel_id=1, source_target_pairs={{0,2},{1,3},{2,4},{3,5},{4,6},{5,7},{6,0},{7,1},{8,10},{9,11},{10,... | collective-permute-start | bytes 786440 | tf_op jit(solution)/shard_map/ppermute | solution.py:29
  61.0 9.9 %collective-permute-start.14 = (bf16[128,1024]{1,0:T(8,128)(2,1)S(1)}, bf16[128,1024]{1,0:T(8,128)(2,1)S(1)}, u32[]{:S(2)}, u32[]{:S(2)}) collective-permute-start(bf16[128,1024]{1,0:T(8,128)(2,1)S(1)} %get-tuple-element.47), channel_id=1, source_target_pairs={{0,1},{1,0},{2,3},{3,2},{4,5},{5,4},{6,7},{7,6},{8,9},{9,8},{10,11... | collective-permute-start | bytes 786440 | tf_op jit(solution)/shard_map/ppermute | solution.py:29
  61.0 12.6 %collective-permute-start.16 = (bf16[128,1024]{1,0:T(8,128)(2,1)S(1)}, bf16[128,1024]{1,0:T(8,128)(2,1)S(1)}, u32[]{:S(2)}, u32[]{:S(2)}) collective-permute-start(bf16[128,1024]{1,0:T(8,128)(2,1)S(1)} %get-tuple-element.49), channel_id=1, source_target_pairs={{0,1},{1,0},{2,3},{3,2},{4,5},{5,4},{6,7},{7,6},{8,9},{9,8},{10,11... | collective-permute-start | bytes 786440 | tf_op jit(solution)/shard_map/ppermute | solution.py:29
  61.6 15.5 %collective-permute-start.11 = (bf16[128,1024]{1,0:T(8,128)(2,1)S(1)}, bf16[128,1024]{1,0:T(8,128)(2,1)S(1)}, u32[]{:S(2)}, u32[]{:S(2)}) collective-permute-start(bf16[128,1024]{1,0:T(8,128)(2,1)S(1)} %add_convert_fusion.4), channel_id=1, source_target_pairs={{0,4},{1,5},{2,6},{3,7},{4,0},{5,1},{6,2},{7,3},{8,12},{9,13},{10,... | collective-permute-start | bytes 786440 | tf_op jit(solution)/shard_map/ppermute | solution.py:29
  70.8 2.8 %collective-permute-start.20 = (bf16[128,1024]{1,0:T(8,128)(2,1)S(1)}, bf16[128,1024]{1,0:T(8,128)(2,1)S(1)}, u32[]{:S(2)}, u32[]{:S(2)}) collective-permute-start(bf16[128,1024]{1,0:T(8,128)(2,1)S(1)} %get-tuple-element.62), channel_id=1, source_target_pairs={{0,1},{1,0},{2,3},{3,2},{4,5},{5,4},{6,7},{7,6},{8,9},{9,8},{10,11... | collective-permute-start | bytes 786440 | tf_op jit(solution)/shard_map/ppermute | solution.py:29
  71.0 11.6 %collective-permute-start.15 = (bf16[128,1024]{1,0:T(8,128)(2,1)S(1)}, bf16[128,1024]{1,0:T(8,128)(2,1)S(1)}, u32[]{:S(2)}, u32[]{:S(2)}) collective-permute-start(bf16[128,1024]{1,0:T(8,128)(2,1)S(1)} %add_convert_fusion.2), channel_id=1, source_target_pairs={{0,6},{1,7},{2,0},{3,1},{4,2},{5,3},{6,4},{7,5},{8,14},{9,15},{10,... | collective-permute-start | bytes 786440 | tf_op jit(solution)/shard_map/ppermute | solution.py:29
  83.2 6.5 %collective-permute-start.22 = (bf16[128,256]{1,0:T(8,128)(2,1)S(1)}, bf16[128,256]{1,0:T(8,128)(2,1)S(1)}, u32[]{:S(2)}, u32[]{:S(2)}) collective-permute-start(bf16[128,256]{1,0:T(8,128)(2,1)S(1)} %get-tuple-element.73), channel_id=1, source_target_pairs={{0,24},{1,25},{2,26},{3,27},{4,28},{5,29},{6,30},{7,31},{8,0},{9,1... | collective-permute-start | bytes 196616 | tf_op jit(solution)/shard_map/ppermute | solution.py:29
  86.4 6.5 %collective-permute-start.23 = (bf16[128,256]{1,0:T(8,128)(2,1)S(1)}, bf16[128,256]{1,0:T(8,128)(2,1)S(1)}, u32[]{:S(2)}, u32[]{:S(2)}) collective-permute-start(bf16[128,256]{1,0:T(8,128)(2,1)S(1)} %get-tuple-element.72), channel_id=1, source_target_pairs={{0,16},{1,17},{2,18},{3,19},{4,20},{5,21},{6,22},{7,23},{8,24},{9,... | collective-permute-start | bytes 196616 | tf_op jit(solution)/shard_map/ppermute | solution.py:29
  86.4 7.2 %collective-permute-start.24 = (bf16[128,256]{1,0:T(8,128)(2,1)S(1)}, bf16[128,256]{1,0:T(8,128)(2,1)S(1)}, u32[]{:S(2)}, u32[]{:S(2)}) collective-permute-start(bf16[128,256]{1,0:T(8,128)(2,1)S(1)} %get-tuple-element.71), channel_id=1, source_target_pairs={{0,8},{1,9},{2,10},{3,11},{4,12},{5,13},{6,14},{7,15},{8,16},{9,17... | collective-permute-start | bytes 196616 | tf_op jit(solution)/shard_map/ppermute | solution.py:29
  93.7 21.1 %copy-start.3 = (bf16[384,512]{1,0:T(8,128)(2,1)S(1)}, bf16[384,512]{1,0:T(8,128)(2,1)}, u32[]{:S(2)}) copy-start(bf16[384,512]{1,0:T(8,128)(2,1)} %param.23) | copy-start | bytes 1179652
  93.7 21.1 %copy-start.5 = (bf16[384,512]{1,0:T(8,128)(2,1)S(1)}, bf16[384,512]{1,0:T(8,128)(2,1)}, u32[]{:S(2)}) copy-start(bf16[384,512]{1,0:T(8,128)(2,1)} %param.17) | copy-start | bytes 1179652
  93.8 5.3 %collective-permute-start.25 = (bf16[128,512]{1,0:T(8,128)(2,1)S(1)}, bf16[128,512]{1,0:T(8,128)(2,1)S(1)}, u32[]{:S(2)}, u32[]{:S(2)}) collective-permute-start(bf16[128,512]{1,0:T(8,128)(2,1)S(1)} %get-tuple-element.70), channel_id=1, source_target_pairs={{0,1},{1,0},{2,3},{3,2},{4,5},{5,4},{6,7},{7,6},{8,9},{9,8},{10,11... | collective-permute-start | bytes 393224 | tf_op jit(solution)/shard_map/ppermute | solution.py:29
  93.9 18.4 %collective-permute-start.26 = (bf16[4,128,256]{2,1,0:T(8,128)(2,1)S(1)}, bf16[4,128,256]{2,1,0:T(8,128)(2,1)S(1)}, u32[]{:S(2)}, u32[]{:S(2)}) collective-permute-start(bf16[4,128,256]{2,1,0:T(8,128)(2,1)S(1)} %constant_dynamic-slice_fusion), channel_id=1, source_target_pairs={{0,1},{1,0},{2,3},{3,2},{4,5},{5,4},{6,7},{7,6},{8,9},{9,8},{10,11... | collective-permute-start | bytes 786440 | tf_op jit(solution)/shard_map/ppermute | solution.py:29
  94.4 14.2 %collective-permute-start.27 = (bf16[4,128,256]{2,1,0:T(8,128)(2,1)S(1)}, bf16[4,128,256]{2,1,0:T(8,128)(2,1)S(1)}, u32[]{:S(2)}, u32[]{:S(2)}) collective-permute-start(bf16[4,128,256]{2,1,0:T(8,128)(2,1)S(1)} %constant_dynamic-slice_fusion), channel_id=1, source_target_pairs={{0,6},{1,7},{2,0},{3,1},{4,2},{5,3},{6,4},{7,5},{8,14},{9,15},{10,... | collective-permute-start | bytes 786440 | tf_op jit(solution)/shard_map/ppermute | solution.py:29
  97.1 11.5 %collective-permute-start.29 = (bf16[4,128,256]{2,1,0:T(8,128)(2,1)S(1)}, bf16[4,128,256]{2,1,0:T(8,128)(2,1)S(1)}, u32[]{:S(2)}, u32[]{:S(2)}) collective-permute-start(bf16[4,128,256]{2,1,0:T(8,128)(2,1)S(1)} %constant_dynamic-slice_fusion), channel_id=1, source_target_pairs={{0,4},{1,5},{2,6},{3,7},{4,0},{5,1},{6,2},{7,3},{8,12},{9,13},{10,... | collective-permute-start | bytes 786440 | tf_op jit(solution)/shard_map/ppermute | solution.py:29
  98.1 14.2 %collective-permute-start.31 = (bf16[4,128,256]{2,1,0:T(8,128)(2,1)S(1)}, bf16[4,128,256]{2,1,0:T(8,128)(2,1)S(1)}, u32[]{:S(2)}, u32[]{:S(2)}) collective-permute-start(bf16[4,128,256]{2,1,0:T(8,128)(2,1)S(1)} %constant_dynamic-slice_fusion), channel_id=1, source_target_pairs={{0,2},{1,3},{2,4},{3,5},{4,6},{5,7},{6,0},{7,1},{8,10},{9,11},{10,... | collective-permute-start | bytes 786440 | tf_op jit(solution)/shard_map/ppermute | solution.py:29
  100.2 14.7 %all-to-all-start.1 = ((bf16[16,24,512]{2,1,0:T(8,128)(2,1)}), bf16[16,24,512]{2,1,0:T(8,128)(2,1)S(1)}, u32[]{:S(2)}, u32[]{:S(2)}) async-start(bf16[16,24,512]{2,1,0:T(8,128)(2,1)} %bitcast.30), calls=%async_computation.1 | async-start | bytes 786432 | tf_op jit(solution)/shard_map/all_to_all | solution.py:239
  108.6 7.7 %collective-permute-start.28 = (bf16[4,128,256]{2,1,0:T(8,128)(2,1)S(1)}, bf16[4,128,256]{2,1,0:T(8,128)(2,1)S(1)}, u32[]{:S(2)}, u32[]{:S(2)}) collective-permute-start(bf16[4,128,256]{2,1,0:T(8,128)(2,1)S(1)} %collective-permute-done.27), channel_id=1, source_target_pairs={{0,1},{1,0},{2,3},{3,2},{4,5},{5,4},{6,7},{7,6},{8,9},{9,8},{10,11... | collective-permute-start | bytes 786440 | tf_op jit(solution)/shard_map/ppermute | solution.py:29
  108.6 8.0 %collective-permute-start.30 = (bf16[4,128,256]{2,1,0:T(8,128)(2,1)S(1)}, bf16[4,128,256]{2,1,0:T(8,128)(2,1)S(1)}, u32[]{:S(2)}, u32[]{:S(2)}) collective-permute-start(bf16[4,128,256]{2,1,0:T(8,128)(2,1)S(1)} %collective-permute-done.29), channel_id=1, source_target_pairs={{0,1},{1,0},{2,3},{3,2},{4,5},{5,4},{6,7},{7,6},{8,9},{9,8},{10,11... | collective-permute-start | bytes 786440 | tf_op jit(solution)/shard_map/ppermute | solution.py:29
  112.2 4.5 %collective-permute-start.32 = (bf16[4,128,256]{2,1,0:T(8,128)(2,1)S(1)}, bf16[4,128,256]{2,1,0:T(8,128)(2,1)}, u32[]{:S(2)}, u32[]{:S(2)}) collective-permute-start(bf16[4,128,256]{2,1,0:T(8,128)(2,1)S(1)} %collective-permute-done.31), channel_id=1, source_target_pairs={{0,1},{1,0},{2,3},{3,2},{4,5},{5,4},{6,7},{7,6},{8,9},{9,8},{10,11... | collective-permute-start | bytes 786440 | tf_op jit(solution)/shard_map/ppermute | solution.py:29
  118.3 3.2 %copy-start.13 = (bf16[1024,1024]{1,0:T(8,128)(2,1)S(1)}, bf16[1024,1024]{1,0:T(8,128)(2,1)}, u32[]{:S(2)}) copy-start(bf16[1024,1024]{1,0:T(8,128)(2,1)} %all-gather.2.cloned.1.call-done) | copy-start | bytes 6291460
  120.2 16.8 %collective-permute-start.33 = (bf16[512,256]{1,0:T(8,128)(2,1)S(1)}, bf16[512,256]{1,0:T(8,128)(2,1)S(1)}, u32[]{:S(2)}, u32[]{:S(2)}) collective-permute-start(bf16[512,256]{1,0:T(8,128)(2,1)S(1)} %convolution_convert_fusion.5), channel_id=1, source_target_pairs={{0,96},{1,97},{2,98},{3,99},{4,100},{5,101},{6,102},{7,103},{8,104... | collective-permute-start | bytes 786440 | tf_op jit(solution)/shard_map/ppermute | solution.py:29
  122.0 10.5 %collective-permute-start.34 = (bf16[512,256]{1,0:T(8,128)(2,1)S(1)}, bf16[512,256]{1,0:T(8,128)(2,1)S(1)}, u32[]{:S(2)}, u32[]{:S(2)}) collective-permute-start(bf16[512,256]{1,0:T(8,128)(2,1)S(1)} %convolution_convert_fusion.4), channel_id=1, source_target_pairs={{0,32},{1,33},{2,34},{3,35},{4,36},{5,37},{6,38},{7,39},{8,40},{9,... | collective-permute-start | bytes 786440 | tf_op jit(solution)/shard_map/ppermute | solution.py:29
  123.3 19.2 %collective-permute-start.36 = (bf16[512,256]{1,0:T(8,128)(2,1)S(1)}, bf16[512,256]{1,0:T(8,128)(2,1)S(1)}, u32[]{:S(2)}, u32[]{:S(2)}) collective-permute-start(bf16[512,256]{1,0:T(8,128)(2,1)S(1)} %convolution_convert_fusion.3), channel_id=1, source_target_pairs={{0,32},{1,33},{2,34},{3,35},{4,36},{5,37},{6,38},{7,39},{8,40},{9,... | collective-permute-start | bytes 786440 | tf_op jit(solution)/shard_map/ppermute | solution.py:29
  124.0 9.2 %collective-permute-start.37 = (bf16[512,256]{1,0:T(8,128)(2,1)S(1)}, bf16[512,256]{1,0:T(8,128)(2,1)S(1)}, u32[]{:S(2)}, u32[]{:S(2)}) collective-permute-start(bf16[512,256]{1,0:T(8,128)(2,1)S(1)} %convolution_convert_fusion.2), channel_id=1, source_target_pairs={{0,96},{1,97},{2,98},{3,99},{4,100},{5,101},{6,102},{7,103},{8,104... | collective-permute-start | bytes 786440 | tf_op jit(solution)/shard_map/ppermute | solution.py:29
  133.1 9.0 %collective-permute-start.35 = (bf16[512,256]{1,0:T(8,128)(2,1)S(1)}, bf16[512,256]{1,0:T(8,128)(2,1)S(1)}, u32[]{:S(2)}, u32[]{:S(2)}) collective-permute-start(bf16[512,256]{1,0:T(8,128)(2,1)S(1)} %add_convert_fusion.1), channel_id=1, source_target_pairs={{0,32},{1,33},{2,34},{3,35},{4,36},{5,37},{6,38},{7,39},{8,40},{9,... | collective-permute-start | bytes 786440 | tf_op jit(solution)/shard_map/ppermute | solution.py:29
  133.7 8.9 %collective-permute-start.38 = (bf16[512,256]{1,0:T(8,128)(2,1)S(1)}, bf16[512,256]{1,0:T(8,128)(2,1)S(1)}, u32[]{:S(2)}, u32[]{:S(2)}) collective-permute-start(bf16[512,256]{1,0:T(8,128)(2,1)S(1)} %add_convert_fusion), channel_id=1, source_target_pairs={{0,96},{1,97},{2,98},{3,99},{4,100},{5,101},{6,102},{7,103},{8,104... | collective-permute-start | bytes 786440 | tf_op jit(solution)/shard_map/ppermute | solution.py:29
Sparse Core Ops, SparseCore 0:
  59.0 34.3 all-gather.1

commit v4 on v3

--- a/solution.py
+++ b/solution.py
@@ -7,6 +7,7 @@
 from jax.experimental.pallas import tpu as pltpu
 from jax.sharding import Mesh, PartitionSpec as P
 
+LINES = 8
 AXES = ("x", "z", "y", "c")
 N = 4
 BF = jnp.bfloat16
@@ -89,53 +90,45 @@
     return jax.ShapeDtypeStruct((rows, columns), dtype)
 
 
-def project(context, w_out, width):
+def project(context, w_out, width, exchange):
     y, c = lax.axis_index("y"), lax.axis_index("c")
-    tokens = context.shape[0]
-    half = tokens // 2
     steps = (2, 1, -1, 0)
 
     def emit(i, value, starts, extra, outs):
-        value = value.astype(BF)
-        if i < N:
-            outs[i][...] = value
-        else:
-            outs[2 * i - N][...] = value[:half]
-            outs[2 * i - N + 1][...] = value[half:]
+        outs[i][...] = value.astype(BF)
 
     starts = jnp.stack(
         [(lax.rem(y + d + N, N) * 2 + core) * width for core in (1 - c, c) for d in steps]
     ).astype(jnp.int32)
-    shapes = [shape(tokens, width, BF)] * N + [shape(half, width, BF)] * (2 * N)
-    outs = products(context, w_out, starts, 2 * N, width, emit, shapes)
+    outs = products(context, w_out, starts, 2 * N, width, emit, [shape(context.shape[0], width, BF)] * (2 * N))
     got = [swap(out) for out in outs[:N]]
-    far, right, left, own = [
-        (add(outs[N + 2 * i], got[i][:half]), add(outs[N + 2 * i + 1], got[i][half:])) for i in range(N)
-    ]
-    from_left, from_right = along_y(far[0].astype(BF), 1), along_y(far[1].astype(BF), -1)
-    right_b, left_a = right[1].astype(BF), left[0].astype(BF)
-    low_b, up_a = along_y(right_b, 1), along_y(left_a, -1)
-    last = add(right[0], from_left).astype(BF), add(left[1], from_right).astype(BF)
-    low_a, up_b = along_y(last[0], 1), along_y(last[1], -1)
-    return add(own[0], up_a, low_a), add(own[1], low_b, up_b), last
-
-
-def join(rows, w_join, width):
-    y, c = lax.axis_index("y"), lax.axis_index("c")
+    sums = [add(outs[N + i], got[i]) for i in range(N)]
+    sends = [value.astype(BF) for value in sums[:-1]]
+    terms = [along_y(value, d) for value, d in zip(sends, steps)]
+    return add(sums[-1], *terms), exchange(*sends)
+
+
+def join(rows, w_join, width, squares):
+    y = lax.axis_index("y")
     half = rows.shape[0] // 2
     steps = (2, 1, -1, 0)
 
     def emit(i, value, starts, extra, outs):
-        first, second = value[:half].astype(BF), value[half:].astype(BF)
-        mine = starts[N] == 0
-        outs[2 * i][...] = jnp.where(mine, second, first)
-        outs[2 * i + 1][...] = jnp.where(mine, first, second)
-
-    starts = jnp.stack([lax.rem(y + d + N, N) * width for d in steps] + [c]).astype(jnp.int32)
+        outs[2 * i][...] = value[half:].astype(BF)
+        outs[2 * i + 1][...] = value[:half].astype(BF)
+
+    starts = jnp.stack([lax.rem(y + d + N, N) * width for d in steps]).astype(jnp.int32)
     outs = products(rows, w_join, starts, N, width, emit, [shape(half, width, BF)] * (2 * N))
     got = [swap(out) for out in outs[::2]]
-    terms = [along_y(add(outs[2 * i + 1], got[i]).astype(BF), steps[i]) for i in range(N - 1)]
-    return [*terms, outs[-1], got[-1]]
+    squares = squares[0] + swap(after(squares[1], outs[-1]))
+    high = lax.reduce_precision(squares, 8, 7)
+    middle = lax.reduce_precision(squares - high, 8, 7)
+    lines = jnp.stack([high, middle, squares - high - middle])
+    lines = jnp.pad(lines, ((0, LINES - 3), (0, width - half))).astype(BF)
+    sends = [jnp.concatenate([add(outs[2 * i + 1], got[i]).astype(BF), lines], axis=0) for i in range(N - 1)]
+    terms = [along_y(sends[i], steps[i]) for i in range(N - 1)]
+    total = squares + sum(jnp.sum(term[half : half + 3, :half].astype(F32), axis=0) for term in terms)
+    return [outs[-1], got[-1], *[term[:half] for term in terms]], total, sends
 
 
 def body(
@@ -158,25 +151,25 @@
 
     both = jnp.concatenate([dec_state, cotangent], axis=1).reshape(n_owner, most, 2 * features)
 
-    sum_a, sum_b, last = project(context, w_out, width)
-    both = lax.all_to_all(after(both, *last), ("x", "z"), 0, 0, tiled=True).reshape(slot_rows, 2 * features)
+    summed, both = project(
+        context, w_out, width, lambda *others: lax.all_to_all(after(both, *others), ("x", "z"), 0, 0, tiled=True)
+    )
+    both = both.reshape(slot_rows, 2 * features)
     gain, mask = norm_gain[None, :], pad_mask.astype(F32)[:, None]
     residual = residual.astype(F32)
-    mixed = jnp.concatenate([residual[:half] + sum_a, residual[half:] + sum_b], axis=0)
+    mixed = residual + summed
     squares = jnp.sum(mixed * mixed, axis=1)
     rows = (mixed * gain * mask).astype(BF)
-    rows_z = lax.all_gather(rows, "z", axis=0, tiled=True)
-
-    total = squares.reshape(2, -1)
-    total = total + swap(total)
-    total = total + move(total, lambda x, z, y, c: (x, z, y ^ 1, c))
-    total = total + move(total, lambda x, z, y, c: (x, z, y ^ 2, c))
-    scale = lax.rsqrt(total / (width * N * 2) + 1e-05)
-    scale = jnp.where(first, scale[0], scale[1])[:, None]
+    rows = jnp.where(first, rows, jnp.concatenate([rows[half:], rows[:half]], axis=0))
 
     gated, both = lax.optimization_barrier((rows, both))
-    terms = join(gated, w_join, 2 * features)
-    both = jnp.dot(select, after(both, terms[1]), preferred_element_type=F32).astype(BF)
+    squares = squares.reshape(2, half)
+    squares = jnp.where(first, squares[0], squares[1]), jnp.where(first, squares[1], squares[0])
+    terms, total, sends = join(gated, w_join, 2 * features, squares)
+    *terms, rows_1, rows_3 = lax.optimization_barrier((*terms, along_z(rows, -1), along_z(rows, 1)))
+    hidden = add(*terms)
+    scale = lax.rsqrt(total / (width * N * 2) + 1e-05)[:, None]
+    both = jnp.dot(select, after(both, *sends), preferred_element_type=F32).astype(BF)
     keep = jnp.where(first, both[:half], both[half:])
     got = swap(jnp.where(first, both[half:], both[:half]))
 
@@ -190,7 +183,7 @@
     params = jnp.stack([gate_s, gate_h, gate_bias])
     params_t = widen(params, swap(params))
 
-    hidden = (add(*terms) * scale).astype(BF)
+    hidden = (hidden * scale).astype(BF)
 
     def gates(params, state, hidden):
         gate = jax.nn.sigmoid(params[0][None, :] * state + params[1][None, :] * hidden + params[2][None, :])
@@ -205,30 +198,21 @@
         return lax.dynamic_slice_in_dim(grad, lax.rem(z + step + N, N) * quarter, quarter, 1)
 
     others = {f: along_z(quarter_for(-f), -f) for f in (2, 1, 3)}
-    block = jnp.stack([quarter_for(0), others[1], others[2], others[3]] * 2)
-    block = lax.dynamic_slice_in_dim(block, lax.rem(N - z, N), N, 0)
+    block = jnp.stack([quarter_for(0), others[1], others[2], others[3]])
+    rows_2 = along_z(after(rows, block), 2)
     arrived = {d: along_y(block, -d) for d in (2, 1, 3)}
+    arrived[2], rows_2 = lax.optimization_barrier((arrived[2], rows_2))
     pieces = [block, arrived[1], arrived[2], arrived[3]]
     swapped = [swap(piece) for piece in pieces]
-    grads = jnp.stack(
-        [jnp.where(first, jnp.concatenate([a, b], axis=1), jnp.concatenate([b, a], axis=1)) for a, b in zip(pieces, swapped)]
-    )
-    grads = grads.reshape(N, N * tokens, -1)
-
-    def grad_term(step, part):
+    grads = jnp.stack([jnp.stack(pair, axis=1) for pair in zip(pieces, swapped)]).reshape(N, N * tokens, quarter)
+    rows_z = lax.optimization_barrier(jnp.concatenate([rows, rows_1, rows_2, rows_3], axis=0))
+
+    def grad_term(step):
         columns = lax.dynamic_index_in_dim(grads, lax.rem(x + step - y + 2 * N, N), 0, keepdims=False)
-        rows = rows_z[:, : width // 2] if part == 0 else rows_z[:, width // 2 :]
-        return lax.dot_general(rows, columns, (((0,), (0,)), ((), ())), preferred_element_type=F32)
-
-    from_left = along_x(grad_term(2, 0).astype(BF), 1)
-    from_right = along_x(grad_term(2, 1).astype(BF), -1)
-    near = grad_term(1, 1).astype(BF), grad_term(-1, 0).astype(BF)
-    low_b, up_a = along_x(near[0], 1), along_x(near[1], -1)
-    low_a = along_x(add(grad_term(1, 0), from_left).astype(BF), 1)
-    up_b = along_x(add(grad_term(-1, 1), from_right).astype(BF), -1)
-    join_grad = jnp.concatenate(
-        [add(grad_term(0, 0), up_a, low_a), add(grad_term(0, 1), low_b, up_b)], axis=0
-    )
+        return lax.dot_general(rows_z, columns, (((0,), (0,)), ((), ())), preferred_element_type=F32)
+
+    sends = [grad_term(d).astype(BF) for d in (2, 1, -1)]
+    sums = [along_x(value, d) for value, d in zip(sends, (2, 1, -1))]
 
     late_hidden = after(hidden, block)
     keep = jnp.where(first, late_hidden[:, :features], late_hidden[:, features:])
@@ -236,11 +220,13 @@
     rows_h = jnp.where(first, jnp.concatenate([keep, got], axis=0), jnp.concatenate([got, keep], axis=0))
     placed = lax.dot_general(select, rows_h, (((0,), (0,)), ((), ())), preferred_element_type=F32)
     placed = placed.astype(BF).reshape(n_owner, most, features)
-    placed = lax.all_to_all(placed, ("x", "z"), 0, 0, tiled=True).reshape(slot_rows, features).astype(F32)
+    placed = lax.all_to_all(placed, ("x", "z"), 0, 0, tiled=True)
+    placed = placed.reshape(slot_rows, features).astype(F32)
     state = dec_state.astype(F32)
     gate, slope = gates(params, state, placed)
     joined = (state + gate * placed).astype(BF)
     state_grad = (cotangent.astype(F32) * (1.0 + slope * gate_s[None, :])).astype(BF)
+    join_grad = add(grad_term(0), *sums)
     return joined, state_grad, join_grad
 
 

time: 151 us -> 138 us (0.914)
  between operations: 14.8 us -> 1.17 us
  starting transfers between devices: 52.8 us -> 46.5 us
  waiting for transfers between devices: 53.4 us -> 56.5 us
  matrix products: 7.13 us -> 9.88 us
  other arithmetic: 11 us -> 9.13 us
  local copies, waits for them, and re-layouts: 1.38 us -> 2.97 us
    ppermute x39 -> x34, starting transfers between devices: 39.4 us -> 33.2 us  [move(): return lax.ppermute(value, AXES, pairs)]
    ppermute x39 -> x34, waiting for transfers between devices: 50 us -> 55.4 us  [move(): return lax.ppermute(value, AXES, pairs)]
    dot_general x9 -> x5, matrix products: 5.73 us -> 8.48 us  [the longest x4 8 us: grad_term(): lax.dot_general(rows_z, columns, (((0,), (0,)), ((), ())), preferred_elem...]
    all_to_all x2, waiting for transfers between devices: 3.32 us -> 1.08 us  [the longest x1 1.08 us: body(): lax.all_to_all(after(both, *others), ('x', 'z'), 0, 0, tiled=True)]
    reduce_sum x1, other arithmetic: 0.34 us -> 2.24 us  [body(): squares = jnp.sum(mixed * mixed, axis=1)]
    add x3 -> x0, other arithmetic: 1.75 us -> none  [the longest x1 1.74 us: body(): residual[:half] + sum_a]
    select_n x5 -> x2, other arithmetic: 1.88 us -> 0.2 us  [the longest x1 0.19 us: body(): jnp.where(first, rows, jnp.concatenate([rows[half:], rows[:half]], axis=0))]
  transfers between devices with their start and end apart: 42 -> 36, of which waited for: 19 -> 20; matrix products, arithmetic and copies ran while one was open for 10% -> 11% of each run, Pallas kernels for 3% -> 4%
where the time goes in v4:
time: 138 us; the launch traced here: 137 us
  waiting for transfers between devices  56.5 us (41%)
  starting transfers between devices  46.5 us (34%)
  Pallas kernels  10.4 us (8%)
  matrix products  9.88 us (7%)
  other arithmetic  9.13 us (7%)
  local copies, waits for them, and re-layouts  2.97 us (2%)
    ppermute x34, waiting for transfers between devices, move(): return lax.ppermute(value, AXES, pairs)  55.4 us
    ppermute x34, starting transfers between devices, move(): return lax.ppermute(value, AXES, pairs)  33.2 us
    pallas_call x2, Pallas kernels, products(): pl.pallas_call(functools.partial(product_kernel, n, width, len(extra), em...  10.4 us
    dot_general x4, matrix products, grad_term(): lax.dot_general(rows_z, columns, (((0,), (0,)), ((), ())), preferred_elem...  8 us
    all_to_all x1, starting transfers between devices, body(): lax.all_to_all(after(both, *others), ('x', 'z'), 0, 0, tiled=True)  7.88 us
    all_to_all x1, starting transfers between devices, body(): placed = lax.all_to_all(placed, ('x', 'z'), 0, 0, tiled=True)  5.46 us
  transfers between devices with their start and end apart: 36, of which 20 were waited for; matrix products, arithmetic and copies ran while one was open for 11% of the time, Pallas kernels for 4%

profile of v4, /device:TPU:0, one launch (start us, length us, event | category | flops | bytes accessed | tf_op | source)
XLA Modules:
  0.0 136.5 jit_solution(2640307260078566352)
XLA Ops:
  0.7 1.0 copy-done
  1.7 5.4 %shard_map.139 = (bf16[256,1024]{1,0:T(8,128)(2,1)S(1)}, bf16[256,1024]{1,0:T(8,128)(2,1)S(1)}, bf16[256,1024]{1,0:T(8,128)(2,1)S(1)}, bf16[256,1024]{1,0:T(8,12...) custom-call(s32[8]{0:T(128)S(1)} %stack.149.starts, ...), custom_call_target="tpu_custom_call" | custom-call | flops 2147483648 | bytes 8388608 | tf_op jit(solution)/shard_map/pallas_call | solution.py:76
  7.2 0.5 collective-permute-start.3
  7.8 0.4 collective-permute-start
  8.4 0.7 collective-permute-done.1
  9.3 3.4 %collective-permute-start.2 = (bf16[256,1024]{1,0:T(8,128)(2,1)S(1)}, bf16[256,1024]{1,0:T(8,128)(2,1)}, u32[]{:S(2)}, u32[]{:S(2)}) collective-permute-start(bf16[256,1024]{1,0:T(8,128)(2,1)S(1)} %add_convert_fusion.2), channel_id=1, source_target_pairs={{0,4},{1,5},{2,6},{3,7},{4,0},{5,1},{6,2},{7,3},{8,12},{9,13},{10,... | collective-permute-start | bytes 1572872 | tf_op jit(solution)/shard_map/ppermute | solution.py:30
  12.7 0.2 add_convert_fusion.1
  12.9 0.7 collective-permute-start.4
  13.6 1.0 add_convert_fusion
  14.6 2.6 %collective-permute-start.6 = (bf16[256,1024]{1,0:T(8,128)(2,1)}, bf16[256,1024]{1,0:T(8,128)(2,1)}, u32[]{:S(2)}, u32[]{:S(2)}) collective-permute-start(bf16[256,1024]{1,0:T(8,128)(2,1)} %add_convert_fusion), channel_id=1, source_target_pairs={{0,6},{1,7},{2,0},{3,1},{4,2},{5,3},{6,4},{7,5},{8,14},{9,15},{10,... | collective-permute-start | bytes 1572872 | tf_op jit(solution)/shard_map/ppermute | solution.py:30
  17.2 0.3 fusion
  17.6 1.0 pad_maximum_fusion.2
  18.6 7.9 %all-to-all-start = ((bf16[16,24,1024]{2,1,0:T(8,128)(2,1)}), bf16[16,24,1024]{2,1,0:T(8,128)(2,1)S(1)}, u32[]{:S(2)}, u32[]{:S(2)}) async-start(bf16[16,24,1024]{2,1,0:T(8,128)(2,1)} %bitcast.15), calls=%async_computation | async-start | bytes 1572864 | tf_op jit(solution)/shard_map/all_to_all | solution.py:155
  26.5 9.7 %collective-permute-done.4 = bf16[256,1024]{1,0:T(8,128)(2,1)} collective-permute-done((bf16[256,1024]{1,0:T(8,128)(2,1)S(1)}, bf16[256,1024]{1,0:T(8,128)(2,1)}, u32[]{:S(2)}, u32[]{:S(2)}) %collective-permute-start.4) | collective-permute-done | bytes 524320 | tf_op jit(solution)/shard_map/ppermute | solution.py:30
  36.2 0.4 collective-permute-done.6
  36.7 2.2 %multiply_reduce_fusion = (f32[256]{0:T(256)S(1)}, bf16[256,1024]{1,0:T(8,128)(2,1)S(1)}) fusion(bf16[256,1024]{1,0:T(8,128)(2,1)} %collective-permute-done.6, bf16[256,1024]{1,0:T(8,128)(2,1)} %collective-permute-done.4, bf16[256,1024]{1,0:T(8,128)(2,1)} %collective-permute-done.2, bf16[256,1024]{1,0:T(8,128)(2,1)} %collective-permute-done, ...), kind=kLoop, calls=%fused_computation.14 | loop fusion | flops 4194048 | bytes 3676160 | tf_op jit(solution)/shard_map/reduce_sum | solution.py:161
  39.2 1.1 all-to-all-done
  40.2 5.0 %shard_map.140 = (bf16[128,1024]{1,0:T(8,128)(2,1)S(1)}, bf16[128,1024]{1,0:T(8,128)(2,1)S(1)}, bf16[128,1024]{1,0:T(8,128)(2,1)S(1)}, bf16[128,1024]{1,0:T(8,12...) custom-call(s32[4]{0:T(128)S(1)} %pad_add_fusion.starts, ...), custom_call_target="tpu_custom_call" | custom-call | flops 2147483648 | bytes 8388608 | tf_op jit(solution)/shard_map/pallas_call | solution.py:76
  45.4 0.5 collective-permute-start.8
  46.0 0.4 collective-permute-start.13
  46.5 0.5 collective-permute-done.8
  47.1 0.3 collective-permute-done.11
  47.5 0.3 collective-permute-done.13
  47.9 1.8 %collective-permute-start.10 = (bf16[136,1024]{1,0:T(8,128)(2,1)S(1)}, bf16[136,1024]{1,0:T(8,128)(2,1)S(1)}, u32[]{:S(2)}, u32[]{:S(2)}) collective-permute-start(bf16[136,1024]{1,0:T(8,128)(2,1)S(1)} %get-tuple-element.96), channel_id=1, source_target_pairs={{0,4},{1,5},{2,6},{3,7},{4,0},{5,1},{6,2},{7,3},{8,12},{9,13},{10,... | collective-permute-start | bytes 835592 | tf_op jit(solution)/shard_map/ppermute | solution.py:30
  49.7 0.5 convolution_convert_fusion
  50.4 4.1 %collective-permute-start.15 = (bf16[256,1024]{1,0:T(8,128)(2,1)S(1)}, bf16[256,1024]{1,0:T(8,128)(2,1)S(1)}, u32[]{:S(2)}, u32[]{:S(2)}) collective-permute-start(bf16[256,1024]{1,0:T(8,128)(2,1)S(1)} %maximum_select_fusion.rows), channel_id=1, source_target_pairs={{0,24},{1,25},{2,26},{3,27},{4,28},{5,29},{6,30},{7,31},{8,0},{9,1... | collective-permute-start | bytes 1572872 | tf_op jit(solution)/shard_map/ppermute | solution.py:30
  54.5 0.4 collective-permute-start.7
  55.0 0.7 collective-permute-start.12
  55.7 2.7 %collective-permute-done.10 = bf16[136,1024]{1,0:T(8,128)(2,1)S(1)} collective-permute-done((bf16[136,1024]{1,0:T(8,128)(2,1)S(1)}, bf16[136,1024]{1,0:T(8,128)(2,1)S(1)}, u32[]{:S(2)}, u32[]{:S(2)}) %collective-permute-start.10) | collective-permute-done | bytes 278560 | tf_op jit(solution)/shard_map/ppermute | solution.py:30
  58.4 1.6 %collective-permute-start.14 = (bf16[136,1024]{1,0:T(8,128)(2,1)S(1)}, bf16[136,1024]{1,0:T(8,128)(2,1)S(1)}, u32[]{:S(2)}, u32[]{:S(2)}) collective-permute-start(bf16[136,1024]{1,0:T(8,128)(2,1)S(1)} %get-tuple-element.94), channel_id=1, source_target_pairs={{0,6},{1,7},{2,0},{3,1},{4,2},{5,3},{6,4},{7,5},{8,14},{9,15},{10,... | collective-permute-start | bytes 835592 | tf_op jit(solution)/shard_map/ppermute | solution.py:30
  60.1 5.0 %collective-permute-done.12 = bf16[136,1024]{1,0:T(8,128)(2,1)S(1)} collective-permute-done((bf16[136,1024]{1,0:T(8,128)(2,1)S(1)}, bf16[136,1024]{1,0:T(8,128)(2,1)S(1)}, u32[]{:S(2)}, u32[]{:S(2)}) %collective-permute-start.12) | collective-permute-done | bytes 278560 | tf_op jit(solution)/shard_map/ppermute | solution.py:30
  65.1 1.4 %collective-permute-done.14 = bf16[136,1024]{1,0:T(8,128)(2,1)S(1)} collective-permute-done((bf16[136,1024]{1,0:T(8,128)(2,1)S(1)}, bf16[136,1024]{1,0:T(8,128)(2,1)S(1)}, u32[]{:S(2)}, u32[]{:S(2)}) %collective-permute-start.14) | collective-permute-done | bytes 278560 | tf_op jit(solution)/shard_map/ppermute | solution.py:30
  66.6 3.1 %collective-permute-done.16 = bf16[256,1024]{1,0:T(8,128)(2,1)S(1)} collective-permute-done((bf16[256,1024]{1,0:T(8,128)(2,1)S(1)}, bf16[256,1024]{1,0:T(8,128)(2,1)S(1)}, u32[]{:S(2)}, u32[]{:S(2)}) %collective-permute-start.16) | collective-permute-done | bytes 524320 | tf_op jit(solution)/shard_map/ppermute | solution.py:30
  69.8 0.7 copy-done.8
  70.5 0.6 fusion.22
  71.2 0.5 collective-permute-start.19
  71.7 0.7 collective-permute-start.20
  72.4 0.9 collective-permute-start.21
  73.3 2.2 %collective-permute-done.19 = bf16[128,256]{1,0:T(8,128)(2,1)S(1)} collective-permute-done((bf16[128,256]{1,0:T(8,128)(2,1)S(1)}, bf16[128,256]{1,0:T(8,128)(2,1)S(1)}, u32[]{:S(2)}, u32[]{:S(2)}) %collective-permute-start.19) | collective-permute-done | bytes 65568 | tf_op jit(solution)/shard_map/ppermute | solution.py:30
  75.5 2.6 %collective-permute-done.20 = bf16[128,256]{1,0:T(8,128)(2,1)S(1)} collective-permute-done((bf16[128,256]{1,0:T(8,128)(2,1)S(1)}, bf16[128,256]{1,0:T(8,128)(2,1)S(1)}, u32[]{:S(2)}, u32[]{:S(2)}) %collective-permute-start.20) | collective-permute-done | bytes 65568 | tf_op jit(solution)/shard_map/ppermute | solution.py:30
  78.2 0.4 collective-permute-done.21
  78.6 2.8 %collective-permute-start.26 = (bf16[4,128,256]{2,1,0:T(8,128)(2,1)S(1)}, bf16[4,128,256]{2,1,0:T(8,128)(2,1)S(1)}, u32[]{:S(2)}, u32[]{:S(2)}) collective-permute-start(bf16[4,128,256]{2,1,0:T(8,128)(2,1)S(1)} %get-tuple-element.80), channel_id=1, source_target_pairs={{0,6},{1,7},{2,0},{3,1},{4,2},{5,3},{6,4},{7,5},{8,14},{9,15},{10,... | collective-permute-start | bytes 786440 | tf_op jit(solution)/shard_map/ppermute | solution.py:30
  81.5 1.7 %collective-permute-start.24 = (bf16[256,1024]{1,0:T(8,128)(2,1)S(1)}, bf16[256,1024]{1,0:T(8,128)(2,1)S(1)}, u32[]{:S(2)}, u32[]{:S(2)}) collective-permute-start(bf16[256,1024]{1,0:T(8,128)(2,1)S(1)} %maximum_select_fusion.rows), channel_id=1, source_target_pairs={{0,16},{1,17},{2,18},{3,19},{4,20},{5,21},{6,22},{7,23},{8,24},{9,... | collective-permute-start | bytes 1572872 | tf_op jit(solution)/shard_map/ppermute | solution.py:30
  83.4 1.6 %collective-permute-start.23 = (bf16[4,128,256]{2,1,0:T(8,128)(2,1)S(1)}, bf16[4,128,256]{2,1,0:T(8,128)(2,1)S(1)}, u32[]{:S(2)}, u32[]{:S(2)}) collective-permute-start(bf16[4,128,256]{2,1,0:T(8,128)(2,1)S(1)} %get-tuple-element.80), channel_id=1, source_target_pairs={{0,4},{1,5},{2,6},{3,7},{4,0},{5,1},{6,2},{7,3},{8,12},{9,13},{10,... | collective-permute-start | bytes 786440 | tf_op jit(solution)/shard_map/ppermute | solution.py:30
  84.9 0.4 collective-permute-done.26
  85.3 9.3 %collective-permute-done.29 = bf16[4,128,256]{2,1,0:T(8,128)(2,1)S(1)} collective-permute-done((bf16[4,128,256]{2,1,0:T(8,128)(2,1)S(1)}, bf16[4,128,256]{2,1,0:T(8,128)(2,1)S(1)}, u32[]{:S(2)}, u32[]{:S(2)}) %collective-permute-start.29) | collective-permute-done | bytes 262176 | tf_op jit(solution)/shard_map/ppermute | solution.py:30
  94.6 1.1 convolution_convert_fusion.4
  95.7 5.5 %all-to-all-start.1 = ((bf16[16,24,512]{2,1,0:T(8,128)(2,1)}), bf16[16,24,512]{2,1,0:T(8,128)(2,1)S(1)}, u32[]{:S(2)}, u32[]{:S(2)}) async-start(bf16[16,24,512]{2,1,0:T(8,128)(2,1)} %bitcast.30), calls=%async_computation.1 | async-start | bytes 786432 | tf_op jit(solution)/shard_map/all_to_all | solution.py:223
  101.5 0.3 collective-permute-start.28
  101.9 0.4 copy-done.10
  102.4 0.3 copy-done.9
  102.7 1.2 pad_maximum_fusion
  104.1 0.3 pad_maximum_fusion.1
  104.3 1.6 %convolution_convert_fusion.3 = bf16[1024,256]{1,0:T(8,128)(2,1)} fusion(bf16[1024,1024]{1,0:T(8,128)(2,1)S(1)} %pad_maximum_fusion, bf16[4,1024,256]{2,1,0:T(8,128)(2,1)S(1)} %pad_maximum_fusion.1, s32[]{:T(128)S(6)} %select_n.120), kind=kOutput, calls=%fused_computation.5 | convolution fusion | flops 537133056 | bytes 3145732 | tf_op jit(solution)/shard_map/dot_general | solution.py:212
  105.9 3.4 %collective-permute-start.31 = (bf16[1024,256]{1,0:T(8,128)(2,1)}, bf16[1024,256]{1,0:T(8,128)(2,1)}, u32[]{:S(2)}, u32[]{:S(2)}) collective-permute-start(bf16[1024,256]{1,0:T(8,128)(2,1)} %convolution_convert_fusion.3), channel_id=1, source_target_pairs={{0,64},{1,65},{2,66},{3,67},{4,68},{5,69},{6,70},{7,71},{8,72},{9,... | collective-permute-start | bytes 1572872 | tf_op jit(solution)/shard_map/ppermute | solution.py:30
  109.4 1.6 %convolution_convert_fusion.2 = bf16[1024,256]{1,0:T(8,128)(2,1)} fusion(bf16[1024,1024]{1,0:T(8,128)(2,1)S(1)} %pad_maximum_fusion, bf16[4,1024,256]{2,1,0:T(8,128)(2,1)S(1)} %pad_maximum_fusion.1, s32[]{:T(128)S(6)} %select_n.121), kind=kOutput, calls=%fused_computation.4 | convolution fusion | flops 537133056 | bytes 3145732 | tf_op jit(solution)/shard_map/dot_general | solution.py:212
  111.0 0.6 collective-permute-start.32
  111.5 1.6 %convolution_convert_fusion.1 = bf16[1024,256]{1,0:T(8,128)(2,1)} fusion(bf16[1024,1024]{1,0:T(8,128)(2,1)S(1)} %pad_maximum_fusion, bf16[4,1024,256]{2,1,0:T(8,128)(2,1)S(1)} %pad_maximum_fusion.1, s32[]{:T(128)S(6)} %select_n.122), kind=kOutput, calls=%fused_computation.3 | convolution fusion | flops 537133056 | bytes 3145732 | tf_op jit(solution)/shard_map/dot_general | solution.py:212
  113.1 2.7 %collective-permute-start.33 = (bf16[1024,256]{1,0:T(8,128)(2,1)}, bf16[1024,256]{1,0:T(8,128)(2,1)}, u32[]{:S(2)}, u32[]{:S(2)}) collective-permute-start(bf16[1024,256]{1,0:T(8,128)(2,1)} %convolution_convert_fusion.1), channel_id=1, source_target_pairs={{0,96},{1,97},{2,98},{3,99},{4,100},{5,101},{6,102},{7,103},{8,104... | collective-permute-start | bytes 1572872 | tf_op jit(solution)/shard_map/ppermute | solution.py:30
  115.8 1.4 %fusion.11 = (bf16[384,512]{1,0:T(8,128)(2,1)}, bf16[384,512]{1,0:T(8,128)(2,1)}) fusion(bf16[384,512]{1,0:T(8,128)(2,1)S(1)} %copy-done.3, bf16[16,24,512]{2,1,0:T(8,128)(2,1)S(1)} %all-to-all-done.1, bf16[384,512]{1,0:T(8,128)(2,1)S(1)} %copy-done.5, f32[512]{0:T(512)S(1)} %copy-done.11, f32[512]{0:T(512)S(1)} %copy-done.12, f32[512]{0:T(512)S(1)} %copy-done.13), kind=kLoop, calls=%fused_computation.32 | loop fusion | flops 3932160 | bytes 1972224 | tf_op jit(solution)/shard_map/convert_element_type | solution.py:228
  117.2 5.3 %collective-permute-done.31 = bf16[1024,256]{1,0:T(8,128)(2,1)} collective-permute-done((bf16[1024,256]{1,0:T(8,128)(2,1)}, bf16[1024,256]{1,0:T(8,128)(2,1)}, u32[]{:S(2)}, u32[]{:S(2)}) %collective-permute-start.31) | collective-permute-done | bytes 524320 | tf_op jit(solution)/shard_map/ppermute | solution.py:30
  122.5 10.5 %collective-permute-done.32 = bf16[1024,256]{1,0:T(8,128)(2,1)} collective-permute-done((bf16[1024,256]{1,0:T(8,128)(2,1)}, bf16[1024,256]{1,0:T(8,128)(2,1)}, u32[]{:S(2)}, u32[]{:S(2)}) %collective-permute-start.32) | collective-permute-done | bytes 524320 | tf_op jit(solution)/shard_map/ppermute | solution.py:30
  133.0 0.2 collective-permute-done.33
  133.3 3.2 %convert_add_fusion = f32[1024,256]{1,0:T(8,128)} fusion(bf16[1024,256]{1,0:T(8,128)(2,1)} %collective-permute-done.33, bf16[1024,256]{1,0:T(8,128)(2,1)} %collective-permute-done.32, bf16[1024,256]{1,0:T(8,128)(2,1)} %collective-permute-done.31, bf16[1024,1024]{1,0:T(8,128)(2,1)S(1)} %pad_maximum_fusion, bf16[4,1024,256]{2,1,0:T(8,128)(2,1)} %copy-done.1, ...), kind=kOutput, calls=%fused_computation.13 | convolution fusion | flops 538443776 | bytes 5242884 | tf_op jit(solution)/shard_map/dot_general | solution.py:212
  (100 shorter events, 2.8 us)
Async XLA Ops:
  0.7 1.0 copy-start
  1.7 6.5 %copy-start.11 = (f32[512]{0:T(512)S(1)}, f32[512]{0:T(512)}, u32[]{:S(2)}) copy-start(f32[512]{0:T(512)} %param.20) | copy-start | bytes 6148
  1.7 6.5 %copy-start.12 = (f32[512]{0:T(512)S(1)}, f32[512]{0:T(512)}, u32[]{:S(2)}) copy-start(f32[512]{0:T(512)} %param.19) | copy-start | bytes 6148
  1.7 6.5 %copy-start.13 = (f32[512]{0:T(512)S(1)}, f32[512]{0:T(512)}, u32[]{:S(2)}) copy-start(f32[512]{0:T(512)} %param.18) | copy-start | bytes 6148
  7.1 2.0 %collective-permute-start.1 = (bf16[256,1024]{1,0:T(8,128)(2,1)S(1)}, bf16[256,1024]{1,0:T(8,128)(2,1)S(1)}, u32[]{:S(2)}, u32[]{:S(2)}) collective-permute-start(bf16[256,1024]{1,0:T(8,128)(2,1)S(1)} %get-tuple-element.38), channel_id=1, source_target_pairs={{0,1},{1,0},{2,3},{3,2},{4,5},{5,4},{6,7},{7,6},{8,9},{9,8},{10,11... | collective-permute-start | bytes 1572872 | tf_op jit(solution)/shard_map/ppermute | solution.py:30
  7.2 5.5 %collective-permute-start.3 = (bf16[256,1024]{1,0:T(8,128)(2,1)S(1)}, bf16[256,1024]{1,0:T(8,128)(2,1)S(1)}, u32[]{:S(2)}, u32[]{:S(2)}) collective-permute-start(bf16[256,1024]{1,0:T(8,128)(2,1)S(1)} %get-tuple-element.40), channel_id=1, source_target_pairs={{0,1},{1,0},{2,3},{3,2},{4,5},{5,4},{6,7},{7,6},{8,9},{9,8},{10,11... | collective-permute-start | bytes 1572872 | tf_op jit(solution)/shard_map/ppermute | solution.py:30
  7.7 5.9 %collective-permute-start.5 = (bf16[256,1024]{1,0:T(8,128)(2,1)S(1)}, bf16[256,1024]{1,0:T(8,128)(2,1)S(1)}, u32[]{:S(2)}, u32[]{:S(2)}) collective-permute-start(bf16[256,1024]{1,0:T(8,128)(2,1)S(1)} %get-tuple-element.42), channel_id=1, source_target_pairs={{0,1},{1,0},{2,3},{3,2},{4,5},{5,4},{6,7},{7,6},{8,9},{9,8},{10,11... | collective-permute-start | bytes 1572872 | tf_op jit(solution)/shard_map/ppermute | solution.py:30
  7.8 18.7 %collective-permute-start = (bf16[256,1024]{1,0:T(8,128)(2,1)S(1)}, bf16[256,1024]{1,0:T(8,128)(2,1)}, u32[]{:S(2)}, u32[]{:S(2)}) collective-permute-start(bf16[256,1024]{1,0:T(8,128)(2,1)S(1)} %get-tuple-element.36), channel_id=1, source_target_pairs={{0,1},{1,0},{2,3},{3,2},{4,5},{5,4},{6,7},{7,6},{8,9},{9,8},{10,11... | collective-permute-start | bytes 1572872 | tf_op jit(solution)/shard_map/ppermute | solution.py:30
  8.2 42.2 %collective-permute-start.18 = (f32[3,512]{1,0:T(4,128)S(1)}, f32[3,512]{1,0:T(4,128)S(1)}, u32[]{:S(2)}, u32[]{:S(2)}) collective-permute-start(f32[3,512]{1,0:T(4,128)S(1)} %pad_maximum_fusion.11), channel_id=1, source_target_pairs={{0,1},{1,0},{2,3},{3,2},{4,5},{5,4},{6,7},{7,6},{8,9},{9,8},{10,11... | collective-permute-start | bytes 18440 | tf_op jit(solution)/shard_map/ppermute | solution.py:30
  9.1 8.1 %copy-start.15 = (s32[256,1]{0,1:T(1,128)S(1)}, s32[256,1]{0,1:T(1,128)}, u32[]{:S(2)}) copy-start(s32[256,1]{0,1:T(1,128)} %param.21) | copy-start | bytes 3076
  9.3 8.2 %copy-start.16 = (s32[256]{0:T(256)S(1)}, s32[256]{0:T(256)}, u32[]{:S(2)}) copy-start(s32[256]{0:T(256)} %param.22) | copy-start | bytes 3076
  9.3 8.3 %copy-start.2 = (bf16[384,512]{1,0:T(8,128)(2,1)S(1)}, bf16[384,512]{1,0:T(8,128)(2,1)}, u32[]{:S(2)}) copy-start(bf16[384,512]{1,0:T(8,128)(2,1)} %param.23) | copy-start | bytes 1179652
  9.3 8.3 %copy-start.4 = (bf16[384,512]{1,0:T(8,128)(2,1)S(1)}, bf16[384,512]{1,0:T(8,128)(2,1)}, u32[]{:S(2)}) copy-start(bf16[384,512]{1,0:T(8,128)(2,1)} %param.17) | copy-start | bytes 1179652
  9.3 17.2 %collective-permute-start.2 = (bf16[256,1024]{1,0:T(8,128)(2,1)S(1)}, bf16[256,1024]{1,0:T(8,128)(2,1)}, u32[]{:S(2)}, u32[]{:S(2)}) collective-permute-start(bf16[256,1024]{1,0:T(8,128)(2,1)S(1)} %add_convert_fusion.2), channel_id=1, source_target_pairs={{0,4},{1,5},{2,6},{3,7},{4,0},{5,1},{6,2},{7,3},{8,12},{9,13},{10,... | collective-permute-start | bytes 1572872 | tf_op jit(solution)/shard_map/ppermute | solution.py:30
  12.9 23.4 %collective-permute-start.4 = (bf16[256,1024]{1,0:T(8,128)(2,1)S(1)}, bf16[256,1024]{1,0:T(8,128)(2,1)}, u32[]{:S(2)}, u32[]{:S(2)}) collective-permute-start(bf16[256,1024]{1,0:T(8,128)(2,1)S(1)} %add_convert_fusion.1), channel_id=1, source_target_pairs={{0,2},{1,3},{2,4},{3,5},{4,6},{5,7},{6,0},{7,1},{8,10},{9,11},{10,... | collective-permute-start | bytes 1572872 | tf_op jit(solution)/shard_map/ppermute | solution.py:30
  14.6 22.1 %copy-start.14 = (f32[1024]{0:T(1024)S(1)}, f32[1024]{0:T(1024)}, u32[]{:S(2)}) copy-start(f32[1024]{0:T(1024)} %param.15) | copy-start | bytes 12292
  14.6 22.1 %collective-permute-start.6 = (bf16[256,1024]{1,0:T(8,128)(2,1)}, bf16[256,1024]{1,0:T(8,128)(2,1)}, u32[]{:S(2)}, u32[]{:S(2)}) collective-permute-start(bf16[256,1024]{1,0:T(8,128)(2,1)} %add_convert_fusion), channel_id=1, source_target_pairs={{0,6},{1,7},{2,0},{3,1},{4,2},{5,3},{6,4},{7,5},{8,14},{9,15},{10,... | collective-permute-start | bytes 1572872 | tf_op jit(solution)/shard_map/ppermute | solution.py:30
  18.6 21.6 %all-to-all-start = ((bf16[16,24,1024]{2,1,0:T(8,128)(2,1)}), bf16[16,24,1024]{2,1,0:T(8,128)(2,1)S(1)}, u32[]{:S(2)}, u32[]{:S(2)}) async-start(bf16[16,24,1024]{2,1,0:T(8,128)(2,1)} %bitcast.15), calls=%async_computation | async-start | bytes 1572864 | tf_op jit(solution)/shard_map/all_to_all | solution.py:155
  45.3 1.2 collective-permute-start.9
  45.4 1.6 %collective-permute-start.8 = (bf16[128,1024]{1,0:T(8,128)(2,1)S(1)}, bf16[128,1024]{1,0:T(8,128)(2,1)S(1)}, u32[]{:S(2)}, u32[]{:S(2)}) collective-permute-start(bf16[128,1024]{1,0:T(8,128)(2,1)S(1)} %get-tuple-element.48), channel_id=1, source_target_pairs={{0,1},{1,0},{2,3},{3,2},{4,5},{5,4},{6,7},{7,6},{8,9},{9,8},{10,11... | collective-permute-start | bytes 786440 | tf_op jit(solution)/shard_map/ppermute | solution.py:30
  45.9 1.5 %collective-permute-start.11 = (bf16[128,1024]{1,0:T(8,128)(2,1)S(1)}, bf16[128,1024]{1,0:T(8,128)(2,1)S(1)}, u32[]{:S(2)}, u32[]{:S(2)}) collective-permute-start(bf16[128,1024]{1,0:T(8,128)(2,1)S(1)} %get-tuple-element.51), channel_id=1, source_target_pairs={{0,1},{1,0},{2,3},{3,2},{4,5},{5,4},{6,7},{7,6},{8,9},{9,8},{10,11... | collective-permute-start | bytes 786440 | tf_op jit(solution)/shard_map/ppermute | solution.py:30
  46.0 1.8 %collective-permute-start.13 = (bf16[128,1024]{1,0:T(8,128)(2,1)S(1)}, bf16[128,1024]{1,0:T(8,128)(2,1)S(1)}, u32[]{:S(2)}, u32[]{:S(2)}) collective-permute-start(bf16[128,1024]{1,0:T(8,128)(2,1)S(1)} %get-tuple-element.53), channel_id=1, source_target_pairs={{0,1},{1,0},{2,3},{3,2},{4,5},{5,4},{6,7},{7,6},{8,9},{9,8},{10,11... | collective-permute-start | bytes 786440 | tf_op jit(solution)/shard_map/ppermute | solution.py:30
  47.9 10.5 %collective-permute-start.10 = (bf16[136,1024]{1,0:T(8,128)(2,1)S(1)}, bf16[136,1024]{1,0:T(8,128)(2,1)S(1)}, u32[]{:S(2)}, u32[]{:S(2)}) collective-permute-start(bf16[136,1024]{1,0:T(8,128)(2,1)S(1)} %get-tuple-element.96), channel_id=1, source_target_pairs={{0,4},{1,5},{2,6},{3,7},{4,0},{5,1},{6,2},{7,3},{8,12},{9,13},{10,... | collective-permute-start | bytes 835592 | tf_op jit(solution)/shard_map/ppermute | solution.py:30
  50.2 4.7 %collective-permute-start.17 = (bf16[128,1024]{1,0:T(8,128)(2,1)S(1)}, bf16[128,1024]{1,0:T(8,128)(2,1)S(1)}, u32[]{:S(2)}, u32[]{:S(2)}) collective-permute-start(bf16[128,1024]{1,0:T(8,128)(2,1)S(1)} %get-tuple-element.76), channel_id=1, source_target_pairs={{0,1},{1,0},{2,3},{3,2},{4,5},{5,4},{6,7},{7,6},{8,9},{9,8},{10,11... | collective-permute-start | bytes 786440 | tf_op jit(solution)/shard_map/ppermute | solution.py:30
  50.4 16.2 %collective-permute-start.15 = (bf16[256,1024]{1,0:T(8,128)(2,1)S(1)}, bf16[256,1024]{1,0:T(8,128)(2,1)S(1)}, u32[]{:S(2)}, u32[]{:S(2)}) collective-permute-start(bf16[256,1024]{1,0:T(8,128)(2,1)S(1)} %maximum_select_fusion.rows), channel_id=1, source_target_pairs={{0,24},{1,25},{2,26},{3,27},{4,28},{5,29},{6,30},{7,31},{8,0},{9,1... | collective-permute-start | bytes 1572872 | tf_op jit(solution)/shard_map/ppermute | solution.py:30
  54.5 15.2 %collective-permute-start.16 = (bf16[256,1024]{1,0:T(8,128)(2,1)S(1)}, bf16[256,1024]{1,0:T(8,128)(2,1)S(1)}, u32[]{:S(2)}, u32[]{:S(2)}) collective-permute-start(bf16[256,1024]{1,0:T(8,128)(2,1)S(1)} %maximum_select_fusion.rows), channel_id=1, source_target_pairs={{0,8},{1,9},{2,10},{3,11},{4,12},{5,13},{6,14},{7,15},{8,16},{9,17... | collective-permute-start | bytes 1572872 | tf_op jit(solution)/shard_map/ppermute | solution.py:30
  54.5 12.0 %collective-permute-start.7 = (bf16[128,1024]{1,0:T(8,128)(2,1)S(1)}, bf16[128,1024]{1,0:T(8,128)(2,1)S(1)}, u32[]{:S(2)}, u32[]{:S(2)}) collective-permute-start(bf16[128,1024]{1,0:T(8,128)(2,1)S(1)} %get-tuple-element.46), channel_id=1, source_target_pairs={{0,1},{1,0},{2,3},{3,2},{4,5},{5,4},{6,7},{7,6},{8,9},{9,8},{10,11... | collective-permute-start | bytes 786440 | tf_op jit(solution)/shard_map/ppermute | solution.py:30
  55.0 10.1 %collective-permute-start.12 = (bf16[136,1024]{1,0:T(8,128)(2,1)S(1)}, bf16[136,1024]{1,0:T(8,128)(2,1)S(1)}, u32[]{:S(2)}, u32[]{:S(2)}) collective-permute-start(bf16[136,1024]{1,0:T(8,128)(2,1)S(1)} %get-tuple-element.95), channel_id=1, source_target_pairs={{0,2},{1,3},{2,4},{3,5},{4,6},{5,7},{6,0},{7,1},{8,10},{9,11},{10,... | collective-permute-start | bytes 835592 | tf_op jit(solution)/shard_map/ppermute | solution.py:30
  58.4 8.1 %collective-permute-start.14 = (bf16[136,1024]{1,0:T(8,128)(2,1)S(1)}, bf16[136,1024]{1,0:T(8,128)(2,1)S(1)}, u32[]{:S(2)}, u32[]{:S(2)}) collective-permute-start(bf16[136,1024]{1,0:T(8,128)(2,1)S(1)} %get-tuple-element.94), channel_id=1, source_target_pairs={{0,6},{1,7},{2,0},{3,1},{4,2},{5,3},{6,4},{7,5},{8,14},{9,15},{10,... | collective-permute-start | bytes 835592 | tf_op jit(solution)/shard_map/ppermute | solution.py:30
  66.6 3.2 %copy-start.6 = (bf16[256,1024]{1,0:T(8,128)(2,1)}, bf16[256,1024]{1,0:T(8,128)(2,1)S(1)}, u32[]{:S(2)}) copy-start(bf16[256,1024]{1,0:T(8,128)(2,1)S(1)} %collective-permute-done.15) | copy-start | bytes 1572868
  69.7 0.8 copy-start.8
  71.2 4.3 %collective-permute-start.19 = (bf16[128,256]{1,0:T(8,128)(2,1)S(1)}, bf16[128,256]{1,0:T(8,128)(2,1)S(1)}, u32[]{:S(2)}, u32[]{:S(2)}) collective-permute-start(bf16[128,256]{1,0:T(8,128)(2,1)S(1)} %get-tuple-element.86), channel_id=1, source_target_pairs={{0,24},{1,25},{2,26},{3,27},{4,28},{5,29},{6,30},{7,31},{8,0},{9,1... | collective-permute-start | bytes 196616 | tf_op jit(solution)/shard_map/ppermute | solution.py:30
  71.7 6.5 %collective-permute-start.20 = (bf16[128,256]{1,0:T(8,128)(2,1)S(1)}, bf16[128,256]{1,0:T(8,128)(2,1)S(1)}, u32[]{:S(2)}, u32[]{:S(2)}) collective-permute-start(bf16[128,256]{1,0:T(8,128)(2,1)S(1)} %get-tuple-element.85), channel_id=1, source_target_pairs={{0,16},{1,17},{2,18},{3,19},{4,20},{5,21},{6,22},{7,23},{8,24},{9,... | collective-permute-start | bytes 196616 | tf_op jit(solution)/shard_map/ppermute | solution.py:30
  72.4 6.1 %collective-permute-start.21 = (bf16[128,256]{1,0:T(8,128)(2,1)S(1)}, bf16[128,256]{1,0:T(8,128)(2,1)S(1)}, u32[]{:S(2)}, u32[]{:S(2)}) collective-permute-start(bf16[128,256]{1,0:T(8,128)(2,1)S(1)} %get-tuple-element.84), channel_id=1, source_target_pairs={{0,8},{1,9},{2,10},{3,11},{4,12},{5,13},{6,14},{7,15},{8,16},{9,17... | collective-permute-start | bytes 196616 | tf_op jit(solution)/shard_map/ppermute | solution.py:30
  78.6 6.7 %collective-permute-start.26 = (bf16[4,128,256]{2,1,0:T(8,128)(2,1)S(1)}, bf16[4,128,256]{2,1,0:T(8,128)(2,1)S(1)}, u32[]{:S(2)}, u32[]{:S(2)}) collective-permute-start(bf16[4,128,256]{2,1,0:T(8,128)(2,1)S(1)} %get-tuple-element.80), channel_id=1, source_target_pairs={{0,6},{1,7},{2,0},{3,1},{4,2},{5,3},{6,4},{7,5},{8,14},{9,15},{10,... | collective-permute-start | bytes 786440 | tf_op jit(solution)/shard_map/ppermute | solution.py:30
  81.4 13.2 %collective-permute-start.29 = (bf16[4,128,256]{2,1,0:T(8,128)(2,1)S(1)}, bf16[4,128,256]{2,1,0:T(8,128)(2,1)S(1)}, u32[]{:S(2)}, u32[]{:S(2)}) collective-permute-start(bf16[4,128,256]{2,1,0:T(8,128)(2,1)S(1)} %get-tuple-element.80), channel_id=1, source_target_pairs={{0,2},{1,3},{2,4},{3,5},{4,6},{5,7},{6,0},{7,1},{8,10},{9,11},{10,... | collective-permute-start | bytes 786440 | tf_op jit(solution)/shard_map/ppermute | solution.py:30
  81.4 1.9 %collective-permute-start.22 = (bf16[128,512]{1,0:T(8,128)(2,1)S(1)}, bf16[128,512]{1,0:T(8,128)(2,1)S(1)}, u32[]{:S(2)}, u32[]{:S(2)}) collective-permute-start(bf16[128,512]{1,0:T(8,128)(2,1)S(1)} %get-tuple-element.82), channel_id=1, source_target_pairs={{0,1},{1,0},{2,3},{3,2},{4,5},{5,4},{6,7},{7,6},{8,9},{9,8},{10,11... | collective-permute-start | bytes 393224 | tf_op jit(solution)/shard_map/ppermute | solution.py:30
  81.5 19.9 %collective-permute-start.24 = (bf16[256,1024]{1,0:T(8,128)(2,1)S(1)}, bf16[256,1024]{1,0:T(8,128)(2,1)S(1)}, u32[]{:S(2)}, u32[]{:S(2)}) collective-permute-start(bf16[256,1024]{1,0:T(8,128)(2,1)S(1)} %maximum_select_fusion.rows), channel_id=1, source_target_pairs={{0,16},{1,17},{2,18},{3,19},{4,20},{5,21},{6,22},{7,23},{8,24},{9,... | collective-permute-start | bytes 1572872 | tf_op jit(solution)/shard_map/ppermute | solution.py:30
  83.2 18.0 %collective-permute-start.25 = (bf16[4,128,256]{2,1,0:T(8,128)(2,1)S(1)}, bf16[4,128,256]{2,1,0:T(8,128)(2,1)S(1)}, u32[]{:S(2)}, u32[]{:S(2)}) collective-permute-start(bf16[4,128,256]{2,1,0:T(8,128)(2,1)S(1)} %get-tuple-element.80), channel_id=1, source_target_pairs={{0,1},{1,0},{2,3},{3,2},{4,5},{5,4},{6,7},{7,6},{8,9},{9,8},{10,11... | collective-permute-start | bytes 786440 | tf_op jit(solution)/shard_map/ppermute | solution.py:30
  83.4 18.1 %collective-permute-start.23 = (bf16[4,128,256]{2,1,0:T(8,128)(2,1)S(1)}, bf16[4,128,256]{2,1,0:T(8,128)(2,1)S(1)}, u32[]{:S(2)}, u32[]{:S(2)}) collective-permute-start(bf16[4,128,256]{2,1,0:T(8,128)(2,1)S(1)} %get-tuple-element.80), channel_id=1, source_target_pairs={{0,4},{1,5},{2,6},{3,7},{4,0},{5,1},{6,2},{7,3},{8,12},{9,13},{10,... | collective-permute-start | bytes 786440 | tf_op jit(solution)/shard_map/ppermute | solution.py:30
  85.3 16.0 %collective-permute-start.27 = (bf16[4,128,256]{2,1,0:T(8,128)(2,1)S(1)}, bf16[4,128,256]{2,1,0:T(8,128)(2,1)S(1)}, u32[]{:S(2)}, u32[]{:S(2)}) collective-permute-start(bf16[4,128,256]{2,1,0:T(8,128)(2,1)S(1)} %collective-permute-done.26), channel_id=1, source_target_pairs={{0,1},{1,0},{2,3},{3,2},{4,5},{5,4},{6,7},{7,6},{8,9},{9,8},{10,11... | collective-permute-start | bytes 786440 | tf_op jit(solution)/shard_map/ppermute | solution.py:30
  94.6 7.2 %collective-permute-start.30 = (bf16[4,128,256]{2,1,0:T(8,128)(2,1)S(1)}, bf16[4,128,256]{2,1,0:T(8,128)(2,1)S(1)}, u32[]{:S(2)}, u32[]{:S(2)}) collective-permute-start(bf16[4,128,256]{2,1,0:T(8,128)(2,1)S(1)} %collective-permute-done.29), channel_id=1, source_target_pairs={{0,1},{1,0},{2,3},{3,2},{4,5},{5,4},{6,7},{7,6},{8,9},{9,8},{10,11... | collective-permute-start | bytes 786440 | tf_op jit(solution)/shard_map/ppermute | solution.py:30
  95.7 20.0 %all-to-all-start.1 = ((bf16[16,24,512]{2,1,0:T(8,128)(2,1)}), bf16[16,24,512]{2,1,0:T(8,128)(2,1)S(1)}, u32[]{:S(2)}, u32[]{:S(2)}) async-start(bf16[16,24,512]{2,1,0:T(8,128)(2,1)} %bitcast.30), calls=%async_computation.1 | async-start | bytes 786432 | tf_op jit(solution)/shard_map/all_to_all | solution.py:223
  101.3 1.0 copy-start.7
  101.3 1.4 %copy-start.9 = (bf16[256,1024]{1,0:T(8,128)(2,1)S(1)}, bf16[256,1024]{1,0:T(8,128)(2,1)}, u32[]{:S(2)}) copy-start(bf16[256,1024]{1,0:T(8,128)(2,1)} %copy-done.8) | copy-start | bytes 1572868
  101.5 0.8 copy-start.10
  101.5 2.5 %collective-permute-start.28 = (bf16[4,128,256]{2,1,0:T(8,128)(2,1)S(1)}, bf16[4,128,256]{2,1,0:T(8,128)(2,1)S(1)}, u32[]{:S(2)}, u32[]{:S(2)}) collective-permute-start(bf16[4,128,256]{2,1,0:T(8,128)(2,1)S(1)} %collective-permute-done.23), channel_id=1, source_target_pairs={{0,1},{1,0},{2,3},{3,2},{4,5},{5,4},{6,7},{7,6},{8,9},{9,8},{10,11... | collective-permute-start | bytes 786440 | tf_op jit(solution)/shard_map/ppermute | solution.py:30
  104.3 7.2 %copy-start.1 = (bf16[4,1024,256]{2,1,0:T(8,128)(2,1)}, bf16[4,1024,256]{2,1,0:T(8,128)(2,1)S(1)}, u32[]{:S(2)}) copy-start(bf16[4,1024,256]{2,1,0:T(8,128)(2,1)S(1)} %pad_maximum_fusion.1) | copy-start | bytes 6291460
  105.9 16.6 %collective-permute-start.31 = (bf16[1024,256]{1,0:T(8,128)(2,1)}, bf16[1024,256]{1,0:T(8,128)(2,1)}, u32[]{:S(2)}, u32[]{:S(2)}) collective-permute-start(bf16[1024,256]{1,0:T(8,128)(2,1)} %convolution_convert_fusion.3), channel_id=1, source_target_pairs={{0,64},{1,65},{2,66},{3,67},{4,68},{5,69},{6,70},{7,71},{8,72},{9,... | collective-permute-start | bytes 1572872 | tf_op jit(solution)/shard_map/ppermute | solution.py:30
  111.0 4.8 %copy-start.3 = (bf16[384,512]{1,0:T(8,128)(2,1)S(1)}, bf16[384,512]{1,0:T(8,128)(2,1)}, u32[]{:S(2)}) copy-start(bf16[384,512]{1,0:T(8,128)(2,1)} %param.23) | copy-start | bytes 1179652
  111.0 4.8 %copy-start.5 = (bf16[384,512]{1,0:T(8,128)(2,1)S(1)}, bf16[384,512]{1,0:T(8,128)(2,1)}, u32[]{:S(2)}) copy-start(bf16[384,512]{1,0:T(8,128)(2,1)} %param.17) | copy-start | bytes 1179652
  111.0 22.1 %collective-permute-start.32 = (bf16[1024,256]{1,0:T(8,128)(2,1)}, bf16[1024,256]{1,0:T(8,128)(2,1)}, u32[]{:S(2)}, u32[]{:S(2)}) collective-permute-start(bf16[1024,256]{1,0:T(8,128)(2,1)} %convolution_convert_fusion.2), channel_id=1, source_target_pairs={{0,32},{1,33},{2,34},{3,35},{4,36},{5,37},{6,38},{7,39},{8,40},{9,... | collective-permute-start | bytes 1572872 | tf_op jit(solution)/shard_map/ppermute | solution.py:30
  113.1 20.2 %collective-permute-start.33 = (bf16[1024,256]{1,0:T(8,128)(2,1)}, bf16[1024,256]{1,0:T(8,128)(2,1)}, u32[]{:S(2)}, u32[]{:S(2)}) collective-permute-start(bf16[1024,256]{1,0:T(8,128)(2,1)} %convolution_convert_fusion.1), channel_id=1, source_target_pairs={{0,96},{1,97},{2,98},{3,99},{4,100},{5,101},{6,102},{7,103},{8,104... | collective-permute-start | bytes 1572872 | tf_op jit(solution)/shard_map/ppermute | solution.py:30

commit v5 on v4

--- a/solution.py
+++ b/solution.py
@@ -126,9 +126,11 @@
     lines = jnp.stack([high, middle, squares - high - middle])
     lines = jnp.pad(lines, ((0, LINES - 3), (0, width - half))).astype(BF)
     sends = [jnp.concatenate([add(outs[2 * i + 1], got[i]).astype(BF), lines], axis=0) for i in range(N - 1)]
+    own = add(outs[-1], got[-1])
+    *sends, own = lax.optimization_barrier((*sends, own))
     terms = [along_y(sends[i], steps[i]) for i in range(N - 1)]
     total = squares + sum(jnp.sum(term[half : half + 3, :half].astype(F32), axis=0) for term in terms)
-    return [outs[-1], got[-1], *[term[:half] for term in terms]], total, sends
+    return [own, *[term[:half] for term in terms]], total, sends
 
 
 def body(
@@ -166,7 +168,8 @@
     squares = squares.reshape(2, half)
     squares = jnp.where(first, squares[0], squares[1]), jnp.where(first, squares[1], squares[0])
     terms, total, sends = join(gated, w_join, 2 * features, squares)
-    *terms, rows_1, rows_3 = lax.optimization_barrier((*terms, along_z(rows, -1), along_z(rows, 1)))
+    rows_sent = after(rows, *sends)
+    rows_1, rows_3 = along_z(rows_sent, -1), along_z(rows_sent, 1)
     hidden = add(*terms)
     scale = lax.rsqrt(total / (width * N * 2) + 1e-05)[:, None]
     both = jnp.dot(select, after(both, *sends), preferred_element_type=F32).astype(BF)
@@ -199,34 +202,42 @@
 
     others = {f: along_z(quarter_for(-f), -f) for f in (2, 1, 3)}
     block = jnp.stack([quarter_for(0), others[1], others[2], others[3]])
+    block, rows_1, rows_3 = lax.optimization_barrier((block, rows_1, rows_3))
     rows_2 = along_z(after(rows, block), 2)
     arrived = {d: along_y(block, -d) for d in (2, 1, 3)}
-    arrived[2], rows_2 = lax.optimization_barrier((arrived[2], rows_2))
+    arrived[1], arrived[2], arrived[3], rows_2 = lax.optimization_barrier((arrived[1], arrived[2], arrived[3], rows_2))
     pieces = [block, arrived[1], arrived[2], arrived[3]]
     swapped = [swap(piece) for piece in pieces]
     grads = jnp.stack([jnp.stack(pair, axis=1) for pair in zip(pieces, swapped)]).reshape(N, N * tokens, quarter)
     rows_z = lax.optimization_barrier(jnp.concatenate([rows, rows_1, rows_2, rows_3], axis=0))
 
-    def grad_term(step):
-        columns = lax.dynamic_index_in_dim(grads, lax.rem(x + step - y + 2 * N, N), 0, keepdims=False)
-        return lax.dot_general(rows_z, columns, (((0,), (0,)), ((), ())), preferred_element_type=F32)
-
-    sends = [grad_term(d).astype(BF) for d in (2, 1, -1)]
-    sums = [along_x(value, d) for value, d in zip(sends, (2, 1, -1))]
-
-    late_hidden = after(hidden, block)
-    keep = jnp.where(first, late_hidden[:, :features], late_hidden[:, features:])
-    got = swap(jnp.where(first, late_hidden[:, features:], late_hidden[:, :features]))
+    keep = jnp.where(first, hidden[:, :features], hidden[:, features:])
+    got = swap(jnp.where(first, hidden[:, features:], hidden[:, :features]))
     rows_h = jnp.where(first, jnp.concatenate([keep, got], axis=0), jnp.concatenate([got, keep], axis=0))
     placed = lax.dot_general(select, rows_h, (((0,), (0,)), ((), ())), preferred_element_type=F32)
-    placed = placed.astype(BF).reshape(n_owner, most, features)
+    placed = after(placed.astype(BF), block).reshape(n_owner, most, features)
     placed = lax.all_to_all(placed, ("x", "z"), 0, 0, tiled=True)
     placed = placed.reshape(slot_rows, features).astype(F32)
+
+    def grad_term(step, part):
+        columns = lax.dynamic_index_in_dim(grads, lax.rem(x + step - y + 2 * N, N), 0, keepdims=False)
+        lines = rows_z[:, : width // 2] if part == 0 else rows_z[:, width // 2 :]
+        return lax.dot_general(lines, columns, (((0,), (0,)), ((), ())), preferred_element_type=F32)
+
+    from_left = along_x(grad_term(2, 0).astype(BF), 1)
+    from_right = along_x(grad_term(2, 1).astype(BF), -1)
+    near = grad_term(1, 1).astype(BF), grad_term(-1, 0).astype(BF)
+    low_b, up_a = along_x(near[0], 1), along_x(near[1], -1)
+    last = add(grad_term(1, 0), from_left).astype(BF), add(grad_term(-1, 1), from_right).astype(BF)
+    low_a, up_b = along_x(last[0], 1), along_x(last[1], -1)
+    placed = placed + from_left[0, 0] * 0.0
     state = dec_state.astype(F32)
     gate, slope = gates(params, state, placed)
     joined = (state + gate * placed).astype(BF)
     state_grad = (cotangent.astype(F32) * (1.0 + slope * gate_s[None, :])).astype(BF)
-    join_grad = add(grad_term(0), *sums)
+    join_grad = jnp.concatenate(
+        [add(grad_term(0, 0), up_a, low_a), add(grad_term(0, 1), low_b, up_b)], axis=0
+    )
     return joined, state_grad, join_grad
 
 

time: 138 us -> 133 us (0.964)
  waiting for transfers between devices: 56.5 us -> 41.7 us
  other arithmetic: 9.13 us -> 15.5 us
  starting transfers between devices: 46.5 us -> 48.4 us
  matrix products: 9.88 us -> 11.4 us
    ppermute x34 -> x37, waiting for transfers between devices: 55.4 us -> 41.7 us  [move(): return lax.ppermute(value, AXES, pairs)]
    another operation x5 -> x4, other arithmetic: 0.25 us -> 3.05 us  [body(): jnp.stack(pair, axis=1)]
    add x0 -> x4, other arithmetic: none -> 2.27 us  [the longest x3 2.18 us: add(): total = total + term.astype(F32)]
    ppermute x34 -> x37, starting transfers between devices: 33.2 us -> 34.7 us  [move(): return lax.ppermute(value, AXES, pairs)]
    dot_general x4 -> x8, matrix products: 8 us -> 9.51 us  [grad_term(): lax.dot_general(lines, columns, (((0,), (0,)), ((), ())), preferred_eleme...]
  transfers between devices with their start and end apart: 36 -> 39, of which waited for: 20 -> 17; matrix products, arithmetic and copies ran while one was open for 11% -> 19% of each run, Pallas kernels for 4% -> 4%
where the time goes in v5:
time: 133 us; the launch traced here: 132 us
  starting transfers between devices  48.4 us (36%)
  waiting for transfers between devices  41.7 us (31%)
  other arithmetic  15.5 us (12%)
  matrix products  11.4 us (9%)
  Pallas kernels  10.4 us (8%)
  local copies, waits for them, and re-layouts  2.77 us (2%)
  between operations  1.91 us (1%)
    ppermute x37, waiting for transfers between devices, move(): return lax.ppermute(value, AXES, pairs)  41.7 us
    ppermute x37, starting transfers between devices, move(): return lax.ppermute(value, AXES, pairs)  34.7 us
    pallas_call x2, Pallas kernels, products(): pl.pallas_call(functools.partial(product_kernel, n, width, len(extra), em...  10.4 us
    dot_general x8, matrix products, grad_term(): lax.dot_general(lines, columns, (((0,), (0,)), ((), ())), preferred_eleme...  9.51 us
    all_to_all x1, starting transfers between devices, body(): lax.all_to_all(after(both, *others), ('x', 'z'), 0, 0, tiled=True)  7.88 us
    all_to_all x1, starting transfers between devices, body(): placed = lax.all_to_all(placed, ('x', 'z'), 0, 0, tiled=True)  5.86 us
    another operation x4, other arithmetic, body(): jnp.stack(pair, axis=1)  3.05 us
  transfers between devices with their start and end apart: 39, of which 17 were waited for; matrix products, arithmetic and copies ran while one was open for 19% of the time, Pallas kernels for 4%

profile of v5, /device:TPU:0, one launch (start us, length us, event | category | flops | bytes accessed | tf_op | source)
XLA Modules:
  0.0 132.1 jit_solution(1617292681514850875)
XLA Ops:
  0.7 1.0 copy-done
  1.7 5.4 %shard_map.139 = (bf16[256,1024]{1,0:T(8,128)(2,1)S(1)}, bf16[256,1024]{1,0:T(8,128)(2,1)S(1)}, bf16[256,1024]{1,0:T(8,128)(2,1)S(1)}, bf16[256,1024]{1,0:T(8,12...) custom-call(s32[8]{0:T(128)S(1)} %stack.149.starts, ...), custom_call_target="tpu_custom_call" | custom-call | flops 2147483648 | bytes 8388608 | tf_op jit(solution)/shard_map/pallas_call | solution.py:76
  7.2 0.5 collective-permute-start.3
  7.8 0.4 collective-permute-start
  8.4 0.7 collective-permute-done.5
  9.3 3.2 %collective-permute-start.6 = (bf16[256,1024]{1,0:T(8,128)(2,1)S(1)}, bf16[256,1024]{1,0:T(8,128)(2,1)}, u32[]{:S(2)}, u32[]{:S(2)}) collective-permute-start(bf16[256,1024]{1,0:T(8,128)(2,1)S(1)} %add_convert_fusion), channel_id=1, source_target_pairs={{0,6},{1,7},{2,0},{3,1},{4,2},{5,3},{6,4},{7,5},{8,14},{9,15},{10,... | collective-permute-start | bytes 1572872 | tf_op jit(solution)/shard_map/ppermute | solution.py:30
  12.8 1.0 add_convert_fusion.2
  13.8 2.6 %collective-permute-start.2 = (bf16[256,1024]{1,0:T(8,128)(2,1)}, bf16[256,1024]{1,0:T(8,128)(2,1)}, u32[]{:S(2)}, u32[]{:S(2)}) collective-permute-start(bf16[256,1024]{1,0:T(8,128)(2,1)} %add_convert_fusion.2), channel_id=1, source_target_pairs={{0,4},{1,5},{2,6},{3,7},{4,0},{5,1},{6,2},{7,3},{8,12},{9,13},{10,... | collective-permute-start | bytes 1572872 | tf_op jit(solution)/shard_map/ppermute | solution.py:30
  16.9 1.0 pad_maximum_fusion.3
  17.9 7.9 %all-to-all-start = ((bf16[16,24,1024]{2,1,0:T(8,128)(2,1)}), bf16[16,24,1024]{2,1,0:T(8,128)(2,1)S(1)}, u32[]{:S(2)}, u32[]{:S(2)}) async-start(bf16[16,24,1024]{2,1,0:T(8,128)(2,1)} %bitcast.15), calls=%async_computation | async-start | bytes 1572864 | tf_op jit(solution)/shard_map/all_to_all | solution.py:157
  25.7 9.5 %collective-permute-done.6 = bf16[256,1024]{1,0:T(8,128)(2,1)} collective-permute-done((bf16[256,1024]{1,0:T(8,128)(2,1)S(1)}, bf16[256,1024]{1,0:T(8,128)(2,1)}, u32[]{:S(2)}, u32[]{:S(2)}) %collective-permute-start.6) | collective-permute-done | bytes 524320 | tf_op jit(solution)/shard_map/ppermute | solution.py:30
  35.2 3.8 %collective-permute-done.4 = bf16[256,1024]{1,0:T(8,128)(2,1)} collective-permute-done((bf16[256,1024]{1,0:T(8,128)(2,1)S(1)}, bf16[256,1024]{1,0:T(8,128)(2,1)}, u32[]{:S(2)}, u32[]{:S(2)}) %collective-permute-start.4) | collective-permute-done | bytes 524320 | tf_op jit(solution)/shard_map/ppermute | solution.py:30
  39.0 2.2 %multiply_reduce_fusion = (f32[256]{0:T(256)S(1)}, bf16[256,1024]{1,0:T(8,128)(2,1)S(1)}) fusion(bf16[256,1024]{1,0:T(8,128)(2,1)} %collective-permute-done.6, bf16[256,1024]{1,0:T(8,128)(2,1)} %collective-permute-done.4, bf16[256,1024]{1,0:T(8,128)(2,1)} %collective-permute-done.2, bf16[256,1024]{1,0:T(8,128)(2,1)} %collective-permute-done, ...), kind=kLoop, calls=%fused_computation.12 | loop fusion | flops 4194048 | bytes 3676160 | tf_op jit(solution)/shard_map/reduce_sum | solution.py:163
  41.5 5.0 %shard_map.140 = (bf16[128,1024]{1,0:T(8,128)(2,1)S(1)}, bf16[128,1024]{1,0:T(8,128)(2,1)S(1)}, bf16[128,1024]{1,0:T(8,128)(2,1)S(1)}, bf16[128,1024]{1,0:T(8,12...) custom-call(s32[4]{0:T(128)S(1)} %pad_add_fusion.starts, ...), custom_call_target="tpu_custom_call" | custom-call | flops 2147483648 | bytes 8388608 | tf_op jit(solution)/shard_map/pallas_call | solution.py:76
  46.7 0.6 collective-permute-start.10
  47.3 0.4 collective-permute-start.7
  47.9 0.5 collective-permute-done.10
  49.6 0.5 convolution_convert_fusion
  50.1 0.5 collective-permute-start.16
  50.7 1.5 %collective-permute-start.12 = (bf16[136,1024]{1,0:T(8,128)(2,1)S(1)}, bf16[136,1024]{1,0:T(8,128)(2,1)S(1)}, u32[]{:S(2)}, u32[]{:S(2)}) collective-permute-start(bf16[136,1024]{1,0:T(8,128)(2,1)S(1)} %get-tuple-element.58), channel_id=1, source_target_pairs={{0,4},{1,5},{2,6},{3,7},{4,0},{5,1},{6,2},{7,3},{8,12},{9,13},{10,... | collective-permute-start | bytes 835592 | tf_op jit(solution)/shard_map/ppermute | solution.py:30
  52.1 0.5 collective-permute-start.13
  52.7 4.1 %collective-permute-start.21 = (bf16[256,1024]{1,0:T(8,128)(2,1)S(1)}, bf16[256,1024]{1,0:T(8,128)(2,1)S(1)}, u32[]{:S(2)}, u32[]{:S(2)}) collective-permute-start(bf16[256,1024]{1,0:T(8,128)(2,1)S(1)} %maximum_select_fusion.rows), channel_id=1, source_target_pairs={{0,24},{1,25},{2,26},{3,27},{4,28},{5,29},{6,30},{7,31},{8,0},{9,1... | collective-permute-start | bytes 1572872 | tf_op jit(solution)/shard_map/ppermute | solution.py:30
  56.8 3.3 %collective-permute-done.14 = bf16[136,1024]{1,0:T(8,128)(2,1)S(1)} collective-permute-done((bf16[136,1024]{1,0:T(8,128)(2,1)S(1)}, bf16[136,1024]{1,0:T(8,128)(2,1)S(1)}, u32[]{:S(2)}, u32[]{:S(2)}) %collective-permute-start.14) | collective-permute-done | bytes 278560 | tf_op jit(solution)/shard_map/ppermute | solution.py:30
  60.2 1.6 %collective-permute-done.12 = bf16[136,1024]{1,0:T(8,128)(2,1)S(1)} collective-permute-done((bf16[136,1024]{1,0:T(8,128)(2,1)S(1)}, bf16[136,1024]{1,0:T(8,128)(2,1)S(1)}, u32[]{:S(2)}, u32[]{:S(2)}) %collective-permute-start.12) | collective-permute-done | bytes 278560 | tf_op jit(solution)/shard_map/ppermute | solution.py:30
  61.8 5.1 %collective-permute-done.13 = bf16[136,1024]{1,0:T(8,128)(2,1)S(1)} collective-permute-done((bf16[136,1024]{1,0:T(8,128)(2,1)S(1)}, bf16[136,1024]{1,0:T(8,128)(2,1)S(1)}, u32[]{:S(2)}, u32[]{:S(2)}) %collective-permute-start.13) | collective-permute-done | bytes 278560 | tf_op jit(solution)/shard_map/ppermute | solution.py:30
  66.9 0.6 fusion.35
  67.6 2.0 %collective-permute-start.20 = (bf16[128,256]{1,0:T(8,128)(2,1)S(1)}, bf16[128,256]{1,0:T(8,128)(2,1)S(1)}, u32[]{:S(2)}, u32[]{:S(2)}) collective-permute-start(bf16[128,256]{1,0:T(8,128)(2,1)S(1)} %get-tuple-element.86), channel_id=1, source_target_pairs={{0,8},{1,9},{2,10},{3,11},{4,12},{5,13},{6,14},{7,15},{8,16},{9,17... | collective-permute-start | bytes 196616 | tf_op jit(solution)/shard_map/ppermute | solution.py:30
  69.5 3.6 %collective-permute-start.19 = (bf16[128,256]{1,0:T(8,128)(2,1)S(1)}, bf16[128,256]{1,0:T(8,128)(2,1)S(1)}, u32[]{:S(2)}, u32[]{:S(2)}) collective-permute-start(bf16[128,256]{1,0:T(8,128)(2,1)S(1)} %get-tuple-element.87), channel_id=1, source_target_pairs={{0,16},{1,17},{2,18},{3,19},{4,20},{5,21},{6,22},{7,23},{8,24},{9,... | collective-permute-start | bytes 196616 | tf_op jit(solution)/shard_map/ppermute | solution.py:30
  73.1 1.0 collective-permute-start.18
  74.2 2.4 %collective-permute-done.19 = bf16[128,256]{1,0:T(8,128)(2,1)S(1)} collective-permute-done((bf16[128,256]{1,0:T(8,128)(2,1)S(1)}, bf16[128,256]{1,0:T(8,128)(2,1)S(1)}, u32[]{:S(2)}, u32[]{:S(2)}) %collective-permute-start.19) | collective-permute-done | bytes 65568 | tf_op jit(solution)/shard_map/ppermute | solution.py:30
  76.5 0.9 collective-permute-done.18
  77.5 1.6 %collective-permute-start.26 = (bf16[256,1024]{1,0:T(8,128)(2,1)S(1)}, bf16[256,1024]{1,0:T(8,128)(2,1)S(1)}, u32[]{:S(2)}, u32[]{:S(2)}) collective-permute-start(bf16[256,1024]{1,0:T(8,128)(2,1)S(1)} %maximum_select_fusion.rows), channel_id=1, source_target_pairs={{0,16},{1,17},{2,18},{3,19},{4,20},{5,21},{6,22},{7,23},{8,24},{9,... | collective-permute-start | bytes 1572872 | tf_op jit(solution)/shard_map/ppermute | solution.py:30
  79.2 1.2 collective-permute-start.23
  80.4 0.9 collective-permute-start.25
  81.3 1.1 convolution_convert_fusion.1
  82.4 5.9 %all-to-all-start.1 = ((bf16[16,24,512]{2,1,0:T(8,128)(2,1)}), bf16[16,24,512]{2,1,0:T(8,128)(2,1)S(1)}, u32[]{:S(2)}, u32[]{:S(2)}) async-start(bf16[16,24,512]{2,1,0:T(8,128)(2,1)} %bitcast.92), calls=%async_computation.1 | async-start | bytes 786432 | tf_op jit(solution)/shard_map/all_to_all | solution.py:219
  88.5 2.7 %collective-permute-done.24 = bf16[4,128,256]{2,1,0:T(8,128)(2,1)} collective-permute-done((bf16[4,128,256]{2,1,0:T(8,128)(2,1)S(1)}, bf16[4,128,256]{2,1,0:T(8,128)(2,1)}, u32[]{:S(2)}, u32[]{:S(2)}) %collective-permute-start.24) | collective-permute-done | bytes 262176 | tf_op jit(solution)/shard_map/ppermute | solution.py:30
  91.2 4.8 %collective-permute-done.25 = bf16[4,128,256]{2,1,0:T(8,128)(2,1)} collective-permute-done((bf16[4,128,256]{2,1,0:T(8,128)(2,1)S(1)}, bf16[4,128,256]{2,1,0:T(8,128)(2,1)}, u32[]{:S(2)}, u32[]{:S(2)}) %collective-permute-start.25) | collective-permute-done | bytes 262176 | tf_op jit(solution)/shard_map/ppermute | solution.py:30
  96.1 0.6 collective-permute-start.29
  96.8 1.5 %pad_maximum_fusion = bf16[1024,1024]{1,0:T(8,128)(2,1)S(1)} fusion(bf16[256,1024]{1,0:T(8,128)(2,1)} %copy-done.8, bf16[256,1024]{1,0:T(8,128)(2,1)} %copy-done.9, bf16[256,1024]{1,0:T(8,128)(2,1)} %copy-done.7, bf16[256,1024]{1,0:T(8,128)(2,1)S(1)} %maximum_select_fusion.rows), kind=kLoop, calls=%fused_computation | loop fusion | flops 8388608 | bytes 4194304 | tf_op jit(solution)/shard_map/concatenate | solution.py:212
  98.4 1.0 pad_maximum_fusion.7
  99.4 1.0 pad_maximum_fusion.6
  100.5 1.0 pad_maximum_fusion.5
  101.8 0.5 convolution_convert_fusion.5
  102.3 0.5 convolution_convert_fusion.2
  102.8 1.6 %collective-permute-start.31 = (bf16[512,256]{1,0:T(8,128)(2,1)S(1)}, bf16[512,256]{1,0:T(8,128)(2,1)S(1)}, u32[]{:S(2)}, u32[]{:S(2)}) collective-permute-start(bf16[512,256]{1,0:T(8,128)(2,1)S(1)} %convolution_convert_fusion.5), channel_id=1, source_target_pairs={{0,32},{1,33},{2,34},{3,35},{4,36},{5,37},{6,38},{7,39},{8,40},{9,... | collective-permute-start | bytes 786440 | tf_op jit(solution)/shard_map/ppermute | solution.py:30
  104.4 1.7 %collective-permute-start.35 = (bf16[512,256]{1,0:T(8,128)(2,1)S(1)}, bf16[512,256]{1,0:T(8,128)(2,1)S(1)}, u32[]{:S(2)}, u32[]{:S(2)}) collective-permute-start(bf16[512,256]{1,0:T(8,128)(2,1)S(1)} %convolution_convert_fusion.2), channel_id=1, source_target_pairs={{0,96},{1,97},{2,98},{3,99},{4,100},{5,101},{6,102},{7,103},{8,104... | collective-permute-start | bytes 786440 | tf_op jit(solution)/shard_map/ppermute | solution.py:30
  106.1 1.3 fusion.17
  107.4 1.2 convolution_convert_fusion.3
  108.9 1.2 convolution_convert_fusion.4
  110.1 3.0 %collective-permute-start.32 = (bf16[512,256]{1,0:T(8,128)(2,1)}, bf16[512,256]{1,0:T(8,128)(2,1)}, u32[]{:S(2)}, u32[]{:S(2)}) collective-permute-start(bf16[512,256]{1,0:T(8,128)(2,1)} %convolution_convert_fusion.4), channel_id=1, source_target_pairs={{0,96},{1,97},{2,98},{3,99},{4,100},{5,101},{6,102},{7,103},{8,104... | collective-permute-start | bytes 786440 | tf_op jit(solution)/shard_map/ppermute | solution.py:30
  113.1 1.3 fusion.22
  114.4 1.2 add_convert_fusion.3
  115.6 0.7 copy-done.16
  116.3 0.6 slice.131
  117.6 1.5 %collective-permute-start.36 = (bf16[512,256]{1,0:T(8,128)(2,1)}, bf16[512,256]{1,0:T(8,128)(2,1)}, u32[]{:S(2)}, u32[]{:S(2)}) collective-permute-start(bf16[512,256]{1,0:T(8,128)(2,1)} %add_convert_fusion.3), channel_id=1, source_target_pairs={{0,96},{1,97},{2,98},{3,99},{4,100},{5,101},{6,102},{7,103},{8,104... | collective-permute-start | bytes 786440 | tf_op jit(solution)/shard_map/ppermute | solution.py:30
  119.0 2.3 %add_convert_fusion.4 = bf16[512,256]{1,0:T(8,128)(2,1)} fusion(bf16[512,256]{1,0:T(8,128)(2,1)} %copy-done.16, bf16[4,1024,256]{2,1,0:T(8,128)(2,1)} %copy-done.1, s32[]{:T(128)S(6)} %select_n.126, bf16[1024,1024]{1,0:T(8,128)(2,1)S(1)} %pad_maximum_fusion), kind=kOutput, calls=%fused_computation.78 | convolution fusion | flops 268828672 | bytes 2097156 | tf_op jit(solution)/shard_map/dot_general | solution.py:225
  121.3 0.6 collective-permute-start.33
  122.1 1.4 %fusion.12 = (bf16[384,512]{1,0:T(8,128)(2,1)}, bf16[384,512]{1,0:T(8,128)(2,1)}) fusion(f32[16,24,512]{2,1,0:T(8,128)S(1)} %convert_add_fusion.1, bf16[384,512]{1,0:T(8,128)(2,1)S(1)} %copy-done.2, bf16[384,512]{1,0:T(8,128)(2,1)S(1)} %copy-done.4, f32[512]{0:T(512)S(1)} %copy-done.10, f32[512]{0:T(512)S(1)} %copy-done.11, f32[512]{0:T(512)S(1)} %copy-done.12), kind=kLoop, calls=%fused_computation.31 | loop fusion | flops 3735552 | bytes 2365440 | tf_op jit(solution)/shard_map/convert_element_type | solution.py:237
  123.5 2.0 %collective-permute-done.36 = bf16[512,256]{1,0:T(8,128)(2,1)} collective-permute-done((bf16[512,256]{1,0:T(8,128)(2,1)}, bf16[512,256]{1,0:T(8,128)(2,1)}, u32[]{:S(2)}, u32[]{:S(2)}) %collective-permute-start.36) | collective-permute-done | bytes 262176 | tf_op jit(solution)/shard_map/ppermute | solution.py:30
  125.5 1.1 convert_add_fusion.2
  126.6 3.4 %collective-permute-done.33 = bf16[512,256]{1,0:T(8,128)(2,1)S(1)} collective-permute-done((bf16[512,256]{1,0:T(8,128)(2,1)}, bf16[512,256]{1,0:T(8,128)(2,1)S(1)}, u32[]{:S(2)}, u32[]{:S(2)}) %collective-permute-start.33) | collective-permute-done | bytes 262176 | tf_op jit(solution)/shard_map/ppermute | solution.py:30
  130.1 1.0 convert_add_fusion.3
  131.1 1.0 pad_maximum_fusion.2
  (113 shorter events, 4.8 us)
Async XLA Ops:
  0.7 1.0 copy-start
  1.7 6.5 %copy-start.10 = (f32[512]{0:T(512)S(1)}, f32[512]{0:T(512)}, u32[]{:S(2)}) copy-start(f32[512]{0:T(512)} %param.20) | copy-start | bytes 6148
  1.7 6.5 %copy-start.11 = (f32[512]{0:T(512)S(1)}, f32[512]{0:T(512)}, u32[]{:S(2)}) copy-start(f32[512]{0:T(512)} %param.19) | copy-start | bytes 6148
  1.7 6.5 %copy-start.12 = (f32[512]{0:T(512)S(1)}, f32[512]{0:T(512)}, u32[]{:S(2)}) copy-start(f32[512]{0:T(512)} %param.18) | copy-start | bytes 6148
  7.1 2.0 %collective-permute-start.5 = (bf16[256,1024]{1,0:T(8,128)(2,1)S(1)}, bf16[256,1024]{1,0:T(8,128)(2,1)S(1)}, u32[]{:S(2)}, u32[]{:S(2)}) collective-permute-start(bf16[256,1024]{1,0:T(8,128)(2,1)S(1)} %get-tuple-element.45), channel_id=1, source_target_pairs={{0,1},{1,0},{2,3},{3,2},{4,5},{5,4},{6,7},{7,6},{8,9},{9,8},{10,11... | collective-permute-start | bytes 1572872 | tf_op jit(solution)/shard_map/ppermute | solution.py:30
  7.2 5.3 %collective-permute-start.3 = (bf16[256,1024]{1,0:T(8,128)(2,1)S(1)}, bf16[256,1024]{1,0:T(8,128)(2,1)S(1)}, u32[]{:S(2)}, u32[]{:S(2)}) collective-permute-start(bf16[256,1024]{1,0:T(8,128)(2,1)S(1)} %get-tuple-element.43), channel_id=1, source_target_pairs={{0,1},{1,0},{2,3},{3,2},{4,5},{5,4},{6,7},{7,6},{8,9},{9,8},{10,11... | collective-permute-start | bytes 1572872 | tf_op jit(solution)/shard_map/ppermute | solution.py:30
  7.7 5.1 %collective-permute-start.1 = (bf16[256,1024]{1,0:T(8,128)(2,1)S(1)}, bf16[256,1024]{1,0:T(8,128)(2,1)S(1)}, u32[]{:S(2)}, u32[]{:S(2)}) collective-permute-start(bf16[256,1024]{1,0:T(8,128)(2,1)S(1)} %get-tuple-element.41), channel_id=1, source_target_pairs={{0,1},{1,0},{2,3},{3,2},{4,5},{5,4},{6,7},{7,6},{8,9},{9,8},{10,11... | collective-permute-start | bytes 1572872 | tf_op jit(solution)/shard_map/ppermute | solution.py:30
  7.8 18.0 %collective-permute-start = (bf16[256,1024]{1,0:T(8,128)(2,1)S(1)}, bf16[256,1024]{1,0:T(8,128)(2,1)}, u32[]{:S(2)}, u32[]{:S(2)}) collective-permute-start(bf16[256,1024]{1,0:T(8,128)(2,1)S(1)} %get-tuple-element.39), channel_id=1, source_target_pairs={{0,1},{1,0},{2,3},{3,2},{4,5},{5,4},{6,7},{7,6},{8,9},{9,8},{10,11... | collective-permute-start | bytes 1572872 | tf_op jit(solution)/shard_map/ppermute | solution.py:30
  8.2 38.4 %collective-permute-start.17 = (f32[3,512]{1,0:T(4,128)S(1)}, f32[3,512]{1,0:T(4,128)S(1)}, u32[]{:S(2)}, u32[]{:S(2)}) collective-permute-start(f32[3,512]{1,0:T(4,128)S(1)} %pad_maximum_fusion.12), channel_id=1, source_target_pairs={{0,1},{1,0},{2,3},{3,2},{4,5},{5,4},{6,7},{7,6},{8,9},{9,8},{10,11... | collective-permute-start | bytes 18440 | tf_op jit(solution)/shard_map/ppermute | solution.py:30
  9.1 7.3 %copy-start.14 = (s32[256,1]{0,1:T(1,128)S(1)}, s32[256,1]{0,1:T(1,128)}, u32[]{:S(2)}) copy-start(s32[256,1]{0,1:T(1,128)} %param.21) | copy-start | bytes 3076
  9.3 7.4 %copy-start.15 = (s32[256]{0:T(256)S(1)}, s32[256]{0:T(256)}, u32[]{:S(2)}) copy-start(s32[256]{0:T(256)} %param.22) | copy-start | bytes 3076
  9.3 7.6 %copy-start.2 = (bf16[384,512]{1,0:T(8,128)(2,1)S(1)}, bf16[384,512]{1,0:T(8,128)(2,1)}, u32[]{:S(2)}) copy-start(bf16[384,512]{1,0:T(8,128)(2,1)} %param.23) | copy-start | bytes 1179652
  9.3 7.5 %copy-start.3 = (bf16[384,512]{1,0:T(8,128)(2,1)S(1)}, bf16[384,512]{1,0:T(8,128)(2,1)}, u32[]{:S(2)}) copy-start(bf16[384,512]{1,0:T(8,128)(2,1)} %param.17) | copy-start | bytes 1179652
  9.3 25.9 %collective-permute-start.6 = (bf16[256,1024]{1,0:T(8,128)(2,1)S(1)}, bf16[256,1024]{1,0:T(8,128)(2,1)}, u32[]{:S(2)}, u32[]{:S(2)}) collective-permute-start(bf16[256,1024]{1,0:T(8,128)(2,1)S(1)} %add_convert_fusion), channel_id=1, source_target_pairs={{0,6},{1,7},{2,0},{3,1},{4,2},{5,3},{6,4},{7,5},{8,14},{9,15},{10,... | collective-permute-start | bytes 1572872 | tf_op jit(solution)/shard_map/ppermute | solution.py:30
  12.7 26.3 %collective-permute-start.4 = (bf16[256,1024]{1,0:T(8,128)(2,1)S(1)}, bf16[256,1024]{1,0:T(8,128)(2,1)}, u32[]{:S(2)}, u32[]{:S(2)}) collective-permute-start(bf16[256,1024]{1,0:T(8,128)(2,1)S(1)} %add_convert_fusion.1), channel_id=1, source_target_pairs={{0,2},{1,3},{2,4},{3,5},{4,6},{5,7},{6,0},{7,1},{8,10},{9,11},{10,... | collective-permute-start | bytes 1572872 | tf_op jit(solution)/shard_map/ppermute | solution.py:30
  13.8 25.2 %copy-start.13 = (f32[1024]{0:T(1024)S(1)}, f32[1024]{0:T(1024)}, u32[]{:S(2)}) copy-start(f32[1024]{0:T(1024)} %param.15) | copy-start | bytes 12292
  13.8 25.2 %collective-permute-start.2 = (bf16[256,1024]{1,0:T(8,128)(2,1)}, bf16[256,1024]{1,0:T(8,128)(2,1)}, u32[]{:S(2)}, u32[]{:S(2)}) collective-permute-start(bf16[256,1024]{1,0:T(8,128)(2,1)} %add_convert_fusion.2), channel_id=1, source_target_pairs={{0,4},{1,5},{2,6},{3,7},{4,0},{5,1},{6,2},{7,3},{8,12},{9,13},{10,... | collective-permute-start | bytes 1572872 | tf_op jit(solution)/shard_map/ppermute | solution.py:30
  17.9 23.6 %all-to-all-start = ((bf16[16,24,1024]{2,1,0:T(8,128)(2,1)}), bf16[16,24,1024]{2,1,0:T(8,128)(2,1)S(1)}, u32[]{:S(2)}, u32[]{:S(2)}) async-start(bf16[16,24,1024]{2,1,0:T(8,128)(2,1)} %bitcast.15), calls=%async_computation | async-start | bytes 1572864 | tf_op jit(solution)/shard_map/all_to_all | solution.py:157
  46.5 1.3 collective-permute-start.8
  46.7 1.7 %collective-permute-start.10 = (bf16[128,1024]{1,0:T(8,128)(2,1)S(1)}, bf16[128,1024]{1,0:T(8,128)(2,1)S(1)}, u32[]{:S(2)}, u32[]{:S(2)}) collective-permute-start(bf16[128,1024]{1,0:T(8,128)(2,1)S(1)} %get-tuple-element.55), channel_id=1, source_target_pairs={{0,1},{1,0},{2,3},{3,2},{4,5},{5,4},{6,7},{7,6},{8,9},{9,8},{10,11... | collective-permute-start | bytes 786440 | tf_op jit(solution)/shard_map/ppermute | solution.py:30
  47.2 1.5 %collective-permute-start.9 = (bf16[128,1024]{1,0:T(8,128)(2,1)S(1)}, bf16[128,1024]{1,0:T(8,128)(2,1)S(1)}, u32[]{:S(2)}, u32[]{:S(2)}) collective-permute-start(bf16[128,1024]{1,0:T(8,128)(2,1)S(1)} %get-tuple-element.53), channel_id=1, source_target_pairs={{0,1},{1,0},{2,3},{3,2},{4,5},{5,4},{6,7},{7,6},{8,9},{9,8},{10,11... | collective-permute-start | bytes 786440 | tf_op jit(solution)/shard_map/ppermute | solution.py:30
  47.3 1.8 %collective-permute-start.7 = (bf16[128,1024]{1,0:T(8,128)(2,1)S(1)}, bf16[128,1024]{1,0:T(8,128)(2,1)S(1)}, u32[]{:S(2)}, u32[]{:S(2)}) collective-permute-start(bf16[128,1024]{1,0:T(8,128)(2,1)S(1)} %get-tuple-element.49), channel_id=1, source_target_pairs={{0,1},{1,0},{2,3},{3,2},{4,5},{5,4},{6,7},{7,6},{8,9},{9,8},{10,11... | collective-permute-start | bytes 786440 | tf_op jit(solution)/shard_map/ppermute | solution.py:30
  47.7 1.8 %collective-permute-start.11 = (bf16[128,1024]{1,0:T(8,128)(2,1)S(1)}, bf16[128,1024]{1,0:T(8,128)(2,1)S(1)}, u32[]{:S(2)}, u32[]{:S(2)}) collective-permute-start(bf16[128,1024]{1,0:T(8,128)(2,1)S(1)} %get-tuple-element.56), channel_id=1, source_target_pairs={{0,1},{1,0},{2,3},{3,2},{4,5},{5,4},{6,7},{7,6},{8,9},{9,8},{10,11... | collective-permute-start | bytes 786440 | tf_op jit(solution)/shard_map/ppermute | solution.py:30
  50.1 6.7 %collective-permute-start.16 = (bf16[128,1024]{1,0:T(8,128)(2,1)S(1)}, bf16[128,1024]{1,0:T(8,128)(2,1)S(1)}, u32[]{:S(2)}, u32[]{:S(2)}) collective-permute-start(bf16[128,1024]{1,0:T(8,128)(2,1)S(1)} %get-tuple-element.82), channel_id=1, source_target_pairs={{0,1},{1,0},{2,3},{3,2},{4,5},{5,4},{6,7},{7,6},{8,9},{9,8},{10,11... | collective-permute-start | bytes 786440 | tf_op jit(solution)/shard_map/ppermute | solution.py:30
  50.6 9.6 %collective-permute-start.14 = (bf16[136,1024]{1,0:T(8,128)(2,1)S(1)}, bf16[136,1024]{1,0:T(8,128)(2,1)S(1)}, u32[]{:S(2)}, u32[]{:S(2)}) collective-permute-start(bf16[136,1024]{1,0:T(8,128)(2,1)S(1)} %get-tuple-element.60), channel_id=1, source_target_pairs={{0,6},{1,7},{2,0},{3,1},{4,2},{5,3},{6,4},{7,5},{8,14},{9,15},{10,... | collective-permute-start | bytes 835592 | tf_op jit(solution)/shard_map/ppermute | solution.py:30
  50.7 11.1 %collective-permute-start.12 = (bf16[136,1024]{1,0:T(8,128)(2,1)S(1)}, bf16[136,1024]{1,0:T(8,128)(2,1)S(1)}, u32[]{:S(2)}, u32[]{:S(2)}) collective-permute-start(bf16[136,1024]{1,0:T(8,128)(2,1)S(1)} %get-tuple-element.58), channel_id=1, source_target_pairs={{0,4},{1,5},{2,6},{3,7},{4,0},{5,1},{6,2},{7,3},{8,12},{9,13},{10,... | collective-permute-start | bytes 835592 | tf_op jit(solution)/shard_map/ppermute | solution.py:30
  52.1 14.8 %collective-permute-start.13 = (bf16[136,1024]{1,0:T(8,128)(2,1)S(1)}, bf16[136,1024]{1,0:T(8,128)(2,1)S(1)}, u32[]{:S(2)}, u32[]{:S(2)}) collective-permute-start(bf16[136,1024]{1,0:T(8,128)(2,1)S(1)} %get-tuple-element.59), channel_id=1, source_target_pairs={{0,2},{1,3},{2,4},{3,5},{4,6},{5,7},{6,0},{7,1},{8,10},{9,11},{10,... | collective-permute-start | bytes 835592 | tf_op jit(solution)/shard_map/ppermute | solution.py:30
  52.7 24.7 %collective-permute-start.21 = (bf16[256,1024]{1,0:T(8,128)(2,1)S(1)}, bf16[256,1024]{1,0:T(8,128)(2,1)S(1)}, u32[]{:S(2)}, u32[]{:S(2)}) collective-permute-start(bf16[256,1024]{1,0:T(8,128)(2,1)S(1)} %maximum_select_fusion.rows), channel_id=1, source_target_pairs={{0,24},{1,25},{2,26},{3,27},{4,28},{5,29},{6,30},{7,31},{8,0},{9,1... | collective-permute-start | bytes 1572872 | tf_op jit(solution)/shard_map/ppermute | solution.py:30
  56.8 20.7 %collective-permute-start.22 = (bf16[256,1024]{1,0:T(8,128)(2,1)S(1)}, bf16[256,1024]{1,0:T(8,128)(2,1)S(1)}, u32[]{:S(2)}, u32[]{:S(2)}) collective-permute-start(bf16[256,1024]{1,0:T(8,128)(2,1)S(1)} %maximum_select_fusion.rows), channel_id=1, source_target_pairs={{0,8},{1,9},{2,10},{3,11},{4,12},{5,13},{6,14},{7,15},{8,16},{9,17... | collective-permute-start | bytes 1572872 | tf_op jit(solution)/shard_map/ppermute | solution.py:30
  67.6 6.6 %collective-permute-start.20 = (bf16[128,256]{1,0:T(8,128)(2,1)S(1)}, bf16[128,256]{1,0:T(8,128)(2,1)S(1)}, u32[]{:S(2)}, u32[]{:S(2)}) collective-permute-start(bf16[128,256]{1,0:T(8,128)(2,1)S(1)} %get-tuple-element.86), channel_id=1, source_target_pairs={{0,8},{1,9},{2,10},{3,11},{4,12},{5,13},{6,14},{7,15},{8,16},{9,17... | collective-permute-start | bytes 196616 | tf_op jit(solution)/shard_map/ppermute | solution.py:30
  69.5 7.0 %collective-permute-start.19 = (bf16[128,256]{1,0:T(8,128)(2,1)S(1)}, bf16[128,256]{1,0:T(8,128)(2,1)S(1)}, u32[]{:S(2)}, u32[]{:S(2)}) collective-permute-start(bf16[128,256]{1,0:T(8,128)(2,1)S(1)} %get-tuple-element.87), channel_id=1, source_target_pairs={{0,16},{1,17},{2,18},{3,19},{4,20},{5,21},{6,22},{7,23},{8,24},{9,... | collective-permute-start | bytes 196616 | tf_op jit(solution)/shard_map/ppermute | solution.py:30
  73.1 4.3 %collective-permute-start.18 = (bf16[128,256]{1,0:T(8,128)(2,1)S(1)}, bf16[128,256]{1,0:T(8,128)(2,1)S(1)}, u32[]{:S(2)}, u32[]{:S(2)}) collective-permute-start(bf16[128,256]{1,0:T(8,128)(2,1)S(1)} %get-tuple-element.88), channel_id=1, source_target_pairs={{0,24},{1,25},{2,26},{3,27},{4,28},{5,29},{6,30},{7,31},{8,0},{9,1... | collective-permute-start | bytes 196616 | tf_op jit(solution)/shard_map/ppermute | solution.py:30
  77.5 19.2 %copy-start.7 = (bf16[256,1024]{1,0:T(8,128)(2,1)}, bf16[256,1024]{1,0:T(8,128)(2,1)S(1)}, u32[]{:S(2)}) copy-start(bf16[256,1024]{1,0:T(8,128)(2,1)S(1)} %collective-permute-done.21) | copy-start | bytes 1572868
  77.5 19.2 %copy-start.8 = (bf16[256,1024]{1,0:T(8,128)(2,1)}, bf16[256,1024]{1,0:T(8,128)(2,1)S(1)}, u32[]{:S(2)}) copy-start(bf16[256,1024]{1,0:T(8,128)(2,1)S(1)} %collective-permute-done.22) | copy-start | bytes 1572868
  77.5 18.5 %collective-permute-start.26 = (bf16[256,1024]{1,0:T(8,128)(2,1)S(1)}, bf16[256,1024]{1,0:T(8,128)(2,1)S(1)}, u32[]{:S(2)}, u32[]{:S(2)}) collective-permute-start(bf16[256,1024]{1,0:T(8,128)(2,1)S(1)} %maximum_select_fusion.rows), channel_id=1, source_target_pairs={{0,16},{1,17},{2,18},{3,19},{4,20},{5,21},{6,22},{7,23},{8,24},{9,... | collective-permute-start | bytes 1572872 | tf_op jit(solution)/shard_map/ppermute | solution.py:30
  79.1 2.2 %collective-permute-start.15 = (bf16[128,512]{1,0:T(8,128)(2,1)S(1)}, bf16[128,512]{1,0:T(8,128)(2,1)S(1)}, u32[]{:S(2)}, u32[]{:S(2)}) collective-permute-start(bf16[128,512]{1,0:T(8,128)(2,1)S(1)} %get-tuple-element.90), channel_id=1, source_target_pairs={{0,1},{1,0},{2,3},{3,2},{4,5},{5,4},{6,7},{7,6},{8,9},{9,8},{10,11... | collective-permute-start | bytes 393224 | tf_op jit(solution)/shard_map/ppermute | solution.py:30
  79.2 9.3 %collective-permute-start.23 = (bf16[4,128,256]{2,1,0:T(8,128)(2,1)S(1)}, bf16[4,128,256]{2,1,0:T(8,128)(2,1)}, u32[]{:S(2)}, u32[]{:S(2)}) collective-permute-start(bf16[4,128,256]{2,1,0:T(8,128)(2,1)S(1)} %pad_maximum_fusion.11), channel_id=1, source_target_pairs={{0,6},{1,7},{2,0},{3,1},{4,2},{5,3},{6,4},{7,5},{8,14},{9,15},{10,... | collective-permute-start | bytes 786440 | tf_op jit(solution)/shard_map/ppermute | solution.py:30
  80.4 10.8 %collective-permute-start.24 = (bf16[4,128,256]{2,1,0:T(8,128)(2,1)S(1)}, bf16[4,128,256]{2,1,0:T(8,128)(2,1)}, u32[]{:S(2)}, u32[]{:S(2)}) collective-permute-start(bf16[4,128,256]{2,1,0:T(8,128)(2,1)S(1)} %pad_maximum_fusion.11), channel_id=1, source_target_pairs={{0,4},{1,5},{2,6},{3,7},{4,0},{5,1},{6,2},{7,3},{8,12},{9,13},{10,... | collective-permute-start | bytes 786440 | tf_op jit(solution)/shard_map/ppermute | solution.py:30
  80.4 15.5 %collective-permute-start.25 = (bf16[4,128,256]{2,1,0:T(8,128)(2,1)S(1)}, bf16[4,128,256]{2,1,0:T(8,128)(2,1)}, u32[]{:S(2)}, u32[]{:S(2)}) collective-permute-start(bf16[4,128,256]{2,1,0:T(8,128)(2,1)S(1)} %pad_maximum_fusion.11), channel_id=1, source_target_pairs={{0,2},{1,3},{2,4},{3,5},{4,6},{5,7},{6,0},{7,1},{8,10},{9,11},{10,... | collective-permute-start | bytes 786440 | tf_op jit(solution)/shard_map/ppermute | solution.py:30
  81.3 14.7 %collective-permute-start.27 = (bf16[4,128,256]{2,1,0:T(8,128)(2,1)S(1)}, bf16[4,128,256]{2,1,0:T(8,128)(2,1)S(1)}, u32[]{:S(2)}, u32[]{:S(2)}) collective-permute-start(bf16[4,128,256]{2,1,0:T(8,128)(2,1)S(1)} %pad_maximum_fusion.11), channel_id=1, source_target_pairs={{0,1},{1,0},{2,3},{3,2},{4,5},{5,4},{6,7},{7,6},{8,9},{9,8},{10,11... | collective-permute-start | bytes 786440 | tf_op jit(solution)/shard_map/ppermute | solution.py:30
  82.4 39.5 %all-to-all-start.1 = ((bf16[16,24,512]{2,1,0:T(8,128)(2,1)}), bf16[16,24,512]{2,1,0:T(8,128)(2,1)S(1)}, u32[]{:S(2)}, u32[]{:S(2)}) async-start(bf16[16,24,512]{2,1,0:T(8,128)(2,1)} %bitcast.92), calls=%async_computation.1 | async-start | bytes 786432 | tf_op jit(solution)/shard_map/all_to_all | solution.py:219
  96.0 0.8 copy-start.9
  96.0 2.4 %collective-permute-start.30 = (bf16[4,128,256]{2,1,0:T(8,128)(2,1)}, bf16[4,128,256]{2,1,0:T(8,128)(2,1)S(1)}, u32[]{:S(2)}, u32[]{:S(2)}) collective-permute-start(bf16[4,128,256]{2,1,0:T(8,128)(2,1)} %collective-permute-done.25), channel_id=1, source_target_pairs={{0,1},{1,0},{2,3},{3,2},{4,5},{5,4},{6,7},{7,6},{8,9},{9,8},{10,11... | collective-permute-start | bytes 786440 | tf_op jit(solution)/shard_map/ppermute | solution.py:30
  96.1 3.3 %collective-permute-start.29 = (bf16[4,128,256]{2,1,0:T(8,128)(2,1)}, bf16[4,128,256]{2,1,0:T(8,128)(2,1)S(1)}, u32[]{:S(2)}, u32[]{:S(2)}) collective-permute-start(bf16[4,128,256]{2,1,0:T(8,128)(2,1)} %collective-permute-done.24), channel_id=1, source_target_pairs={{0,1},{1,0},{2,3},{3,2},{4,5},{5,4},{6,7},{7,6},{8,9},{9,8},{10,11... | collective-permute-start | bytes 786440 | tf_op jit(solution)/shard_map/ppermute | solution.py:30
  96.8 3.7 %collective-permute-start.28 = (bf16[4,128,256]{2,1,0:T(8,128)(2,1)}, bf16[4,128,256]{2,1,0:T(8,128)(2,1)S(1)}, u32[]{:S(2)}, u32[]{:S(2)}) collective-permute-start(bf16[4,128,256]{2,1,0:T(8,128)(2,1)} %collective-permute-done.23), channel_id=1, source_target_pairs={{0,1},{1,0},{2,3},{3,2},{4,5},{5,4},{6,7},{7,6},{8,9},{9,8},{10,11... | collective-permute-start | bytes 786440 | tf_op jit(solution)/shard_map/ppermute | solution.py:30
  101.8 12.6 %copy-start.1 = (bf16[4,1024,256]{2,1,0:T(8,128)(2,1)}, bf16[4,1024,256]{2,1,0:T(8,128)(2,1)S(1)}, u32[]{:S(2)}) copy-start(bf16[4,1024,256]{2,1,0:T(8,128)(2,1)S(1)} %pad_maximum_fusion.1) | copy-start | bytes 6291460
  102.8 12.7 %collective-permute-start.31 = (bf16[512,256]{1,0:T(8,128)(2,1)S(1)}, bf16[512,256]{1,0:T(8,128)(2,1)S(1)}, u32[]{:S(2)}, u32[]{:S(2)}) collective-permute-start(bf16[512,256]{1,0:T(8,128)(2,1)S(1)} %convolution_convert_fusion.5), channel_id=1, source_target_pairs={{0,32},{1,33},{2,34},{3,35},{4,36},{5,37},{6,38},{7,39},{8,40},{9,... | collective-permute-start | bytes 786440 | tf_op jit(solution)/shard_map/ppermute | solution.py:30
  104.4 10.0 %collective-permute-start.35 = (bf16[512,256]{1,0:T(8,128)(2,1)S(1)}, bf16[512,256]{1,0:T(8,128)(2,1)S(1)}, u32[]{:S(2)}, u32[]{:S(2)}) collective-permute-start(bf16[512,256]{1,0:T(8,128)(2,1)S(1)} %convolution_convert_fusion.2), channel_id=1, source_target_pairs={{0,96},{1,97},{2,98},{3,99},{4,100},{5,101},{6,102},{7,103},{8,104... | collective-permute-start | bytes 786440 | tf_op jit(solution)/shard_map/ppermute | solution.py:30
  108.6 14.9 %collective-permute-start.34 = (bf16[512,256]{1,0:T(8,128)(2,1)}, bf16[512,256]{1,0:T(8,128)(2,1)}, u32[]{:S(2)}, u32[]{:S(2)}) collective-permute-start(bf16[512,256]{1,0:T(8,128)(2,1)} %convolution_convert_fusion.3), channel_id=1, source_target_pairs={{0,32},{1,33},{2,34},{3,35},{4,36},{5,37},{6,38},{7,39},{8,40},{9,... | collective-permute-start | bytes 786440 | tf_op jit(solution)/shard_map/ppermute | solution.py:30
  110.1 16.5 %collective-permute-start.32 = (bf16[512,256]{1,0:T(8,128)(2,1)}, bf16[512,256]{1,0:T(8,128)(2,1)}, u32[]{:S(2)}, u32[]{:S(2)}) collective-permute-start(bf16[512,256]{1,0:T(8,128)(2,1)} %convolution_convert_fusion.4), channel_id=1, source_target_pairs={{0,96},{1,97},{2,98},{3,99},{4,100},{5,101},{6,102},{7,103},{8,104... | collective-permute-start | bytes 786440 | tf_op jit(solution)/shard_map/ppermute | solution.py:30
  115.6 0.7 copy-start.16
  117.5 4.5 %copy-start.4 = (bf16[384,512]{1,0:T(8,128)(2,1)S(1)}, bf16[384,512]{1,0:T(8,128)(2,1)}, u32[]{:S(2)}) copy-start(bf16[384,512]{1,0:T(8,128)(2,1)} %param.17) | copy-start | bytes 1179652
  117.6 7.9 %collective-permute-start.36 = (bf16[512,256]{1,0:T(8,128)(2,1)}, bf16[512,256]{1,0:T(8,128)(2,1)}, u32[]{:S(2)}, u32[]{:S(2)}) collective-permute-start(bf16[512,256]{1,0:T(8,128)(2,1)} %add_convert_fusion.3), channel_id=1, source_target_pairs={{0,96},{1,97},{2,98},{3,99},{4,100},{5,101},{6,102},{7,103},{8,104... | collective-permute-start | bytes 786440 | tf_op jit(solution)/shard_map/ppermute | solution.py:30
  121.3 4.2 %copy-start.6 = (f32[512,256]{1,0:T(8,128)S(1)}, f32[512,256]{1,0:T(8,128)}, u32[]{:S(2)}) copy-start(f32[512,256]{1,0:T(8,128)} %fusion.17) | copy-start | bytes 1572868
  121.3 8.7 %collective-permute-start.33 = (bf16[512,256]{1,0:T(8,128)(2,1)}, bf16[512,256]{1,0:T(8,128)(2,1)S(1)}, u32[]{:S(2)}, u32[]{:S(2)}) collective-permute-start(bf16[512,256]{1,0:T(8,128)(2,1)} %add_convert_fusion.4), channel_id=1, source_target_pairs={{0,32},{1,33},{2,34},{3,35},{4,36},{5,37},{6,38},{7,39},{8,40},{9,... | collective-permute-start | bytes 786440 | tf_op jit(solution)/shard_map/ppermute | solution.py:30
  122.1 8.0 %copy-start.5 = (f32[512,256]{1,0:T(8,128)S(1)}, f32[512,256]{1,0:T(8,128)}, u32[]{:S(2)}) copy-start(f32[512,256]{1,0:T(8,128)} %fusion.22) | copy-start | bytes 1572868

commit v6 on v5

--- a/solution.py
+++ b/solution.py
@@ -92,7 +92,7 @@
 
 def project(context, w_out, width, exchange):
     y, c = lax.axis_index("y"), lax.axis_index("c")
-    steps = (2, 1, -1, 0)
+    steps = (-1, 1, 2, 0)
 
     def emit(i, value, starts, extra, outs):
         outs[i][...] = value.astype(BF)

time: 133 us -> 132 us (level)
  waiting for transfers between devices: 41.7 us -> 39.2 us
  starting transfers between devices: 48.4 us -> 50.5 us
    ppermute x37, waiting for transfers between devices: 41.7 us -> 38.1 us  [move(): return lax.ppermute(value, AXES, pairs)]
    ppermute x37, starting transfers between devices: 34.7 us -> 36.7 us  [move(): return lax.ppermute(value, AXES, pairs)]
where the time goes in v6:
time: 132 us
  starting transfers between devices  50.5 us (38%)
  waiting for transfers between devices  39.2 us (30%)
  other arithmetic  15.5 us (12%)
  matrix products  11.4 us (9%)
  Pallas kernels  10.4 us (8%)
  local copies, waits for them, and re-layouts  2.77 us (2%)
  between operations  1.9 us (1%)
    ppermute x37, waiting for transfers between devices, move(): return lax.ppermute(value, AXES, pairs)  38.1 us
    ppermute x37, starting transfers between devices, move(): return lax.ppermute(value, AXES, pairs)  36.7 us
    pallas_call x2, Pallas kernels, products(): pl.pallas_call(functools.partial(product_kernel, n, width, len(extra), em...  10.4 us
    dot_general x8, matrix products, grad_term(): lax.dot_general(lines, columns, (((0,), (0,)), ((), ())), preferred_eleme...  9.5 us
    all_to_all x1, starting transfers between devices, body(): lax.all_to_all(after(both, *others), ('x', 'z'), 0, 0, tiled=True)  7.87 us
    all_to_all x1, starting transfers between devices, body(): placed = lax.all_to_all(placed, ('x', 'z'), 0, 0, tiled=True)  5.87 us
    another operation x4, other arithmetic, body(): jnp.stack(pair, axis=1)  3.05 us
  transfers between devices with their start and end apart: 39, of which 17 were waited for; matrix products, arithmetic and copies ran while one was open for 19% of the time, Pallas kernels for 4%

profile of v6, /device:TPU:0, one launch (start us, length us, event | category | flops | bytes accessed | tf_op | source)
XLA Modules:
  0.0 131.5 jit_solution(234087869505916793)
XLA Ops:
  0.7 1.0 copy-done
  1.7 5.4 %shard_map.139 = (bf16[256,1024]{1,0:T(8,128)(2,1)S(1)}, bf16[256,1024]{1,0:T(8,128)(2,1)S(1)}, bf16[256,1024]{1,0:T(8,128)(2,1)S(1)}, bf16[256,1024]{1,0:T(8,12...) custom-call(s32[8]{0:T(128)S(1)} %stack.149.starts, ...), custom_call_target="tpu_custom_call" | custom-call | flops 2147483648 | bytes 8388608 | tf_op jit(solution)/shard_map/pallas_call | solution.py:76
  7.2 0.5 collective-permute-start.3
  8.4 0.7 collective-permute-done.5
  9.3 3.4 %collective-permute-start.6 = (bf16[256,1024]{1,0:T(8,128)(2,1)S(1)}, bf16[256,1024]{1,0:T(8,128)(2,1)}, u32[]{:S(2)}, u32[]{:S(2)}) collective-permute-start(bf16[256,1024]{1,0:T(8,128)(2,1)S(1)} %add_convert_fusion), channel_id=1, source_target_pairs={{0,4},{1,5},{2,6},{3,7},{4,0},{5,1},{6,2},{7,3},{8,12},{9,13},{10,... | collective-permute-start | bytes 1572872 | tf_op jit(solution)/shard_map/ppermute | solution.py:30
  12.9 0.7 collective-permute-start.4
  13.6 1.0 add_convert_fusion.2
  14.6 2.6 %collective-permute-start.2 = (bf16[256,1024]{1,0:T(8,128)(2,1)}, bf16[256,1024]{1,0:T(8,128)(2,1)}, u32[]{:S(2)}, u32[]{:S(2)}) collective-permute-start(bf16[256,1024]{1,0:T(8,128)(2,1)} %add_convert_fusion.2), channel_id=1, source_target_pairs={{0,6},{1,7},{2,0},{3,1},{4,2},{5,3},{6,4},{7,5},{8,14},{9,15},{10,... | collective-permute-start | bytes 1572872 | tf_op jit(solution)/shard_map/ppermute | solution.py:30
  17.6 1.0 pad_maximum_fusion.3
  18.6 7.9 %all-to-all-start = ((bf16[16,24,1024]{2,1,0:T(8,128)(2,1)}), bf16[16,24,1024]{2,1,0:T(8,128)(2,1)S(1)}, u32[]{:S(2)}, u32[]{:S(2)}) async-start(bf16[16,24,1024]{2,1,0:T(8,128)(2,1)} %bitcast.15), calls=%async_computation | async-start | bytes 1572864 | tf_op jit(solution)/shard_map/all_to_all | solution.py:157
  26.5 9.7 %collective-permute-done.4 = bf16[256,1024]{1,0:T(8,128)(2,1)} collective-permute-done((bf16[256,1024]{1,0:T(8,128)(2,1)S(1)}, bf16[256,1024]{1,0:T(8,128)(2,1)}, u32[]{:S(2)}, u32[]{:S(2)}) %collective-permute-start.4) | collective-permute-done | bytes 524320 | tf_op jit(solution)/shard_map/ppermute | solution.py:30
  36.7 2.2 %multiply_reduce_fusion = (f32[256]{0:T(256)S(1)}, bf16[256,1024]{1,0:T(8,128)(2,1)S(1)}) fusion(bf16[256,1024]{1,0:T(8,128)(2,1)} %collective-permute-done.6, bf16[256,1024]{1,0:T(8,128)(2,1)} %collective-permute-done.4, bf16[256,1024]{1,0:T(8,128)(2,1)} %collective-permute-done.2, bf16[256,1024]{1,0:T(8,128)(2,1)} %collective-permute-done, ...), kind=kLoop, calls=%fused_computation.12 | loop fusion | flops 4194048 | bytes 3676160 | tf_op jit(solution)/shard_map/reduce_sum | solution.py:163
  39.2 1.1 all-to-all-done
  40.3 5.0 %shard_map.140 = (bf16[128,1024]{1,0:T(8,128)(2,1)S(1)}, bf16[128,1024]{1,0:T(8,128)(2,1)S(1)}, bf16[128,1024]{1,0:T(8,128)(2,1)S(1)}, bf16[128,1024]{1,0:T(8,12...) custom-call(s32[4]{0:T(128)S(1)} %pad_add_fusion.starts, ...), custom_call_target="tpu_custom_call" | custom-call | flops 2147483648 | bytes 8388608 | tf_op jit(solution)/shard_map/pallas_call | solution.py:76
  45.4 0.6 collective-permute-start.10
  46.6 0.5 collective-permute-done.10
  48.3 0.5 convolution_convert_fusion
  49.3 1.6 %collective-permute-start.14 = (bf16[136,1024]{1,0:T(8,128)(2,1)S(1)}, bf16[136,1024]{1,0:T(8,128)(2,1)S(1)}, u32[]{:S(2)}, u32[]{:S(2)}) collective-permute-start(bf16[136,1024]{1,0:T(8,128)(2,1)S(1)} %get-tuple-element.60), channel_id=1, source_target_pairs={{0,6},{1,7},{2,0},{3,1},{4,2},{5,3},{6,4},{7,5},{8,14},{9,15},{10,... | collective-permute-start | bytes 835592 | tf_op jit(solution)/shard_map/ppermute | solution.py:30
  51.0 0.8 collective-permute-start.12
  51.7 0.8 collective-permute-start.13
  52.5 4.1 %collective-permute-start.21 = (bf16[256,1024]{1,0:T(8,128)(2,1)S(1)}, bf16[256,1024]{1,0:T(8,128)(2,1)S(1)}, u32[]{:S(2)}, u32[]{:S(2)}) collective-permute-start(bf16[256,1024]{1,0:T(8,128)(2,1)S(1)} %maximum_select_fusion.rows), channel_id=1, source_target_pairs={{0,24},{1,25},{2,26},{3,27},{4,28},{5,29},{6,30},{7,31},{8,0},{9,1... | collective-permute-start | bytes 1572872 | tf_op jit(solution)/shard_map/ppermute | solution.py:30
  56.7 2.3 %collective-permute-done.14 = bf16[136,1024]{1,0:T(8,128)(2,1)S(1)} collective-permute-done((bf16[136,1024]{1,0:T(8,128)(2,1)S(1)}, bf16[136,1024]{1,0:T(8,128)(2,1)S(1)}, u32[]{:S(2)}, u32[]{:S(2)}) %collective-permute-start.14) | collective-permute-done | bytes 278560 | tf_op jit(solution)/shard_map/ppermute | solution.py:30
  58.9 3.1 %collective-permute-done.12 = bf16[136,1024]{1,0:T(8,128)(2,1)S(1)} collective-permute-done((bf16[136,1024]{1,0:T(8,128)(2,1)S(1)}, bf16[136,1024]{1,0:T(8,128)(2,1)S(1)}, u32[]{:S(2)}, u32[]{:S(2)}) %collective-permute-start.12) | collective-permute-done | bytes 278560 | tf_op jit(solution)/shard_map/ppermute | solution.py:30
  62.1 4.8 %collective-permute-done.13 = bf16[136,1024]{1,0:T(8,128)(2,1)S(1)} collective-permute-done((bf16[136,1024]{1,0:T(8,128)(2,1)S(1)}, bf16[136,1024]{1,0:T(8,128)(2,1)S(1)}, u32[]{:S(2)}, u32[]{:S(2)}) %collective-permute-start.13) | collective-permute-done | bytes 278560 | tf_op jit(solution)/shard_map/ppermute | solution.py:30
  66.9 0.6 fusion.35
  67.5 2.0 %collective-permute-start.20 = (bf16[128,256]{1,0:T(8,128)(2,1)S(1)}, bf16[128,256]{1,0:T(8,128)(2,1)S(1)}, u32[]{:S(2)}, u32[]{:S(2)}) collective-permute-start(bf16[128,256]{1,0:T(8,128)(2,1)S(1)} %get-tuple-element.86), channel_id=1, source_target_pairs={{0,8},{1,9},{2,10},{3,11},{4,12},{5,13},{6,14},{7,15},{8,16},{9,17... | collective-permute-start | bytes 196616 | tf_op jit(solution)/shard_map/ppermute | solution.py:30
  69.5 3.6 %collective-permute-start.19 = (bf16[128,256]{1,0:T(8,128)(2,1)S(1)}, bf16[128,256]{1,0:T(8,128)(2,1)S(1)}, u32[]{:S(2)}, u32[]{:S(2)}) collective-permute-start(bf16[128,256]{1,0:T(8,128)(2,1)S(1)} %get-tuple-element.87), channel_id=1, source_target_pairs={{0,16},{1,17},{2,18},{3,19},{4,20},{5,21},{6,22},{7,23},{8,24},{9,... | collective-permute-start | bytes 196616 | tf_op jit(solution)/shard_map/ppermute | solution.py:30
  73.1 1.0 collective-permute-start.18
  74.1 2.4 %collective-permute-done.19 = bf16[128,256]{1,0:T(8,128)(2,1)S(1)} collective-permute-done((bf16[128,256]{1,0:T(8,128)(2,1)S(1)}, bf16[128,256]{1,0:T(8,128)(2,1)S(1)}, u32[]{:S(2)}, u32[]{:S(2)}) %collective-permute-start.19) | collective-permute-done | bytes 65568 | tf_op jit(solution)/shard_map/ppermute | solution.py:30
  76.5 0.9 collective-permute-done.18
  77.4 1.6 %collective-permute-start.26 = (bf16[256,1024]{1,0:T(8,128)(2,1)S(1)}, bf16[256,1024]{1,0:T(8,128)(2,1)S(1)}, u32[]{:S(2)}, u32[]{:S(2)}) collective-permute-start(bf16[256,1024]{1,0:T(8,128)(2,1)S(1)} %maximum_select_fusion.rows), channel_id=1, source_target_pairs={{0,16},{1,17},{2,18},{3,19},{4,20},{5,21},{6,22},{7,23},{8,24},{9,... | collective-permute-start | bytes 1572872 | tf_op jit(solution)/shard_map/ppermute | solution.py:30
  79.1 0.7 collective-permute-start.23
  79.8 0.8 collective-permute-start.24
  80.6 0.8 collective-permute-start.25
  81.4 1.1 convolution_convert_fusion.1
  82.5 5.9 %all-to-all-start.1 = ((bf16[16,24,512]{2,1,0:T(8,128)(2,1)}), bf16[16,24,512]{2,1,0:T(8,128)(2,1)S(1)}, u32[]{:S(2)}, u32[]{:S(2)}) async-start(bf16[16,24,512]{2,1,0:T(8,128)(2,1)} %bitcast.92), calls=%async_computation.1 | async-start | bytes 786432 | tf_op jit(solution)/shard_map/all_to_all | solution.py:219
  88.4 2.2 %collective-permute-done.24 = bf16[4,128,256]{2,1,0:T(8,128)(2,1)} collective-permute-done((bf16[4,128,256]{2,1,0:T(8,128)(2,1)S(1)}, bf16[4,128,256]{2,1,0:T(8,128)(2,1)}, u32[]{:S(2)}, u32[]{:S(2)}) %collective-permute-start.24) | collective-permute-done | bytes 262176 | tf_op jit(solution)/shard_map/ppermute | solution.py:30
  90.6 4.8 %collective-permute-done.25 = bf16[4,128,256]{2,1,0:T(8,128)(2,1)} collective-permute-done((bf16[4,128,256]{2,1,0:T(8,128)(2,1)S(1)}, bf16[4,128,256]{2,1,0:T(8,128)(2,1)}, u32[]{:S(2)}, u32[]{:S(2)}) %collective-permute-start.25) | collective-permute-done | bytes 262176 | tf_op jit(solution)/shard_map/ppermute | solution.py:30
  95.5 0.6 collective-permute-start.29
  96.3 1.5 %pad_maximum_fusion = bf16[1024,1024]{1,0:T(8,128)(2,1)S(1)} fusion(bf16[256,1024]{1,0:T(8,128)(2,1)} %copy-done.8, bf16[256,1024]{1,0:T(8,128)(2,1)} %copy-done.9, bf16[256,1024]{1,0:T(8,128)(2,1)} %copy-done.7, bf16[256,1024]{1,0:T(8,128)(2,1)S(1)} %maximum_select_fusion.rows), kind=kLoop, calls=%fused_computation | loop fusion | flops 8388608 | bytes 4194304 | tf_op jit(solution)/shard_map/concatenate | solution.py:212
  97.8 1.0 pad_maximum_fusion.7
  98.9 1.0 pad_maximum_fusion.6
  99.9 1.0 pad_maximum_fusion.5
  101.2 0.5 convolution_convert_fusion.5
  101.8 0.5 convolution_convert_fusion.2
  102.3 1.6 %collective-permute-start.31 = (bf16[512,256]{1,0:T(8,128)(2,1)S(1)}, bf16[512,256]{1,0:T(8,128)(2,1)S(1)}, u32[]{:S(2)}, u32[]{:S(2)}) collective-permute-start(bf16[512,256]{1,0:T(8,128)(2,1)S(1)} %convolution_convert_fusion.5), channel_id=1, source_target_pairs={{0,32},{1,33},{2,34},{3,35},{4,36},{5,37},{6,38},{7,39},{8,40},{9,... | collective-permute-start | bytes 786440 | tf_op jit(solution)/shard_map/ppermute | solution.py:30
  103.8 1.7 %collective-permute-start.35 = (bf16[512,256]{1,0:T(8,128)(2,1)S(1)}, bf16[512,256]{1,0:T(8,128)(2,1)S(1)}, u32[]{:S(2)}, u32[]{:S(2)}) collective-permute-start(bf16[512,256]{1,0:T(8,128)(2,1)S(1)} %convolution_convert_fusion.2), channel_id=1, source_target_pairs={{0,96},{1,97},{2,98},{3,99},{4,100},{5,101},{6,102},{7,103},{8,104... | collective-permute-start | bytes 786440 | tf_op jit(solution)/shard_map/ppermute | solution.py:30
  105.6 1.3 fusion.17
  106.8 1.2 convolution_convert_fusion.3
  108.3 1.2 convolution_convert_fusion.4
  109.6 3.0 %collective-permute-start.32 = (bf16[512,256]{1,0:T(8,128)(2,1)}, bf16[512,256]{1,0:T(8,128)(2,1)}, u32[]{:S(2)}, u32[]{:S(2)}) collective-permute-start(bf16[512,256]{1,0:T(8,128)(2,1)} %convolution_convert_fusion.4), channel_id=1, source_target_pairs={{0,96},{1,97},{2,98},{3,99},{4,100},{5,101},{6,102},{7,103},{8,104... | collective-permute-start | bytes 786440 | tf_op jit(solution)/shard_map/ppermute | solution.py:30
  112.5 1.3 fusion.22
  113.8 1.2 add_convert_fusion.3
  115.0 0.7 copy-done.16
  115.7 0.6 slice.131
  117.0 1.5 %collective-permute-start.36 = (bf16[512,256]{1,0:T(8,128)(2,1)}, bf16[512,256]{1,0:T(8,128)(2,1)}, u32[]{:S(2)}, u32[]{:S(2)}) collective-permute-start(bf16[512,256]{1,0:T(8,128)(2,1)} %add_convert_fusion.3), channel_id=1, source_target_pairs={{0,96},{1,97},{2,98},{3,99},{4,100},{5,101},{6,102},{7,103},{8,104... | collective-permute-start | bytes 786440 | tf_op jit(solution)/shard_map/ppermute | solution.py:30
  118.5 2.3 %add_convert_fusion.4 = bf16[512,256]{1,0:T(8,128)(2,1)} fusion(bf16[512,256]{1,0:T(8,128)(2,1)} %copy-done.16, bf16[4,1024,256]{2,1,0:T(8,128)(2,1)} %copy-done.1, s32[]{:T(128)S(6)} %select_n.126, bf16[1024,1024]{1,0:T(8,128)(2,1)S(1)} %pad_maximum_fusion), kind=kOutput, calls=%fused_computation.78 | convolution fusion | flops 268828672 | bytes 2097156 | tf_op jit(solution)/shard_map/dot_general | solution.py:225
  120.8 0.6 collective-permute-start.33
  121.5 1.4 %fusion.12 = (bf16[384,512]{1,0:T(8,128)(2,1)}, bf16[384,512]{1,0:T(8,128)(2,1)}) fusion(f32[16,24,512]{2,1,0:T(8,128)S(1)} %convert_add_fusion.1, bf16[384,512]{1,0:T(8,128)(2,1)S(1)} %copy-done.2, bf16[384,512]{1,0:T(8,128)(2,1)S(1)} %copy-done.4, f32[512]{0:T(512)S(1)} %copy-done.10, f32[512]{0:T(512)S(1)} %copy-done.11, f32[512]{0:T(512)S(1)} %copy-done.12), kind=kLoop, calls=%fused_computation.31 | loop fusion | flops 3735552 | bytes 2365440 | tf_op jit(solution)/shard_map/convert_element_type | solution.py:237
  122.9 2.0 %collective-permute-done.36 = bf16[512,256]{1,0:T(8,128)(2,1)} collective-permute-done((bf16[512,256]{1,0:T(8,128)(2,1)}, bf16[512,256]{1,0:T(8,128)(2,1)}, u32[]{:S(2)}, u32[]{:S(2)}) %collective-permute-start.36) | collective-permute-done | bytes 262176 | tf_op jit(solution)/shard_map/ppermute | solution.py:30
  124.9 1.1 convert_add_fusion.2
  126.0 3.4 %collective-permute-done.33 = bf16[512,256]{1,0:T(8,128)(2,1)S(1)} collective-permute-done((bf16[512,256]{1,0:T(8,128)(2,1)}, bf16[512,256]{1,0:T(8,128)(2,1)S(1)}, u32[]{:S(2)}, u32[]{:S(2)}) %collective-permute-start.33) | collective-permute-done | bytes 262176 | tf_op jit(solution)/shard_map/ppermute | solution.py:30
  129.5 1.0 convert_add_fusion.3
  130.5 1.0 pad_maximum_fusion.2
  (113 shorter events, 6.1 us)
Async XLA Ops:
  0.7 1.0 copy-start
  1.7 6.5 %copy-start.10 = (f32[512]{0:T(512)S(1)}, f32[512]{0:T(512)}, u32[]{:S(2)}) copy-start(f32[512]{0:T(512)} %param.20) | copy-start | bytes 6148
  1.7 6.5 %copy-start.11 = (f32[512]{0:T(512)S(1)}, f32[512]{0:T(512)}, u32[]{:S(2)}) copy-start(f32[512]{0:T(512)} %param.19) | copy-start | bytes 6148
  1.7 6.5 %copy-start.12 = (f32[512]{0:T(512)S(1)}, f32[512]{0:T(512)}, u32[]{:S(2)}) copy-start(f32[512]{0:T(512)} %param.18) | copy-start | bytes 6148
  7.1 2.0 %collective-permute-start.5 = (bf16[256,1024]{1,0:T(8,128)(2,1)S(1)}, bf16[256,1024]{1,0:T(8,128)(2,1)S(1)}, u32[]{:S(2)}, u32[]{:S(2)}) collective-permute-start(bf16[256,1024]{1,0:T(8,128)(2,1)S(1)} %get-tuple-element.45), channel_id=1, source_target_pairs={{0,1},{1,0},{2,3},{3,2},{4,5},{5,4},{6,7},{7,6},{8,9},{9,8},{10,11... | collective-permute-start | bytes 1572872 | tf_op jit(solution)/shard_map/ppermute | solution.py:30
  7.2 5.5 %collective-permute-start.3 = (bf16[256,1024]{1,0:T(8,128)(2,1)S(1)}, bf16[256,1024]{1,0:T(8,128)(2,1)S(1)}, u32[]{:S(2)}, u32[]{:S(2)}) collective-permute-start(bf16[256,1024]{1,0:T(8,128)(2,1)S(1)} %get-tuple-element.43), channel_id=1, source_target_pairs={{0,1},{1,0},{2,3},{3,2},{4,5},{5,4},{6,7},{7,6},{8,9},{9,8},{10,11... | collective-permute-start | bytes 1572872 | tf_op jit(solution)/shard_map/ppermute | solution.py:30
  7.7 6.0 %collective-permute-start.1 = (bf16[256,1024]{1,0:T(8,128)(2,1)S(1)}, bf16[256,1024]{1,0:T(8,128)(2,1)S(1)}, u32[]{:S(2)}, u32[]{:S(2)}) collective-permute-start(bf16[256,1024]{1,0:T(8,128)(2,1)S(1)} %get-tuple-element.41), channel_id=1, source_target_pairs={{0,1},{1,0},{2,3},{3,2},{4,5},{5,4},{6,7},{7,6},{8,9},{9,8},{10,11... | collective-permute-start | bytes 1572872 | tf_op jit(solution)/shard_map/ppermute | solution.py:30
  7.8 18.7 %collective-permute-start = (bf16[256,1024]{1,0:T(8,128)(2,1)S(1)}, bf16[256,1024]{1,0:T(8,128)(2,1)}, u32[]{:S(2)}, u32[]{:S(2)}) collective-permute-start(bf16[256,1024]{1,0:T(8,128)(2,1)S(1)} %get-tuple-element.39), channel_id=1, source_target_pairs={{0,1},{1,0},{2,3},{3,2},{4,5},{5,4},{6,7},{7,6},{8,9},{9,8},{10,11... | collective-permute-start | bytes 1572872 | tf_op jit(solution)/shard_map/ppermute | solution.py:30
  8.2 37.2 %collective-permute-start.17 = (f32[3,512]{1,0:T(4,128)S(1)}, f32[3,512]{1,0:T(4,128)S(1)}, u32[]{:S(2)}, u32[]{:S(2)}) collective-permute-start(f32[3,512]{1,0:T(4,128)S(1)} %pad_maximum_fusion.12), channel_id=1, source_target_pairs={{0,1},{1,0},{2,3},{3,2},{4,5},{5,4},{6,7},{7,6},{8,9},{9,8},{10,11... | collective-permute-start | bytes 18440 | tf_op jit(solution)/shard_map/ppermute | solution.py:30
  9.1 8.1 %copy-start.14 = (s32[256,1]{0,1:T(1,128)S(1)}, s32[256,1]{0,1:T(1,128)}, u32[]{:S(2)}) copy-start(s32[256,1]{0,1:T(1,128)} %param.21) | copy-start | bytes 3076
  9.3 8.2 %copy-start.15 = (s32[256]{0:T(256)S(1)}, s32[256]{0:T(256)}, u32[]{:S(2)}) copy-start(s32[256]{0:T(256)} %param.22) | copy-start | bytes 3076
  9.3 8.3 %copy-start.2 = (bf16[384,512]{1,0:T(8,128)(2,1)S(1)}, bf16[384,512]{1,0:T(8,128)(2,1)}, u32[]{:S(2)}) copy-start(bf16[384,512]{1,0:T(8,128)(2,1)} %param.23) | copy-start | bytes 1179652
  9.3 8.3 %copy-start.3 = (bf16[384,512]{1,0:T(8,128)(2,1)S(1)}, bf16[384,512]{1,0:T(8,128)(2,1)}, u32[]{:S(2)}) copy-start(bf16[384,512]{1,0:T(8,128)(2,1)} %param.17) | copy-start | bytes 1179652
  9.3 17.2 %collective-permute-start.6 = (bf16[256,1024]{1,0:T(8,128)(2,1)S(1)}, bf16[256,1024]{1,0:T(8,128)(2,1)}, u32[]{:S(2)}, u32[]{:S(2)}) collective-permute-start(bf16[256,1024]{1,0:T(8,128)(2,1)S(1)} %add_convert_fusion), channel_id=1, source_target_pairs={{0,4},{1,5},{2,6},{3,7},{4,0},{5,1},{6,2},{7,3},{8,12},{9,13},{10,... | collective-permute-start | bytes 1572872 | tf_op jit(solution)/shard_map/ppermute | solution.py:30
  12.9 23.4 %collective-permute-start.4 = (bf16[256,1024]{1,0:T(8,128)(2,1)S(1)}, bf16[256,1024]{1,0:T(8,128)(2,1)}, u32[]{:S(2)}, u32[]{:S(2)}) collective-permute-start(bf16[256,1024]{1,0:T(8,128)(2,1)S(1)} %add_convert_fusion.1), channel_id=1, source_target_pairs={{0,2},{1,3},{2,4},{3,5},{4,6},{5,7},{6,0},{7,1},{8,10},{9,11},{10,... | collective-permute-start | bytes 1572872 | tf_op jit(solution)/shard_map/ppermute | solution.py:30
  14.6 22.1 %copy-start.13 = (f32[1024]{0:T(1024)S(1)}, f32[1024]{0:T(1024)}, u32[]{:S(2)}) copy-start(f32[1024]{0:T(1024)} %param.15) | copy-start | bytes 12292
  14.6 22.0 %collective-permute-start.2 = (bf16[256,1024]{1,0:T(8,128)(2,1)}, bf16[256,1024]{1,0:T(8,128)(2,1)}, u32[]{:S(2)}, u32[]{:S(2)}) collective-permute-start(bf16[256,1024]{1,0:T(8,128)(2,1)} %add_convert_fusion.2), channel_id=1, source_target_pairs={{0,6},{1,7},{2,0},{3,1},{4,2},{5,3},{6,4},{7,5},{8,14},{9,15},{10,... | collective-permute-start | bytes 1572872 | tf_op jit(solution)/shard_map/ppermute | solution.py:30
  18.6 21.6 %all-to-all-start = ((bf16[16,24,1024]{2,1,0:T(8,128)(2,1)}), bf16[16,24,1024]{2,1,0:T(8,128)(2,1)S(1)}, u32[]{:S(2)}, u32[]{:S(2)}) async-start(bf16[16,24,1024]{2,1,0:T(8,128)(2,1)} %bitcast.15), calls=%async_computation | async-start | bytes 1572864 | tf_op jit(solution)/shard_map/all_to_all | solution.py:157
  45.3 1.3 collective-permute-start.8
  45.4 1.7 %collective-permute-start.10 = (bf16[128,1024]{1,0:T(8,128)(2,1)S(1)}, bf16[128,1024]{1,0:T(8,128)(2,1)S(1)}, u32[]{:S(2)}, u32[]{:S(2)}) collective-permute-start(bf16[128,1024]{1,0:T(8,128)(2,1)S(1)} %get-tuple-element.55), channel_id=1, source_target_pairs={{0,1},{1,0},{2,3},{3,2},{4,5},{5,4},{6,7},{7,6},{8,9},{9,8},{10,11... | collective-permute-start | bytes 786440 | tf_op jit(solution)/shard_map/ppermute | solution.py:30
  46.0 1.5 %collective-permute-start.9 = (bf16[128,1024]{1,0:T(8,128)(2,1)S(1)}, bf16[128,1024]{1,0:T(8,128)(2,1)S(1)}, u32[]{:S(2)}, u32[]{:S(2)}) collective-permute-start(bf16[128,1024]{1,0:T(8,128)(2,1)S(1)} %get-tuple-element.53), channel_id=1, source_target_pairs={{0,1},{1,0},{2,3},{3,2},{4,5},{5,4},{6,7},{7,6},{8,9},{9,8},{10,11... | collective-permute-start | bytes 786440 | tf_op jit(solution)/shard_map/ppermute | solution.py:30
  46.1 1.8 %collective-permute-start.7 = (bf16[128,1024]{1,0:T(8,128)(2,1)S(1)}, bf16[128,1024]{1,0:T(8,128)(2,1)S(1)}, u32[]{:S(2)}, u32[]{:S(2)}) collective-permute-start(bf16[128,1024]{1,0:T(8,128)(2,1)S(1)} %get-tuple-element.49), channel_id=1, source_target_pairs={{0,1},{1,0},{2,3},{3,2},{4,5},{5,4},{6,7},{7,6},{8,9},{9,8},{10,11... | collective-permute-start | bytes 786440 | tf_op jit(solution)/shard_map/ppermute | solution.py:30
  46.5 1.8 %collective-permute-start.11 = (bf16[128,1024]{1,0:T(8,128)(2,1)S(1)}, bf16[128,1024]{1,0:T(8,128)(2,1)S(1)}, u32[]{:S(2)}, u32[]{:S(2)}) collective-permute-start(bf16[128,1024]{1,0:T(8,128)(2,1)S(1)} %get-tuple-element.56), channel_id=1, source_target_pairs={{0,1},{1,0},{2,3},{3,2},{4,5},{5,4},{6,7},{7,6},{8,9},{9,8},{10,11... | collective-permute-start | bytes 786440 | tf_op jit(solution)/shard_map/ppermute | solution.py:30
  48.9 7.8 %collective-permute-start.16 = (bf16[128,1024]{1,0:T(8,128)(2,1)S(1)}, bf16[128,1024]{1,0:T(8,128)(2,1)S(1)}, u32[]{:S(2)}, u32[]{:S(2)}) collective-permute-start(bf16[128,1024]{1,0:T(8,128)(2,1)S(1)} %get-tuple-element.82), channel_id=1, source_target_pairs={{0,1},{1,0},{2,3},{3,2},{4,5},{5,4},{6,7},{7,6},{8,9},{9,8},{10,11... | collective-permute-start | bytes 786440 | tf_op jit(solution)/shard_map/ppermute | solution.py:30
  49.3 9.6 %collective-permute-start.14 = (bf16[136,1024]{1,0:T(8,128)(2,1)S(1)}, bf16[136,1024]{1,0:T(8,128)(2,1)S(1)}, u32[]{:S(2)}, u32[]{:S(2)}) collective-permute-start(bf16[136,1024]{1,0:T(8,128)(2,1)S(1)} %get-tuple-element.60), channel_id=1, source_target_pairs={{0,6},{1,7},{2,0},{3,1},{4,2},{5,3},{6,4},{7,5},{8,14},{9,15},{10,... | collective-permute-start | bytes 835592 | tf_op jit(solution)/shard_map/ppermute | solution.py:30
  51.0 11.1 %collective-permute-start.12 = (bf16[136,1024]{1,0:T(8,128)(2,1)S(1)}, bf16[136,1024]{1,0:T(8,128)(2,1)S(1)}, u32[]{:S(2)}, u32[]{:S(2)}) collective-permute-start(bf16[136,1024]{1,0:T(8,128)(2,1)S(1)} %get-tuple-element.58), channel_id=1, source_target_pairs={{0,4},{1,5},{2,6},{3,7},{4,0},{5,1},{6,2},{7,3},{8,12},{9,13},{10,... | collective-permute-start | bytes 835592 | tf_op jit(solution)/shard_map/ppermute | solution.py:30
  51.7 15.1 %collective-permute-start.13 = (bf16[136,1024]{1,0:T(8,128)(2,1)S(1)}, bf16[136,1024]{1,0:T(8,128)(2,1)S(1)}, u32[]{:S(2)}, u32[]{:S(2)}) collective-permute-start(bf16[136,1024]{1,0:T(8,128)(2,1)S(1)} %get-tuple-element.59), channel_id=1, source_target_pairs={{0,2},{1,3},{2,4},{3,5},{4,6},{5,7},{6,0},{7,1},{8,10},{9,11},{10,... | collective-permute-start | bytes 835592 | tf_op jit(solution)/shard_map/ppermute | solution.py:30
  52.5 24.8 %collective-permute-start.21 = (bf16[256,1024]{1,0:T(8,128)(2,1)S(1)}, bf16[256,1024]{1,0:T(8,128)(2,1)S(1)}, u32[]{:S(2)}, u32[]{:S(2)}) collective-permute-start(bf16[256,1024]{1,0:T(8,128)(2,1)S(1)} %maximum_select_fusion.rows), channel_id=1, source_target_pairs={{0,24},{1,25},{2,26},{3,27},{4,28},{5,29},{6,30},{7,31},{8,0},{9,1... | collective-permute-start | bytes 1572872 | tf_op jit(solution)/shard_map/ppermute | solution.py:30
  56.6 20.8 %collective-permute-start.22 = (bf16[256,1024]{1,0:T(8,128)(2,1)S(1)}, bf16[256,1024]{1,0:T(8,128)(2,1)S(1)}, u32[]{:S(2)}, u32[]{:S(2)}) collective-permute-start(bf16[256,1024]{1,0:T(8,128)(2,1)S(1)} %maximum_select_fusion.rows), channel_id=1, source_target_pairs={{0,8},{1,9},{2,10},{3,11},{4,12},{5,13},{6,14},{7,15},{8,16},{9,17... | collective-permute-start | bytes 1572872 | tf_op jit(solution)/shard_map/ppermute | solution.py:30
  67.5 6.6 %collective-permute-start.20 = (bf16[128,256]{1,0:T(8,128)(2,1)S(1)}, bf16[128,256]{1,0:T(8,128)(2,1)S(1)}, u32[]{:S(2)}, u32[]{:S(2)}) collective-permute-start(bf16[128,256]{1,0:T(8,128)(2,1)S(1)} %get-tuple-element.86), channel_id=1, source_target_pairs={{0,8},{1,9},{2,10},{3,11},{4,12},{5,13},{6,14},{7,15},{8,16},{9,17... | collective-permute-start | bytes 196616 | tf_op jit(solution)/shard_map/ppermute | solution.py:30
  69.5 7.0 %collective-permute-start.19 = (bf16[128,256]{1,0:T(8,128)(2,1)S(1)}, bf16[128,256]{1,0:T(8,128)(2,1)S(1)}, u32[]{:S(2)}, u32[]{:S(2)}) collective-permute-start(bf16[128,256]{1,0:T(8,128)(2,1)S(1)} %get-tuple-element.87), channel_id=1, source_target_pairs={{0,16},{1,17},{2,18},{3,19},{4,20},{5,21},{6,22},{7,23},{8,24},{9,... | collective-permute-start | bytes 196616 | tf_op jit(solution)/shard_map/ppermute | solution.py:30
  73.1 4.3 %collective-permute-start.18 = (bf16[128,256]{1,0:T(8,128)(2,1)S(1)}, bf16[128,256]{1,0:T(8,128)(2,1)S(1)}, u32[]{:S(2)}, u32[]{:S(2)}) collective-permute-start(bf16[128,256]{1,0:T(8,128)(2,1)S(1)} %get-tuple-element.88), channel_id=1, source_target_pairs={{0,24},{1,25},{2,26},{3,27},{4,28},{5,29},{6,30},{7,31},{8,0},{9,1... | collective-permute-start | bytes 196616 | tf_op jit(solution)/shard_map/ppermute | solution.py:30
  77.4 18.7 %copy-start.7 = (bf16[256,1024]{1,0:T(8,128)(2,1)}, bf16[256,1024]{1,0:T(8,128)(2,1)S(1)}, u32[]{:S(2)}) copy-start(bf16[256,1024]{1,0:T(8,128)(2,1)S(1)} %collective-permute-done.21) | copy-start | bytes 1572868
  77.4 18.7 %copy-start.8 = (bf16[256,1024]{1,0:T(8,128)(2,1)}, bf16[256,1024]{1,0:T(8,128)(2,1)S(1)}, u32[]{:S(2)}) copy-start(bf16[256,1024]{1,0:T(8,128)(2,1)S(1)} %collective-permute-done.22) | copy-start | bytes 1572868
  77.4 18.0 %collective-permute-start.26 = (bf16[256,1024]{1,0:T(8,128)(2,1)S(1)}, bf16[256,1024]{1,0:T(8,128)(2,1)S(1)}, u32[]{:S(2)}, u32[]{:S(2)}) collective-permute-start(bf16[256,1024]{1,0:T(8,128)(2,1)S(1)} %maximum_select_fusion.rows), channel_id=1, source_target_pairs={{0,16},{1,17},{2,18},{3,19},{4,20},{5,21},{6,22},{7,23},{8,24},{9,... | collective-permute-start | bytes 1572872 | tf_op jit(solution)/shard_map/ppermute | solution.py:30
  79.0 2.4 %collective-permute-start.15 = (bf16[128,512]{1,0:T(8,128)(2,1)S(1)}, bf16[128,512]{1,0:T(8,128)(2,1)S(1)}, u32[]{:S(2)}, u32[]{:S(2)}) collective-permute-start(bf16[128,512]{1,0:T(8,128)(2,1)S(1)} %get-tuple-element.90), channel_id=1, source_target_pairs={{0,1},{1,0},{2,3},{3,2},{4,5},{5,4},{6,7},{7,6},{8,9},{9,8},{10,11... | collective-permute-start | bytes 393224 | tf_op jit(solution)/shard_map/ppermute | solution.py:30
  79.1 9.3 %collective-permute-start.23 = (bf16[4,128,256]{2,1,0:T(8,128)(2,1)S(1)}, bf16[4,128,256]{2,1,0:T(8,128)(2,1)}, u32[]{:S(2)}, u32[]{:S(2)}) collective-permute-start(bf16[4,128,256]{2,1,0:T(8,128)(2,1)S(1)} %pad_maximum_fusion.11), channel_id=1, source_target_pairs={{0,6},{1,7},{2,0},{3,1},{4,2},{5,3},{6,4},{7,5},{8,14},{9,15},{10,... | collective-permute-start | bytes 786440 | tf_op jit(solution)/shard_map/ppermute | solution.py:30
  79.8 10.8 %collective-permute-start.24 = (bf16[4,128,256]{2,1,0:T(8,128)(2,1)S(1)}, bf16[4,128,256]{2,1,0:T(8,128)(2,1)}, u32[]{:S(2)}, u32[]{:S(2)}) collective-permute-start(bf16[4,128,256]{2,1,0:T(8,128)(2,1)S(1)} %pad_maximum_fusion.11), channel_id=1, source_target_pairs={{0,4},{1,5},{2,6},{3,7},{4,0},{5,1},{6,2},{7,3},{8,12},{9,13},{10,... | collective-permute-start | bytes 786440 | tf_op jit(solution)/shard_map/ppermute | solution.py:30
  80.6 14.8 %collective-permute-start.25 = (bf16[4,128,256]{2,1,0:T(8,128)(2,1)S(1)}, bf16[4,128,256]{2,1,0:T(8,128)(2,1)}, u32[]{:S(2)}, u32[]{:S(2)}) collective-permute-start(bf16[4,128,256]{2,1,0:T(8,128)(2,1)S(1)} %pad_maximum_fusion.11), channel_id=1, source_target_pairs={{0,2},{1,3},{2,4},{3,5},{4,6},{5,7},{6,0},{7,1},{8,10},{9,11},{10,... | collective-permute-start | bytes 786440 | tf_op jit(solution)/shard_map/ppermute | solution.py:30
  81.4 14.0 %collective-permute-start.27 = (bf16[4,128,256]{2,1,0:T(8,128)(2,1)S(1)}, bf16[4,128,256]{2,1,0:T(8,128)(2,1)S(1)}, u32[]{:S(2)}, u32[]{:S(2)}) collective-permute-start(bf16[4,128,256]{2,1,0:T(8,128)(2,1)S(1)} %pad_maximum_fusion.11), channel_id=1, source_target_pairs={{0,1},{1,0},{2,3},{3,2},{4,5},{5,4},{6,7},{7,6},{8,9},{9,8},{10,11... | collective-permute-start | bytes 786440 | tf_op jit(solution)/shard_map/ppermute | solution.py:30
  82.5 38.9 %all-to-all-start.1 = ((bf16[16,24,512]{2,1,0:T(8,128)(2,1)}), bf16[16,24,512]{2,1,0:T(8,128)(2,1)S(1)}, u32[]{:S(2)}, u32[]{:S(2)}) async-start(bf16[16,24,512]{2,1,0:T(8,128)(2,1)} %bitcast.92), calls=%async_computation.1 | async-start | bytes 786432 | tf_op jit(solution)/shard_map/all_to_all | solution.py:219
  95.4 0.8 copy-start.9
  95.4 2.4 %collective-permute-start.30 = (bf16[4,128,256]{2,1,0:T(8,128)(2,1)}, bf16[4,128,256]{2,1,0:T(8,128)(2,1)S(1)}, u32[]{:S(2)}, u32[]{:S(2)}) collective-permute-start(bf16[4,128,256]{2,1,0:T(8,128)(2,1)} %collective-permute-done.25), channel_id=1, source_target_pairs={{0,1},{1,0},{2,3},{3,2},{4,5},{5,4},{6,7},{7,6},{8,9},{9,8},{10,11... | collective-permute-start | bytes 786440 | tf_op jit(solution)/shard_map/ppermute | solution.py:30
  95.5 3.3 %collective-permute-start.29 = (bf16[4,128,256]{2,1,0:T(8,128)(2,1)}, bf16[4,128,256]{2,1,0:T(8,128)(2,1)S(1)}, u32[]{:S(2)}, u32[]{:S(2)}) collective-permute-start(bf16[4,128,256]{2,1,0:T(8,128)(2,1)} %collective-permute-done.24), channel_id=1, source_target_pairs={{0,1},{1,0},{2,3},{3,2},{4,5},{5,4},{6,7},{7,6},{8,9},{9,8},{10,11... | collective-permute-start | bytes 786440 | tf_op jit(solution)/shard_map/ppermute | solution.py:30
  96.2 3.7 %collective-permute-start.28 = (bf16[4,128,256]{2,1,0:T(8,128)(2,1)}, bf16[4,128,256]{2,1,0:T(8,128)(2,1)S(1)}, u32[]{:S(2)}, u32[]{:S(2)}) collective-permute-start(bf16[4,128,256]{2,1,0:T(8,128)(2,1)} %collective-permute-done.23), channel_id=1, source_target_pairs={{0,1},{1,0},{2,3},{3,2},{4,5},{5,4},{6,7},{7,6},{8,9},{9,8},{10,11... | collective-permute-start | bytes 786440 | tf_op jit(solution)/shard_map/ppermute | solution.py:30
  101.2 12.6 %copy-start.1 = (bf16[4,1024,256]{2,1,0:T(8,128)(2,1)}, bf16[4,1024,256]{2,1,0:T(8,128)(2,1)S(1)}, u32[]{:S(2)}) copy-start(bf16[4,1024,256]{2,1,0:T(8,128)(2,1)S(1)} %pad_maximum_fusion.1) | copy-start | bytes 6291460
  102.3 12.8 %collective-permute-start.31 = (bf16[512,256]{1,0:T(8,128)(2,1)S(1)}, bf16[512,256]{1,0:T(8,128)(2,1)S(1)}, u32[]{:S(2)}, u32[]{:S(2)}) collective-permute-start(bf16[512,256]{1,0:T(8,128)(2,1)S(1)} %convolution_convert_fusion.5), channel_id=1, source_target_pairs={{0,32},{1,33},{2,34},{3,35},{4,36},{5,37},{6,38},{7,39},{8,40},{9,... | collective-permute-start | bytes 786440 | tf_op jit(solution)/shard_map/ppermute | solution.py:30
  103.8 10.0 %collective-permute-start.35 = (bf16[512,256]{1,0:T(8,128)(2,1)S(1)}, bf16[512,256]{1,0:T(8,128)(2,1)S(1)}, u32[]{:S(2)}, u32[]{:S(2)}) collective-permute-start(bf16[512,256]{1,0:T(8,128)(2,1)S(1)} %convolution_convert_fusion.2), channel_id=1, source_target_pairs={{0,96},{1,97},{2,98},{3,99},{4,100},{5,101},{6,102},{7,103},{8,104... | collective-permute-start | bytes 786440 | tf_op jit(solution)/shard_map/ppermute | solution.py:30
  108.0 14.9 %collective-permute-start.34 = (bf16[512,256]{1,0:T(8,128)(2,1)}, bf16[512,256]{1,0:T(8,128)(2,1)}, u32[]{:S(2)}, u32[]{:S(2)}) collective-permute-start(bf16[512,256]{1,0:T(8,128)(2,1)} %convolution_convert_fusion.3), channel_id=1, source_target_pairs={{0,32},{1,33},{2,34},{3,35},{4,36},{5,37},{6,38},{7,39},{8,40},{9,... | collective-permute-start | bytes 786440 | tf_op jit(solution)/shard_map/ppermute | solution.py:30
  109.6 16.5 %collective-permute-start.32 = (bf16[512,256]{1,0:T(8,128)(2,1)}, bf16[512,256]{1,0:T(8,128)(2,1)}, u32[]{:S(2)}, u32[]{:S(2)}) collective-permute-start(bf16[512,256]{1,0:T(8,128)(2,1)} %convolution_convert_fusion.4), channel_id=1, source_target_pairs={{0,96},{1,97},{2,98},{3,99},{4,100},{5,101},{6,102},{7,103},{8,104... | collective-permute-start | bytes 786440 | tf_op jit(solution)/shard_map/ppermute | solution.py:30
  115.0 0.7 copy-start.16
  117.0 4.5 %copy-start.4 = (bf16[384,512]{1,0:T(8,128)(2,1)S(1)}, bf16[384,512]{1,0:T(8,128)(2,1)}, u32[]{:S(2)}) copy-start(bf16[384,512]{1,0:T(8,128)(2,1)} %param.17) | copy-start | bytes 1179652
  117.0 7.9 %collective-permute-start.36 = (bf16[512,256]{1,0:T(8,128)(2,1)}, bf16[512,256]{1,0:T(8,128)(2,1)}, u32[]{:S(2)}, u32[]{:S(2)}) collective-permute-start(bf16[512,256]{1,0:T(8,128)(2,1)} %add_convert_fusion.3), channel_id=1, source_target_pairs={{0,96},{1,97},{2,98},{3,99},{4,100},{5,101},{6,102},{7,103},{8,104... | collective-permute-start | bytes 786440 | tf_op jit(solution)/shard_map/ppermute | solution.py:30
  120.8 4.2 %copy-start.6 = (f32[512,256]{1,0:T(8,128)S(1)}, f32[512,256]{1,0:T(8,128)}, u32[]{:S(2)}) copy-start(f32[512,256]{1,0:T(8,128)} %fusion.17) | copy-start | bytes 1572868
  120.8 8.7 %collective-permute-start.33 = (bf16[512,256]{1,0:T(8,128)(2,1)}, bf16[512,256]{1,0:T(8,128)(2,1)S(1)}, u32[]{:S(2)}, u32[]{:S(2)}) collective-permute-start(bf16[512,256]{1,0:T(8,128)(2,1)} %add_convert_fusion.4), channel_id=1, source_target_pairs={{0,32},{1,33},{2,34},{3,35},{4,36},{5,37},{6,38},{7,39},{8,40},{9,... | collective-permute-start | bytes 786440 | tf_op jit(solution)/shard_map/ppermute | solution.py:30
  121.5 8.0 %copy-start.5 = (f32[512,256]{1,0:T(8,128)S(1)}, f32[512,256]{1,0:T(8,128)}, u32[]{:S(2)}) copy-start(f32[512,256]{1,0:T(8,128)} %fusion.22) | copy-start | bytes 1572868

commit v7 on v6

--- a/solution.py
+++ b/solution.py
@@ -111,7 +111,7 @@
 def join(rows, w_join, width, squares):
     y = lax.axis_index("y")
     half = rows.shape[0] // 2
-    steps = (2, 1, -1, 0)
+    steps = (1, -1, 2, 0)
 
     def emit(i, value, starts, extra, outs):
         outs[2 * i][...] = value[half:].astype(BF)

time: 132 us -> 132 us (level)
  waiting for transfers between devices: 39.2 us -> 37.2 us
  starting transfers between devices: 50.5 us -> 52.2 us
    ppermute x37, waiting for transfers between devices: 38.1 us -> 36 us  [move(): return lax.ppermute(value, AXES, pairs)]
    ppermute x37, starting transfers between devices: 36.7 us -> 38.4 us  [move(): return lax.ppermute(value, AXES, pairs)]
  transfers between devices with their start and end apart: 39 -> 39, of which waited for: 17 -> 15; matrix products, arithmetic and copies ran while one was open for 19% -> 19% of each run, Pallas kernels for 4% -> 4%
where the time goes in v7:
time: 132 us; the launch traced here: 131 us
  starting transfers between devices  52.2 us (40%)
  waiting for transfers between devices  37.2 us (28%)
  other arithmetic  15.5 us (12%)
  matrix products  11.4 us (9%)
  Pallas kernels  10.4 us (8%)
  local copies, waits for them, and re-layouts  2.77 us (2%)
  between operations  1.89 us (1%)
    ppermute x37, starting transfers between devices, move(): return lax.ppermute(value, AXES, pairs)  38.4 us
    ppermute x37, waiting for transfers between devices, move(): return lax.ppermute(value, AXES, pairs)  36 us
    pallas_call x2, Pallas kernels, products(): pl.pallas_call(functools.partial(product_kernel, n, width, len(extra), em...  10.4 us
    dot_general x8, matrix products, grad_term(): lax.dot_general(lines, columns, (((0,), (0,)), ((), ())), preferred_eleme...  9.51 us
    all_to_all x1, starting transfers between devices, body(): lax.all_to_all(after(both, *others), ('x', 'z'), 0, 0, tiled=True)  7.87 us
    all_to_all x1, starting transfers between devices, body(): placed = lax.all_to_all(placed, ('x', 'z'), 0, 0, tiled=True)  5.87 us
    another operation x4, other arithmetic, body(): jnp.stack(pair, axis=1)  3.05 us
  transfers between devices with their start and end apart: 39, of which 15 were waited for; matrix products, arithmetic and copies ran while one was open for 19% of the time, Pallas kernels for 4%

profile of v7, /device:TPU:0, one launch (start us, length us, event | category | flops | bytes accessed | tf_op | source)
XLA Modules:
  0.0 131.3 jit_solution(3675730789365279815)
XLA Ops:
  0.7 1.0 copy-done
  1.7 5.4 %shard_map.139 = (bf16[256,1024]{1,0:T(8,128)(2,1)S(1)}, bf16[256,1024]{1,0:T(8,128)(2,1)S(1)}, bf16[256,1024]{1,0:T(8,128)(2,1)S(1)}, bf16[256,1024]{1,0:T(8,12...) custom-call(s32[8]{0:T(128)S(1)} %stack.149.starts, ...), custom_call_target="tpu_custom_call" | custom-call | flops 2147483648 | bytes 8388608 | tf_op jit(solution)/shard_map/pallas_call | solution.py:76
  7.2 0.5 collective-permute-start.3
  7.8 0.4 collective-permute-start
  8.4 0.7 collective-permute-done.5
  9.3 3.4 %collective-permute-start.6 = (bf16[256,1024]{1,0:T(8,128)(2,1)S(1)}, bf16[256,1024]{1,0:T(8,128)(2,1)}, u32[]{:S(2)}, u32[]{:S(2)}) collective-permute-start(bf16[256,1024]{1,0:T(8,128)(2,1)S(1)} %add_convert_fusion), channel_id=1, source_target_pairs={{0,4},{1,5},{2,6},{3,7},{4,0},{5,1},{6,2},{7,3},{8,12},{9,13},{10,... | collective-permute-start | bytes 1572872 | tf_op jit(solution)/shard_map/ppermute | solution.py:30
  12.9 0.7 collective-permute-start.4
  13.6 1.0 add_convert_fusion.2
  14.6 2.6 %collective-permute-start.2 = (bf16[256,1024]{1,0:T(8,128)(2,1)}, bf16[256,1024]{1,0:T(8,128)(2,1)}, u32[]{:S(2)}, u32[]{:S(2)}) collective-permute-start(bf16[256,1024]{1,0:T(8,128)(2,1)} %add_convert_fusion.2), channel_id=1, source_target_pairs={{0,6},{1,7},{2,0},{3,1},{4,2},{5,3},{6,4},{7,5},{8,14},{9,15},{10,... | collective-permute-start | bytes 1572872 | tf_op jit(solution)/shard_map/ppermute | solution.py:30
  17.6 1.0 pad_maximum_fusion.3
  18.6 7.9 %all-to-all-start = ((bf16[16,24,1024]{2,1,0:T(8,128)(2,1)}), bf16[16,24,1024]{2,1,0:T(8,128)(2,1)S(1)}, u32[]{:S(2)}, u32[]{:S(2)}) async-start(bf16[16,24,1024]{2,1,0:T(8,128)(2,1)} %bitcast.15), calls=%async_computation | async-start | bytes 1572864 | tf_op jit(solution)/shard_map/all_to_all | solution.py:157
  26.5 9.7 %collective-permute-done.4 = bf16[256,1024]{1,0:T(8,128)(2,1)} collective-permute-done((bf16[256,1024]{1,0:T(8,128)(2,1)S(1)}, bf16[256,1024]{1,0:T(8,128)(2,1)}, u32[]{:S(2)}, u32[]{:S(2)}) %collective-permute-start.4) | collective-permute-done | bytes 524320 | tf_op jit(solution)/shard_map/ppermute | solution.py:30
  36.2 0.4 collective-permute-done.2
  36.7 2.2 %multiply_reduce_fusion = (f32[256]{0:T(256)S(1)}, bf16[256,1024]{1,0:T(8,128)(2,1)S(1)}) fusion(bf16[256,1024]{1,0:T(8,128)(2,1)} %collective-permute-done.6, bf16[256,1024]{1,0:T(8,128)(2,1)} %collective-permute-done.4, bf16[256,1024]{1,0:T(8,128)(2,1)} %collective-permute-done.2, bf16[256,1024]{1,0:T(8,128)(2,1)} %collective-permute-done, ...), kind=kLoop, calls=%fused_computation.12 | loop fusion | flops 4194048 | bytes 3676160 | tf_op jit(solution)/shard_map/reduce_sum | solution.py:163
  39.2 1.1 all-to-all-done
  40.3 5.0 %shard_map.140 = (bf16[128,1024]{1,0:T(8,128)(2,1)S(1)}, bf16[128,1024]{1,0:T(8,128)(2,1)S(1)}, bf16[128,1024]{1,0:T(8,128)(2,1)S(1)}, bf16[128,1024]{1,0:T(8,12...) custom-call(s32[4]{0:T(128)S(1)} %pad_add_fusion.starts, ...), custom_call_target="tpu_custom_call" | custom-call | flops 2147483648 | bytes 8388608 | tf_op jit(solution)/shard_map/pallas_call | solution.py:76
  45.4 0.6 collective-permute-start.10
  46.6 0.5 collective-permute-done.10
  48.3 0.5 convolution_convert_fusion
  48.9 0.5 collective-permute-start.16
  49.3 1.8 %collective-permute-start.14 = (bf16[136,1024]{1,0:T(8,128)(2,1)S(1)}, bf16[136,1024]{1,0:T(8,128)(2,1)S(1)}, u32[]{:S(2)}, u32[]{:S(2)}) collective-permute-start(bf16[136,1024]{1,0:T(8,128)(2,1)S(1)} %get-tuple-element.60), channel_id=1, source_target_pairs={{0,4},{1,5},{2,6},{3,7},{4,0},{5,1},{6,2},{7,3},{8,12},{9,13},{10,... | collective-permute-start | bytes 835592 | tf_op jit(solution)/shard_map/ppermute | solution.py:30
  51.1 0.7 collective-permute-start.12
  51.8 2.5 %collective-permute-start.13 = (bf16[136,1024]{1,0:T(8,128)(2,1)S(1)}, bf16[136,1024]{1,0:T(8,128)(2,1)S(1)}, u32[]{:S(2)}, u32[]{:S(2)}) collective-permute-start(bf16[136,1024]{1,0:T(8,128)(2,1)S(1)} %get-tuple-element.59), channel_id=1, source_target_pairs={{0,6},{1,7},{2,0},{3,1},{4,2},{5,3},{6,4},{7,5},{8,14},{9,15},{10,... | collective-permute-start | bytes 835592 | tf_op jit(solution)/shard_map/ppermute | solution.py:30
  54.4 4.1 %collective-permute-start.21 = (bf16[256,1024]{1,0:T(8,128)(2,1)S(1)}, bf16[256,1024]{1,0:T(8,128)(2,1)S(1)}, u32[]{:S(2)}, u32[]{:S(2)}) collective-permute-start(bf16[256,1024]{1,0:T(8,128)(2,1)S(1)} %maximum_select_fusion.rows), channel_id=1, source_target_pairs={{0,24},{1,25},{2,26},{3,27},{4,28},{5,29},{6,30},{7,31},{8,0},{9,1... | collective-permute-start | bytes 1572872 | tf_op jit(solution)/shard_map/ppermute | solution.py:30
  58.5 2.0 %collective-permute-done.14 = bf16[136,1024]{1,0:T(8,128)(2,1)S(1)} collective-permute-done((bf16[136,1024]{1,0:T(8,128)(2,1)S(1)}, bf16[136,1024]{1,0:T(8,128)(2,1)S(1)}, u32[]{:S(2)}, u32[]{:S(2)}) %collective-permute-start.14) | collective-permute-done | bytes 278560 | tf_op jit(solution)/shard_map/ppermute | solution.py:30
  60.5 5.1 %collective-permute-done.12 = bf16[136,1024]{1,0:T(8,128)(2,1)S(1)} collective-permute-done((bf16[136,1024]{1,0:T(8,128)(2,1)S(1)}, bf16[136,1024]{1,0:T(8,128)(2,1)S(1)}, u32[]{:S(2)}, u32[]{:S(2)}) %collective-permute-start.12) | collective-permute-done | bytes 278560 | tf_op jit(solution)/shard_map/ppermute | solution.py:30
  65.7 0.6 fusion.35
  66.3 0.9 collective-permute-start.20
  67.2 3.6 %collective-permute-start.19 = (bf16[128,256]{1,0:T(8,128)(2,1)S(1)}, bf16[128,256]{1,0:T(8,128)(2,1)S(1)}, u32[]{:S(2)}, u32[]{:S(2)}) collective-permute-start(bf16[128,256]{1,0:T(8,128)(2,1)S(1)} %get-tuple-element.87), channel_id=1, source_target_pairs={{0,16},{1,17},{2,18},{3,19},{4,20},{5,21},{6,22},{7,23},{8,24},{9,... | collective-permute-start | bytes 196616 | tf_op jit(solution)/shard_map/ppermute | solution.py:30
  70.7 1.0 collective-permute-start.18
  71.8 3.6 %collective-permute-done.20 = bf16[128,256]{1,0:T(8,128)(2,1)S(1)} collective-permute-done((bf16[128,256]{1,0:T(8,128)(2,1)S(1)}, bf16[128,256]{1,0:T(8,128)(2,1)S(1)}, u32[]{:S(2)}, u32[]{:S(2)}) %collective-permute-start.20) | collective-permute-done | bytes 65568 | tf_op jit(solution)/shard_map/ppermute | solution.py:30
  75.4 1.3 collective-permute-start.26
  76.8 2.7 %collective-permute-start.23 = (bf16[4,128,256]{2,1,0:T(8,128)(2,1)S(1)}, bf16[4,128,256]{2,1,0:T(8,128)(2,1)}, u32[]{:S(2)}, u32[]{:S(2)}) collective-permute-start(bf16[4,128,256]{2,1,0:T(8,128)(2,1)S(1)} %pad_maximum_fusion.11), channel_id=1, source_target_pairs={{0,6},{1,7},{2,0},{3,1},{4,2},{5,3},{6,4},{7,5},{8,14},{9,15},{10,... | collective-permute-start | bytes 786440 | tf_op jit(solution)/shard_map/ppermute | solution.py:30
  79.5 0.8 collective-permute-start.24
  80.4 1.1 convolution_convert_fusion.1
  81.6 5.9 %all-to-all-start.1 = ((bf16[16,24,512]{2,1,0:T(8,128)(2,1)}), bf16[16,24,512]{2,1,0:T(8,128)(2,1)S(1)}, u32[]{:S(2)}, u32[]{:S(2)}) async-start(bf16[16,24,512]{2,1,0:T(8,128)(2,1)} %bitcast.92), calls=%async_computation.1 | async-start | bytes 786432 | tf_op jit(solution)/shard_map/all_to_all | solution.py:219
  87.4 3.9 %collective-permute-done.23 = bf16[4,128,256]{2,1,0:T(8,128)(2,1)} collective-permute-done((bf16[4,128,256]{2,1,0:T(8,128)(2,1)S(1)}, bf16[4,128,256]{2,1,0:T(8,128)(2,1)}, u32[]{:S(2)}, u32[]{:S(2)}) %collective-permute-start.23) | collective-permute-done | bytes 262176 | tf_op jit(solution)/shard_map/ppermute | solution.py:30
  91.3 3.8 %collective-permute-done.25 = bf16[4,128,256]{2,1,0:T(8,128)(2,1)} collective-permute-done((bf16[4,128,256]{2,1,0:T(8,128)(2,1)S(1)}, bf16[4,128,256]{2,1,0:T(8,128)(2,1)}, u32[]{:S(2)}, u32[]{:S(2)}) %collective-permute-start.25) | collective-permute-done | bytes 262176 | tf_op jit(solution)/shard_map/ppermute | solution.py:30
  95.2 0.6 collective-permute-start.29
  95.9 1.5 %pad_maximum_fusion = bf16[1024,1024]{1,0:T(8,128)(2,1)S(1)} fusion(bf16[256,1024]{1,0:T(8,128)(2,1)} %copy-done.8, bf16[256,1024]{1,0:T(8,128)(2,1)} %copy-done.9, bf16[256,1024]{1,0:T(8,128)(2,1)} %copy-done.7, bf16[256,1024]{1,0:T(8,128)(2,1)S(1)} %maximum_select_fusion.rows), kind=kLoop, calls=%fused_computation | loop fusion | flops 8388608 | bytes 4194304 | tf_op jit(solution)/shard_map/concatenate | solution.py:212
  97.5 1.0 pad_maximum_fusion.7
  98.5 1.0 pad_maximum_fusion.6
  99.6 1.0 pad_maximum_fusion.5
  100.9 0.5 convolution_convert_fusion.5
  101.4 0.5 convolution_convert_fusion.2
  101.9 1.6 %collective-permute-start.31 = (bf16[512,256]{1,0:T(8,128)(2,1)S(1)}, bf16[512,256]{1,0:T(8,128)(2,1)S(1)}, u32[]{:S(2)}, u32[]{:S(2)}) collective-permute-start(bf16[512,256]{1,0:T(8,128)(2,1)S(1)} %convolution_convert_fusion.5), channel_id=1, source_target_pairs={{0,32},{1,33},{2,34},{3,35},{4,36},{5,37},{6,38},{7,39},{8,40},{9,... | collective-permute-start | bytes 786440 | tf_op jit(solution)/shard_map/ppermute | solution.py:30
  103.5 1.7 %collective-permute-start.35 = (bf16[512,256]{1,0:T(8,128)(2,1)S(1)}, bf16[512,256]{1,0:T(8,128)(2,1)S(1)}, u32[]{:S(2)}, u32[]{:S(2)}) collective-permute-start(bf16[512,256]{1,0:T(8,128)(2,1)S(1)} %convolution_convert_fusion.2), channel_id=1, source_target_pairs={{0,96},{1,97},{2,98},{3,99},{4,100},{5,101},{6,102},{7,103},{8,104... | collective-permute-start | bytes 786440 | tf_op jit(solution)/shard_map/ppermute | solution.py:30
  105.2 1.3 fusion.17
  106.5 1.2 convolution_convert_fusion.3
  108.0 1.2 convolution_convert_fusion.4
  109.2 2.9 %collective-permute-start.32 = (bf16[512,256]{1,0:T(8,128)(2,1)}, bf16[512,256]{1,0:T(8,128)(2,1)}, u32[]{:S(2)}, u32[]{:S(2)}) collective-permute-start(bf16[512,256]{1,0:T(8,128)(2,1)} %convolution_convert_fusion.4), channel_id=1, source_target_pairs={{0,96},{1,97},{2,98},{3,99},{4,100},{5,101},{6,102},{7,103},{8,104... | collective-permute-start | bytes 786440 | tf_op jit(solution)/shard_map/ppermute | solution.py:30
  112.2 1.3 fusion.22
  113.4 1.2 add_convert_fusion.3
  114.7 0.7 copy-done.16
  115.4 0.6 slice.131
  116.6 1.5 %collective-permute-start.36 = (bf16[512,256]{1,0:T(8,128)(2,1)}, bf16[512,256]{1,0:T(8,128)(2,1)}, u32[]{:S(2)}, u32[]{:S(2)}) collective-permute-start(bf16[512,256]{1,0:T(8,128)(2,1)} %add_convert_fusion.3), channel_id=1, source_target_pairs={{0,96},{1,97},{2,98},{3,99},{4,100},{5,101},{6,102},{7,103},{8,104... | collective-permute-start | bytes 786440 | tf_op jit(solution)/shard_map/ppermute | solution.py:30
  118.1 2.3 %add_convert_fusion.4 = bf16[512,256]{1,0:T(8,128)(2,1)} fusion(bf16[512,256]{1,0:T(8,128)(2,1)} %copy-done.16, bf16[4,1024,256]{2,1,0:T(8,128)(2,1)} %copy-done.1, s32[]{:T(128)S(6)} %select_n.126, bf16[1024,1024]{1,0:T(8,128)(2,1)S(1)} %pad_maximum_fusion), kind=kOutput, calls=%fused_computation.78 | convolution fusion | flops 268828672 | bytes 2097156 | tf_op jit(solution)/shard_map/dot_general | solution.py:225
  120.4 0.6 collective-permute-start.33
  121.2 1.4 %fusion.12 = (bf16[384,512]{1,0:T(8,128)(2,1)}, bf16[384,512]{1,0:T(8,128)(2,1)}) fusion(f32[16,24,512]{2,1,0:T(8,128)S(1)} %convert_add_fusion.1, bf16[384,512]{1,0:T(8,128)(2,1)S(1)} %copy-done.2, bf16[384,512]{1,0:T(8,128)(2,1)S(1)} %copy-done.4, f32[512]{0:T(512)S(1)} %copy-done.10, f32[512]{0:T(512)S(1)} %copy-done.11, f32[512]{0:T(512)S(1)} %copy-done.12), kind=kLoop, calls=%fused_computation.31 | loop fusion | flops 3735552 | bytes 2365440 | tf_op jit(solution)/shard_map/convert_element_type | solution.py:237
  122.6 2.1 %collective-permute-done.36 = bf16[512,256]{1,0:T(8,128)(2,1)} collective-permute-done((bf16[512,256]{1,0:T(8,128)(2,1)}, bf16[512,256]{1,0:T(8,128)(2,1)}, u32[]{:S(2)}, u32[]{:S(2)}) %collective-permute-start.36) | collective-permute-done | bytes 262176 | tf_op jit(solution)/shard_map/ppermute | solution.py:30
  124.6 1.1 convert_add_fusion.2
  125.7 3.5 %collective-permute-done.33 = bf16[512,256]{1,0:T(8,128)(2,1)S(1)} collective-permute-done((bf16[512,256]{1,0:T(8,128)(2,1)}, bf16[512,256]{1,0:T(8,128)(2,1)S(1)}, u32[]{:S(2)}, u32[]{:S(2)}) %collective-permute-start.33) | collective-permute-done | bytes 262176 | tf_op jit(solution)/shard_map/ppermute | solution.py:30
  129.2 1.0 convert_add_fusion.3
  130.2 1.0 pad_maximum_fusion.2
  (113 shorter events, 4.9 us)
Async XLA Ops:
  0.7 1.0 copy-start
  1.7 6.5 %copy-start.10 = (f32[512]{0:T(512)S(1)}, f32[512]{0:T(512)}, u32[]{:S(2)}) copy-start(f32[512]{0:T(512)} %param.20) | copy-start | bytes 6148
  1.7 6.5 %copy-start.11 = (f32[512]{0:T(512)S(1)}, f32[512]{0:T(512)}, u32[]{:S(2)}) copy-start(f32[512]{0:T(512)} %param.19) | copy-start | bytes 6148
  1.7 6.5 %copy-start.12 = (f32[512]{0:T(512)S(1)}, f32[512]{0:T(512)}, u32[]{:S(2)}) copy-start(f32[512]{0:T(512)} %param.18) | copy-start | bytes 6148
  7.1 2.0 %collective-permute-start.5 = (bf16[256,1024]{1,0:T(8,128)(2,1)S(1)}, bf16[256,1024]{1,0:T(8,128)(2,1)S(1)}, u32[]{:S(2)}, u32[]{:S(2)}) collective-permute-start(bf16[256,1024]{1,0:T(8,128)(2,1)S(1)} %get-tuple-element.45), channel_id=1, source_target_pairs={{0,1},{1,0},{2,3},{3,2},{4,5},{5,4},{6,7},{7,6},{8,9},{9,8},{10,11... | collective-permute-start | bytes 1572872 | tf_op jit(solution)/shard_map/ppermute | solution.py:30
  7.2 5.5 %collective-permute-start.3 = (bf16[256,1024]{1,0:T(8,128)(2,1)S(1)}, bf16[256,1024]{1,0:T(8,128)(2,1)S(1)}, u32[]{:S(2)}, u32[]{:S(2)}) collective-permute-start(bf16[256,1024]{1,0:T(8,128)(2,1)S(1)} %get-tuple-element.43), channel_id=1, source_target_pairs={{0,1},{1,0},{2,3},{3,2},{4,5},{5,4},{6,7},{7,6},{8,9},{9,8},{10,11... | collective-permute-start | bytes 1572872 | tf_op jit(solution)/shard_map/ppermute | solution.py:30
  7.7 6.0 %collective-permute-start.1 = (bf16[256,1024]{1,0:T(8,128)(2,1)S(1)}, bf16[256,1024]{1,0:T(8,128)(2,1)S(1)}, u32[]{:S(2)}, u32[]{:S(2)}) collective-permute-start(bf16[256,1024]{1,0:T(8,128)(2,1)S(1)} %get-tuple-element.41), channel_id=1, source_target_pairs={{0,1},{1,0},{2,3},{3,2},{4,5},{5,4},{6,7},{7,6},{8,9},{9,8},{10,11... | collective-permute-start | bytes 1572872 | tf_op jit(solution)/shard_map/ppermute | solution.py:30
  7.8 18.7 %collective-permute-start = (bf16[256,1024]{1,0:T(8,128)(2,1)S(1)}, bf16[256,1024]{1,0:T(8,128)(2,1)}, u32[]{:S(2)}, u32[]{:S(2)}) collective-permute-start(bf16[256,1024]{1,0:T(8,128)(2,1)S(1)} %get-tuple-element.39), channel_id=1, source_target_pairs={{0,1},{1,0},{2,3},{3,2},{4,5},{5,4},{6,7},{7,6},{8,9},{9,8},{10,11... | collective-permute-start | bytes 1572872 | tf_op jit(solution)/shard_map/ppermute | solution.py:30
  8.2 37.2 %collective-permute-start.17 = (f32[3,512]{1,0:T(4,128)S(1)}, f32[3,512]{1,0:T(4,128)S(1)}, u32[]{:S(2)}, u32[]{:S(2)}) collective-permute-start(f32[3,512]{1,0:T(4,128)S(1)} %pad_maximum_fusion.12), channel_id=1, source_target_pairs={{0,1},{1,0},{2,3},{3,2},{4,5},{5,4},{6,7},{7,6},{8,9},{9,8},{10,11... | collective-permute-start | bytes 18440 | tf_op jit(solution)/shard_map/ppermute | solution.py:30
  9.1 8.1 %copy-start.14 = (s32[256,1]{0,1:T(1,128)S(1)}, s32[256,1]{0,1:T(1,128)}, u32[]{:S(2)}) copy-start(s32[256,1]{0,1:T(1,128)} %param.21) | copy-start | bytes 3076
  9.3 8.2 %copy-start.15 = (s32[256]{0:T(256)S(1)}, s32[256]{0:T(256)}, u32[]{:S(2)}) copy-start(s32[256]{0:T(256)} %param.22) | copy-start | bytes 3076
  9.3 8.3 %copy-start.2 = (bf16[384,512]{1,0:T(8,128)(2,1)S(1)}, bf16[384,512]{1,0:T(8,128)(2,1)}, u32[]{:S(2)}) copy-start(bf16[384,512]{1,0:T(8,128)(2,1)} %param.23) | copy-start | bytes 1179652
  9.3 8.3 %copy-start.3 = (bf16[384,512]{1,0:T(8,128)(2,1)S(1)}, bf16[384,512]{1,0:T(8,128)(2,1)}, u32[]{:S(2)}) copy-start(bf16[384,512]{1,0:T(8,128)(2,1)} %param.17) | copy-start | bytes 1179652
  9.3 17.2 %collective-permute-start.6 = (bf16[256,1024]{1,0:T(8,128)(2,1)S(1)}, bf16[256,1024]{1,0:T(8,128)(2,1)}, u32[]{:S(2)}, u32[]{:S(2)}) collective-permute-start(bf16[256,1024]{1,0:T(8,128)(2,1)S(1)} %add_convert_fusion), channel_id=1, source_target_pairs={{0,4},{1,5},{2,6},{3,7},{4,0},{5,1},{6,2},{7,3},{8,12},{9,13},{10,... | collective-permute-start | bytes 1572872 | tf_op jit(solution)/shard_map/ppermute | solution.py:30
  12.9 23.4 %collective-permute-start.4 = (bf16[256,1024]{1,0:T(8,128)(2,1)S(1)}, bf16[256,1024]{1,0:T(8,128)(2,1)}, u32[]{:S(2)}, u32[]{:S(2)}) collective-permute-start(bf16[256,1024]{1,0:T(8,128)(2,1)S(1)} %add_convert_fusion.1), channel_id=1, source_target_pairs={{0,2},{1,3},{2,4},{3,5},{4,6},{5,7},{6,0},{7,1},{8,10},{9,11},{10,... | collective-permute-start | bytes 1572872 | tf_op jit(solution)/shard_map/ppermute | solution.py:30
  14.6 22.1 %copy-start.13 = (f32[1024]{0:T(1024)S(1)}, f32[1024]{0:T(1024)}, u32[]{:S(2)}) copy-start(f32[1024]{0:T(1024)} %param.15) | copy-start | bytes 12292
  14.6 22.0 %collective-permute-start.2 = (bf16[256,1024]{1,0:T(8,128)(2,1)}, bf16[256,1024]{1,0:T(8,128)(2,1)}, u32[]{:S(2)}, u32[]{:S(2)}) collective-permute-start(bf16[256,1024]{1,0:T(8,128)(2,1)} %add_convert_fusion.2), channel_id=1, source_target_pairs={{0,6},{1,7},{2,0},{3,1},{4,2},{5,3},{6,4},{7,5},{8,14},{9,15},{10,... | collective-permute-start | bytes 1572872 | tf_op jit(solution)/shard_map/ppermute | solution.py:30
  18.6 21.6 %all-to-all-start = ((bf16[16,24,1024]{2,1,0:T(8,128)(2,1)}), bf16[16,24,1024]{2,1,0:T(8,128)(2,1)S(1)}, u32[]{:S(2)}, u32[]{:S(2)}) async-start(bf16[16,24,1024]{2,1,0:T(8,128)(2,1)} %bitcast.15), calls=%async_computation | async-start | bytes 1572864 | tf_op jit(solution)/shard_map/all_to_all | solution.py:157
  45.3 1.3 collective-permute-start.8
  45.4 1.7 %collective-permute-start.10 = (bf16[128,1024]{1,0:T(8,128)(2,1)S(1)}, bf16[128,1024]{1,0:T(8,128)(2,1)S(1)}, u32[]{:S(2)}, u32[]{:S(2)}) collective-permute-start(bf16[128,1024]{1,0:T(8,128)(2,1)S(1)} %get-tuple-element.55), channel_id=1, source_target_pairs={{0,1},{1,0},{2,3},{3,2},{4,5},{5,4},{6,7},{7,6},{8,9},{9,8},{10,11... | collective-permute-start | bytes 786440 | tf_op jit(solution)/shard_map/ppermute | solution.py:30
  46.0 1.5 %collective-permute-start.9 = (bf16[128,1024]{1,0:T(8,128)(2,1)S(1)}, bf16[128,1024]{1,0:T(8,128)(2,1)S(1)}, u32[]{:S(2)}, u32[]{:S(2)}) collective-permute-start(bf16[128,1024]{1,0:T(8,128)(2,1)S(1)} %get-tuple-element.53), channel_id=1, source_target_pairs={{0,1},{1,0},{2,3},{3,2},{4,5},{5,4},{6,7},{7,6},{8,9},{9,8},{10,11... | collective-permute-start | bytes 786440 | tf_op jit(solution)/shard_map/ppermute | solution.py:30
  46.1 1.8 %collective-permute-start.7 = (bf16[128,1024]{1,0:T(8,128)(2,1)S(1)}, bf16[128,1024]{1,0:T(8,128)(2,1)S(1)}, u32[]{:S(2)}, u32[]{:S(2)}) collective-permute-start(bf16[128,1024]{1,0:T(8,128)(2,1)S(1)} %get-tuple-element.49), channel_id=1, source_target_pairs={{0,1},{1,0},{2,3},{3,2},{4,5},{5,4},{6,7},{7,6},{8,9},{9,8},{10,11... | collective-permute-start | bytes 786440 | tf_op jit(solution)/shard_map/ppermute | solution.py:30
  46.5 1.8 %collective-permute-start.11 = (bf16[128,1024]{1,0:T(8,128)(2,1)S(1)}, bf16[128,1024]{1,0:T(8,128)(2,1)S(1)}, u32[]{:S(2)}, u32[]{:S(2)}) collective-permute-start(bf16[128,1024]{1,0:T(8,128)(2,1)S(1)} %get-tuple-element.56), channel_id=1, source_target_pairs={{0,1},{1,0},{2,3},{3,2},{4,5},{5,4},{6,7},{7,6},{8,9},{9,8},{10,11... | collective-permute-start | bytes 786440 | tf_op jit(solution)/shard_map/ppermute | solution.py:30
  48.9 9.6 %collective-permute-start.16 = (bf16[128,1024]{1,0:T(8,128)(2,1)S(1)}, bf16[128,1024]{1,0:T(8,128)(2,1)S(1)}, u32[]{:S(2)}, u32[]{:S(2)}) collective-permute-start(bf16[128,1024]{1,0:T(8,128)(2,1)S(1)} %get-tuple-element.82), channel_id=1, source_target_pairs={{0,1},{1,0},{2,3},{3,2},{4,5},{5,4},{6,7},{7,6},{8,9},{9,8},{10,11... | collective-permute-start | bytes 786440 | tf_op jit(solution)/shard_map/ppermute | solution.py:30
  49.3 11.1 %collective-permute-start.14 = (bf16[136,1024]{1,0:T(8,128)(2,1)S(1)}, bf16[136,1024]{1,0:T(8,128)(2,1)S(1)}, u32[]{:S(2)}, u32[]{:S(2)}) collective-permute-start(bf16[136,1024]{1,0:T(8,128)(2,1)S(1)} %get-tuple-element.60), channel_id=1, source_target_pairs={{0,4},{1,5},{2,6},{3,7},{4,0},{5,1},{6,2},{7,3},{8,12},{9,13},{10,... | collective-permute-start | bytes 835592 | tf_op jit(solution)/shard_map/ppermute | solution.py:30
  51.1 14.5 %collective-permute-start.12 = (bf16[136,1024]{1,0:T(8,128)(2,1)S(1)}, bf16[136,1024]{1,0:T(8,128)(2,1)S(1)}, u32[]{:S(2)}, u32[]{:S(2)}) collective-permute-start(bf16[136,1024]{1,0:T(8,128)(2,1)S(1)} %get-tuple-element.58), channel_id=1, source_target_pairs={{0,2},{1,3},{2,4},{3,5},{4,6},{5,7},{6,0},{7,1},{8,10},{9,11},{10,... | collective-permute-start | bytes 835592 | tf_op jit(solution)/shard_map/ppermute | solution.py:30
  51.8 13.8 %collective-permute-start.13 = (bf16[136,1024]{1,0:T(8,128)(2,1)S(1)}, bf16[136,1024]{1,0:T(8,128)(2,1)S(1)}, u32[]{:S(2)}, u32[]{:S(2)}) collective-permute-start(bf16[136,1024]{1,0:T(8,128)(2,1)S(1)} %get-tuple-element.59), channel_id=1, source_target_pairs={{0,6},{1,7},{2,0},{3,1},{4,2},{5,3},{6,4},{7,5},{8,14},{9,15},{10,... | collective-permute-start | bytes 835592 | tf_op jit(solution)/shard_map/ppermute | solution.py:30
  54.4 21.0 %collective-permute-start.21 = (bf16[256,1024]{1,0:T(8,128)(2,1)S(1)}, bf16[256,1024]{1,0:T(8,128)(2,1)S(1)}, u32[]{:S(2)}, u32[]{:S(2)}) collective-permute-start(bf16[256,1024]{1,0:T(8,128)(2,1)S(1)} %maximum_select_fusion.rows), channel_id=1, source_target_pairs={{0,24},{1,25},{2,26},{3,27},{4,28},{5,29},{6,30},{7,31},{8,0},{9,1... | collective-permute-start | bytes 1572872 | tf_op jit(solution)/shard_map/ppermute | solution.py:30
  58.5 16.9 %collective-permute-start.22 = (bf16[256,1024]{1,0:T(8,128)(2,1)S(1)}, bf16[256,1024]{1,0:T(8,128)(2,1)S(1)}, u32[]{:S(2)}, u32[]{:S(2)}) collective-permute-start(bf16[256,1024]{1,0:T(8,128)(2,1)S(1)} %maximum_select_fusion.rows), channel_id=1, source_target_pairs={{0,8},{1,9},{2,10},{3,11},{4,12},{5,13},{6,14},{7,15},{8,16},{9,17... | collective-permute-start | bytes 1572872 | tf_op jit(solution)/shard_map/ppermute | solution.py:30
  66.3 9.1 %collective-permute-start.20 = (bf16[128,256]{1,0:T(8,128)(2,1)S(1)}, bf16[128,256]{1,0:T(8,128)(2,1)S(1)}, u32[]{:S(2)}, u32[]{:S(2)}) collective-permute-start(bf16[128,256]{1,0:T(8,128)(2,1)S(1)} %get-tuple-element.86), channel_id=1, source_target_pairs={{0,8},{1,9},{2,10},{3,11},{4,12},{5,13},{6,14},{7,15},{8,16},{9,17... | collective-permute-start | bytes 196616 | tf_op jit(solution)/shard_map/ppermute | solution.py:30
  67.2 8.2 %collective-permute-start.19 = (bf16[128,256]{1,0:T(8,128)(2,1)S(1)}, bf16[128,256]{1,0:T(8,128)(2,1)S(1)}, u32[]{:S(2)}, u32[]{:S(2)}) collective-permute-start(bf16[128,256]{1,0:T(8,128)(2,1)S(1)} %get-tuple-element.87), channel_id=1, source_target_pairs={{0,16},{1,17},{2,18},{3,19},{4,20},{5,21},{6,22},{7,23},{8,24},{9,... | collective-permute-start | bytes 196616 | tf_op jit(solution)/shard_map/ppermute | solution.py:30
  70.7 4.6 %collective-permute-start.18 = (bf16[128,256]{1,0:T(8,128)(2,1)S(1)}, bf16[128,256]{1,0:T(8,128)(2,1)S(1)}, u32[]{:S(2)}, u32[]{:S(2)}) collective-permute-start(bf16[128,256]{1,0:T(8,128)(2,1)S(1)} %get-tuple-element.88), channel_id=1, source_target_pairs={{0,24},{1,25},{2,26},{3,27},{4,28},{5,29},{6,30},{7,31},{8,0},{9,1... | collective-permute-start | bytes 196616 | tf_op jit(solution)/shard_map/ppermute | solution.py:30
  75.4 20.4 %copy-start.7 = (bf16[256,1024]{1,0:T(8,128)(2,1)}, bf16[256,1024]{1,0:T(8,128)(2,1)S(1)}, u32[]{:S(2)}) copy-start(bf16[256,1024]{1,0:T(8,128)(2,1)S(1)} %collective-permute-done.21) | copy-start | bytes 1572868
  75.4 20.4 %copy-start.8 = (bf16[256,1024]{1,0:T(8,128)(2,1)}, bf16[256,1024]{1,0:T(8,128)(2,1)S(1)}, u32[]{:S(2)}) copy-start(bf16[256,1024]{1,0:T(8,128)(2,1)S(1)} %collective-permute-done.22) | copy-start | bytes 1572868
  75.4 19.7 %collective-permute-start.26 = (bf16[256,1024]{1,0:T(8,128)(2,1)S(1)}, bf16[256,1024]{1,0:T(8,128)(2,1)S(1)}, u32[]{:S(2)}, u32[]{:S(2)}) collective-permute-start(bf16[256,1024]{1,0:T(8,128)(2,1)S(1)} %maximum_select_fusion.rows), channel_id=1, source_target_pairs={{0,16},{1,17},{2,18},{3,19},{4,20},{5,21},{6,22},{7,23},{8,24},{9,... | collective-permute-start | bytes 1572872 | tf_op jit(solution)/shard_map/ppermute | solution.py:30
  76.7 3.7 %collective-permute-start.15 = (bf16[128,512]{1,0:T(8,128)(2,1)S(1)}, bf16[128,512]{1,0:T(8,128)(2,1)S(1)}, u32[]{:S(2)}, u32[]{:S(2)}) collective-permute-start(bf16[128,512]{1,0:T(8,128)(2,1)S(1)} %get-tuple-element.90), channel_id=1, source_target_pairs={{0,1},{1,0},{2,3},{3,2},{4,5},{5,4},{6,7},{7,6},{8,9},{9,8},{10,11... | collective-permute-start | bytes 393224 | tf_op jit(solution)/shard_map/ppermute | solution.py:30
  76.8 14.5 %collective-permute-start.23 = (bf16[4,128,256]{2,1,0:T(8,128)(2,1)S(1)}, bf16[4,128,256]{2,1,0:T(8,128)(2,1)}, u32[]{:S(2)}, u32[]{:S(2)}) collective-permute-start(bf16[4,128,256]{2,1,0:T(8,128)(2,1)S(1)} %pad_maximum_fusion.11), channel_id=1, source_target_pairs={{0,6},{1,7},{2,0},{3,1},{4,2},{5,3},{6,4},{7,5},{8,14},{9,15},{10,... | collective-permute-start | bytes 786440 | tf_op jit(solution)/shard_map/ppermute | solution.py:30
  79.5 11.8 %collective-permute-start.24 = (bf16[4,128,256]{2,1,0:T(8,128)(2,1)S(1)}, bf16[4,128,256]{2,1,0:T(8,128)(2,1)}, u32[]{:S(2)}, u32[]{:S(2)}) collective-permute-start(bf16[4,128,256]{2,1,0:T(8,128)(2,1)S(1)} %pad_maximum_fusion.11), channel_id=1, source_target_pairs={{0,4},{1,5},{2,6},{3,7},{4,0},{5,1},{6,2},{7,3},{8,12},{9,13},{10,... | collective-permute-start | bytes 786440 | tf_op jit(solution)/shard_map/ppermute | solution.py:30
  80.3 14.8 %collective-permute-start.25 = (bf16[4,128,256]{2,1,0:T(8,128)(2,1)S(1)}, bf16[4,128,256]{2,1,0:T(8,128)(2,1)}, u32[]{:S(2)}, u32[]{:S(2)}) collective-permute-start(bf16[4,128,256]{2,1,0:T(8,128)(2,1)S(1)} %pad_maximum_fusion.11), channel_id=1, source_target_pairs={{0,2},{1,3},{2,4},{3,5},{4,6},{5,7},{6,0},{7,1},{8,10},{9,11},{10,... | collective-permute-start | bytes 786440 | tf_op jit(solution)/shard_map/ppermute | solution.py:30
  80.4 14.7 %collective-permute-start.27 = (bf16[4,128,256]{2,1,0:T(8,128)(2,1)S(1)}, bf16[4,128,256]{2,1,0:T(8,128)(2,1)S(1)}, u32[]{:S(2)}, u32[]{:S(2)}) collective-permute-start(bf16[4,128,256]{2,1,0:T(8,128)(2,1)S(1)} %pad_maximum_fusion.11), channel_id=1, source_target_pairs={{0,1},{1,0},{2,3},{3,2},{4,5},{5,4},{6,7},{7,6},{8,9},{9,8},{10,11... | collective-permute-start | bytes 786440 | tf_op jit(solution)/shard_map/ppermute | solution.py:30
  81.6 39.5 %all-to-all-start.1 = ((bf16[16,24,512]{2,1,0:T(8,128)(2,1)}), bf16[16,24,512]{2,1,0:T(8,128)(2,1)S(1)}, u32[]{:S(2)}, u32[]{:S(2)}) async-start(bf16[16,24,512]{2,1,0:T(8,128)(2,1)} %bitcast.92), calls=%async_computation.1 | async-start | bytes 786432 | tf_op jit(solution)/shard_map/all_to_all | solution.py:219
  95.1 0.8 copy-start.9
  95.1 2.4 %collective-permute-start.30 = (bf16[4,128,256]{2,1,0:T(8,128)(2,1)}, bf16[4,128,256]{2,1,0:T(8,128)(2,1)S(1)}, u32[]{:S(2)}, u32[]{:S(2)}) collective-permute-start(bf16[4,128,256]{2,1,0:T(8,128)(2,1)} %collective-permute-done.25), channel_id=1, source_target_pairs={{0,1},{1,0},{2,3},{3,2},{4,5},{5,4},{6,7},{7,6},{8,9},{9,8},{10,11... | collective-permute-start | bytes 786440 | tf_op jit(solution)/shard_map/ppermute | solution.py:30
  95.2 3.3 %collective-permute-start.29 = (bf16[4,128,256]{2,1,0:T(8,128)(2,1)}, bf16[4,128,256]{2,1,0:T(8,128)(2,1)S(1)}, u32[]{:S(2)}, u32[]{:S(2)}) collective-permute-start(bf16[4,128,256]{2,1,0:T(8,128)(2,1)} %collective-permute-done.24), channel_id=1, source_target_pairs={{0,1},{1,0},{2,3},{3,2},{4,5},{5,4},{6,7},{7,6},{8,9},{9,8},{10,11... | collective-permute-start | bytes 786440 | tf_op jit(solution)/shard_map/ppermute | solution.py:30
  95.9 3.7 %collective-permute-start.28 = (bf16[4,128,256]{2,1,0:T(8,128)(2,1)}, bf16[4,128,256]{2,1,0:T(8,128)(2,1)S(1)}, u32[]{:S(2)}, u32[]{:S(2)}) collective-permute-start(bf16[4,128,256]{2,1,0:T(8,128)(2,1)} %collective-permute-done.23), channel_id=1, source_target_pairs={{0,1},{1,0},{2,3},{3,2},{4,5},{5,4},{6,7},{7,6},{8,9},{9,8},{10,11... | collective-permute-start | bytes 786440 | tf_op jit(solution)/shard_map/ppermute | solution.py:30
  100.9 12.6 %copy-start.1 = (bf16[4,1024,256]{2,1,0:T(8,128)(2,1)}, bf16[4,1024,256]{2,1,0:T(8,128)(2,1)S(1)}, u32[]{:S(2)}) copy-start(bf16[4,1024,256]{2,1,0:T(8,128)(2,1)S(1)} %pad_maximum_fusion.1) | copy-start | bytes 6291460
  101.9 12.7 %collective-permute-start.31 = (bf16[512,256]{1,0:T(8,128)(2,1)S(1)}, bf16[512,256]{1,0:T(8,128)(2,1)S(1)}, u32[]{:S(2)}, u32[]{:S(2)}) collective-permute-start(bf16[512,256]{1,0:T(8,128)(2,1)S(1)} %convolution_convert_fusion.5), channel_id=1, source_target_pairs={{0,32},{1,33},{2,34},{3,35},{4,36},{5,37},{6,38},{7,39},{8,40},{9,... | collective-permute-start | bytes 786440 | tf_op jit(solution)/shard_map/ppermute | solution.py:30
  103.5 10.0 %collective-permute-start.35 = (bf16[512,256]{1,0:T(8,128)(2,1)S(1)}, bf16[512,256]{1,0:T(8,128)(2,1)S(1)}, u32[]{:S(2)}, u32[]{:S(2)}) collective-permute-start(bf16[512,256]{1,0:T(8,128)(2,1)S(1)} %convolution_convert_fusion.2), channel_id=1, source_target_pairs={{0,96},{1,97},{2,98},{3,99},{4,100},{5,101},{6,102},{7,103},{8,104... | collective-permute-start | bytes 786440 | tf_op jit(solution)/shard_map/ppermute | solution.py:30
  107.7 14.9 %collective-permute-start.34 = (bf16[512,256]{1,0:T(8,128)(2,1)}, bf16[512,256]{1,0:T(8,128)(2,1)}, u32[]{:S(2)}, u32[]{:S(2)}) collective-permute-start(bf16[512,256]{1,0:T(8,128)(2,1)} %convolution_convert_fusion.3), channel_id=1, source_target_pairs={{0,32},{1,33},{2,34},{3,35},{4,36},{5,37},{6,38},{7,39},{8,40},{9,... | collective-permute-start | bytes 786440 | tf_op jit(solution)/shard_map/ppermute | solution.py:30
  109.2 16.5 %collective-permute-start.32 = (bf16[512,256]{1,0:T(8,128)(2,1)}, bf16[512,256]{1,0:T(8,128)(2,1)}, u32[]{:S(2)}, u32[]{:S(2)}) collective-permute-start(bf16[512,256]{1,0:T(8,128)(2,1)} %convolution_convert_fusion.4), channel_id=1, source_target_pairs={{0,96},{1,97},{2,98},{3,99},{4,100},{5,101},{6,102},{7,103},{8,104... | collective-permute-start | bytes 786440 | tf_op jit(solution)/shard_map/ppermute | solution.py:30
  114.7 0.7 copy-start.16
  116.6 4.5 %copy-start.4 = (bf16[384,512]{1,0:T(8,128)(2,1)S(1)}, bf16[384,512]{1,0:T(8,128)(2,1)}, u32[]{:S(2)}) copy-start(bf16[384,512]{1,0:T(8,128)(2,1)} %param.17) | copy-start | bytes 1179652
  116.6 8.0 %collective-permute-start.36 = (bf16[512,256]{1,0:T(8,128)(2,1)}, bf16[512,256]{1,0:T(8,128)(2,1)}, u32[]{:S(2)}, u32[]{:S(2)}) collective-permute-start(bf16[512,256]{1,0:T(8,128)(2,1)} %add_convert_fusion.3), channel_id=1, source_target_pairs={{0,96},{1,97},{2,98},{3,99},{4,100},{5,101},{6,102},{7,103},{8,104... | collective-permute-start | bytes 786440 | tf_op jit(solution)/shard_map/ppermute | solution.py:30
  120.4 4.2 %copy-start.6 = (f32[512,256]{1,0:T(8,128)S(1)}, f32[512,256]{1,0:T(8,128)}, u32[]{:S(2)}) copy-start(f32[512,256]{1,0:T(8,128)} %fusion.17) | copy-start | bytes 1572868
  120.4 8.7 %collective-permute-start.33 = (bf16[512,256]{1,0:T(8,128)(2,1)}, bf16[512,256]{1,0:T(8,128)(2,1)S(1)}, u32[]{:S(2)}, u32[]{:S(2)}) collective-permute-start(bf16[512,256]{1,0:T(8,128)(2,1)} %add_convert_fusion.4), channel_id=1, source_target_pairs={{0,32},{1,33},{2,34},{3,35},{4,36},{5,37},{6,38},{7,39},{8,40},{9,... | collective-permute-start | bytes 786440 | tf_op jit(solution)/shard_map/ppermute | solution.py:30
  121.2 8.0 %copy-start.5 = (f32[512,256]{1,0:T(8,128)S(1)}, f32[512,256]{1,0:T(8,128)}, u32[]{:S(2)}) copy-start(f32[512,256]{1,0:T(8,128)} %fusion.22) | copy-start | bytes 1572868
